TPU v7x, 32 devices: a whole 2x2x4 slice. The times are simulated.
32 devices in a mesh: row: 4 (over y, x), seq: 8 (over z, core).
Axes of the slice: x: 2, y: 2, z: 4, core: 2. Of those that a mesh axis runs over, the one named last changes fastest.
Arguments:
- tokens: bfloat16 [8192, 768], P(('row', 'seq')), may hold values from -6 to 6
- lengths: int32 [4, 4], P('row'), may hold values from 1 to 1280, 2048 in all within a row
- w_query: bfloat16 [768, 768], replicated, may hold values from -0.21875 to 0.21875
- w_key: bfloat16 [768, 768], replicated, may hold values from -0.21875 to 0.21875
- w_value: bfloat16 [768, 768], replicated, may hold values from -0.21875 to 0.21875
- w_out: bfloat16 [768, 768], replicated, may hold values from -0.21875 to 0.21875
- w_up: bfloat16 [768, 3072], replicated, may hold values from -0.21875 to 0.21875
- w_down: bfloat16 [3072, 768], replicated, may hold values from -0.109375 to 0.109375
- gain_attend: float32 [768], replicated, may hold values from 0.5 to 1.5
- gain_inner: float32 [768], replicated, may hold values from 0.5 to 1.5
- gain_feed: float32 [768], replicated, may hold values from 0.5 to 1.5
- gain_hidden: float32 [3072], replicated, may hold values from 0.5 to 1.5
- cotangent: bfloat16 [8192, 768], P(('row', 'seq')), may hold values from -6 to 6
Outputs:
- result: bfloat16 [8192, 768], P(('row', 'seq'))
- grad_input: bfloat16 [8192, 768], P(('row', 'seq'))
- grad_query: float32 [589824], P(('row', 'seq'))
- grad_key: float32 [589824], P(('row', 'seq'))
- grad_value: float32 [589824], P(('row', 'seq'))
- grad_out: float32 [589824], P(('row', 'seq'))
- grad_up: float32 [2359296], P(('row', 'seq'))
- grad_down: float32 [2359296], P(('row', 'seq'))
- grad_gains: float32 [5376], P(('row', 'seq'))
Inputs may be any that keep to these rules, and one draw needn't show every extreme that they name: The 4 lengths of each row sum to 2048; the longest is exactly 1280.
All inputs are finite; a program needn't handle non-finite values.
Results may differ from a plain program's by a relative error of at most 0.015.
Values may be sent and summed in bfloat16 or wider, within the bound.
No kernel may reach another device: no remote copies, remote signals or barrier semaphores. Data moves between devices by JAX's collectives and lax.ppermute only.
A program may use at most 192 MiB of HBM per device.

v0:
```python
from functools import partial
from functools import reduce
import math

import jax
import jax.numpy as jnp
from jax import lax
from jax.sharding import PartitionSpec as P

HEADS = 12
SEGMENT = 2048
PATTERNS = 5


big_negative = -1e30


def shifted_2(shard, axis, by):
    length = lax.axis_size(axis)
    pairs = [(i, i + by) for i in range(length) if 0 <= i + by < length]
    return lax.ppermute(shard, axis, pairs)


def shifted_3(value, axis, steps):
    count = lax.axis_size(axis)
    pairs = [(source, (source + steps) % count) for source in range(count)]
    return lax.ppermute(value, axis, pairs)


def layer_norm(values, gain_vector):
    centre = jnp.mean(values, axis=-1, keepdims=True)
    shifted = values - centre
    variance = jnp.mean(shifted * shifted, axis=-1, keepdims=True)
    return shifted * lax.rsqrt(variance + 1e-05) * gain_vector


def hidden_norm(hidden_pre, gain_vector):
    return layer_norm(jax.nn.gelu(hidden_pre, approximate=True), gain_vector)


def selector(stride, head_count):
    return jnp.arange(stride)[:, None] == (jnp.arange(head_count) % stride)[None, :]


def compact(full_array, stride):
    length_in, head_count, inner_size = full_array.shape
    shaped = full_array.reshape(length_in // stride, stride, head_count, inner_size)
    picked = jnp.where(
        selector(stride, head_count)[None, :, :, None], shaped, jnp.zeros((), full_array.dtype)
    )
    return jnp.sum(picked, axis=1)


def expand(part_array, stride, fill_value):
    part_rows, head_count, inner_size = part_array.shape
    widened = jnp.where(
        selector(stride, head_count)[None, :, :, None],
        part_array[:, None],
        jnp.asarray(fill_value, part_array.dtype),
    )
    return widened.reshape(part_rows * stride, head_count, inner_size)


def positions(start_pos, part_rows, stride, head_count):
    row_ids = jnp.arange(part_rows, dtype=jnp.int32)[:, None] * stride
    head_ids = (jnp.arange(head_count, dtype=jnp.int32) % stride)[None, :]
    return start_pos + row_ids + head_ids


def doc_index(places, doc_bounds):
    return jnp.sum((places[..., None] >= doc_bounds).astype(jnp.int32), axis=-1)


def block_mask(doc_query, doc_key, local_block):
    allowed = doc_query.T[:, :, None] == doc_key.T[:, None, :]
    if local_block:
        rank_ids = jnp.arange(doc_query.shape[0])
        allowed = allowed & (rank_ids[:, None] >= rank_ids[None, :])[None]
    return allowed


def forward_block(query_part, key_part, value_part, allowed, score_scale):
    scores = (
        jnp.einsum("qhd,khd->hqk", query_part, key_part, preferred_element_type=jnp.float32)
        * score_scale
    )
    scores = jnp.where(allowed, scores, big_negative)
    row_peak = jnp.max(scores, axis=-1)
    weights = jnp.where(allowed, jnp.exp(scores - row_peak[..., None]), 0.0)
    row_total = jnp.sum(weights, axis=-1)
    mixed = jnp.einsum(
        "hqk,khd->qhd", weights.astype(jnp.bfloat16), value_part, preferred_element_type=jnp.float32
    )
    return (row_peak.T, row_total.T, mixed)


def merge(carried, new_block):
    best_peak = jnp.maximum(carried[0], new_block[0])
    keep_factor = jnp.exp(carried[0] - best_peak)
    take_factor = jnp.exp(new_block[0] - best_peak)
    new_total = carried[1] * keep_factor + new_block[1] * take_factor
    new_mixed = carried[2] * keep_factor[..., None] + new_block[2] * take_factor[..., None]
    return (best_peak, new_total, new_mixed)


def backward_block(
    query_part, grad_part, lse_part, delta_part, key_part, value_part, allowed, score_scale
):
    scores = (
        jnp.einsum("qhd,khd->hqk", query_part, key_part, preferred_element_type=jnp.float32)
        * score_scale
    )
    probs = jnp.where(allowed, jnp.exp(scores - lse_part.T[:, :, None]), 0.0)
    dots = jnp.einsum("qhd,khd->hqk", grad_part, value_part, preferred_element_type=jnp.float32)
    grad_scores = (probs * (dots - delta_part.T[:, :, None])).astype(jnp.bfloat16)
    query_grad = (
        jnp.einsum("hqk,khd->qhd", grad_scores, key_part, preferred_element_type=jnp.float32)
        * score_scale
    )
    key_grad = (
        jnp.einsum("hqk,qhd->khd", grad_scores, query_part, preferred_element_type=jnp.float32)
        * score_scale
    )
    value_grad = jnp.einsum(
        "hqk,qhd->khd", probs.astype(jnp.bfloat16), grad_part, preferred_element_type=jnp.float32
    )
    return (query_grad, key_grad, value_grad)


def keep_state(carried):
    return carried


def local(
    tokens,
    lengths,
    w_query,
    w_key,
    w_value,
    w_out,
    w_up,
    w_down,
    gain_attend,
    gain_inner,
    gain_feed,
    gain_hidden,
    cotangent,
):
    block_rows, model_width = tokens.shape
    head_count = HEADS
    head_size = model_width // head_count
    score_scale = head_size ** (-0.5)
    seq_devices = lax.axis_size("seq")
    all_devices = seq_devices * lax.axis_size("row")
    my_index = lax.axis_index("seq")
    seq_total = block_rows * seq_devices
    doc_bounds = jnp.cumsum(lengths[0])[:-1]
    patterns = [
        (2**pattern, min(SEGMENT * 2**pattern, seq_total) // block_rows)
        for pattern in range(PATTERNS)
    ]
    near_ids = [0, 1]
    far_ids = list(range(2, PATTERNS))
    reach = patterns[1][1]
    far_rows = [block_rows // patterns[pattern][0] for pattern in far_ids]
    far_starts = [sum(far_rows[:slot_id]) for slot_id in range(len(far_ids))]
    far_total = sum(far_rows)

    def key_docs(pattern, source):
        stride = patterns[pattern][0]
        return doc_index(
            positions(source * block_rows, block_rows // stride, stride, head_count), doc_bounds
        )

    def is_live(pattern, cycle_step):
        group_size = patterns[pattern][1]
        return (cycle_step < group_size) & (my_index % group_size >= cycle_step)

    source_x = tokens.astype(jnp.float32)
    normed, attend_back = jax.vjp(layer_norm, source_x, gain_attend)
    normed_b = normed.astype(jnp.bfloat16)
    query_b = jnp.dot(normed_b, w_query, preferred_element_type=jnp.float32).astype(jnp.bfloat16)
    key_b = jnp.dot(normed_b, w_key, preferred_element_type=jnp.float32).astype(jnp.bfloat16)
    value_b = jnp.dot(normed_b, w_value, preferred_element_type=jnp.float32).astype(jnp.bfloat16)
    query_heads = query_b.reshape(block_rows, head_count, head_size)
    key_heads = key_b.reshape(block_rows, head_count, head_size)
    value_heads = value_b.reshape(block_rows, head_count, head_size)
    query_parts = [compact(query_heads, stride) for stride, group_size in patterns]
    key_parts = [compact(key_heads, stride) for stride, group_size in patterns]
    value_parts = [compact(value_heads, stride) for stride, group_size in patterns]
    own_docs = [key_docs(pattern, my_index) for pattern in range(PATTERNS)]
    states = [
        forward_block(
            query_parts[pattern],
            key_parts[pattern],
            value_parts[pattern],
            block_mask(own_docs[pattern], own_docs[pattern], True),
            score_scale,
        )
        for pattern in range(PATTERNS)
    ]

    def unpack_near(key_block):
        key_full = key_block[:, :model_width].reshape(block_rows, head_count, head_size)
        value_full = key_block[:, model_width:].reshape(block_rows, head_count, head_size)
        return (key_full, value_full)

    def near_fold_parts(pattern, key_part, value_part, source, carried):
        new_block = forward_block(
            query_parts[pattern],
            key_part,
            value_part,
            block_mask(own_docs[pattern], key_docs(pattern, source), False),
            score_scale,
        )
        return merge(carried, new_block)

    def near_fold(pattern, key_full, value_full, source, carried):
        stride = patterns[pattern][0]
        return near_fold_parts(
            pattern, compact(key_full, stride), compact(value_full, stride), source, carried
        )

    pair_block = jnp.concatenate([key_b, value_b], axis=1)
    kept_blocks = jnp.zeros((max(reach - 1, 1), block_rows, 2 * model_width), jnp.bfloat16)

    def near_forward(cycle_step, loop_state):
        key_block, near_now, kept_store = loop_state
        key_block = shifted_2(key_block, "seq", 1)
        key_full, value_full = unpack_near(key_block)
        new_states = []
        for pattern in near_ids:
            new_states.append(
                lax.cond(
                    is_live(pattern, cycle_step),
                    partial(near_fold, pattern, key_full, value_full, my_index - cycle_step),
                    keep_state,
                    near_now[pattern],
                )
            )
        return (key_block, tuple(new_states), kept_store)

    _, near_states, kept_blocks = lax.fori_loop(
        1, reach, near_forward, (pair_block, (states[0], states[1]), kept_blocks)
    )
    far_block = jnp.concatenate(
        [
            jnp.concatenate(
                [
                    key_parts[pattern].reshape(rows_here, model_width),
                    value_parts[pattern].reshape(rows_here, model_width),
                ],
                axis=1,
            )
            for pattern, rows_here in zip(far_ids, far_rows)
        ],
        axis=0,
    )

    def unpack_far(key_block, slot_id):
        rows_here = far_rows[slot_id]
        row_begin = far_starts[slot_id]
        piece_rows = key_block[row_begin : row_begin + rows_here]
        key_part = piece_rows[:, :model_width].reshape(rows_here, head_count, head_size)
        value_part = piece_rows[:, model_width:].reshape(rows_here, head_count, head_size)
        return (key_part, value_part)

    def far_fold(pattern, key_part, value_part, source, carried):
        new_block = forward_block(
            query_parts[pattern],
            key_part,
            value_part,
            block_mask(own_docs[pattern], key_docs(pattern, source), False),
            score_scale,
        )
        return merge(carried, new_block)

    def far_update(far_now, key_block, cycle_step):
        new_states = []
        for slot_id, pattern in enumerate(far_ids):
            key_part, value_part = unpack_far(key_block, slot_id)
            new_states.append(
                lax.cond(
                    is_live(pattern, cycle_step),
                    partial(far_fold, pattern, key_part, value_part, my_index - cycle_step),
                    keep_state,
                    far_now[slot_id],
                )
            )
        return tuple(new_states)

    far_states = tuple((states[pattern] for pattern in far_ids))

    def far_forward(cycle_step, loop_state):
        key_block, far_now = loop_state
        key_block = shifted_2(key_block, "seq", 1)
        return (key_block, far_update(far_now, key_block, cycle_step))

    _, far_states = lax.fori_loop(1, seq_devices, far_forward, (far_block, far_states))
    ordered = list(near_states) + list(far_states)
    peaks = [
        expand(ordered[pattern][0][..., None], patterns[pattern][0], big_negative)[..., 0]
        for pattern in range(PATTERNS)
    ]
    best_peak = reduce(jnp.maximum, peaks)
    weight_sum = jnp.zeros((block_rows, head_count), jnp.float32)
    mixed_sum = jnp.zeros((block_rows, head_count, head_size), jnp.float32)
    for pattern in range(PATTERNS):
        stride = patterns[pattern][0]
        factor = jnp.exp(peaks[pattern] - best_peak)
        weight_sum = (
            weight_sum + expand(ordered[pattern][1][..., None], stride, 0.0)[..., 0] * factor
        )
        mixed_sum = mixed_sum + expand(ordered[pattern][2], stride, 0.0) * factor[..., None]
    attended = mixed_sum / weight_sum[..., None]
    log_total = best_peak + jnp.log(weight_sum)
    inner_out, inner_back = jax.vjp(
        layer_norm, attended.reshape(block_rows, model_width), gain_inner
    )
    inner_b = inner_out.astype(jnp.bfloat16)
    middle = source_x + jnp.dot(inner_b, w_out, preferred_element_type=jnp.float32)
    normed_two, feed_back = jax.vjp(layer_norm, middle, gain_feed)
    normed_two_b = normed_two.astype(jnp.bfloat16)
    hidden_pre = jnp.dot(normed_two_b, w_up, preferred_element_type=jnp.float32)
    hidden, hidden_back = jax.vjp(hidden_norm, hidden_pre, gain_hidden)
    hidden_b = hidden.astype(jnp.bfloat16)
    result = (middle + jnp.dot(hidden_b, w_down, preferred_element_type=jnp.float32)).astype(
        jnp.bfloat16
    )
    grad_down = jnp.einsum("tf,tg->fg", hidden_b, cotangent, preferred_element_type=jnp.float32)
    grad_hidden = jnp.einsum("tg,fg->tf", cotangent, w_down, preferred_element_type=jnp.float32)
    grad_pre, grad_gain_hidden = hidden_back(grad_hidden)
    grad_pre_b = grad_pre.astype(jnp.bfloat16)
    grad_up = jnp.einsum("tf,tg->fg", normed_two_b, grad_pre_b, preferred_element_type=jnp.float32)
    grad_normed_two = jnp.einsum("tg,fg->tf", grad_pre_b, w_up, preferred_element_type=jnp.float32)
    grad_middle_part, grad_gain_feed = feed_back(grad_normed_two)
    grad_middle = cotangent.astype(jnp.float32) + grad_middle_part
    grad_middle_b = grad_middle.astype(jnp.bfloat16)
    grad_out = jnp.einsum("tf,tg->fg", inner_b, grad_middle_b, preferred_element_type=jnp.float32)
    grad_inner = jnp.einsum("tg,fg->tf", grad_middle_b, w_out, preferred_element_type=jnp.float32)
    grad_attended, grad_gain_inner = inner_back(grad_inner)
    grad_heads = grad_attended.astype(jnp.bfloat16).reshape(block_rows, head_count, head_size)
    delta_rows = jnp.sum(grad_heads.astype(jnp.float32) * attended, axis=-1)
    grad_parts = [compact(grad_heads, stride) for stride, group_size in patterns]
    lse_parts = [compact(log_total[..., None], stride)[..., 0] for stride, group_size in patterns]
    delta_parts = [
        compact(delta_rows[..., None], stride)[..., 0] for stride, group_size in patterns
    ]
    query_grads = []
    home_keys = []
    home_values = []
    for pattern in range(PATTERNS):
        part_query, part_key, part_value = backward_block(
            query_parts[pattern],
            grad_parts[pattern],
            lse_parts[pattern],
            delta_parts[pattern],
            key_parts[pattern],
            value_parts[pattern],
            block_mask(own_docs[pattern], own_docs[pattern], True),
            score_scale,
        )
        query_grads.append(part_query)
        home_keys.append(part_key)
        home_values.append(part_value)

    def fetch_full(key_block):
        return shifted_2(key_block, "seq", 1)

    def near_grad(pattern, key_full, value_full, source, operands):
        query_grad, travel = operands
        stride = patterns[pattern][0]
        part_query, part_key, part_value = backward_block(
            query_parts[pattern],
            grad_parts[pattern],
            lse_parts[pattern],
            delta_parts[pattern],
            compact(key_full, stride),
            compact(value_full, stride),
            block_mask(own_docs[pattern], key_docs(pattern, source), False),
            score_scale,
        )
        spread_rows = jnp.concatenate(
            [
                expand(part_key, stride, 0.0).reshape(block_rows, model_width),
                expand(part_value, stride, 0.0).reshape(block_rows, model_width),
            ],
            axis=1,
        )
        return (query_grad + part_query, travel + spread_rows)

    def near_backward(cycle_step, loop_state):
        key_block, grads_now, travel = loop_state
        key_block = fetch_full(key_block)
        travel = shifted_3(travel.astype(jnp.bfloat16), "seq", 1).astype(travel.dtype)
        key_full, value_full = unpack_near(key_block)
        new_grads = list(grads_now)
        for pattern in near_ids:
            new_grads[pattern], travel = lax.cond(
                is_live(pattern, cycle_step),
                partial(near_grad, pattern, key_full, value_full, my_index - cycle_step),
                keep_state,
                (new_grads[pattern], travel),
            )
        return (key_block, tuple(new_grads), travel)

    own_key_near = expand(home_keys[0], 1, 0.0) + expand(home_keys[1], 2, 0.0)
    own_value_near = expand(home_values[0], 1, 0.0) + expand(home_values[1], 2, 0.0)
    near_start = jnp.concatenate(
        [
            own_key_near.reshape(block_rows, model_width),
            own_value_near.reshape(block_rows, model_width),
        ],
        axis=1,
    )
    _, near_query, travel_near = lax.fori_loop(
        1, reach, near_backward, (pair_block, (query_grads[0], query_grads[1]), near_start)
    )
    near_home = shifted_3(travel_near.astype(jnp.bfloat16), "seq", 1 - reach).astype(
        travel_near.dtype
    )
    near_key_add = near_home[:, :model_width].reshape(block_rows, head_count, head_size)
    near_value_add = near_home[:, model_width:].reshape(block_rows, head_count, head_size)

    def far_grad(slot_id, key_part, value_part, source, operands):
        query_grad, travel = operands
        pattern = far_ids[slot_id]
        rows_here = far_rows[slot_id]
        row_begin = far_starts[slot_id]
        part_query, part_key, part_value = backward_block(
            query_parts[pattern],
            grad_parts[pattern],
            lse_parts[pattern],
            delta_parts[pattern],
            key_part,
            value_part,
            block_mask(own_docs[pattern], key_docs(pattern, source), False),
            score_scale,
        )
        spread_rows = jnp.concatenate(
            [part_key.reshape(rows_here, model_width), part_value.reshape(rows_here, model_width)],
            axis=1,
        )
        return (
            query_grad + part_query,
            travel.at[row_begin : row_begin + rows_here].add(spread_rows),
        )

    def far_back_update(grads_now, travel, key_block, cycle_step):
        new_grads = list(grads_now)
        for slot_id, pattern in enumerate(far_ids):
            key_part, value_part = unpack_far(key_block, slot_id)
            new_grads[slot_id], travel = lax.cond(
                is_live(pattern, cycle_step),
                partial(far_grad, slot_id, key_part, value_part, my_index - cycle_step),
                keep_state,
                (new_grads[slot_id], travel),
            )
        return (tuple(new_grads), travel)

    far_query = tuple((query_grads[pattern] for pattern in far_ids))
    far_empty = jnp.zeros((far_total, 2 * model_width), jnp.float32)

    def far_send(travel):
        return shifted_3(travel.astype(jnp.bfloat16), "seq", 1).astype(travel.dtype)

    def far_backward(cycle_step, loop_state):
        key_block, grads_now, travel = loop_state
        key_block = shifted_2(key_block, "seq", 1)
        travel = far_send(travel)
        grads_now, travel = far_back_update(grads_now, travel, key_block, cycle_step)
        return (key_block, grads_now, travel)

    _, far_query, travel_far = lax.fori_loop(
        1, seq_devices, far_backward, (far_block, far_query, far_empty)
    )
    far_home = far_send(travel_far)
    all_query = list(near_query) + list(far_query)
    query_grad = jnp.zeros((block_rows, head_count, head_size), jnp.float32)
    key_grad = near_key_add
    value_grad = near_value_add
    for pattern in range(PATTERNS):
        stride = patterns[pattern][0]
        query_grad = query_grad + expand(all_query[pattern], stride, 0.0)
    for pattern in far_ids:
        stride = patterns[pattern][0]
        key_grad = key_grad + expand(home_keys[pattern], stride, 0.0)
        value_grad = value_grad + expand(home_values[pattern], stride, 0.0)
    for slot_id, pattern in enumerate(far_ids):
        stride = patterns[pattern][0]
        rows_here = far_rows[slot_id]
        row_begin = far_starts[slot_id]
        piece_rows = far_home[row_begin : row_begin + rows_here]
        key_grad = key_grad + expand(
            piece_rows[:, :model_width].reshape(rows_here, head_count, head_size), stride, 0.0
        )
        value_grad = value_grad + expand(
            piece_rows[:, model_width:].reshape(rows_here, head_count, head_size), stride, 0.0
        )
    grad_query_b = query_grad.reshape(block_rows, model_width).astype(jnp.bfloat16)
    grad_key_b = key_grad.reshape(block_rows, model_width).astype(jnp.bfloat16)
    grad_value_b = value_grad.reshape(block_rows, model_width).astype(jnp.bfloat16)
    grad_w_query = jnp.einsum(
        "tf,tg->fg", normed_b, grad_query_b, preferred_element_type=jnp.float32
    )
    grad_w_key = jnp.einsum("tf,tg->fg", normed_b, grad_key_b, preferred_element_type=jnp.float32)
    grad_w_value = jnp.einsum(
        "tf,tg->fg", normed_b, grad_value_b, preferred_element_type=jnp.float32
    )
    grad_normed = jnp.einsum("tg,fg->tf", grad_query_b, w_query, preferred_element_type=jnp.float32)
    grad_normed = grad_normed + jnp.einsum(
        "tg,fg->tf", grad_key_b, w_key, preferred_element_type=jnp.float32
    )
    grad_normed = grad_normed + jnp.einsum(
        "tg,fg->tf", grad_value_b, w_value, preferred_element_type=jnp.float32
    )
    grad_x_part, grad_gain_attend = attend_back(grad_normed)
    grad_input = (grad_middle + grad_x_part).astype(jnp.bfloat16)
    gains_all = jnp.concatenate(
        [grad_gain_attend, grad_gain_inner, grad_gain_feed, grad_gain_hidden]
    )
    summed = (
        lax.psum_scatter(grad_w_query.reshape(-1), ("row", "seq"), scatter_dimension=0, tiled=True),
        lax.psum_scatter(grad_w_key.reshape(-1), ("row", "seq"), scatter_dimension=0, tiled=True),
        lax.psum_scatter(grad_w_value.reshape(-1), ("row", "seq"), scatter_dimension=0, tiled=True),
        lax.psum_scatter(grad_out.reshape(-1), ("row", "seq"), scatter_dimension=0, tiled=True),
        lax.psum_scatter(grad_up.reshape(-1), ("row", "seq"), scatter_dimension=0, tiled=True),
        lax.psum_scatter(grad_down.reshape(-1), ("row", "seq"), scatter_dimension=0, tiled=True),
        lax.psum_scatter(gains_all, ("row", "seq"), scatter_dimension=0, tiled=True),
    )
    factor = 1.0 / math.sqrt(block_rows * all_devices)
    return (result, grad_input) + tuple((summed_part * factor for summed_part in summed))


def solution(mesh):
    return jax.shard_map(
        local,
        mesh=mesh,
        in_specs=(
            P(("row", "seq"), None),
            P("row", None),
            P(),
            P(),
            P(),
            P(),
            P(),
            P(),
            P(),
            P(),
            P(),
            P(),
            P(("row", "seq"), None),
        ),
        out_specs=(
            P(("row", "seq"), None),
            P(("row", "seq"), None),
            P(("row", "seq")),
            P(("row", "seq")),
            P(("row", "seq")),
            P(("row", "seq")),
            P(("row", "seq")),
            P(("row", "seq")),
            P(("row", "seq")),
        ),
        check_vma=False,
    )
```

profile of v0, /device:TPU:0, one launch (start us, length us, event | category | flops | bytes accessed | tf_op | source)
XLA Modules:
  0.0 1872.8 jit_solution(18335964295018214245)
XLA Ops:
  76.4 93.1 %while.108 = (s32[]{:T(128)}, bf16[112,1536]{1,0:T(8,128)(2,1)}, f32[64,12]{0,1:T(8,128)}, f32[64,12]{0,1:T(8,128)}, f32[64,12,64]{2,0,1:T(8,128)S(1)}, /*index=...) while((s32[]{:T(128)}, bf16[112,1536]{1,0:T(8,128)(2,1)}, ...), condition=%wide.region_60.61_spmd, body=%wide.region_44.60_spmd.sunk | while | flops 17565184 | bytes 5546095 | solution.py:299
  81.0 20.0 %collective-permute-start.1 = (bf16[112,1536]{1,0:T(8,128)(2,1)}, bf16[112,1536]{1,0:T(8,128)(2,1)S(1)}, u32[]{:S(2)}, u32[]{:S(2)}) collective-permute-start(bf16[112,1536]{1,0:T(8,128)(2,1)} %get-tuple-element.3613), channel_id=1, source_target_pairs={{0,1},{1,2},{2,3},{3,4},{4,5},{5,6},{6,7},{8,9},{9,10},{10,11},{11... | collective-permute-start | bytes 1032200 | tf_op jit(solution)/shard_map/while/body/eval_jaxpr/ppermute | solution.py:21
  112.8 19.7 %collective-permute-start.1 = (bf16[112,1536]{1,0:T(8,128)(2,1)}, bf16[112,1536]{1,0:T(8,128)(2,1)S(1)}, u32[]{:S(2)}, u32[]{:S(2)}) collective-permute-start(bf16[112,1536]{1,0:T(8,128)(2,1)} %get-tuple-element.3613), channel_id=1, source_target_pairs={{0,1},{1,2},{2,3},{3,4},{4,5},{5,6},{6,7},{8,9},{9,10},{10,11},{11... | collective-permute-start | bytes 1032200 | tf_op jit(solution)/shard_map/while/body/eval_jaxpr/ppermute | solution.py:21
  144.2 13.6 collective-permute-start.1
  199.7 194.8 %while.107 = (s32[]{:T(128)}, bf16[256,1536]{1,0:T(8,128)(2,1)S(1)}, f32[256,12]{0,1:T(8,128)S(1)}, f32[256,12]{0,1:T(8,128)}, f32[256,12,64]{0,2,1:T(8,128)}, /...) while((s32[]{:T(128)}, bf16[256,1536]{1,0:T(8,128)(2,1)S(1)}, ...), condition=%wide.region_25.26_spmd, body=%wide.region_12.25_spmd.sunk | while | flops 268132448 | bytes 39528272 | solution.py:243
  199.7 19.7 %collective-permute-start = (bf16[256,1536]{1,0:T(8,128)(2,1)S(1)}, bf16[256,1536]{1,0:T(8,128)(2,1)S(1)}, u32[]{:S(2)}, u32[]{:S(2)}) collective-permute-start(bf16[256,1536]{1,0:T(8,128)(2,1)S(1)} %get-tuple-element.3674), channel_id=1, source_target_pairs={{0,1},{1,2},{2,3},{3,4},{4,5},{5,6},{6,7},{8,9},{9,10},{10,11},{11... | collective-permute-start | bytes 2359304 | tf_op jit(solution)/shard_map/while/body/eval_jaxpr/ppermute | solution.py:21
  223.6 33.5 %collective-permute-start = (bf16[256,1536]{1,0:T(8,128)(2,1)S(1)}, bf16[256,1536]{1,0:T(8,128)(2,1)S(1)}, u32[]{:S(2)}, u32[]{:S(2)}) collective-permute-start(bf16[256,1536]{1,0:T(8,128)(2,1)S(1)} %get-tuple-element.3674), channel_id=1, source_target_pairs={{0,1},{1,2},{2,3},{3,4},{4,5},{5,6},{6,7},{8,9},{9,10},{10,11},{11... | collective-permute-start | bytes 2359304 | tf_op jit(solution)/shard_map/while/body/eval_jaxpr/ppermute | solution.py:21
  261.4 13.6 collective-permute-start
  279.2 33.6 %collective-permute-start = (bf16[256,1536]{1,0:T(8,128)(2,1)S(1)}, bf16[256,1536]{1,0:T(8,128)(2,1)S(1)}, u32[]{:S(2)}, u32[]{:S(2)}) collective-permute-start(bf16[256,1536]{1,0:T(8,128)(2,1)S(1)} %get-tuple-element.3674), channel_id=1, source_target_pairs={{0,1},{1,2},{2,3},{3,4},{4,5},{5,6},{6,7},{8,9},{9,10},{10,11},{11... | collective-permute-start | bytes 2359304 | tf_op jit(solution)/shard_map/while/body/eval_jaxpr/ppermute | solution.py:21
  317.1 19.6 %collective-permute-start = (bf16[256,1536]{1,0:T(8,128)(2,1)S(1)}, bf16[256,1536]{1,0:T(8,128)(2,1)S(1)}, u32[]{:S(2)}, u32[]{:S(2)}) collective-permute-start(bf16[256,1536]{1,0:T(8,128)(2,1)S(1)} %get-tuple-element.3674), channel_id=1, source_target_pairs={{0,1},{1,2},{2,3},{3,4},{4,5},{5,6},{6,7},{8,9},{9,10},{10,11},{11... | collective-permute-start | bytes 2359304 | tf_op jit(solution)/shard_map/while/body/eval_jaxpr/ppermute | solution.py:21
  340.9 33.6 %collective-permute-start = (bf16[256,1536]{1,0:T(8,128)(2,1)S(1)}, bf16[256,1536]{1,0:T(8,128)(2,1)S(1)}, u32[]{:S(2)}, u32[]{:S(2)}) collective-permute-start(bf16[256,1536]{1,0:T(8,128)(2,1)S(1)} %get-tuple-element.3674), channel_id=1, source_target_pairs={{0,1},{1,2},{2,3},{3,4},{4,5},{5,6},{6,7},{8,9},{9,10},{10,11},{11... | collective-permute-start | bytes 2359304 | tf_op jit(solution)/shard_map/while/body/eval_jaxpr/ppermute | solution.py:21
  378.7 11.5 collective-permute-start
  527.4 264.5 %while.110 = (s32[]{:T(128)}, bf16[112,1536]{1,0:T(8,128)(2,1)}, f32[64,12,64]{2,0,1:T(8,128)S(1)}, f32[32,12,64]{2,0,1:T(8,128)}, f32[16,12,64]{2,0,1:T(8,128)}...) while((s32[]{:T(128)}, bf16[112,1536]{1,0:T(8,128)(2,1)}, ...), condition=%wide.region_106.107_spmd, body=%wide.region_96.106_spmd.sunk | while | flops 42762496 | bytes 16015791 | solution.py:474
  527.9 31.7 %collective-permute-start.5 = (bf16[112,1536]{1,0:T(8,128)(2,1)S(1)}, bf16[112,1536]{1,0:T(8,128)(2,1)S(1)}, u32[]{:S(2)}, u32[]{:S(2)}) collective-permute-start(bf16[112,1536]{1,0:T(8,128)(2,1)S(1)} %convert_element_type.558), channel_id=1, source_target_pairs={{0,1},{1,2},{2,3},{3,4},{4,5},{5,6},{6,7},{7,0},{8,9},{9,10},{10,1... | collective-permute-start | bytes 1032200 | tf_op jit(solution)/shard_map/while/body/eval_jaxpr/ppermute | solution.py:27
  564.1 82.3 %collective-permute-done.5 = bf16[112,1536]{1,0:T(8,128)(2,1)S(1)} collective-permute-done((bf16[112,1536]{1,0:T(8,128)(2,1)S(1)}, bf16[112,1536]{1,0:T(8,128)(2,1)S(1)}, u32[]{:S(2)}, u32[]{:S(2)}) %collective-permute-start.5) | collective-permute-done | bytes 344096 | tf_op jit(solution)/shard_map/while/body/eval_jaxpr/ppermute | solution.py:27
  649.7 16.0 collective-permute-done.5
  674.8 14.0 collective-permute-done.5
  698.5 15.6 collective-permute-done.5
  723.8 15.6 collective-permute-done.5
  746.1 18.6 collective-permute-done.5
  768.0 22.0 %collective-permute-done.5 = bf16[112,1536]{1,0:T(8,128)(2,1)S(1)} collective-permute-done((bf16[112,1536]{1,0:T(8,128)(2,1)S(1)}, bf16[112,1536]{1,0:T(8,128)(2,1)S(1)}, u32[]{:S(2)}, u32[]{:S(2)}) %collective-permute-start.5) | collective-permute-done | bytes 344096 | tf_op jit(solution)/shard_map/while/body/eval_jaxpr/ppermute | solution.py:27
  839.5 384.1 %while.109 = (s32[]{:T(128)}, bf16[256,1536]{1,0:T(8,128)(2,1)}, f32[256,12,64]{0,2,1:T(8,128)}, f32[128,12,64]{0,2,1:T(8,128)}, bf16[256,1536]{1,0:T(8,128)(2,1...) while((s32[]{:T(128)}, bf16[256,1536]{1,0:T(8,128)(2,1)}, ...), condition=%wide.region_86.87_spmd, body=%wide.region_77.86_spmd.sunk | while | flops 644421760 | bytes 74832136 | solution.py:416
  842.6 26.8 %collective-permute-done.3 = bf16[256,1536]{0,1:T(8,128)(2,1)S(1)} collective-permute-done((bf16[256,1536]{0,1:T(8,128)(2,1)S(1)}, bf16[256,1536]{0,1:T(8,128)(2,1)S(1)}, u32[]{:S(2)}, u32[]{:S(2)}) %collective-permute-start.3) | collective-permute-done | bytes 786464 | tf_op jit(solution)/shard_map/while/body/eval_jaxpr/ppermute | solution.py:27
  875.1 25.1 %collective-permute-start.3 = (bf16[256,1536]{0,1:T(8,128)(2,1)S(1)}, bf16[256,1536]{0,1:T(8,128)(2,1)S(1)}, u32[]{:S(2)}, u32[]{:S(2)}) collective-permute-start(bf16[256,1536]{0,1:T(8,128)(2,1)S(1)} %copy.1235), channel_id=1, source_target_pairs={{0,1},{1,2},{2,3},{3,4},{4,5},{5,6},{6,7},{7,0},{8,9},{9,10},{10,1... | collective-permute-start | bytes 2359304 | tf_op jit(solution)/shard_map/while/body/eval_jaxpr/ppermute | solution.py:27
  904.5 15.0 collective-permute-done.3
  927.8 39.7 %collective-permute-start.2 = (bf16[256,1536]{1,0:T(8,128)(2,1)}, bf16[256,1536]{1,0:T(8,128)(2,1)S(1)}, u32[]{:S(2)}, u32[]{:S(2)}) collective-permute-start(bf16[256,1536]{1,0:T(8,128)(2,1)} %get-tuple-element.3806), channel_id=1, source_target_pairs={{0,1},{1,2},{2,3},{3,4},{4,5},{5,6},{6,7},{8,9},{9,10},{10,11},{11... | collective-permute-start | bytes 2359304 | tf_op jit(solution)/shard_map/while/body/eval_jaxpr/ppermute | solution.py:21
  993.3 43.3 %collective-permute-done.3 = bf16[256,1536]{0,1:T(8,128)(2,1)S(1)} collective-permute-done((bf16[256,1536]{0,1:T(8,128)(2,1)S(1)}, bf16[256,1536]{0,1:T(8,128)(2,1)S(1)}, u32[]{:S(2)}, u32[]{:S(2)}) %collective-permute-start.3) | collective-permute-done | bytes 786464 | tf_op jit(solution)/shard_map/while/body/eval_jaxpr/ppermute | solution.py:27
  1054.2 43.3 %collective-permute-done.3 = bf16[256,1536]{0,1:T(8,128)(2,1)S(1)} collective-permute-done((bf16[256,1536]{0,1:T(8,128)(2,1)S(1)}, bf16[256,1536]{0,1:T(8,128)(2,1)S(1)}, u32[]{:S(2)}, u32[]{:S(2)}) %collective-permute-start.3) | collective-permute-done | bytes 786464 | tf_op jit(solution)/shard_map/while/body/eval_jaxpr/ppermute | solution.py:27
  1108.0 50.4 %collective-permute-done.3 = bf16[256,1536]{0,1:T(8,128)(2,1)S(1)} collective-permute-done((bf16[256,1536]{0,1:T(8,128)(2,1)S(1)}, bf16[256,1536]{0,1:T(8,128)(2,1)S(1)}, u32[]{:S(2)}, u32[]{:S(2)}) %collective-permute-start.3) | collective-permute-done | bytes 786464 | tf_op jit(solution)/shard_map/while/body/eval_jaxpr/ppermute | solution.py:27
  1165.6 53.8 %collective-permute-done.3 = bf16[256,1536]{0,1:T(8,128)(2,1)S(1)} collective-permute-done((bf16[256,1536]{0,1:T(8,128)(2,1)S(1)}, bf16[256,1536]{0,1:T(8,128)(2,1)S(1)}, u32[]{:S(2)}, u32[]{:S(2)}) %collective-permute-start.3) | collective-permute-done | bytes 786464 | tf_op jit(solution)/shard_map/while/body/eval_jaxpr/ppermute | solution.py:27
  1391.6 84.2 %all-reduce.6 = f32[5376]{0:T(1024)S(1)} all-reduce(f32[5376]{0:T(1024)S(1)} %pad_maximum_fusion.2), channel_id=8, replica_groups=mesh['row'=4,'seq'=8] {'row','seq'}, use_global_device_ids=true, to_apply=%region_119.120.clone | all-reduce | flops 5376 | bytes 43008
  1478.6 382.0 %all-reduce.10.cloned.1.call-done = (f32[589824]{0:T(1024)}, f32[589824]{0:T(1024)}, f32[589824]{0:T(1024)}, f32[589824]{0:T(1024)}, f32[2359296]{0:T(1024)}, /*index=5*/f32[2359296]{0:T(1024)}) async-done(((f32[589824]{0:T(1024)}, f32[589824]{0:T(1024)}, f32[589824]{0:T(1024)}, f32[589824]{0:T(1024)}, f32[2359296]{0:T(1024)}, /*index=5*/f32[2359296]{0:T(1024)}), (f32[589824]{0:T(1024)}, f32[589824]{0:T(1024)}, ...) | async-done | bytes 28311568
  (1186 shorter events, 662.9 us)
Async XLA Ops:
  7.2 1853.4 %all-reduce.10.cloned.1.call-start = ((), (), s32[]{:S(2)}) async-start(), calls=%async_computation | async-start | bytes 56623104
  81.0 21.4 %collective-permute-start.1 = (bf16[112,1536]{1,0:T(8,128)(2,1)}, bf16[112,1536]{1,0:T(8,128)(2,1)S(1)}, u32[]{:S(2)}, u32[]{:S(2)}) collective-permute-start(bf16[112,1536]{1,0:T(8,128)(2,1)} %get-tuple-element.3613), channel_id=1, source_target_pairs={{0,1},{1,2},{2,3},{3,4},{4,5},{5,6},{6,7},{8,9},{9,10},{10,11},{11... | collective-permute-start | bytes 1032200 | tf_op jit(solution)/shard_map/while/body/eval_jaxpr/ppermute | solution.py:21
  199.7 21.5 %collective-permute-start = (bf16[256,1536]{1,0:T(8,128)(2,1)S(1)}, bf16[256,1536]{1,0:T(8,128)(2,1)S(1)}, u32[]{:S(2)}, u32[]{:S(2)}) collective-permute-start(bf16[256,1536]{1,0:T(8,128)(2,1)S(1)} %get-tuple-element.3674), channel_id=1, source_target_pairs={{0,1},{1,2},{2,3},{3,4},{4,5},{5,6},{6,7},{8,9},{9,10},{10,11},{11... | collective-permute-start | bytes 2359304 | tf_op jit(solution)/shard_map/while/body/eval_jaxpr/ppermute | solution.py:21
  223.6 35.4 %collective-permute-start = (bf16[256,1536]{1,0:T(8,128)(2,1)S(1)}, bf16[256,1536]{1,0:T(8,128)(2,1)S(1)}, u32[]{:S(2)}, u32[]{:S(2)}) collective-permute-start(bf16[256,1536]{1,0:T(8,128)(2,1)S(1)} %get-tuple-element.3674), channel_id=1, source_target_pairs={{0,1},{1,2},{2,3},{3,4},{4,5},{5,6},{6,7},{8,9},{9,10},{10,11},{11... | collective-permute-start | bytes 2359304 | tf_op jit(solution)/shard_map/while/body/eval_jaxpr/ppermute | solution.py:21
  279.2 35.5 %collective-permute-start = (bf16[256,1536]{1,0:T(8,128)(2,1)S(1)}, bf16[256,1536]{1,0:T(8,128)(2,1)S(1)}, u32[]{:S(2)}, u32[]{:S(2)}) collective-permute-start(bf16[256,1536]{1,0:T(8,128)(2,1)S(1)} %get-tuple-element.3674), channel_id=1, source_target_pairs={{0,1},{1,2},{2,3},{3,4},{4,5},{5,6},{6,7},{8,9},{9,10},{10,11},{11... | collective-permute-start | bytes 2359304 | tf_op jit(solution)/shard_map/while/body/eval_jaxpr/ppermute | solution.py:21
  317.1 21.4 %collective-permute-start = (bf16[256,1536]{1,0:T(8,128)(2,1)S(1)}, bf16[256,1536]{1,0:T(8,128)(2,1)S(1)}, u32[]{:S(2)}, u32[]{:S(2)}) collective-permute-start(bf16[256,1536]{1,0:T(8,128)(2,1)S(1)} %get-tuple-element.3674), channel_id=1, source_target_pairs={{0,1},{1,2},{2,3},{3,4},{4,5},{5,6},{6,7},{8,9},{9,10},{10,11},{11... | collective-permute-start | bytes 2359304 | tf_op jit(solution)/shard_map/while/body/eval_jaxpr/ppermute | solution.py:21
  340.9 35.5 %collective-permute-start = (bf16[256,1536]{1,0:T(8,128)(2,1)S(1)}, bf16[256,1536]{1,0:T(8,128)(2,1)S(1)}, u32[]{:S(2)}, u32[]{:S(2)}) collective-permute-start(bf16[256,1536]{1,0:T(8,128)(2,1)S(1)} %get-tuple-element.3674), channel_id=1, source_target_pairs={{0,1},{1,2},{2,3},{3,4},{4,5},{5,6},{6,7},{8,9},{9,10},{10,11},{11... | collective-permute-start | bytes 2359304 | tf_op jit(solution)/shard_map/while/body/eval_jaxpr/ppermute | solution.py:21
  527.9 118.5 %collective-permute-start.5 = (bf16[112,1536]{1,0:T(8,128)(2,1)S(1)}, bf16[112,1536]{1,0:T(8,128)(2,1)S(1)}, u32[]{:S(2)}, u32[]{:S(2)}) collective-permute-start(bf16[112,1536]{1,0:T(8,128)(2,1)S(1)} %convert_element_type.558), channel_id=1, source_target_pairs={{0,1},{1,2},{2,3},{3,4},{4,5},{5,6},{6,7},{7,0},{8,9},{9,10},{10,1... | collective-permute-start | bytes 1032200 | tf_op jit(solution)/shard_map/while/body/eval_jaxpr/ppermute | solution.py:27
  559.7 86.8 %collective-permute-start.4 = (bf16[112,1536]{1,0:T(8,128)(2,1)}, bf16[112,1536]{1,0:T(8,128)(2,1)S(1)}, u32[]{:S(2)}, u32[]{:S(2)}) collective-permute-start(bf16[112,1536]{1,0:T(8,128)(2,1)} %get-tuple-element.3734), channel_id=1, source_target_pairs={{0,1},{1,2},{2,3},{3,4},{4,5},{5,6},{6,7},{8,9},{9,10},{10,11},{11... | collective-permute-start | bytes 1032200 | tf_op jit(solution)/shard_map/while/body/eval_jaxpr/ppermute | solution.py:21
  667.5 21.3 %collective-permute-start.5 = (bf16[112,1536]{1,0:T(8,128)(2,1)S(1)}, bf16[112,1536]{1,0:T(8,128)(2,1)S(1)}, u32[]{:S(2)}, u32[]{:S(2)}) collective-permute-start(bf16[112,1536]{1,0:T(8,128)(2,1)S(1)} %convert_element_type.558), channel_id=1, source_target_pairs={{0,1},{1,2},{2,3},{3,4},{4,5},{5,6},{6,7},{7,0},{8,9},{9,10},{10,1... | collective-permute-start | bytes 1032200 | tf_op jit(solution)/shard_map/while/body/eval_jaxpr/ppermute | solution.py:27
  667.6 21.3 %collective-permute-start.4 = (bf16[112,1536]{1,0:T(8,128)(2,1)}, bf16[112,1536]{1,0:T(8,128)(2,1)S(1)}, u32[]{:S(2)}, u32[]{:S(2)}) collective-permute-start(bf16[112,1536]{1,0:T(8,128)(2,1)} %get-tuple-element.3734), channel_id=1, source_target_pairs={{0,1},{1,2},{2,3},{3,4},{4,5},{5,6},{6,7},{8,9},{9,10},{10,11},{11... | collective-permute-start | bytes 1032200 | tf_op jit(solution)/shard_map/while/body/eval_jaxpr/ppermute | solution.py:21
  690.7 23.4 %collective-permute-start.5 = (bf16[112,1536]{1,0:T(8,128)(2,1)S(1)}, bf16[112,1536]{1,0:T(8,128)(2,1)S(1)}, u32[]{:S(2)}, u32[]{:S(2)}) collective-permute-start(bf16[112,1536]{1,0:T(8,128)(2,1)S(1)} %convert_element_type.558), channel_id=1, source_target_pairs={{0,1},{1,2},{2,3},{3,4},{4,5},{5,6},{6,7},{7,0},{8,9},{9,10},{10,1... | collective-permute-start | bytes 1032200 | tf_op jit(solution)/shard_map/while/body/eval_jaxpr/ppermute | solution.py:27
  716.0 23.4 %collective-permute-start.5 = (bf16[112,1536]{1,0:T(8,128)(2,1)S(1)}, bf16[112,1536]{1,0:T(8,128)(2,1)S(1)}, u32[]{:S(2)}, u32[]{:S(2)}) collective-permute-start(bf16[112,1536]{1,0:T(8,128)(2,1)S(1)} %convert_element_type.558), channel_id=1, source_target_pairs={{0,1},{1,2},{2,3},{3,4},{4,5},{5,6},{6,7},{7,0},{8,9},{9,10},{10,1... | collective-permute-start | bytes 1032200 | tf_op jit(solution)/shard_map/while/body/eval_jaxpr/ppermute | solution.py:27
  741.3 23.4 %collective-permute-start.5 = (bf16[112,1536]{1,0:T(8,128)(2,1)S(1)}, bf16[112,1536]{1,0:T(8,128)(2,1)S(1)}, u32[]{:S(2)}, u32[]{:S(2)}) collective-permute-start(bf16[112,1536]{1,0:T(8,128)(2,1)S(1)} %convert_element_type.558), channel_id=1, source_target_pairs={{0,1},{1,2},{2,3},{3,4},{4,5},{5,6},{6,7},{7,0},{8,9},{9,10},{10,1... | collective-permute-start | bytes 1032200 | tf_op jit(solution)/shard_map/while/body/eval_jaxpr/ppermute | solution.py:27
  741.4 23.4 %collective-permute-start.4 = (bf16[112,1536]{1,0:T(8,128)(2,1)}, bf16[112,1536]{1,0:T(8,128)(2,1)S(1)}, u32[]{:S(2)}, u32[]{:S(2)}) collective-permute-start(bf16[112,1536]{1,0:T(8,128)(2,1)} %get-tuple-element.3734), channel_id=1, source_target_pairs={{0,1},{1,2},{2,3},{3,4},{4,5},{5,6},{6,7},{8,9},{9,10},{10,11},{11... | collective-permute-start | bytes 1032200 | tf_op jit(solution)/shard_map/while/body/eval_jaxpr/ppermute | solution.py:21
  766.6 23.4 %collective-permute-start.5 = (bf16[112,1536]{1,0:T(8,128)(2,1)S(1)}, bf16[112,1536]{1,0:T(8,128)(2,1)S(1)}, u32[]{:S(2)}, u32[]{:S(2)}) collective-permute-start(bf16[112,1536]{1,0:T(8,128)(2,1)S(1)} %convert_element_type.558), channel_id=1, source_target_pairs={{0,1},{1,2},{2,3},{3,4},{4,5},{5,6},{6,7},{7,0},{8,9},{9,10},{10,1... | collective-permute-start | bytes 1032200 | tf_op jit(solution)/shard_map/while/body/eval_jaxpr/ppermute | solution.py:27
  766.7 23.5 %collective-permute-start.4 = (bf16[112,1536]{1,0:T(8,128)(2,1)}, bf16[112,1536]{1,0:T(8,128)(2,1)S(1)}, u32[]{:S(2)}, u32[]{:S(2)}) collective-permute-start(bf16[112,1536]{1,0:T(8,128)(2,1)} %get-tuple-element.3734), channel_id=1, source_target_pairs={{0,1},{1,2},{2,3},{3,4},{4,5},{5,6},{6,7},{8,9},{9,10},{10,11},{11... | collective-permute-start | bytes 1032200 | tf_op jit(solution)/shard_map/while/body/eval_jaxpr/ppermute | solution.py:21
  792.9 535.2 %collective-permute-start.7 = (bf16[112,1536]{1,0:T(8,128)(2,1)}, bf16[112,1536]{1,0:T(8,128)(2,1)}, u32[]{:S(2)}, u32[]{:S(2)}) collective-permute-start(bf16[112,1536]{1,0:T(8,128)(2,1)} %convert_element_type.393), channel_id=1, source_target_pairs={{0,1},{1,2},{2,3},{3,4},{4,5},{5,6},{6,7},{7,0},{8,9},{9,10},{10,1... | collective-permute-start | bytes 1032200 | tf_op jit(solution)/shard_map/ppermute | solution.py:27
  841.1 28.2 %collective-permute-start.3 = (bf16[256,1536]{0,1:T(8,128)(2,1)S(1)}, bf16[256,1536]{0,1:T(8,128)(2,1)S(1)}, u32[]{:S(2)}, u32[]{:S(2)}) collective-permute-start(bf16[256,1536]{0,1:T(8,128)(2,1)S(1)} %copy.1235), channel_id=1, source_target_pairs={{0,1},{1,2},{2,3},{3,4},{4,5},{5,6},{6,7},{7,0},{8,9},{9,10},{10,1... | collective-permute-start | bytes 2359304 | tf_op jit(solution)/shard_map/while/body/eval_jaxpr/ppermute | solution.py:27
  841.2 28.2 %collective-permute-start.2 = (bf16[256,1536]{1,0:T(8,128)(2,1)}, bf16[256,1536]{1,0:T(8,128)(2,1)S(1)}, u32[]{:S(2)}, u32[]{:S(2)}) collective-permute-start(bf16[256,1536]{1,0:T(8,128)(2,1)} %get-tuple-element.3806), channel_id=1, source_target_pairs={{0,1},{1,2},{2,3},{3,4},{4,5},{5,6},{6,7},{8,9},{9,10},{10,11},{11... | collective-permute-start | bytes 2359304 | tf_op jit(solution)/shard_map/while/body/eval_jaxpr/ppermute | solution.py:21
  875.1 44.4 %collective-permute-start.3 = (bf16[256,1536]{0,1:T(8,128)(2,1)S(1)}, bf16[256,1536]{0,1:T(8,128)(2,1)S(1)}, u32[]{:S(2)}, u32[]{:S(2)}) collective-permute-start(bf16[256,1536]{0,1:T(8,128)(2,1)S(1)} %copy.1235), channel_id=1, source_target_pairs={{0,1},{1,2},{2,3},{3,4},{4,5},{5,6},{6,7},{7,0},{8,9},{9,10},{10,1... | collective-permute-start | bytes 2359304 | tf_op jit(solution)/shard_map/while/body/eval_jaxpr/ppermute | solution.py:27
  925.2 50.5 %collective-permute-start.3 = (bf16[256,1536]{0,1:T(8,128)(2,1)S(1)}, bf16[256,1536]{0,1:T(8,128)(2,1)S(1)}, u32[]{:S(2)}, u32[]{:S(2)}) collective-permute-start(bf16[256,1536]{0,1:T(8,128)(2,1)S(1)} %copy.1235), channel_id=1, source_target_pairs={{0,1},{1,2},{2,3},{3,4},{4,5},{5,6},{6,7},{7,0},{8,9},{9,10},{10,1... | collective-permute-start | bytes 2359304 | tf_op jit(solution)/shard_map/while/body/eval_jaxpr/ppermute | solution.py:27
  927.8 47.9 %collective-permute-start.2 = (bf16[256,1536]{1,0:T(8,128)(2,1)}, bf16[256,1536]{1,0:T(8,128)(2,1)S(1)}, u32[]{:S(2)}, u32[]{:S(2)}) collective-permute-start(bf16[256,1536]{1,0:T(8,128)(2,1)} %get-tuple-element.3806), channel_id=1, source_target_pairs={{0,1},{1,2},{2,3},{3,4},{4,5},{5,6},{6,7},{8,9},{9,10},{10,11},{11... | collective-permute-start | bytes 2359304 | tf_op jit(solution)/shard_map/while/body/eval_jaxpr/ppermute | solution.py:21
  981.4 55.2 %collective-permute-start.3 = (bf16[256,1536]{0,1:T(8,128)(2,1)S(1)}, bf16[256,1536]{0,1:T(8,128)(2,1)S(1)}, u32[]{:S(2)}, u32[]{:S(2)}) collective-permute-start(bf16[256,1536]{0,1:T(8,128)(2,1)S(1)} %copy.1235), channel_id=1, source_target_pairs={{0,1},{1,2},{2,3},{3,4},{4,5},{5,6},{6,7},{7,0},{8,9},{9,10},{10,1... | collective-permute-start | bytes 2359304 | tf_op jit(solution)/shard_map/while/body/eval_jaxpr/ppermute | solution.py:27
  989.0 47.7 %collective-permute-start.2 = (bf16[256,1536]{1,0:T(8,128)(2,1)}, bf16[256,1536]{1,0:T(8,128)(2,1)S(1)}, u32[]{:S(2)}, u32[]{:S(2)}) collective-permute-start(bf16[256,1536]{1,0:T(8,128)(2,1)} %get-tuple-element.3806), channel_id=1, source_target_pairs={{0,1},{1,2},{2,3},{3,4},{4,5},{5,6},{6,7},{8,9},{9,10},{10,11},{11... | collective-permute-start | bytes 2359304 | tf_op jit(solution)/shard_map/while/body/eval_jaxpr/ppermute | solution.py:21
  1042.3 55.2 %collective-permute-start.3 = (bf16[256,1536]{0,1:T(8,128)(2,1)S(1)}, bf16[256,1536]{0,1:T(8,128)(2,1)S(1)}, u32[]{:S(2)}, u32[]{:S(2)}) collective-permute-start(bf16[256,1536]{0,1:T(8,128)(2,1)S(1)} %copy.1235), channel_id=1, source_target_pairs={{0,1},{1,2},{2,3},{3,4},{4,5},{5,6},{6,7},{7,0},{8,9},{9,10},{10,1... | collective-permute-start | bytes 2359304 | tf_op jit(solution)/shard_map/while/body/eval_jaxpr/ppermute | solution.py:27
  1049.9 47.7 %collective-permute-start.2 = (bf16[256,1536]{1,0:T(8,128)(2,1)}, bf16[256,1536]{1,0:T(8,128)(2,1)S(1)}, u32[]{:S(2)}, u32[]{:S(2)}) collective-permute-start(bf16[256,1536]{1,0:T(8,128)(2,1)} %get-tuple-element.3806), channel_id=1, source_target_pairs={{0,1},{1,2},{2,3},{3,4},{4,5},{5,6},{6,7},{8,9},{9,10},{10,11},{11... | collective-permute-start | bytes 2359304 | tf_op jit(solution)/shard_map/while/body/eval_jaxpr/ppermute | solution.py:21
  1103.2 55.2 %collective-permute-start.3 = (bf16[256,1536]{0,1:T(8,128)(2,1)S(1)}, bf16[256,1536]{0,1:T(8,128)(2,1)S(1)}, u32[]{:S(2)}, u32[]{:S(2)}) collective-permute-start(bf16[256,1536]{0,1:T(8,128)(2,1)S(1)} %copy.1235), channel_id=1, source_target_pairs={{0,1},{1,2},{2,3},{3,4},{4,5},{5,6},{6,7},{7,0},{8,9},{9,10},{10,1... | collective-permute-start | bytes 2359304 | tf_op jit(solution)/shard_map/while/body/eval_jaxpr/ppermute | solution.py:27
  1103.3 55.3 %collective-permute-start.2 = (bf16[256,1536]{1,0:T(8,128)(2,1)}, bf16[256,1536]{1,0:T(8,128)(2,1)S(1)}, u32[]{:S(2)}, u32[]{:S(2)}) collective-permute-start(bf16[256,1536]{1,0:T(8,128)(2,1)} %get-tuple-element.3806), channel_id=1, source_target_pairs={{0,1},{1,2},{2,3},{3,4},{4,5},{5,6},{6,7},{8,9},{9,10},{10,11},{11... | collective-permute-start | bytes 2359304 | tf_op jit(solution)/shard_map/while/body/eval_jaxpr/ppermute | solution.py:21
  1164.1 55.2 %collective-permute-start.3 = (bf16[256,1536]{0,1:T(8,128)(2,1)S(1)}, bf16[256,1536]{0,1:T(8,128)(2,1)S(1)}, u32[]{:S(2)}, u32[]{:S(2)}) collective-permute-start(bf16[256,1536]{0,1:T(8,128)(2,1)S(1)} %copy.1235), channel_id=1, source_target_pairs={{0,1},{1,2},{2,3},{3,4},{4,5},{5,6},{6,7},{7,0},{8,9},{9,10},{10,1... | collective-permute-start | bytes 2359304 | tf_op jit(solution)/shard_map/while/body/eval_jaxpr/ppermute | solution.py:27
  1164.2 55.3 %collective-permute-start.2 = (bf16[256,1536]{1,0:T(8,128)(2,1)}, bf16[256,1536]{1,0:T(8,128)(2,1)S(1)}, u32[]{:S(2)}, u32[]{:S(2)}) collective-permute-start(bf16[256,1536]{1,0:T(8,128)(2,1)} %get-tuple-element.3806), channel_id=1, source_target_pairs={{0,1},{1,2},{2,3},{3,4},{4,5},{5,6},{6,7},{8,9},{9,10},{10,11},{11... | collective-permute-start | bytes 2359304 | tf_op jit(solution)/shard_map/while/body/eval_jaxpr/ppermute | solution.py:21
  1223.7 140.7 %collective-permute-start.6 = (bf16[256,1536]{1,0:T(8,128)(2,1)}, bf16[256,1536]{1,0:T(8,128)(2,1)}, u32[]{:S(2)}, u32[]{:S(2)}) collective-permute-start(bf16[256,1536]{1,0:T(8,128)(2,1)} %get-tuple-element.2227), channel_id=1, source_target_pairs={{0,1},{1,2},{2,3},{3,4},{4,5},{5,6},{6,7},{7,0},{8,9},{9,10},{10,1... | collective-permute-start | bytes 2359304 | tf_op jit(solution)/shard_map/ppermute | solution.py:27
  (311 other events, 3286.1 us)
Sparse Core Ops, SparseCore 0:
  1381.1 479.4 all-reduce.9
where the time goes:
time: 1900 us; the launch traced here: 1870 us
  waiting for transfers between devices  830 us (44%)
  starting transfers between devices  413 us (22%)
  local copies, waits for them, and re-layouts  344 us (18%)
  matrix products  91.9 us (5%)
  other arithmetic  89.5 us (5%)
  blocking collectives  84.2 us (4%)
    ppermute x16, waiting for transfers between devices, shifted_3(): return lax.ppermute(value, axis, pairs)  425 us
    unnamed x2, waiting for transfers between devices  382 us
    ppermute x28, starting transfers between devices, shifted_2(): return lax.ppermute(shard, axis, pairs)  330 us
    broadcast_in_dim x109, local copies, waits for them, and re-layouts, expand(): jnp.where(selector(stride, head_count)[None, :, :, None], part_array[:, N...  133 us
    unnamed x1, blocking collectives  84.2 us
    ppermute x16, starting transfers between devices, shifted_3(): return lax.ppermute(value, axis, pairs)  82.4 us
    while x182, local copies, waits for them, and re-layouts  46.6 us
  transfers between devices with their start and end apart: 45, of which 29 were waited for; matrix products, arithmetic and copies ran while one was open for 12% of the time, Pallas kernels for 0%

commit v1 on v0

--- a/solution.py
+++ b/solution.py
@@ -4,7 +4,10 @@
 
 import jax
 import jax.numpy as jnp
+import numpy as np
 from jax import lax
+from jax.experimental import pallas as pl
+from jax.experimental.pallas import tpu as pltpu
 from jax.sharding import PartitionSpec as P
 
 HEADS = 12
@@ -131,7 +134,7 @@
     return carried
 
 
-def local(
+def ring_local(
     tokens,
     lengths,
     w_query,
@@ -532,6 +535,999 @@
     return (result, grad_input) + tuple((summed_part * factor for summed_part in summed))
 
 
+def split_log(level):
+    remaining = math.log((level + 1) / level)
+    pieces = []
+    for _ in range(3):
+        piece = float(jnp.bfloat16.dtype.type(remaining))
+        pieces.append(piece)
+        remaining -= piece
+    return pieces
+
+
+def extra_features(heads, size, lanes):
+    masks, owners, query_values, key_values = [], [], [], []
+    for head in range(heads):
+        for lane in range(lanes):
+            level, piece = divmod(lane - size, 3)
+            used = size <= lane < size + 3 * (PATTERNS - 1)
+            masks.append(2 ** (level + 1) - 1 if used else 0)
+            owners.append(head)
+            query_values.append(split_log(level + 1)[piece] if used else 0.0)
+            key_values.append(1.0 if used else 0.0)
+    return (
+        np.array(masks, np.int32),
+        np.array(owners, np.int32),
+        np.array(query_values, np.float32),
+        np.array(key_values, np.float32),
+    )
+
+
+def nt_dot(left, right):
+    return lax.dot_general(
+        left, right, (((1,), (1,)), ((), ())), preferred_element_type=jnp.float32
+    )
+
+
+def nn_dot(left, right):
+    return jnp.dot(left, right, preferred_element_type=jnp.float32)
+
+
+def project_kernel(
+    blocks, own, scale, meta, *refs
+):
+    normed = refs[:blocks]
+    wq_ref, wk_ref, wv_ref, row_ref, col_ref, row_value, col_value = refs[blocks : blocks + 7]
+    q_ref, k_ref, vt_ref = refs[blocks + 7 :]
+    length = normed[0].shape[0]
+    for index in range(blocks):
+        rows = normed[index][...]
+        start = meta[own + index]
+        span = slice(index * length, (index + 1) * length)
+        place = start + lax.broadcasted_iota(jnp.int32, (length, 1), 0)
+        extra = jnp.where(
+            ((place - col_ref[1:2]) & col_ref[0:1]) == 0, col_value[...], 0.0
+        )
+        k_ref[span, :] = (nn_dot(rows, wk_ref[...]) + extra).astype(jnp.bfloat16)
+        vt_ref[:, span] = nt_dot(wv_ref[...], rows).astype(jnp.bfloat16)
+        if index < own:
+            place = start + lax.broadcasted_iota(jnp.int32, (1, length), 1)
+            extra = jnp.where(
+                ((place - row_ref[:, 1:2]) & row_ref[:, 0:1]) == 0, row_value[...], 0.0
+            )
+            query = nt_dot(wq_ref[...], rows).astype(jnp.bfloat16).astype(jnp.float32)
+            q_ref[:, span] = (query * scale + extra).astype(jnp.bfloat16)
+
+
+def project(meta, normed, wq, wk, wv, row_info, col_info, row_value, col_value, own, scale):
+    blocks, length = len(normed), normed[0].shape[0]
+    wide, share = wk.shape[1], wv.shape[0]
+    vmem = pl.BlockSpec(memory_space=pltpu.VMEM)
+    return pl.pallas_call(
+        partial(project_kernel, blocks, own, scale),
+        in_specs=[pl.BlockSpec(memory_space=pltpu.SMEM)] + [vmem] * (blocks + 7),
+        out_specs=[vmem] * 3,
+        out_shape=[
+            jax.ShapeDtypeStruct((wide, own * length), jnp.bfloat16),
+            jax.ShapeDtypeStruct((blocks * length, wide), jnp.bfloat16),
+            jax.ShapeDtypeStruct((share, blocks * length), jnp.bfloat16),
+        ],
+        compiler_params=pltpu.CompilerParams(vmem_limit_bytes=32 << 20),
+        name="project",
+    )(meta, *normed, wq, wk, wv, row_info, col_info, row_value, col_value)
+
+
+def project_back_kernel(blocks, *refs):
+    normed = refs[:blocks]
+    wk_ref, wv_ref, kt_ref, v_ref = refs[blocks:]
+    length = normed[0].shape[0]
+    for index in range(blocks):
+        rows = normed[index][...]
+        span = slice(index * length, (index + 1) * length)
+        kt_ref[:, span] = nt_dot(wk_ref[...], rows).astype(jnp.bfloat16)
+        v_ref[span, :] = nn_dot(rows, wv_ref[...]).astype(jnp.bfloat16)
+
+
+def project_back(normed, wk, wv):
+    blocks, length = len(normed), normed[0].shape[0]
+    vmem = pl.BlockSpec(memory_space=pltpu.VMEM)
+    return pl.pallas_call(
+        partial(project_back_kernel, blocks),
+        in_specs=[vmem] * (blocks + 2),
+        out_specs=[vmem] * 2,
+        out_shape=[
+            jax.ShapeDtypeStruct((wk.shape[0], blocks * length), jnp.bfloat16),
+            jax.ShapeDtypeStruct((blocks * length, wv.shape[1]), jnp.bfloat16),
+        ],
+        compiler_params=pltpu.CompilerParams(vmem_limit_bytes=32 << 20),
+        cost_estimate=pl.CostEstimate(flops=3 * 10**9, bytes_accessed=6 << 20, transcendentals=0),
+        name="project_back",
+    )(*normed, wk, wv)
+
+
+def pair_mask(query_start, key_start, doc_line, block):
+    query_place = query_start + lax.broadcasted_iota(jnp.int32, (1, block), 1)
+    key_place = key_start + lax.broadcasted_iota(jnp.int32, (block, 1), 0)
+    return (key_place <= query_place) & (key_place >= doc_line)
+
+
+def attend_kernel(
+    heads, block, key_blocks, meta, doc_ref, q_ref, k_ref, vt_ref, o_ref, ob_ref, lse_ref, m_ref, l_ref
+):
+    step = pl.program_id(0)
+    steps = pl.num_programs(0)
+    query_start = meta[step]
+    doc_first = meta[steps + key_blocks + step]
+    doc_line = doc_ref[...]
+    size = o_ref.shape[0] // heads
+    lanes = q_ref.shape[0] // heads
+    m_ref[...] = jnp.full_like(m_ref, big_negative)
+    l_ref[...] = jnp.zeros_like(l_ref)
+    o_ref[...] = jnp.zeros_like(o_ref)
+
+    def body(slot, carry):
+        key_start = meta[steps + slot]
+
+        @pl.when((key_start <= query_start) & (key_start + block > doc_first))
+        def _():
+            span = pl.ds(pl.multiple_of(slot * block, block), block)
+            allowed = pair_mask(query_start, key_start, doc_line, block)
+            for head in range(heads):
+                wide = slice(head * lanes, (head + 1) * lanes)
+                rows = slice(head * size, (head + 1) * size)
+                scores = nn_dot(k_ref[span, wide], q_ref[wide, :])
+                scores = jnp.where(allowed, scores, big_negative)
+                old_peak = m_ref[head]
+                new_peak = jnp.maximum(old_peak, jnp.max(scores, axis=0, keepdims=True))
+                weights = jnp.exp(scores - new_peak)
+                fade = jnp.exp(old_peak - new_peak)
+                m_ref[head] = new_peak
+                l_ref[head] = l_ref[head] * fade + jnp.sum(weights, axis=0, keepdims=True)
+                o_ref[rows, :] = o_ref[rows, :] * fade + nn_dot(
+                    vt_ref[rows, span], weights.astype(jnp.bfloat16)
+                )
+
+        return carry
+
+    lax.fori_loop(0, key_blocks, body, 0)
+    for head in range(heads):
+        rows = slice(head * size, (head + 1) * size)
+        total = l_ref[head]
+        mixed = o_ref[rows, :] / total
+        o_ref[rows, :] = mixed
+        ob_ref[0, rows, :] = mixed.astype(jnp.bfloat16)
+        lse_ref[head] = m_ref[head] + jnp.log(total)
+
+
+def attend_back_kernel(
+    heads,
+    block,
+    key_blocks,
+    scale,
+    meta,
+    doc_ref,
+    q_ref,
+    g_ref,
+    o_ref,
+    lse_ref,
+    k_ref,
+    kt_ref,
+    v_ref,
+    dq_ref,
+    dk_ref,
+    dv_ref,
+    acc_ref,
+):
+    step = pl.program_id(0)
+    steps = pl.num_programs(0)
+    query_start = meta[step]
+    doc_first = meta[steps + key_blocks + step]
+    doc_line = doc_ref[...]
+    size = g_ref.shape[0] // heads
+    lanes = q_ref.shape[0] // heads
+
+    @pl.when(step == 0)
+    def _():
+        dk_ref[...] = jnp.zeros_like(dk_ref)
+        dv_ref[...] = jnp.zeros_like(dv_ref)
+
+    acc_ref[...] = jnp.zeros_like(acc_ref)
+
+    def body(slot, carry):
+        key_start = meta[steps + slot]
+
+        @pl.when((key_start <= query_start) & (key_start + block > doc_first))
+        def _():
+            span = pl.ds(pl.multiple_of(slot * block, block), block)
+            allowed = pair_mask(query_start, key_start, doc_line, block)
+            for head in range(heads):
+                wide = slice(head * lanes, (head + 1) * lanes)
+                rows = slice(head * size, (head + 1) * size)
+                grad = g_ref[rows, :]
+                delta = jnp.sum(grad.astype(jnp.float32) * o_ref[rows, :], axis=0, keepdims=True)
+                scores = nn_dot(k_ref[span, wide], q_ref[wide, :])
+                probs = jnp.where(allowed, jnp.exp(scores - lse_ref[head]), 0.0)
+                dots = nn_dot(v_ref[span, head * lanes : head * lanes + size], grad)
+                grad_scores = (probs * (dots - delta)).astype(jnp.bfloat16)
+                dv_ref[rows, span] += nt_dot(grad, probs.astype(jnp.bfloat16))
+                query = q_ref[head * lanes : head * lanes + size, :]
+                dk_ref[rows, span] += nt_dot(query, grad_scores)
+                acc_ref[rows, :] += nn_dot(kt_ref[rows, span], grad_scores)
+
+        return carry
+
+    lax.fori_loop(0, key_blocks, body, 0)
+    dq_ref[...] = (acc_ref[...] * scale).astype(dq_ref.dtype)
+
+
+def whole(shape):
+    return pl.BlockSpec(shape, lambda *index: (0,) * len(shape))
+
+
+def attend(meta, doc_line, q_ext, k_ext, v_t, heads, block):
+    wide, queries = q_ext.shape
+    share, keys = v_t.shape
+    steps, key_blocks = queries // block, keys // block
+    return pl.pallas_call(
+        partial(attend_kernel, heads, block, key_blocks),
+        grid_spec=pltpu.PrefetchScalarGridSpec(
+            num_scalar_prefetch=1,
+            grid=(steps,),
+            in_specs=[
+                pl.BlockSpec((1, block), lambda i, meta: (0, i)),
+                pl.BlockSpec((wide, block), lambda i, meta: (0, i)),
+                whole(k_ext.shape),
+                whole(v_t.shape),
+            ],
+            out_specs=[
+                pl.BlockSpec((share, block), lambda i, meta: (0, i)),
+                pl.BlockSpec((1, share, block), lambda i, meta: (i, 0, 0)),
+                pl.BlockSpec((heads, 1, block), lambda i, meta: (0, 0, i)),
+            ],
+            scratch_shapes=[
+                pltpu.VMEM((heads, 1, block), jnp.float32),
+                pltpu.VMEM((heads, 1, block), jnp.float32),
+            ],
+        ),
+        out_shape=[
+            jax.ShapeDtypeStruct((share, queries), jnp.float32),
+            jax.ShapeDtypeStruct((steps, share, block), jnp.bfloat16),
+            jax.ShapeDtypeStruct((heads, 1, queries), jnp.float32),
+        ],
+        compiler_params=pltpu.CompilerParams(vmem_limit_bytes=24 << 20),
+        cost_estimate=pl.CostEstimate(flops=8 * 10**9, bytes_accessed=8 << 20, transcendentals=0),
+        name="attend",
+    )(meta, doc_line, q_ext, k_ext, v_t)
+
+
+def attend_back(meta, doc_line, q_ext, grad_t, mixed, lse, k_ext, k_t, v_ext, heads, block, scale):
+    wide, queries = q_ext.shape
+    share, keys = k_t.shape
+    steps, key_blocks = queries // block, keys // block
+    return pl.pallas_call(
+        partial(attend_back_kernel, heads, block, key_blocks, scale),
+        grid_spec=pltpu.PrefetchScalarGridSpec(
+            num_scalar_prefetch=1,
+            grid=(steps,),
+            in_specs=[
+                pl.BlockSpec((1, block), lambda i, meta: (0, i)),
+                pl.BlockSpec((wide, block), lambda i, meta: (0, i)),
+                pl.BlockSpec((share, block), lambda i, meta: (0, i)),
+                pl.BlockSpec((share, block), lambda i, meta: (0, i)),
+                pl.BlockSpec((heads, 1, block), lambda i, meta: (0, 0, i)),
+                whole(k_ext.shape),
+                whole(k_t.shape),
+                whole(v_ext.shape),
+            ],
+            out_specs=[
+                pl.BlockSpec((share, block), lambda i, meta: (0, i)),
+                whole(k_t.shape),
+                whole(k_t.shape),
+            ],
+            scratch_shapes=[pltpu.VMEM((share, block), jnp.float32)],
+        ),
+        out_shape=[
+            jax.ShapeDtypeStruct((share, queries), jnp.bfloat16),
+            jax.ShapeDtypeStruct((share, keys), jnp.float32),
+            jax.ShapeDtypeStruct((share, keys), jnp.float32),
+        ],
+        compiler_params=pltpu.CompilerParams(vmem_limit_bytes=32 << 20),
+        cost_estimate=pl.CostEstimate(flops=10**6, bytes_accessed=1 << 10, transcendentals=0),
+        name="attend_back",
+    )(meta, doc_line, q_ext, grad_t, mixed, lse, k_ext, k_t, v_ext)
+
+
+def norm_parts(values):
+    shifted = values - jnp.mean(values, axis=-1, keepdims=True)
+    rate = lax.rsqrt(jnp.mean(shifted * shifted, axis=-1, keepdims=True) + 1e-05)
+    return shifted * rate, rate
+
+
+def norm_back(grad, hat, rate, gain):
+    scaled = grad * gain
+    mean_scaled = jnp.mean(scaled, axis=-1, keepdims=True)
+    mean_product = jnp.mean(scaled * hat, axis=-1, keepdims=True)
+    return (
+        rate * (scaled - mean_scaled - hat * mean_product),
+        jnp.sum(grad * hat, axis=0, keepdims=True),
+    )
+
+
+def middle_kernel(
+    chips,
+    tiles,
+    per,
+    position,
+    *refs,
+):
+    mixed = refs[:chips]
+    (
+        tokens_ref,
+        cot_ref,
+        wout_ref,
+        wup_ref,
+        wdown_ref,
+        perm_ref,
+        ginner_ref,
+        gfeed_ref,
+        ghidden_ref,
+        result_ref,
+        gmid_ref,
+    ) = refs[chips : chips + 11]
+    go_refs = refs[chips + 11 : 2 * chips + 11]
+    (
+        down_keep,
+        down_send,
+        flat_keep,
+        flat_send,
+        dinner_ref,
+        dfeed_ref,
+        dhidden_ref,
+        swap_ref,
+        mid_ref,
+        z_ref,
+        zhat_ref,
+        h2_ref,
+        hat_ref,
+        h2p_ref,
+        act_ref,
+        slope_ref,
+        dact_ref,
+        acc_ref,
+        stat_ref,
+        down_tile,
+        flat_tile,
+        down_sem,
+        flat_sem,
+    ) = refs[2 * chips + 11 :]
+    step = pl.program_id(0)
+    chip, core = position[0], position[1]
+    block, model_width = tokens_ref.shape
+    share = model_width // chips
+    tile = wdown_ref.shape[0]
+    hidden = tile * tiles
+    root = math.sqrt(2.0 / math.pi)
+    phase, index = step // tiles, step % tiles
+    slot = lax.rem(index, 2)
+    chunks = down_keep.shape[0]
+    group = down_tile.shape[1]
+    flat = model_width // (2 * chunks)
+
+    def down_copies(where, tile_index):
+        area = pl.ds(group * tile_index, group)
+        return [
+            pltpu.make_async_copy(
+                down_tile.at[where, :, side], target.at[area], down_sem.at[where, which]
+            )
+            for which, (side, target) in enumerate(((core, down_keep), (1 - core, down_send)))
+        ]
+
+    def flat_copies(where, first_row):
+        area = (slice(None), pl.ds(first_row, flat))
+        return [
+            pltpu.make_async_copy(
+                flat_tile.at[where, which], target.at[area], flat_sem.at[where, which]
+            )
+            for which, target in enumerate((flat_keep, flat_send))
+        ]
+
+    def fill_flat(where, grad):
+        for which in range(2):
+            for chunk in range(chunks):
+                first = (which * chunks + chunk) * flat
+                flat_tile[where, which, chunk] = grad[first : first + flat].astype(jnp.bfloat16)
+
+    @pl.when(step == 0)
+    def _():
+        for near in range(chips):
+            start = pl.multiple_of(share * lax.rem(chip + near, chips), share)
+            swap_ref[pl.ds(start, share), :] = mixed[near][...].astype(jnp.float32)
+        zhat, zrate = norm_parts(swap_ref[...].T)
+        zhat_ref[...] = zhat
+        stat_ref[0] = jnp.broadcast_to(zrate, stat_ref.shape[1:])
+        z = (zhat * ginner_ref[...]).astype(jnp.bfloat16)
+        z_ref[...] = z
+        mid = tokens_ref[...].astype(jnp.float32) + nn_dot(z, wout_ref[...])
+        mid_ref[...] = mid
+        hat, rate = norm_parts(mid)
+        hat_ref[...] = hat
+        stat_ref[1] = jnp.broadcast_to(rate, stat_ref.shape[1:])
+        h2 = (hat * gfeed_ref[...]).astype(jnp.bfloat16)
+        h2_ref[...] = h2
+        h2p_ref[...] = nt_dot(perm_ref[...], h2).astype(jnp.bfloat16)
+
+    @pl.when(phase == 0)
+    def _():
+        u = nn_dot(h2_ref[...], wup_ref[...])
+        squared = u * u
+        bend = jnp.tanh(root * (u + 0.044715 * u * squared))
+        value = 0.5 * u * (1.0 + bend)
+        slope_ref[index] = 0.5 * (1.0 + bend) + 0.5 * u * (1.0 - bend * bend) * root * (
+            1.0 + 3.0 * 0.044715 * squared
+        )
+        act_ref[index] = value
+
+        @pl.when(index == 0)
+        def _():
+            stat_ref[2] = jnp.broadcast_to(
+                jnp.mean(value, axis=-1, keepdims=True), stat_ref.shape[1:]
+            )
+            stat_ref[3] = jnp.zeros_like(stat_ref[3])
+            stat_ref[4] = jnp.zeros_like(stat_ref[4])
+
+        off = value - stat_ref[2][:, :1]
+        stat_ref[3] += jnp.broadcast_to(
+            jnp.sum(off, axis=-1, keepdims=True), stat_ref.shape[1:]
+        )
+        stat_ref[4] += jnp.broadcast_to(
+            jnp.sum(off * off, axis=-1, keepdims=True), stat_ref.shape[1:]
+        )
+
+    @pl.when(step == tiles)
+    def _():
+        drift = stat_ref[3] / hidden
+        stat_ref[2] = stat_ref[2] + drift
+        stat_ref[4] = lax.rsqrt(jnp.maximum(stat_ref[4] / hidden - drift * drift, 0.0) + 1e-05)
+        stat_ref[5] = jnp.zeros_like(stat_ref[5])
+        stat_ref[6] = jnp.zeros_like(stat_ref[6])
+        acc_ref[...] = mid_ref[...]
+
+    @pl.when(phase == 1)
+    def _():
+        gain = ghidden_ref[...]
+        hat = (act_ref[index] - stat_ref[2][:, :1]) * stat_ref[4][:, :1]
+        act_ref[index] = hat
+        act = (hat * gain).astype(jnp.bfloat16)
+        cot = cot_ref[...]
+        acc_ref[...] += nn_dot(act, wdown_ref[...])
+        grad = nt_dot(cot, wdown_ref[...])
+        dhidden_ref[...] = jnp.sum(grad * hat, axis=0, keepdims=True)
+        scaled = grad * gain
+        dact_ref[index] = scaled
+        stat_ref[5] += jnp.broadcast_to(
+            jnp.sum(scaled, axis=-1, keepdims=True), stat_ref.shape[1:]
+        )
+        stat_ref[6] += jnp.broadcast_to(
+            jnp.sum(scaled * hat, axis=-1, keepdims=True), stat_ref.shape[1:]
+        )
+        grad = lax.dot_general(
+            act, cot, (((0,), (0,)), ((), ())), preferred_element_type=jnp.float32
+        )
+
+        @pl.when(index >= 2)
+        def _():
+            for copy in down_copies(slot, index - 2):
+                copy.wait()
+
+        for part in range(group):
+            for side in range(2):
+                first = (2 * part + side) * per
+                down_tile[slot, part, side] = grad[first : first + per].astype(jnp.bfloat16)
+        for copy in down_copies(slot, index):
+            copy.start()
+
+    @pl.when(step == 2 * tiles)
+    def _():
+        result_ref[...] = acc_ref[...].astype(jnp.bfloat16)
+        acc_ref[...] = jnp.zeros_like(acc_ref)
+
+    @pl.when(phase == 2)
+    def _():
+        inner = dact_ref[index] - (stat_ref[5][:, :1] + act_ref[index] * stat_ref[6][:, :1]) / hidden
+        pre = (stat_ref[4][:, :1] * inner * slope_ref[index]).astype(jnp.bfloat16)
+        grad = nn_dot(h2p_ref[...], pre)
+
+        @pl.when(index >= 2)
+        def _():
+            for copy in flat_copies(slot, flat * (index - 2)):
+                copy.wait()
+
+        fill_flat(slot, grad)
+        for copy in flat_copies(slot, flat * index):
+            copy.start()
+
+        acc_ref[...] += nt_dot(pre, wup_ref[...])
+
+    @pl.when(step == 3 * tiles - 1)
+    def _():
+        back, dfeed = norm_back(acc_ref[...], hat_ref[...], stat_ref[1][:, :1], gfeed_ref[...])
+        dfeed_ref[...] = dfeed
+        gmid = cot_ref[...].astype(jnp.float32) + back
+        gmid_ref[...] = gmid
+        gmid_b = gmid.astype(jnp.bfloat16)
+        zp = nt_dot(perm_ref[...], z_ref[...]).astype(jnp.bfloat16)
+        fill_flat(2, nn_dot(zp, gmid_b))
+        for copy in flat_copies(2, flat * tiles):
+            copy.start()
+        go, dinner = norm_back(
+            nt_dot(gmid_b, wout_ref[...]), zhat_ref[...], stat_ref[0][:, :1], ginner_ref[...]
+        )
+        dinner_ref[...] = dinner
+        swap_ref[...] = go.T
+        for near in range(chips):
+            start = pl.multiple_of(share * lax.rem(chip + near, chips), share)
+            go_refs[near][...] = swap_ref[pl.ds(start, share), :].astype(jnp.bfloat16)
+        for late in range(tiles - min(tiles, 2), tiles):
+            for copy in down_copies(late % 2, late) + flat_copies(late % 2, flat * late):
+                copy.wait()
+        for copy in flat_copies(2, flat * tiles):
+            copy.wait()
+
+
+def middle(position, mixed, tokens, cotangent, w_out, w_up, w_down, perm, gains, per):
+    chips = len(mixed)
+    block, model_width = tokens.shape
+    hidden = w_up.shape[1]
+    tile = model_width
+    tiles = hidden // tile
+    share = model_width // chips
+    chunks, last = hidden // (2 * per), tiles - 1
+    flat, group = model_width // (2 * chunks), chunks // tiles
+    down_out = jax.ShapeDtypeStruct((chunks, per, model_width), jnp.bfloat16)
+    flat_out = jax.ShapeDtypeStruct((chunks, flat * (tiles + 1), model_width), jnp.bfloat16)
+
+    def up_index(i, pos):
+        return (0, jnp.where(i < tiles, i, jnp.where(i < 2 * tiles, last, i - 2 * tiles)))
+
+    def down_index(i, pos):
+        return (jnp.clip(i - tiles, 0, last), 0)
+
+    def hidden_index(i, pos):
+        return (0, jnp.clip(i - tiles, 0, last))
+
+    def f32(*shape):
+        return pltpu.VMEM(shape, jnp.float32)
+
+    def b16(*shape):
+        return pltpu.VMEM(shape, jnp.bfloat16)
+
+    square = (model_width, model_width)
+    row = (1, model_width)
+    return pl.pallas_call(
+        partial(middle_kernel, chips, tiles, per),
+        grid_spec=pltpu.PrefetchScalarGridSpec(
+            num_scalar_prefetch=1,
+            grid=(3 * tiles,),
+            in_specs=[whole((share, block))] * chips
+            + [
+                whole((block, model_width)),
+                whole((block, model_width)),
+                whole(square),
+                pl.BlockSpec((model_width, tile), up_index),
+                pl.BlockSpec((tile, model_width), down_index),
+                whole(square),
+                whole(row),
+                whole(row),
+                pl.BlockSpec((1, tile), hidden_index),
+            ],
+            out_specs=[whole((block, model_width)), whole((block, model_width))]
+            + [whole((share, block))] * chips
+            + [
+                pl.BlockSpec(memory_space=pl.ANY),
+                pl.BlockSpec(memory_space=pl.ANY),
+                pl.BlockSpec(memory_space=pl.ANY),
+                pl.BlockSpec(memory_space=pl.ANY),
+                whole(row),
+                whole(row),
+                pl.BlockSpec((1, tile), hidden_index),
+            ],
+            scratch_shapes=[
+                f32(model_width, block),
+                f32(block, model_width),
+                b16(block, model_width),
+                f32(block, model_width),
+                b16(block, model_width),
+                f32(block, model_width),
+                b16(model_width, block),
+                f32(tiles, block, tile),
+                f32(tiles, block, tile),
+                f32(tiles, block, tile),
+                f32(block, model_width),
+                f32(7, block, 128),
+                b16(2, group, 2, per, model_width),
+                b16(3, 2, chunks, flat, model_width),
+                pltpu.SemaphoreType.DMA((2, 2)),
+                pltpu.SemaphoreType.DMA((3, 2)),
+            ],
+        ),
+        out_shape=[
+            jax.ShapeDtypeStruct((block, model_width), jnp.bfloat16),
+            jax.ShapeDtypeStruct((block, model_width), jnp.float32),
+        ]
+        + [jax.ShapeDtypeStruct((share, block), jnp.bfloat16)] * chips
+        + [
+            down_out,
+            down_out,
+            flat_out,
+            flat_out,
+            jax.ShapeDtypeStruct(row, jnp.float32),
+            jax.ShapeDtypeStruct(row, jnp.float32),
+            jax.ShapeDtypeStruct((1, hidden), jnp.float32),
+        ],
+        compiler_params=pltpu.CompilerParams(vmem_limit_bytes=56 << 20),
+        cost_estimate=pl.CostEstimate(flops=16 * 10**9, bytes_accessed=40 << 20, transcendentals=0),
+        name="middle",
+    )(position, *mixed, tokens, cotangent, w_out, w_up, w_down, perm, *gains)
+
+
+def final_kernel(chips, position, *refs):
+    homes = refs[:chips]
+    (
+        tokens_ref,
+        gmid_ref,
+        wq_ref,
+        wk_ref,
+        wv_ref,
+        gain_ref,
+        out_ref,
+        swap_ref,
+    ) = refs[chips:]
+    chip = position[0]
+    block, model_width = tokens_ref.shape
+    share = model_width // chips
+    total = jnp.zeros((block, model_width), jnp.float32)
+    for index, weight in enumerate((wq_ref, wk_ref, wv_ref)):
+        for near in range(chips):
+            start = pl.multiple_of(share * lax.rem(chip + near, chips), share)
+            swap_ref[pl.ds(start, share), :] = homes[near][
+                index * share : (index + 1) * share, :
+            ].astype(jnp.float32)
+        total = total + nt_dot(swap_ref[...].T.astype(jnp.bfloat16), weight[...])
+    hat, rate = norm_parts(tokens_ref[...].astype(jnp.float32))
+    back = norm_back(total, hat, rate, gain_ref[...])[0]
+    out_ref[...] = (gmid_ref[...] + back).astype(jnp.bfloat16)
+
+
+def final(position, homes, tokens, gmid, w_query, w_key, w_value, gain):
+    block, model_width = tokens.shape
+    vmem = pl.BlockSpec(memory_space=pltpu.VMEM)
+    return pl.pallas_call(
+        partial(final_kernel, len(homes)),
+        in_specs=[pl.BlockSpec(memory_space=pltpu.SMEM)] + [vmem] * (len(homes) + 6),
+        out_specs=vmem,
+        out_shape=jax.ShapeDtypeStruct((block, model_width), jnp.bfloat16),
+        scratch_shapes=[pltpu.VMEM((model_width, block), jnp.float32)],
+        compiler_params=pltpu.CompilerParams(vmem_limit_bytes=24 << 20),
+        name="final",
+    )(position, *homes, tokens, gmid, w_query, w_key, w_value, gain)
+
+
+def chip_shift(value, steps):
+    count = lax.axis_size("seq")
+    return lax.ppermute(value, "seq", [(i, (i + 2 * steps) % count) for i in range(count)])
+
+
+def seq_swap(value, bit):
+    return lax.ppermute(value, "seq", [(i, i ^ bit) for i in range(lax.axis_size("seq"))])
+
+
+def row_swap(value, bit):
+    return lax.ppermute(value, "row", [(i, i ^ bit) for i in range(lax.axis_size("row"))])
+
+
+def pick(array, index, axis):
+    return lax.dynamic_index_in_dim(array, index, axis, keepdims=False)
+
+
+def rolled(blocks, start):
+    count = blocks.shape[0]
+    return lax.dynamic_slice_in_dim(jnp.concatenate([blocks, blocks], axis=0), start, count, axis=0)
+
+
+def sent(array):
+    return array.astype(jnp.bfloat16)
+
+
+def wide(array):
+    return array.astype(jnp.float32)
+
+
+def total_of(*terms):
+    result = wide(terms[0])
+    for term in terms[1:]:
+        result = result + wide(term)
+    return sent(result)
+
+
+def corner(term, low, high, second):
+    half = term.shape[1] // 2
+    rest = term.shape[2:]
+    shaped = term.reshape((2, 2) + term.shape[1:])
+    starts = (0 if high is None else high, 0 if low is None else low, half * second)
+    sizes = (2 if high is None else 1, 2 if low is None else 1, half)
+    part = lax.dynamic_slice(shaped, starts + (0,) * len(rest), sizes + rest)
+    return part.reshape((2, half) + rest)
+
+
+def row_first(terms, row):
+    low_bit, high_bit = row % 2, row // 2
+    low = row_swap(total_of(*[corner(term, 1 - low_bit, None, 0) for term in terms]), 1)
+    high = row_swap(total_of(*[corner(term, None, 1 - high_bit, 1) for term in terms]), 2)
+    return low, high
+
+
+def row_middle(terms, low, high, row):
+    low_bit, high_bit = row % 2, row // 2
+    return (
+        total_of(*[corner(term, low_bit, None, 0) for term in terms], low),
+        total_of(*[corner(term, None, high_bit, 1) for term in terms], high),
+    )
+
+
+def row_second(first, second, row):
+    low_bit, high_bit = row % 2, row // 2
+    low = row_swap(pick(first, 1 - high_bit, 0), 2)
+    high = row_swap(pick(second, 1 - low_bit, 0), 1)
+    return jnp.concatenate(
+        [total_of(pick(first, high_bit, 0), low), total_of(pick(second, low_bit, 0), high)], axis=0
+    )
+
+
+def fast_local(
+    tokens,
+    lengths,
+    w_query,
+    w_key,
+    w_value,
+    w_out,
+    w_up,
+    w_down,
+    gain_attend,
+    gain_inner,
+    gain_feed,
+    gain_hidden,
+    cotangent,
+):
+    block, model_width = tokens.shape
+    hidden = w_up.shape[1]
+    size = model_width // HEADS
+    lanes = 2 * size
+    scale = size ** (-0.5)
+    seq_devices, row_devices = lax.axis_size("seq"), lax.axis_size("row")
+    chips = seq_devices // 2
+    heads = HEADS // chips
+    share = heads * size
+    spread = heads * lanes
+    parts = row_devices * seq_devices
+    position, row = lax.axis_index("seq"), lax.axis_index("row")
+    chip, core = position // 2, position % 2
+    place = jnp.stack([chip, core]).astype(jnp.int32)
+    bounds = jnp.cumsum(lengths[0])[:-1]
+    factor = 1.0 / math.sqrt(block * parts)
+
+    normed_b = layer_norm(tokens.astype(jnp.float32), gain_attend).astype(jnp.bfloat16)
+    own = [normed_b] + [chip_shift(normed_b, step) for step in range(1, chips)]
+
+    chip_ids = (chip - jnp.arange(chips, dtype=jnp.int32)) % chips
+    query_starts = block * (2 * chip_ids + core)
+    key_starts = jnp.concatenate([query_starts, block * (2 * chip_ids + 1 - core)])
+    in_block = jnp.arange(block, dtype=jnp.int32)[None, :]
+    query_places = (query_starts[:, None] + in_block).reshape(-1)
+    doc_line = jnp.max(jnp.where(bounds[:, None] <= query_places[None, :], bounds[:, None], 0), axis=0)
+    meta = jnp.concatenate([query_starts, key_starts, doc_line.reshape(chips, block)[:, 0]])
+    doc_line = doc_line[None, :]
+
+    feature = jnp.arange(model_width, dtype=jnp.int32)
+    wide_lane = jnp.arange(spread, dtype=jnp.int32)
+    source = chip * share + wide_lane // lanes * size + wide_lane % lanes
+    pick_wide = ((feature[:, None] == source[None, :]) & (wide_lane % lanes < size)[None, :]).astype(
+        jnp.bfloat16
+    )
+    narrow = chip * share + jnp.arange(share, dtype=jnp.int32)
+    pick_narrow = (feature[:, None] == narrow[None, :]).astype(jnp.bfloat16)
+
+    def picked(weight, choice):
+        return sent(nn_dot(weight, choice))
+
+    def picked_rows(weight, choice):
+        return sent(
+            lax.dot_general(
+                choice, weight, (((0,), (1,)), ((), ())), preferred_element_type=jnp.float32
+            )
+        )
+
+    per = model_width // parts
+    order = jnp.arange(model_width, dtype=jnp.int32)
+    chunk, inside = order // per, order % per
+    chunks = parts // 2
+    parity = jnp.where(chunk < chunks, core, 1 - core)
+    wanted = (2 * (chunk % chunks) + parity) * per + inside
+    perm = (wanted[:, None] == feature[None, :]).astype(jnp.bfloat16)
+
+    masks, owners, query_values, key_values = extra_features(heads, size, lanes)
+    head_ids = heads * chip + jnp.asarray(owners)
+    info = jnp.stack([jnp.asarray(masks), head_ids])
+    early = (
+        jnp.concatenate([query_starts, key_starts]),
+        meta,
+        doc_line,
+        perm,
+        picked_rows(w_query, pick_wide),
+        picked(w_key, pick_wide),
+        picked_rows(w_value, pick_narrow),
+        picked_rows(w_key, pick_narrow),
+        picked(w_value, pick_wide),
+        jnp.concatenate([picked(weight, pick_narrow) for weight in (w_query, w_key, w_value)], axis=1),
+        info,
+        info.T,
+        gain_attend[None, :],
+        gain_inner[None, :],
+        gain_feed[None, :],
+        gain_hidden[None, :],
+        place,
+    )
+    own[1], early = lax.optimization_barrier((own[1], early))
+    starts, meta, doc_line, perm, wq_wide, wk_wide, wv_rows, wk_rows, wv_wide, w_own = early[:10]
+    info, info_t, gain_first, gain_inner, gain_feed, gain_hidden, place = early[10:]
+    sibling = [seq_swap(rows, 1) for rows in own]
+    q_ext, k_ext, v_t = project(
+        starts,
+        own + sibling,
+        wq_wide,
+        wk_wide,
+        wv_rows,
+        info_t,
+        info,
+        jnp.asarray(query_values)[:, None],
+        jnp.asarray(key_values)[None, :],
+        chips,
+        scale,
+    )
+    mixed, mixed_b, lse = attend(meta, doc_line, q_ext, k_ext, v_t, heads, block)
+    back = [mixed_b[0]] + [chip_shift(mixed_b[step], -step) for step in range(1, chips)]
+
+    own_normed = jnp.concatenate(own, axis=0)
+    k_t, v_ext = project_back(own + sibling, wk_rows, wv_wide)
+    normed_p = sent(nt_dot(perm, own_normed))
+    weights_p = sent(nn_dot(perm, w_own))
+    back, k_t, v_ext, normed_p, weights_p = lax.optimization_barrier(
+        (back, k_t, v_ext, normed_p, weights_p)
+    )
+
+    outs = middle(
+        place,
+        back,
+        tokens,
+        cotangent,
+        w_out,
+        w_up,
+        w_down,
+        perm,
+        (gain_inner, gain_feed, gain_hidden),
+        hidden // parts,
+    )
+    result, grad_middle = outs[:2]
+    go = outs[2 : 2 + chips]
+    keep_a, send_a, keep_b, send_b, dinner, dfeed, dhidden = outs[2 + chips :]
+
+    def gridded(array):
+        return array.reshape((row_devices, chips) + array.shape[1:])
+
+    other_a, other_b = seq_swap(send_a, 1), seq_swap(send_b, 1)
+    grad_t = jnp.concatenate(
+        [go[0]] + [chip_shift(go[step], step) for step in range(1, chips)], axis=1
+    )
+    grad_t, keep_a, other_a, keep_b, other_b = lax.optimization_barrier(
+        (grad_t, keep_a, other_a, keep_b, other_b)
+    )
+    terms_a, terms_b = [gridded(keep_a), gridded(other_a)], [gridded(keep_b), gridded(other_b)]
+    low_a, high_a = row_first(terms_a, row)
+    dq, dk, dv = attend_back(
+        meta, doc_line, q_ext, grad_t, mixed, lse, k_ext, k_t, v_ext, heads, block, scale
+    )
+    dq, dk, dv, low_a, high_a, keep_b, other_b = lax.optimization_barrier(
+        (dq, dk, dv, low_a, high_a, keep_b, other_b)
+    )
+    terms_b = [gridded(keep_b), gridded(other_b)]
+    low_b, high_b = row_first(terms_b, row)
+    mine = chips * block
+    pair = jnp.concatenate([dk, dv], axis=0)
+    pair_mine = pair[:, :mine] + wide(seq_swap(sent(pair[:, mine:]), 1))
+    grads_t = jnp.concatenate([dq, sent(pair_mine)], axis=0)
+
+    home = [grads_t[:, :block]] + [
+        chip_shift(grads_t[:, step * block : (step + 1) * block], -step) for step in range(1, chips)
+    ]
+
+    own_grad = nt_dot(normed_p, grads_t)
+    dattend = jnp.sum(own_grad * wide(weights_p), axis=1).reshape(2, parts // 2, 1, per)
+    dattend = jnp.where(core == 0, dattend, dattend[::-1])
+    dattend = jnp.concatenate([dattend[0], dattend[1]], axis=1).reshape(1, model_width)
+    dattend = dattend / gain_first
+    gains_all = jnp.concatenate([dattend, dinner, dfeed, dhidden], axis=1)
+
+    gains_share = gains_all.shape[1] // parts
+    gains_rows = -(-gains_share // 128)
+    gains_all = gains_all.reshape(parts // 2, 2, gains_share)
+    gains_all = jnp.where(core == 0, gains_all, gains_all[:, ::-1]).transpose(1, 0, 2)
+    gains_all = jnp.pad(gains_all, ((0, 0), (0, 0), (0, gains_rows * 128 - gains_share)))
+    gains_all = jnp.pad(
+        gains_all.reshape(parts, gains_rows, 128), ((0, 0), (0, per - gains_rows), (0, 0))
+    ).reshape(model_width, 128)
+    gap = jnp.zeros((model_width, model_width - 128 - 3 * share), jnp.float32)
+    packed = sent(jnp.concatenate([own_grad, gap, gains_all], axis=1))
+    half = model_width // 2
+    mine_grad = packed[:half].reshape(parts // 2, per, model_width)
+    other_grad = seq_swap(packed[half:].reshape(parts // 2, per, model_width), 1)
+    low_a, high_a, low_b, high_b, mine_grad, other_grad, home[1] = lax.optimization_barrier(
+        (low_a, high_a, low_b, high_b, mine_grad, other_grad, home[1])
+    )
+    heads_terms = [gridded(mine_grad), gridded(other_grad)]
+    first, second = row_middle(terms_b, low_b, high_b, row)
+    stage_a = row_second(*row_middle(terms_a, low_a, high_a, row), row)
+    heads_first, heads_second = row_middle(heads_terms, *row_first(heads_terms, row), row)
+    home, stage_a, first, second, heads_first, heads_second = lax.optimization_barrier(
+        (home, stage_a, first, second, heads_first, heads_second)
+    )
+    grad_input = final(
+        place, home, tokens, grad_middle, w_query, w_key, w_value, gain_first
+    )
+    stage_b = row_second(
+        jnp.concatenate([first, heads_first], axis=2),
+        jnp.concatenate([second, heads_second], axis=2),
+        row,
+    )
+
+    def from_chips(stage):
+        return [pick(stage, chip, 0)] + [
+            chip_shift(pick(stage, (chip + step) % chips, 0), step) for step in range(1, chips)
+        ]
+
+    total_a = sum(wide(part) for part in from_chips(stage_a)) * factor
+    arrived = from_chips(stage_b)
+    ends = stage_b.shape[1] - per
+    total_b = sum(wide(part[:ends]) for part in arrived) * factor
+    gains_part = sum(wide(part[ends : ends + gains_rows, -128:]) for part in arrived) * factor
+    gains_part = gains_part.reshape(-1)[:gains_share]
+    home = jnp.stack([part[ends:, : 3 * share] for part in arrived[::-1]])
+    home = rolled(home, (chips - 1 - chip) % chips)
+    home = wide(home.reshape(chips, per, 3, share)).transpose(2, 1, 0, 3)
+    home = home.reshape(3, per * model_width) * factor
+
+    tiles = hidden // model_width
+    done_up = total_b[: per * tiles].reshape(tiles, per, model_width)
+    return (
+        result,
+        grad_input,
+        home[0],
+        home[1],
+        home[2],
+        total_b[per * tiles :].reshape(-1),
+        done_up.transpose(1, 0, 2).reshape(-1),
+        total_a.reshape(-1),
+        gains_part,
+    )
+
+
+def local(*arrays):
+    seq_devices, row_devices = lax.axis_size("seq"), lax.axis_size("row")
+    block = arrays[0].shape[0]
+    one_segment = block * seq_devices <= SEGMENT and block % 2 ** (PATTERNS - 1) == 0
+    if one_segment and seq_devices in (2, 4, 8) and row_devices == 4:
+        return fast_local(*arrays)
+    return ring_local(*arrays)
+
+
 def solution(mesh):
     return jax.shard_map(
         local,

time: 1900 us -> 232 us (0.12); the launches traced: 1870 us -> 231 us
  waiting for transfers between devices: 830 us -> 50.6 us
  starting transfers between devices: 413 us -> 46.7 us
  local copies, waits for them, and re-layouts: 344 us -> 23.5 us
  blocking collectives: 84.2 us -> 0 us
  matrix products: 91.9 us -> 15.9 us
  Pallas kernels: 0 us -> 60.7 us
  other arithmetic: 89.5 us -> 31.7 us
    ppermute x44 -> x36, waiting for transfers between devices: 448 us -> 50.6 us  [the longest x18 36.4 us: chip_shift(): lax.ppermute(value, 'seq', [(i, (i + 2 * steps) % count) for i in range(c...]
    unnamed x2 -> x0, waiting for transfers between devices: 382 us -> none
    ppermute x44 -> x36, starting transfers between devices: 413 us -> 46.7 us  [the longest x18 33.6 us: chip_shift(): lax.ppermute(value, 'seq', [(i, (i + 2 * steps) % count) for i in range(c...]
    broadcast_in_dim x118 -> x4, local copies, waits for them, and re-layouts: 137 us -> 1.17 us  [the longest x1 0.58 us: fast_local(): gain_inner[None, :]]
    unnamed x1 -> x0, blocking collectives: 84.2 us -> none
    dot_general x48 -> x9, matrix products: 91.9 us -> 15.9 us  [the longest x4 7.57 us: nn_dot(): return jnp.dot(left, right, preferred_element_type=jnp.float32)]
    while x203 -> x0, local copies, waits for them, and re-layouts: 67.4 us -> none
    pallas_call x0 -> x6, Pallas kernels: none -> 60.7 us  [the longest x1 26.2 us: middle(): pl.pallas_call(partial(middle_kernel, chips, tiles, per), grid_spec=pltpu...]
  transfers between devices with their start and end apart: 45 -> 36, of which waited for: 29 -> 12; matrix products, arithmetic and copies ran while one was open for 12% -> 21% of each run, Pallas kernels for 0% -> 8%
where the time goes in v1:
time: 232 us; the launch traced here: 231 us
  Pallas kernels  60.7 us (26%)
  waiting for transfers between devices  50.6 us (22%)
  starting transfers between devices  46.7 us (20%)
  other arithmetic  31.7 us (14%)
  local copies, waits for them, and re-layouts  23.5 us (10%)
  matrix products  15.9 us (7%)
    ppermute x18, waiting for transfers between devices, chip_shift(): lax.ppermute(value, 'seq', [(i, (i + 2 * steps) % count) for i in range(c...  36.4 us
    ppermute x18, starting transfers between devices, chip_shift(): lax.ppermute(value, 'seq', [(i, (i + 2 * steps) % count) for i in range(c...  33.6 us
    pallas_call x1, Pallas kernels, middle(): pl.pallas_call(partial(middle_kernel, chips, tiles, per), grid_spec=pltpu...  26.2 us
    convert_element_type x14, other arithmetic, sent(): return array.astype(jnp.bfloat16)  19.5 us
    ppermute x10, waiting for transfers between devices, row_swap(): lax.ppermute(value, 'row', [(i, i ^ bit) for i in range(lax.axis_size('ro...  14.3 us
    pallas_call x1, Pallas kernels, attend_back(): pl.pallas_call(partial(attend_back_kernel, heads, block, key_blocks, scal...  11.7 us
    ppermute x10, starting transfers between devices, row_swap(): lax.ppermute(value, 'row', [(i, i ^ bit) for i in range(lax.axis_size('ro...  11 us
    pallas_call x1, Pallas kernels, attend(): pl.pallas_call(partial(attend_kernel, heads, block, key_blocks), grid_spe...  10.9 us
  transfers between devices with their start and end apart: 36, of which 12 were waited for; matrix products, arithmetic and copies ran while one was open for 21% of the time, Pallas kernels for 8%

profile of v1, /device:TPU:0, one launch (start us, length us, event | category | flops | bytes accessed | tf_op | source)
XLA Modules:
  0.0 230.8 jit_solution(14287287933126716056)
XLA Ops:
  4.4 3.1 %collective-permute-start = (bf16[256,768]{1,0:T(8,128)(2,1)S(1)}, bf16[256,768]{1,0:T(8,128)(2,1)}, u32[]{:S(2)}, u32[]{:S(2)}) collective-permute-start(bf16[256,768]{1,0:T(8,128)(2,1)S(1)} %fusion.27.refs_0_), channel_id=1, source_target_pairs={{0,2},{1,3},{2,4},{3,5},{4,6},{5,7},{6,0},{7,1},{8,10},{9,11},{10,... | collective-permute-start | bytes 1179656 | tf_op jit(solution)/shard_map/ppermute | solution.py:1217
  7.5 2.6 %collective-permute-start.1 = (bf16[256,768]{1,0:T(8,128)(2,1)S(1)}, bf16[256,768]{1,0:T(8,128)(2,1)}, u32[]{:S(2)}, u32[]{:S(2)}) collective-permute-start(bf16[256,768]{1,0:T(8,128)(2,1)S(1)} %fusion.27.refs_0_), channel_id=1, source_target_pairs={{0,4},{1,5},{2,6},{3,7},{4,0},{5,1},{6,2},{7,3},{8,12},{9,13},{10,... | collective-permute-start | bytes 1179656 | tf_op jit(solution)/shard_map/ppermute | solution.py:1217
  18.7 1.9 pad_maximum_fusion.3
  24.8 10.9 %collective-permute-done.1.refs_2_ = bf16[256,768]{1,0:T(8,128)(2,1)} collective-permute-done((bf16[256,768]{1,0:T(8,128)(2,1)S(1)}, bf16[256,768]{1,0:T(8,128)(2,1)}, u32[]{:S(2)}, u32[]{:S(2)}) %collective-permute-start.1) | collective-permute-done | bytes 393248 | tf_op jit(solution)/shard_map/ppermute | solution.py:1217
  35.7 3.0 %convolution_convert_fusion.1 = bf16[768,576]{0,1:T(8,128)(2,1)} fusion(bf16[768,768]{1,0:T(8,128)(2,1)S(1)} %fusion.refs_9_, bf16[768,576]{0,1:T(8,128)(2,1)} %pad_maximum_fusion.3), kind=kOutput, calls=%fused_computation.25 | convolution fusion | flops 679919616 | bytes 2949120 | tf_op jit(solution)/shard_map/dot_general | solution.py:573
  39.3 3.8 %convolution_convert_fusion = bf16[768,1024]{1,0:T(8,128)(2,1)} fusion(bf16[768,768]{1,0:T(8,128)(2,1)S(1)} %fusion.refs_9_, bf16[256,768]{1,0:T(8,128)(2,1)} %collective-permute-done.2.refs_3_, bf16[256,768]{1,0:T(8,128)(2,1)} %collective-permute-done.1.refs_2_, bf16[256,768]{1,0:T(8,128)(2,1)} %collective-permute-done.refs_1_, ...), kind=kOutput, calls=%fused_computation.8 | convolution fusion | flops 1215037440 | bytes 4325376 | tf_op jit(solution)/shard_map/dot_general | solution.py:567
  43.2 4.8 %project.1 = (bf16[384,1024]{1,0:T(8,128)(2,1)S(1)}, bf16[2048,384]{1,0:T(8,128)(2,1)S(1)}, bf16[192,2048]{1,0:T(8,128)(2,1)S(1)}) custom-call(s32[12]{0:T(128)S(1)} %pad_add_fusion.1.meta, bf16[256,768]{1,0:T(8,128)(2,1)S(1)} %fusion.27.refs_0_, bf16[256,768]{1,0:T(8,128)(2,1)} %collective-permute-done.refs_1_, ...), custom_call_target="tpu_custom_call" | custom-call | tf_op jit(solution)/shard_map/project/pallas_call | solution.py:606
  48.1 10.9 %attend.1 = (f32[192,1024]{1,0:T(8,128)S(1)}, bf16[4,192,256]{2,1,0:T(8,128)(2,1)S(1)}, f32[3,1,1024]{2,1,0:T(1,128)S(1)}) custom-call(s32[16]{0:T(128)S(1)} %pad_add_fusion.2.meta, s32[1,1024]{1,0:T(1,128)S(1)} %bitcast.179, bf16[384,1024]{1,0:T(8,128)(2,1)S(1)} %get-tuple-element.97.q_ref, bf16[2048,384]{1,0:T(8,128)(2,1)S(1)} %get-tuple-element.98.k_ref, ...), custom_call_target="tpu_custom_call" | custom-call | flops 8000000000 | bytes 8388608 | tf_op jit(solution)/shard_map/attend/pallas_call | solution.py:771
  60.3 10.0 %collective-permute-start.7 = (bf16[192,256]{1,0:T(8,128)(2,1)S(1)}, bf16[192,256]{1,0:T(8,128)(2,1)S(1)}, u32[]{:S(2)}, u32[]{:S(2)}) collective-permute-start(bf16[192,256]{1,0:T(8,128)(2,1)S(1)} %get-tuple-element.191), channel_id=1, source_target_pairs={{0,6},{1,7},{2,0},{3,1},{4,2},{5,3},{6,4},{7,5},{8,14},{9,15},{10,... | collective-permute-start | bytes 294920 | tf_op jit(solution)/shard_map/ppermute | solution.py:1217
  70.8 4.0 %project_back.1 = (bf16[192,2048]{1,0:T(8,128)(2,1)S(1)}, bf16[2048,384]{1,0:T(8,128)(2,1)S(1)}) custom-call(bf16[256,768]{1,0:T(8,128)(2,1)S(1)} %fusion.27.refs_0_, bf16[256,768]{1,0:T(8,128)(2,1)} %collective-permute-done.refs_1_, bf16[256,768]{1,0:T(8,128)(2,1)} %collective-permute-done.1.refs_2_, bf16[256,768]{1,0:T(8,128)(2,1)} %collective-permute-done.2.refs_3_, ...), custom_call_target="tpu_custom_call" | custom-call | flops 3000000000 | bytes 6291456 | tf_op jit(solution)/shard_map/project_back/pallas_call | solution.py:634
  75.8 3.8 %collective-permute-done.8.refs_2_ = bf16[192,256]{1,0:T(8,128)(2,1)S(1)} collective-permute-done((bf16[192,256]{1,0:T(8,128)(2,1)S(1)}, bf16[192,256]{1,0:T(8,128)(2,1)S(1)}, u32[]{:S(2)}, u32[]{:S(2)}) %collective-permute-start.8) | collective-permute-done | bytes 98336 | tf_op jit(solution)/shard_map/ppermute | solution.py:1217
  80.2 26.2 %middle.1 = (bf16[256,768]{1,0:T(8,128)(2,1)}, f32[256,768]{1,0:T(8,128)}, bf16[192,256]{1,0:T(8,128)(2,1)}, bf16[192,256]{1,0:T(8,128)(2,1)}, bf16[192,256]{1,0...) custom-call(s32[2]{0:T(128)} %pad_add_fusion.3.position, ...), custom_call_target="tpu_custom_call" | custom-call | flops 16000000000 | bytes 41943040 | tf_op jit(solution)/shard_map/middle/pallas_call | solution.py:1106
  106.9 1.9 collective-permute-start.12
  109.1 1.9 collective-permute-start.10
  112.3 6.7 %collective-permute-done.11 = bf16[192,256]{1,0:T(8,128)(2,1)S(1)} collective-permute-done((bf16[192,256]{1,0:T(8,128)(2,1)}, bf16[192,256]{1,0:T(8,128)(2,1)S(1)}, u32[]{:S(2)}, u32[]{:S(2)}) %collective-permute-start.11) | collective-permute-done | bytes 98336 | tf_op jit(solution)/shard_map/ppermute | solution.py:1217
  124.5 11.7 %attend_back.1 = (bf16[192,1024]{1,0:T(8,128)(2,1)S(1)}, f32[192,2048]{1,0:T(8,128)S(1)}, f32[192,2048]{1,0:T(8,128)S(1)}) custom-call(s32[16]{0:T(128)S(1)} %pad_add_fusion.2.meta, s32[1,1024]{1,0:T(1,128)S(1)} %bitcast.180, bf16[384,1024]{1,0:T(8,128)(2,1)S(1)} %copy-done.9, bf16[192,1024]{1,0:T(8,128)(2,1)S(1)} %pad_maximum_fusion.5.g_ref, ...), custom_call_target="tpu_custom_call" | custom-call | flops 1000000 | bytes 1024 | tf_op jit(solution)/shard_map/attend_back/pallas_call | solution.py:807
  140.3 2.5 %fusion.29 = bf16[2,2,120,768]{3,2,1,0:T(8,128)(2,1)} fusion(bf16[2,2,4,120,768]{4,3,2,1,0:T(8,128)(2,1)} %bitcast.21, s32[]{:T(128)S(6)} %select_n.228, bf16[2,2,4,120,768]{4,3,2,1,0:T(8,128)(2,1)} %bitcast.181), kind=kLoop, calls=%fused_computation.72 | loop fusion | flops 1474560 | bytes 2211844 | tf_op jit(solution)/shard_map/convert_element_type | solution.py:1238
  144.1 2.4 %fusion.30 = bf16[2,2,120,768]{3,2,1,0:T(8,128)(2,1)} fusion(bf16[2,2,4,120,768]{4,3,2,1,0:T(8,128)(2,1)} %bitcast.21, s32[]{:T(128)S(6)} %select_n.230, bf16[2,2,4,120,768]{4,3,2,1,0:T(8,128)(2,1)} %bitcast.182), kind=kLoop, calls=%fused_computation.73 | loop fusion | flops 1474560 | bytes 2211844 | tf_op jit(solution)/shard_map/convert_element_type | solution.py:1238
  153.6 1.8 collective-permute-start.21
  156.9 4.7 %collective-permute-done.18 = bf16[2,2,120,768]{3,2,1,0:T(8,128)(2,1)} collective-permute-done((bf16[2,2,120,768]{3,2,1,0:T(8,128)(2,1)}, bf16[2,2,120,768]{3,2,1,0:T(8,128)(2,1)}, u32[]{:S(2)}, u32[]{:S(2)}) %collective-permute-start.18) | collective-permute-done | bytes 737312 | tf_op jit(solution)/shard_map/ppermute | solution.py:1225
  162.8 2.6 %collective-permute-done.19 = bf16[2,2,120,768]{3,2,1,0:T(8,128)(2,1)} collective-permute-done((bf16[2,2,120,768]{3,2,1,0:T(8,128)(2,1)}, bf16[2,2,120,768]{3,2,1,0:T(8,128)(2,1)}, u32[]{:S(2)}, u32[]{:S(2)}) %collective-permute-start.19) | collective-permute-done | bytes 737312 | tf_op jit(solution)/shard_map/ppermute | solution.py:1225
  167.4 2.6 %fusion.15 = (bf16[2,2,96,768]{3,2,1,0:T(8,128)(2,1)S(1)}, bf16[2,2,96,768]{3,2,1,0:T(8,128)(2,1)S(1)}) fusion(bf16[2,2,96,768]{3,2,1,0:T(8,128)(2,1)} %copy-done.40, bf16[2,2,4,96,768]{4,3,2,1,0:T(8,128)(2,1)} %bitcast.17, s32[]{:T(128)S(6)} %select_n.235, bf16[2,2,4,96,768]{4,3,2,1,0:T(8,128)(2,1)} %bitcast.186, bf16[2,2,96,768]{3,2,1,0:T(8,128)(2,1)} %copy-done.41, ...), kind=kLoop, calls=%fused_computation.51 | loop fusion | flops 3538944 | bytes 4718600 | tf_op jit(solution)/shard_map/convert_element_type | solution.py:1238
  171.6 1.7 collective-permute-start.26
  173.4 2.3 %fusion.9 = (bf16[2,2,120,768]{3,2,1,0:T(8,128)(2,1)S(1)}, bf16[2,2,120,768]{3,2,1,0:T(8,128)(2,1)S(1)}) fusion(bf16[2,2,120,768]{3,2,1,0:T(8,128)(2,1)} %collective-permute-done.19, bf16[2,2,4,120,768]{4,3,2,1,0:T(8,128)(2,1)} %bitcast.21, s32[]{:T(128)S(6)} %select_n.236, bf16[2,2,4,120,768]{4,3,2,1,0:T(8,128)(2,1)S(1)} %bitcast.183, ...), kind=kLoop, calls=%fused_computation.20 | loop fusion | flops 4423680 | bytes 5898248 | tf_op jit(solution)/shard_map/convert_element_type | solution.py:1238
  176.8 4.7 %collective-permute-done.26 = bf16[2,2,24,768]{3,2,1,0:T(8,128)(2,1)S(1)} collective-permute-done((bf16[2,2,24,768]{3,2,1,0:T(8,128)(2,1)S(1)}, bf16[2,2,24,768]{3,2,1,0:T(8,128)(2,1)S(1)}, u32[]{:S(2)}, u32[]{:S(2)}) %collective-permute-start.26) | collective-permute-done | bytes 147488 | tf_op jit(solution)/shard_map/ppermute | solution.py:1225
  189.4 1.7 collective-permute-start.29
  192.1 1.9 collective-permute-start.35
  195.3 1.9 collective-permute-start.33
  201.6 3.2 %final.1 = bf16[256,768]{1,0:T(8,128)(2,1)} custom-call(s32[2]{0:T(128)S(1)} %copy-done.28, bf16[576,256]{1,0:T(8,128)(2,1)S(1)} %get-tuple-element.155.refs_0_, bf16[576,256]{1,0:T(8,128)(2,1)S(1)} %collective-permute-done.21.refs_1_, bf16[576,256]{1,0:T(8,128)(2,1)S(1)} %copy-done.19, bf16[576,256]{1,0:T(8,128)(2,1)S(1)} %copy-done.21, ...), custom_call_target="tpu_custom_call" | custom-call | tf_op jit(solution)/shard_map/final/pallas_call | solution.py:1204
  207.5 1.9 collective-permute-start.30
  211.8 5.2 %collective-permute-done.30 = bf16[144,768]{1,0:T(8,128)(2,1)S(1)} collective-permute-done((bf16[144,768]{1,0:T(8,128)(2,1)S(1)}, bf16[144,768]{1,0:T(8,128)(2,1)S(1)}, u32[]{:S(2)}, u32[]{:S(2)}) %collective-permute-start.30) | collective-permute-done | bytes 221216 | tf_op jit(solution)/shard_map/ppermute | solution.py:1217
  217.0 8.5 %collective-permute-done.31 = bf16[144,768]{1,0:T(8,128)(2,1)S(1)} collective-permute-done((bf16[144,768]{1,0:T(8,128)(2,1)S(1)}, bf16[144,768]{1,0:T(8,128)(2,1)S(1)}, u32[]{:S(2)}, u32[]{:S(2)}) %collective-permute-start.31) | collective-permute-done | bytes 221216 | tf_op jit(solution)/shard_map/ppermute | solution.py:1217
  (273 shorter events, 72.4 us)
Async XLA Ops:
  4.4 19.8 %collective-permute-start = (bf16[256,768]{1,0:T(8,128)(2,1)S(1)}, bf16[256,768]{1,0:T(8,128)(2,1)}, u32[]{:S(2)}, u32[]{:S(2)}) collective-permute-start(bf16[256,768]{1,0:T(8,128)(2,1)S(1)} %fusion.27.refs_0_), channel_id=1, source_target_pairs={{0,2},{1,3},{2,4},{3,5},{4,6},{5,7},{6,0},{7,1},{8,10},{9,11},{10,... | collective-permute-start | bytes 1179656 | tf_op jit(solution)/shard_map/ppermute | solution.py:1217
  7.5 28.2 %collective-permute-start.1 = (bf16[256,768]{1,0:T(8,128)(2,1)S(1)}, bf16[256,768]{1,0:T(8,128)(2,1)}, u32[]{:S(2)}, u32[]{:S(2)}) collective-permute-start(bf16[256,768]{1,0:T(8,128)(2,1)S(1)} %fusion.27.refs_0_), channel_id=1, source_target_pairs={{0,4},{1,5},{2,6},{3,7},{4,0},{5,1},{6,2},{7,3},{8,12},{9,13},{10,... | collective-permute-start | bytes 1179656 | tf_op jit(solution)/shard_map/ppermute | solution.py:1217
  10.0 28.7 %collective-permute-start.2 = (bf16[256,768]{1,0:T(8,128)(2,1)S(1)}, bf16[256,768]{1,0:T(8,128)(2,1)}, u32[]{:S(2)}, u32[]{:S(2)}) collective-permute-start(bf16[256,768]{1,0:T(8,128)(2,1)S(1)} %fusion.27.refs_0_), channel_id=1, source_target_pairs={{0,6},{1,7},{2,0},{3,1},{4,2},{5,3},{6,4},{7,5},{8,14},{9,15},{10,... | collective-permute-start | bytes 1179656 | tf_op jit(solution)/shard_map/ppermute | solution.py:1217
  11.4 31.7 %collective-permute-start.3 = (bf16[256,768]{1,0:T(8,128)(2,1)S(1)}, bf16[256,768]{1,0:T(8,128)(2,1)}, u32[]{:S(2)}, u32[]{:S(2)}) collective-permute-start(bf16[256,768]{1,0:T(8,128)(2,1)S(1)} %fusion.27.refs_0_), channel_id=1, source_target_pairs={{0,1},{1,0},{2,3},{3,2},{4,5},{5,4},{6,7},{7,6},{8,9},{9,8},{10,11... | collective-permute-start | bytes 1179656 | tf_op jit(solution)/shard_map/ppermute | solution.py:1221
  24.2 18.9 %collective-permute-start.4 = (bf16[256,768]{1,0:T(8,128)(2,1)}, bf16[256,768]{1,0:T(8,128)(2,1)S(1)}, u32[]{:S(2)}, u32[]{:S(2)}) collective-permute-start(bf16[256,768]{1,0:T(8,128)(2,1)} %collective-permute-done.refs_1_), channel_id=1, source_target_pairs={{0,1},{1,0},{2,3},{3,2},{4,5},{5,4},{6,7},{7,6},{8,9},{9,8},{10,11... | collective-permute-start | bytes 1179656 | tf_op jit(solution)/shard_map/ppermute | solution.py:1221
  60.3 15.5 %collective-permute-start.7 = (bf16[192,256]{1,0:T(8,128)(2,1)S(1)}, bf16[192,256]{1,0:T(8,128)(2,1)S(1)}, u32[]{:S(2)}, u32[]{:S(2)}) collective-permute-start(bf16[192,256]{1,0:T(8,128)(2,1)S(1)} %get-tuple-element.191), channel_id=1, source_target_pairs={{0,6},{1,7},{2,0},{3,1},{4,2},{5,3},{6,4},{7,5},{8,14},{9,15},{10,... | collective-permute-start | bytes 294920 | tf_op jit(solution)/shard_map/ppermute | solution.py:1217
  70.2 9.3 %collective-permute-start.8 = (bf16[192,256]{1,0:T(8,128)(2,1)S(1)}, bf16[192,256]{1,0:T(8,128)(2,1)S(1)}, u32[]{:S(2)}, u32[]{:S(2)}) collective-permute-start(bf16[192,256]{1,0:T(8,128)(2,1)S(1)} %get-tuple-element.190), channel_id=1, source_target_pairs={{0,4},{1,5},{2,6},{3,7},{4,0},{5,1},{6,2},{7,3},{8,12},{9,13},{10,... | collective-permute-start | bytes 294920 | tf_op jit(solution)/shard_map/ppermute | solution.py:1217
  70.3 9.3 %collective-permute-start.9 = (bf16[192,256]{1,0:T(8,128)(2,1)S(1)}, bf16[192,256]{1,0:T(8,128)(2,1)S(1)}, u32[]{:S(2)}, u32[]{:S(2)}) collective-permute-start(bf16[192,256]{1,0:T(8,128)(2,1)S(1)} %get-tuple-element.189), channel_id=1, source_target_pairs={{0,2},{1,3},{2,4},{3,5},{4,6},{5,7},{6,0},{7,1},{8,10},{9,11},{10,... | collective-permute-start | bytes 294920 | tf_op jit(solution)/shard_map/ppermute | solution.py:1217
  106.3 13.7 %collective-permute-start.14 = (bf16[16,120,768]{2,1,0:T(8,128)(2,1)}, bf16[16,120,768]{2,1,0:T(8,128)(2,1)}, u32[]{:S(2)}, u32[]{:S(2)}) collective-permute-start(bf16[16,120,768]{2,1,0:T(8,128)(2,1)} %get-tuple-element.122), channel_id=1, source_target_pairs={{0,1},{1,0},{2,3},{3,2},{4,5},{5,4},{6,7},{7,6},{8,9},{9,8},{10,11... | collective-permute-start | bytes 8847368 | tf_op jit(solution)/shard_map/ppermute | solution.py:1221
  106.7 13.3 %collective-permute-start.13 = (bf16[16,96,768]{2,1,0:T(8,128)(2,1)}, bf16[16,96,768]{2,1,0:T(8,128)(2,1)}, u32[]{:S(2)}, u32[]{:S(2)}) collective-permute-start(bf16[16,96,768]{2,1,0:T(8,128)(2,1)} %get-tuple-element.120), channel_id=1, source_target_pairs={{0,1},{1,0},{2,3},{3,2},{4,5},{5,4},{6,7},{7,6},{8,9},{9,8},{10,11... | collective-permute-start | bytes 7077896 | tf_op jit(solution)/shard_map/ppermute | solution.py:1221
  108.9 10.2 %collective-permute-start.11 = (bf16[192,256]{1,0:T(8,128)(2,1)}, bf16[192,256]{1,0:T(8,128)(2,1)S(1)}, u32[]{:S(2)}, u32[]{:S(2)}) collective-permute-start(bf16[192,256]{1,0:T(8,128)(2,1)} %get-tuple-element.117), channel_id=1, source_target_pairs={{0,4},{1,5},{2,6},{3,7},{4,0},{5,1},{6,2},{7,3},{8,12},{9,13},{10,... | collective-permute-start | bytes 294920 | tf_op jit(solution)/shard_map/ppermute | solution.py:1217
  109.1 10.0 %collective-permute-start.10 = (bf16[192,256]{1,0:T(8,128)(2,1)}, bf16[192,256]{1,0:T(8,128)(2,1)S(1)}, u32[]{:S(2)}, u32[]{:S(2)}) collective-permute-start(bf16[192,256]{1,0:T(8,128)(2,1)} %get-tuple-element.116), channel_id=1, source_target_pairs={{0,2},{1,3},{2,4},{3,5},{4,6},{5,7},{6,0},{7,1},{8,10},{9,11},{10,... | collective-permute-start | bytes 294920 | tf_op jit(solution)/shard_map/ppermute | solution.py:1217
  121.6 14.7 %collective-permute-start.15 = (bf16[2,2,96,768]{3,2,1,0:T(8,128)(2,1)S(1)}, bf16[2,2,96,768]{3,2,1,0:T(8,128)(2,1)S(1)}, u32[]{:S(2)}, u32[]{:S(2)}) collective-permute-start(bf16[2,2,96,768]{3,2,1,0:T(8,128)(2,1)S(1)} %fusion.35), channel_id=1, source_target_pairs={{0,8},{8,0},{16,24},{24,16},{1,9},{9,1},{17,25},{25,17},{2,10},{10... | collective-permute-start | bytes 1769480 | tf_op jit(solution)/shard_map/ppermute | solution.py:1225
  123.1 14.7 %collective-permute-start.16 = (bf16[2,2,96,768]{3,2,1,0:T(8,128)(2,1)S(1)}, bf16[2,2,96,768]{3,2,1,0:T(8,128)(2,1)S(1)}, u32[]{:S(2)}, u32[]{:S(2)}) collective-permute-start(bf16[2,2,96,768]{3,2,1,0:T(8,128)(2,1)S(1)} %fusion.36), channel_id=1, source_target_pairs={{0,16},{8,24},{16,0},{24,8},{1,17},{9,25},{17,1},{25,9},{2,18},{10... | collective-permute-start | bytes 1769480 | tf_op jit(solution)/shard_map/ppermute | solution.py:1225
  139.8 7.9 %collective-permute-start.17 = (bf16[384,1024]{1,0:T(8,128)(2,1)}, bf16[384,1024]{1,0:T(8,128)(2,1)}, u32[]{:S(2)}, u32[]{:S(2)}) collective-permute-start(bf16[384,1024]{1,0:T(8,128)(2,1)} %slice.238), channel_id=1, source_target_pairs={{0,1},{1,0},{2,3},{3,2},{4,5},{5,4},{6,7},{7,6},{8,9},{9,8},{10,11... | collective-permute-start | bytes 2359304 | tf_op jit(solution)/shard_map/ppermute | solution.py:1221
  142.8 18.8 %collective-permute-start.18 = (bf16[2,2,120,768]{3,2,1,0:T(8,128)(2,1)}, bf16[2,2,120,768]{3,2,1,0:T(8,128)(2,1)}, u32[]{:S(2)}, u32[]{:S(2)}) collective-permute-start(bf16[2,2,120,768]{3,2,1,0:T(8,128)(2,1)} %fusion.29), channel_id=1, source_target_pairs={{0,8},{8,0},{16,24},{24,16},{1,9},{9,1},{17,25},{25,17},{2,10},{10... | collective-permute-start | bytes 2211848 | tf_op jit(solution)/shard_map/ppermute | solution.py:1225
  146.5 18.9 %collective-permute-start.19 = (bf16[2,2,120,768]{3,2,1,0:T(8,128)(2,1)}, bf16[2,2,120,768]{3,2,1,0:T(8,128)(2,1)}, u32[]{:S(2)}, u32[]{:S(2)}) collective-permute-start(bf16[2,2,120,768]{3,2,1,0:T(8,128)(2,1)} %fusion.30), channel_id=1, source_target_pairs={{0,16},{8,24},{16,0},{24,8},{1,17},{9,25},{17,1},{25,9},{2,18},{10... | collective-permute-start | bytes 2211848 | tf_op jit(solution)/shard_map/ppermute | solution.py:1225
  152.6 12.8 %collective-permute-start.20 = (bf16[16,24,768]{2,1,0:T(8,128)(2,1)}, bf16[16,24,768]{2,1,0:T(8,128)(2,1)}, u32[]{:S(2)}, u32[]{:S(2)}) collective-permute-start(bf16[16,24,768]{2,1,0:T(8,128)(2,1)} %bitcast.30), channel_id=1, source_target_pairs={{0,1},{1,0},{2,3},{3,2},{4,5},{5,4},{6,7},{7,6},{8,9},{9,8},{10,11... | collective-permute-start | bytes 1769480 | tf_op jit(solution)/shard_map/ppermute | solution.py:1221
  153.6 11.9 %collective-permute-start.21 = (bf16[576,256]{1,0:T(8,128)(2,1)}, bf16[576,256]{1,0:T(8,128)(2,1)S(1)}, u32[]{:S(2)}, u32[]{:S(2)}) collective-permute-start(bf16[576,256]{1,0:T(8,128)(2,1)} %get-tuple-element.175), channel_id=1, source_target_pairs={{0,6},{1,7},{2,0},{3,1},{4,2},{5,3},{6,4},{7,5},{8,14},{9,15},{10,... | collective-permute-start | bytes 884744 | tf_op jit(solution)/shard_map/ppermute | solution.py:1217
  155.7 28.6 %collective-permute-start.22 = (bf16[576,256]{1,0:T(8,128)(2,1)}, bf16[576,256]{1,0:T(8,128)(2,1)S(1)}, u32[]{:S(2)}, u32[]{:S(2)}) collective-permute-start(bf16[576,256]{1,0:T(8,128)(2,1)} %get-tuple-element.176), channel_id=1, source_target_pairs={{0,4},{1,5},{2,6},{3,7},{4,0},{5,1},{6,2},{7,3},{8,12},{9,13},{10,... | collective-permute-start | bytes 884744 | tf_op jit(solution)/shard_map/ppermute | solution.py:1217
  161.6 22.6 %collective-permute-start.23 = (bf16[576,256]{1,0:T(8,128)(2,1)}, bf16[576,256]{1,0:T(8,128)(2,1)S(1)}, u32[]{:S(2)}, u32[]{:S(2)}) collective-permute-start(bf16[576,256]{1,0:T(8,128)(2,1)} %get-tuple-element.173), channel_id=1, source_target_pairs={{0,2},{1,3},{2,4},{3,5},{4,6},{5,7},{6,0},{7,1},{8,10},{9,11},{10,... | collective-permute-start | bytes 884744 | tf_op jit(solution)/shard_map/ppermute | solution.py:1217
  170.0 12.7 %collective-permute-start.25 = (bf16[2,96,768]{2,1,0:T(8,128)(2,1)S(1)}, bf16[2,96,768]{2,1,0:T(8,128)(2,1)S(1)}, u32[]{:S(2)}, u32[]{:S(2)}) collective-permute-start(bf16[2,96,768]{2,1,0:T(8,128)(2,1)S(1)} %dynamic-slice_bitcast_fusion.2), channel_id=1, source_target_pairs={{0,8},{8,0},{16,24},{24,16},{1,9},{9,1},{17,25},{25,17},{2,10},{10... | collective-permute-start | bytes 884744 | tf_op jit(solution)/shard_map/ppermute | solution.py:1225
  171.6 9.9 %collective-permute-start.26 = (bf16[2,2,24,768]{3,2,1,0:T(8,128)(2,1)S(1)}, bf16[2,2,24,768]{3,2,1,0:T(8,128)(2,1)S(1)}, u32[]{:S(2)}, u32[]{:S(2)}) collective-permute-start(bf16[2,2,24,768]{3,2,1,0:T(8,128)(2,1)S(1)} %fusion.67), channel_id=1, source_target_pairs={{0,8},{8,0},{16,24},{24,16},{1,9},{9,1},{17,25},{25,17},{2,10},{10... | collective-permute-start | bytes 442376 | tf_op jit(solution)/shard_map/ppermute | solution.py:1225
  175.7 7.5 %collective-permute-start.24 = (bf16[2,96,768]{2,1,0:T(8,128)(2,1)S(1)}, bf16[2,96,768]{2,1,0:T(8,128)(2,1)S(1)}, u32[]{:S(2)}, u32[]{:S(2)}) collective-permute-start(bf16[2,96,768]{2,1,0:T(8,128)(2,1)S(1)} %dynamic-slice_bitcast_fusion.3), channel_id=1, source_target_pairs={{0,16},{8,24},{16,0},{24,8},{1,17},{9,25},{17,1},{25,9},{2,18},{10... | collective-permute-start | bytes 884744 | tf_op jit(solution)/shard_map/ppermute | solution.py:1225
  186.8 18.0 %collective-permute-start.28 = (bf16[2,144,768]{2,1,0:T(8,128)(2,1)}, bf16[2,144,768]{2,1,0:T(8,128)(2,1)}, u32[]{:S(2)}, u32[]{:S(2)}) collective-permute-start(bf16[2,144,768]{2,1,0:T(8,128)(2,1)} %dynamic-slice_bitcast_fusion.1), channel_id=1, source_target_pairs={{0,16},{8,24},{16,0},{24,8},{1,17},{9,25},{17,1},{25,9},{2,18},{10... | collective-permute-start | bytes 1327112 | tf_op jit(solution)/shard_map/ppermute | solution.py:1225
  189.4 16.6 %collective-permute-start.29 = (bf16[2,144,768]{2,1,0:T(8,128)(2,1)}, bf16[2,144,768]{2,1,0:T(8,128)(2,1)}, u32[]{:S(2)}, u32[]{:S(2)}) collective-permute-start(bf16[2,144,768]{2,1,0:T(8,128)(2,1)} %dynamic-slice_bitcast_fusion), channel_id=1, source_target_pairs={{0,8},{8,0},{16,24},{24,16},{1,9},{9,1},{17,25},{25,17},{2,10},{10... | collective-permute-start | bytes 1327112 | tf_op jit(solution)/shard_map/ppermute | solution.py:1225
  192.1 17.3 %collective-permute-start.35 = (bf16[96,768]{1,0:T(8,128)(2,1)S(1)}, bf16[96,768]{1,0:T(8,128)(2,1)S(1)}, u32[]{:S(2)}, u32[]{:S(2)}) collective-permute-start(bf16[96,768]{1,0:T(8,128)(2,1)S(1)} %get-tuple-element.184), channel_id=1, source_target_pairs={{0,6},{1,7},{2,0},{3,1},{4,2},{5,3},{6,4},{7,5},{8,14},{9,15},{10,... | collective-permute-start | bytes 442376 | tf_op jit(solution)/shard_map/ppermute | solution.py:1217
  194.0 16.1 %collective-permute-start.34 = (bf16[96,768]{1,0:T(8,128)(2,1)S(1)}, bf16[96,768]{1,0:T(8,128)(2,1)S(1)}, u32[]{:S(2)}, u32[]{:S(2)}) collective-permute-start(bf16[96,768]{1,0:T(8,128)(2,1)S(1)} %get-tuple-element.185), channel_id=1, source_target_pairs={{0,4},{1,5},{2,6},{3,7},{4,0},{5,1},{6,2},{7,3},{8,12},{9,13},{10,... | collective-permute-start | bytes 442376 | tf_op jit(solution)/shard_map/ppermute | solution.py:1217
  195.3 14.8 %collective-permute-start.33 = (bf16[96,768]{1,0:T(8,128)(2,1)S(1)}, bf16[96,768]{1,0:T(8,128)(2,1)S(1)}, u32[]{:S(2)}, u32[]{:S(2)}) collective-permute-start(bf16[96,768]{1,0:T(8,128)(2,1)S(1)} %get-tuple-element.183), channel_id=1, source_target_pairs={{0,2},{1,3},{2,4},{3,5},{4,6},{5,7},{6,0},{7,1},{8,10},{9,11},{10,... | collective-permute-start | bytes 442376 | tf_op jit(solution)/shard_map/ppermute | solution.py:1217
  207.5 9.5 %collective-permute-start.30 = (bf16[144,768]{1,0:T(8,128)(2,1)S(1)}, bf16[144,768]{1,0:T(8,128)(2,1)S(1)}, u32[]{:S(2)}, u32[]{:S(2)}) collective-permute-start(bf16[144,768]{1,0:T(8,128)(2,1)S(1)} %get-tuple-element.180), channel_id=1, source_target_pairs={{0,6},{1,7},{2,0},{3,1},{4,2},{5,3},{6,4},{7,5},{8,14},{9,15},{10,... | collective-permute-start | bytes 663560 | tf_op jit(solution)/shard_map/ppermute | solution.py:1217
  209.5 16.0 %collective-permute-start.31 = (bf16[144,768]{1,0:T(8,128)(2,1)S(1)}, bf16[144,768]{1,0:T(8,128)(2,1)S(1)}, u32[]{:S(2)}, u32[]{:S(2)}) collective-permute-start(bf16[144,768]{1,0:T(8,128)(2,1)S(1)} %get-tuple-element.181), channel_id=1, source_target_pairs={{0,4},{1,5},{2,6},{3,7},{4,0},{5,1},{6,2},{7,3},{8,12},{9,13},{10,... | collective-permute-start | bytes 663560 | tf_op jit(solution)/shard_map/ppermute | solution.py:1217
  209.5 16.0 %collective-permute-start.32 = (bf16[144,768]{1,0:T(8,128)(2,1)S(1)}, bf16[144,768]{1,0:T(8,128)(2,1)S(1)}, u32[]{:S(2)}, u32[]{:S(2)}) collective-permute-start(bf16[144,768]{1,0:T(8,128)(2,1)S(1)} %get-tuple-element.182), channel_id=1, source_target_pairs={{0,2},{1,3},{2,4},{3,5},{4,6},{5,7},{6,0},{7,1},{8,10},{9,11},{10,... | collective-permute-start | bytes 663560 | tf_op jit(solution)/shard_map/ppermute | solution.py:1217
  (60 other events, 315.6 us)

commit v2 on v1

--- a/solution.py
+++ b/solution.py
@@ -573,6 +573,29 @@
     return jnp.dot(left, right, preferred_element_type=jnp.float32)
 
 
+def call_whole(kernel, out_shape, name, scalars, *arrays, in_specs=None, scratch=(), cost=None, limit=12):
+    return pl.pallas_call(
+        kernel,
+        grid_spec=pltpu.PrefetchScalarGridSpec(
+            num_scalar_prefetch=1,
+            grid=(1,),
+            in_specs=in_specs or [whole(array.shape) for array in arrays],
+            out_specs=[whole(out.shape) for out in out_shape],
+            scratch_shapes=list(scratch),
+        ),
+        out_shape=list(out_shape),
+        compiler_params=pltpu.CompilerParams(vmem_limit_bytes=limit << 20),
+        cost_estimate=cost,
+        name=name,
+    )(scalars, *arrays)
+
+
+def norm_kernel(unused, rows_ref, gain_ref, out_ref):
+    out_ref[...] = (norm_parts(rows_ref[...].astype(jnp.float32))[0] * gain_ref[...]).astype(
+        jnp.bfloat16
+    )
+
+
 def project_kernel(
     blocks, own, scale, meta, *refs
 ):
@@ -602,22 +625,28 @@
 def project(meta, normed, wq, wk, wv, row_info, col_info, row_value, col_value, own, scale):
     blocks, length = len(normed), normed[0].shape[0]
     wide, share = wk.shape[1], wv.shape[0]
-    vmem = pl.BlockSpec(memory_space=pltpu.VMEM)
-    return pl.pallas_call(
+    return call_whole(
         partial(project_kernel, blocks, own, scale),
-        in_specs=[pl.BlockSpec(memory_space=pltpu.SMEM)] + [vmem] * (blocks + 7),
-        out_specs=[vmem] * 3,
-        out_shape=[
+        [
             jax.ShapeDtypeStruct((wide, own * length), jnp.bfloat16),
             jax.ShapeDtypeStruct((blocks * length, wide), jnp.bfloat16),
             jax.ShapeDtypeStruct((share, blocks * length), jnp.bfloat16),
         ],
-        compiler_params=pltpu.CompilerParams(vmem_limit_bytes=32 << 20),
-        name="project",
-    )(meta, *normed, wq, wk, wv, row_info, col_info, row_value, col_value)
-
-
-def project_back_kernel(blocks, *refs):
+        "project",
+        meta,
+        *normed,
+        wq,
+        wk,
+        wv,
+        row_info,
+        col_info,
+        row_value,
+        col_value,
+        limit=20,
+    )
+
+
+def project_back_kernel(blocks, unused, *refs):
     normed = refs[:blocks]
     wk_ref, wv_ref, kt_ref, v_ref = refs[blocks:]
     length = normed[0].shape[0]
@@ -628,21 +657,21 @@
         v_ref[span, :] = nn_dot(rows, wv_ref[...]).astype(jnp.bfloat16)
 
 
-def project_back(normed, wk, wv):
+def project_back(scalars, normed, wk, wv):
     blocks, length = len(normed), normed[0].shape[0]
-    vmem = pl.BlockSpec(memory_space=pltpu.VMEM)
-    return pl.pallas_call(
+    return call_whole(
         partial(project_back_kernel, blocks),
-        in_specs=[vmem] * (blocks + 2),
-        out_specs=[vmem] * 2,
-        out_shape=[
+        [
             jax.ShapeDtypeStruct((wk.shape[0], blocks * length), jnp.bfloat16),
             jax.ShapeDtypeStruct((blocks * length, wv.shape[1]), jnp.bfloat16),
         ],
-        compiler_params=pltpu.CompilerParams(vmem_limit_bytes=32 << 20),
-        cost_estimate=pl.CostEstimate(flops=3 * 10**9, bytes_accessed=6 << 20, transcendentals=0),
-        name="project_back",
-    )(*normed, wk, wv)
+        "project_back",
+        scalars,
+        *normed,
+        wk,
+        wv,
+        cost=pl.CostEstimate(flops=3 * 10**9, bytes_accessed=6 << 20, transcendentals=0),
+    )
 
 
 def pair_mask(query_start, key_start, doc_line, block):
@@ -714,9 +743,10 @@
     kt_ref,
     v_ref,
     dq_ref,
-    dk_ref,
-    dv_ref,
+    mine_ref,
+    other_ref,
     acc_ref,
+    pair_ref,
 ):
     step = pl.program_id(0)
     steps = pl.num_programs(0)
@@ -726,10 +756,11 @@
     size = g_ref.shape[0] // heads
     lanes = q_ref.shape[0] // heads
 
+    share = g_ref.shape[0]
+
     @pl.when(step == 0)
     def _():
-        dk_ref[...] = jnp.zeros_like(dk_ref)
-        dv_ref[...] = jnp.zeros_like(dv_ref)
+        pair_ref[...] = jnp.zeros_like(pair_ref)
 
     acc_ref[...] = jnp.zeros_like(acc_ref)
 
@@ -749,15 +780,22 @@
                 probs = jnp.where(allowed, jnp.exp(scores - lse_ref[head]), 0.0)
                 dots = nn_dot(v_ref[span, head * lanes : head * lanes + size], grad)
                 grad_scores = (probs * (dots - delta)).astype(jnp.bfloat16)
-                dv_ref[rows, span] += nt_dot(grad, probs.astype(jnp.bfloat16))
+                value_rows = slice(share + head * size, share + (head + 1) * size)
+                pair_ref[value_rows, span] += nt_dot(grad, probs.astype(jnp.bfloat16))
                 query = q_ref[head * lanes : head * lanes + size, :]
-                dk_ref[rows, span] += nt_dot(query, grad_scores)
+                pair_ref[rows, span] += nt_dot(query, grad_scores)
                 acc_ref[rows, :] += nn_dot(kt_ref[rows, span], grad_scores)
 
         return carry
 
     lax.fori_loop(0, key_blocks, body, 0)
     dq_ref[...] = (acc_ref[...] * scale).astype(dq_ref.dtype)
+
+    @pl.when(step == steps - 1)
+    def _():
+        half = mine_ref.shape[1]
+        mine_ref[...] = pair_ref[:, :half]
+        other_ref[...] = pair_ref[:, half:].astype(jnp.bfloat16)
 
 
 def whole(shape):
@@ -794,7 +832,7 @@
             jax.ShapeDtypeStruct((steps, share, block), jnp.bfloat16),
             jax.ShapeDtypeStruct((heads, 1, queries), jnp.float32),
         ],
-        compiler_params=pltpu.CompilerParams(vmem_limit_bytes=24 << 20),
+        compiler_params=pltpu.CompilerParams(vmem_limit_bytes=12 << 20),
         cost_estimate=pl.CostEstimate(flops=8 * 10**9, bytes_accessed=8 << 20, transcendentals=0),
         name="attend",
     )(meta, doc_line, q_ext, k_ext, v_t)
@@ -821,20 +859,46 @@
             ],
             out_specs=[
                 pl.BlockSpec((share, block), lambda i, meta: (0, i)),
-                whole(k_t.shape),
-                whole(k_t.shape),
+                whole((2 * share, keys // 2)),
+                whole((2 * share, keys // 2)),
             ],
-            scratch_shapes=[pltpu.VMEM((share, block), jnp.float32)],
+            scratch_shapes=[
+                pltpu.VMEM((share, block), jnp.float32),
+                pltpu.VMEM((2 * share, keys), jnp.float32),
+            ],
         ),
         out_shape=[
             jax.ShapeDtypeStruct((share, queries), jnp.bfloat16),
-            jax.ShapeDtypeStruct((share, keys), jnp.float32),
-            jax.ShapeDtypeStruct((share, keys), jnp.float32),
+            jax.ShapeDtypeStruct((2 * share, keys // 2), jnp.float32),
+            jax.ShapeDtypeStruct((2 * share, keys // 2), jnp.bfloat16),
         ],
-        compiler_params=pltpu.CompilerParams(vmem_limit_bytes=32 << 20),
+        compiler_params=pltpu.CompilerParams(vmem_limit_bytes=20 << 20),
         cost_estimate=pl.CostEstimate(flops=10**6, bytes_accessed=1 << 10, transcendentals=0),
         name="attend_back",
     )(meta, doc_line, q_ext, grad_t, mixed, lse, k_ext, k_t, v_ext)
+
+
+def join_kernel(chips, unused, dq_ref, mine_ref, other_ref, *out_refs):
+    share = dq_ref.shape[0]
+    block = dq_ref.shape[1] // chips
+    for step in range(chips):
+        span = slice(step * block, (step + 1) * block)
+        pair = (mine_ref[:, span] + other_ref[:, span].astype(jnp.float32)).astype(jnp.bfloat16)
+        out_refs[step][:share, :] = dq_ref[:, span]
+        out_refs[step][share:, :] = pair
+
+
+def join_parts(scalars, dq, mine, other, chips):
+    rows, block = dq.shape[0] + mine.shape[0], dq.shape[1] // chips
+    return call_whole(
+        partial(join_kernel, chips),
+        [jax.ShapeDtypeStruct((rows, block), jnp.bfloat16)] * chips,
+        "join",
+        scalars,
+        dq,
+        mine,
+        other,
+    )
 
 
 def norm_parts(values):
@@ -1164,7 +1228,7 @@
             jax.ShapeDtypeStruct(row, jnp.float32),
             jax.ShapeDtypeStruct((1, hidden), jnp.float32),
         ],
-        compiler_params=pltpu.CompilerParams(vmem_limit_bytes=56 << 20),
+        compiler_params=pltpu.CompilerParams(vmem_limit_bytes=44 << 20),
         cost_estimate=pl.CostEstimate(flops=16 * 10**9, bytes_accessed=40 << 20, transcendentals=0),
         name="middle",
     )(position, *mixed, tokens, cotangent, w_out, w_up, w_down, perm, *gains)
@@ -1200,16 +1264,20 @@
 
 def final(position, homes, tokens, gmid, w_query, w_key, w_value, gain):
     block, model_width = tokens.shape
-    vmem = pl.BlockSpec(memory_space=pltpu.VMEM)
-    return pl.pallas_call(
+    return call_whole(
         partial(final_kernel, len(homes)),
-        in_specs=[pl.BlockSpec(memory_space=pltpu.SMEM)] + [vmem] * (len(homes) + 6),
-        out_specs=vmem,
-        out_shape=jax.ShapeDtypeStruct((block, model_width), jnp.bfloat16),
-        scratch_shapes=[pltpu.VMEM((model_width, block), jnp.float32)],
-        compiler_params=pltpu.CompilerParams(vmem_limit_bytes=24 << 20),
-        name="final",
-    )(position, *homes, tokens, gmid, w_query, w_key, w_value, gain)
+        [jax.ShapeDtypeStruct((block, model_width), jnp.bfloat16)],
+        "final",
+        position,
+        *homes,
+        tokens,
+        gmid,
+        w_query,
+        w_key,
+        w_value,
+        gain,
+        scratch=[pltpu.VMEM((model_width, block), jnp.float32)],
+    )[0]
 
 
 def chip_shift(value, steps):
@@ -1225,15 +1293,6 @@
     return lax.ppermute(value, "row", [(i, i ^ bit) for i in range(lax.axis_size("row"))])
 
 
-def pick(array, index, axis):
-    return lax.dynamic_index_in_dim(array, index, axis, keepdims=False)
-
-
-def rolled(blocks, start):
-    count = blocks.shape[0]
-    return lax.dynamic_slice_in_dim(jnp.concatenate([blocks, blocks], axis=0), start, count, axis=0)
-
-
 def sent(array):
     return array.astype(jnp.bfloat16)
 
@@ -1242,45 +1301,157 @@
     return array.astype(jnp.float32)
 
 
-def total_of(*terms):
-    result = wide(terms[0])
-    for term in terms[1:]:
-        result = result + wide(term)
-    return sent(result)
-
-
-def corner(term, low, high, second):
-    half = term.shape[1] // 2
-    rest = term.shape[2:]
-    shaped = term.reshape((2, 2) + term.shape[1:])
-    starts = (0 if high is None else high, 0 if low is None else low, half * second)
-    sizes = (2 if high is None else 1, 2 if low is None else 1, half)
-    part = lax.dynamic_slice(shaped, starts + (0,) * len(rest), sizes + rest)
-    return part.reshape((2, half) + rest)
-
-
-def row_first(terms, row):
-    low_bit, high_bit = row % 2, row // 2
-    low = row_swap(total_of(*[corner(term, 1 - low_bit, None, 0) for term in terms]), 1)
-    high = row_swap(total_of(*[corner(term, None, 1 - high_bit, 1) for term in terms]), 2)
-    return low, high
-
-
-def row_middle(terms, low, high, row):
-    low_bit, high_bit = row % 2, row // 2
-    return (
-        total_of(*[corner(term, low_bit, None, 0) for term in terms], low),
-        total_of(*[corner(term, None, high_bit, 1) for term in terms], high),
-    )
-
-
-def row_second(first, second, row):
-    low_bit, high_bit = row % 2, row // 2
-    low = row_swap(pick(first, 1 - high_bit, 0), 2)
-    high = row_swap(pick(second, 1 - low_bit, 0), 1)
-    return jnp.concatenate(
-        [total_of(pick(first, high_bit, 0), low), total_of(pick(second, low_bit, 0), high)], axis=0
-    )
+def low_part(shape, keep):
+    def index(i, bits):
+        return (0, bits[2] if keep else 1 - bits[2], 0, 0, 0)
+
+    return pl.BlockSpec((2, 1, shape[2] // 2) + shape[3:], index)
+
+
+def high_part(shape, keep):
+    def index(i, bits):
+        return (bits[3] if keep else 1 - bits[3], 0, 1, 0, 0)
+
+    return pl.BlockSpec((1, 2, shape[2] // 2) + shape[3:], index)
+
+
+def outgoing_kernel(scalars, low_a, low_b, high_a, high_b, low_ref, high_ref):
+    low_ref[...] = sent(wide(low_a[:, 0]) + wide(low_b[:, 0]))
+    high_ref[...] = sent(wide(high_a[0]) + wide(high_b[0]))
+
+
+def outgoing(scalars, keep, other, kept=False):
+    shape = keep.shape
+    out = jax.ShapeDtypeStruct((2, shape[2] // 2) + shape[3:], jnp.bfloat16)
+    low, high = low_part(shape, kept), high_part(shape, kept)
+    return call_whole(
+        outgoing_kernel,
+        [out, out],
+        "kept" if kept else "outgoing",
+        scalars,
+        keep,
+        other,
+        keep,
+        other,
+        in_specs=[low, low, high, high],
+    )
+
+
+def halfway_kernel(groups, scalars, *refs):
+    ins, outs = refs[: 4 * groups], refs[4 * groups :]
+    low_bit, high_bit = scalars[2], scalars[3]
+    low_keep, low_send, high_keep, high_send = outs
+    first = 0
+    for group in range(groups):
+        low, high, low_in, high_in = ins[4 * group : 4 * group + 4]
+        rows = slice(first, first + low.shape[2])
+        for target, side in ((low_keep, high_bit), (low_send, 1 - high_bit)):
+            target[:, rows] = sent(wide(low[side]) + wide(low_in[side]))
+        for target, side in ((high_keep, low_bit), (high_send, 1 - low_bit)):
+            target[:, rows] = sent(wide(high[side]) + wide(high_in[side]))
+        first += low.shape[2]
+
+
+def halfway(scalars, groups):
+    arrays = [array for group in groups for array in group]
+    rows = sum(group[0].shape[2] for group in groups)
+    out = jax.ShapeDtypeStruct((arrays[0].shape[1], rows, arrays[0].shape[3]), jnp.bfloat16)
+    return call_whole(
+        partial(halfway_kernel, len(groups)), [out] * 4, "halfway", scalars, *arrays, limit=24
+    )
+
+
+def split_kernel(chips, groups, scalars, *refs):
+    ins, outs = refs[: 4 * groups], refs[4 * groups : 4 * groups + chips]
+    all_ref = refs[-1]
+    half = chips // 2
+    first = 0
+    for group in range(groups):
+        low_keep, low_in, high_keep, high_in = ins[4 * group : 4 * group + 4]
+        rows = slice(first, first + low_in.shape[1])
+        all_ref[:half, rows] = sent(wide(low_keep[...]) + wide(low_in[...]))
+        all_ref[half:, rows] = sent(wide(high_keep[...]) + wide(high_in[...]))
+        first += low_in.shape[1]
+    for step in range(chips):
+        outs[step][...] = all_ref[lax.rem(scalars[0] + step, chips)]
+
+
+def split(scalars, groups, chips):
+    arrays = [array for group in groups for array in group]
+    rows = sum(group[0].shape[1] for group in groups)
+    width = arrays[0].shape[2]
+    return call_whole(
+        partial(split_kernel, chips, len(groups)),
+        [jax.ShapeDtypeStruct((rows, width), jnp.bfloat16)] * chips,
+        "split",
+        scalars,
+        *arrays,
+        scratch=[pltpu.VMEM((chips, rows, width), jnp.bfloat16)],
+    )
+
+
+def lay_flat(target, values, first, step):
+    for piece in range(values.shape[1] // 128):
+        target[pl.ds(first + piece, values.shape[0], step), :] = values[
+            :, 128 * piece : 128 * (piece + 1)
+        ]
+
+
+def finish_kernel(chips, per, share, factor, scalars, *refs):
+    arrived, heads_in, refs = refs[:chips], refs[chips : 2 * chips], refs[chips:]
+    down_ref, up_ref, out_ref, query_ref, key_ref, value_ref, gains_ref, heads_ref = refs[chips:]
+    width = arrived[0].shape[1]
+    chip, pieces = scalars[0], width // 128
+    tiles = up_ref.shape[0] * 128 // (per * width)
+    down_rows = down_ref.shape[0] * 128 // width
+
+    def total(first, rows):
+        result = wide(arrived[0][first : first + rows, :])
+        for part in arrived[1:]:
+            result = result + wide(part[first : first + rows, :])
+        return result * factor
+
+    lay_flat(down_ref, total(0, down_rows), 0, pieces)
+    for tile in range(tiles):
+        lay_flat(up_ref, total(down_rows + tile * per, per), tile * pieces, tiles * pieces)
+    lay_flat(out_ref, total(down_rows + tiles * per, per), 0, pieces)
+    gains = wide(heads_in[0][:8, -128:])
+    for part in heads_in[1:]:
+        gains = gains + wide(part[:8, -128:])
+    gains_ref[...] = gains * factor
+    for step in range(chips):
+        heads_ref[lax.rem(chip - step + chips, chips)] = wide(heads_in[step][:, : 3 * share])
+    for index, target in enumerate((query_ref, key_ref, value_ref)):
+        values = jnp.concatenate(
+            [heads_ref[near][:, index * share : (index + 1) * share] for near in range(chips)], axis=1
+        )
+        lay_flat(target, values * factor, 0, pieces)
+
+
+def finish(scalars, arrived, hidden, parts, per, share, factor):
+    chips, width = len(arrived) // 2, arrived[0].shape[1]
+    square = jax.ShapeDtypeStruct((per * width // 128, 128), jnp.float32)
+    large = jax.ShapeDtypeStruct((per * hidden // 128, 128), jnp.float32)
+    return call_whole(
+        partial(finish_kernel, chips, per, share, factor),
+        [large, large, square, square, square, square, jax.ShapeDtypeStruct((8, 128), jnp.float32)],
+        "finish",
+        scalars,
+        *arrived,
+        scratch=[pltpu.VMEM((chips, per, 3 * share), jnp.float32)],
+    )
+
+
+def gathered(rows, chips, chip):
+    if chips != 4:
+        return [rows] + [chip_shift(rows, step) for step in range(1, chips)]
+    behind, ahead = chip_shift(rows, 1), chip_shift(rows, -1)
+    up = [(2 * i + core, 2 * i + 2 + core) for i in (1, 2) for core in (0, 1)]
+    down = [(2 * i + core, 2 * i - 2 + core) for i in (1, 2) for core in (0, 1)]
+    across = jnp.where(
+        chip < 2, lax.ppermute(ahead, "seq", down), lax.ppermute(behind, "seq", up)
+    )
+    return [rows, behind, across, ahead]
 
 
 def fast_local(
@@ -1311,12 +1482,19 @@
     parts = row_devices * seq_devices
     position, row = lax.axis_index("seq"), lax.axis_index("row")
     chip, core = position // 2, position % 2
-    place = jnp.stack([chip, core]).astype(jnp.int32)
+    place = jnp.stack([chip, core, row % 2, row // 2]).astype(jnp.int32)
     bounds = jnp.cumsum(lengths[0])[:-1]
     factor = 1.0 / math.sqrt(block * parts)
 
-    normed_b = layer_norm(tokens.astype(jnp.float32), gain_attend).astype(jnp.bfloat16)
-    own = [normed_b] + [chip_shift(normed_b, step) for step in range(1, chips)]
+    normed_b = call_whole(
+        norm_kernel,
+        [jax.ShapeDtypeStruct(tokens.shape, jnp.bfloat16)],
+        "norm",
+        jnp.zeros((1,), jnp.int32),
+        tokens,
+        gain_attend[None, :],
+    )[0]
+    own = gathered(normed_b, chips, chip)
 
     chip_ids = (chip - jnp.arange(chips, dtype=jnp.int32)) % chips
     query_starts = block * (2 * chip_ids + core)
@@ -1394,10 +1572,11 @@
         scale,
     )
     mixed, mixed_b, lse = attend(meta, doc_line, q_ext, k_ext, v_t, heads, block)
+    own, w_own, mixed_b = lax.optimization_barrier((own, w_own, mixed_b))
     back = [mixed_b[0]] + [chip_shift(mixed_b[step], -step) for step in range(1, chips)]
 
     own_normed = jnp.concatenate(own, axis=0)
-    k_t, v_ext = project_back(own + sibling, wk_rows, wv_wide)
+    k_t, v_ext = project_back(place, own + sibling, wk_rows, wv_wide)
     normed_p = sent(nt_dot(perm, own_normed))
     weights_p = sent(nn_dot(perm, w_own))
     back, k_t, v_ext, normed_p, weights_p = lax.optimization_barrier(
@@ -1421,34 +1600,34 @@
     keep_a, send_a, keep_b, send_b, dinner, dfeed, dhidden = outs[2 + chips :]
 
     def gridded(array):
-        return array.reshape((row_devices, chips) + array.shape[1:])
-
-    other_a, other_b = seq_swap(send_a, 1), seq_swap(send_b, 1)
-    grad_t = jnp.concatenate(
-        [go[0]] + [chip_shift(go[step], step) for step in range(1, chips)], axis=1
-    )
-    grad_t, keep_a, other_a, keep_b, other_b = lax.optimization_barrier(
-        (grad_t, keep_a, other_a, keep_b, other_b)
-    )
-    terms_a, terms_b = [gridded(keep_a), gridded(other_a)], [gridded(keep_b), gridded(other_b)]
-    low_a, high_a = row_first(terms_a, row)
-    dq, dk, dv = attend_back(
-        meta, doc_line, q_ext, grad_t, mixed, lse, k_ext, k_t, v_ext, heads, block, scale
-    )
-    dq, dk, dv, low_a, high_a, keep_b, other_b = lax.optimization_barrier(
-        (dq, dk, dv, low_a, high_a, keep_b, other_b)
-    )
-    terms_b = [gridded(keep_b), gridded(other_b)]
-    low_b, high_b = row_first(terms_b, row)
-    mine = chips * block
-    pair = jnp.concatenate([dk, dv], axis=0)
-    pair_mine = pair[:, :mine] + wide(seq_swap(sent(pair[:, mine:]), 1))
-    grads_t = jnp.concatenate([dq, sent(pair_mine)], axis=0)
-
-    home = [grads_t[:, :block]] + [
-        chip_shift(grads_t[:, step * block : (step + 1) * block], -step) for step in range(1, chips)
-    ]
-
+        return array.reshape((2, 2, chips) + array.shape[1:])
+
+    keep_a, other_a = gridded(keep_a), gridded(seq_swap(send_a, 1))
+    keep_b, other_b = gridded(keep_b), gridded(seq_swap(send_b, 1))
+    out_a, out_b = outgoing(place, keep_a, other_a), outgoing(place, keep_b, other_b)
+    go = [go[0]] + [chip_shift(go[step], step) for step in range(1, chips)]
+    go, out_a, out_b = lax.optimization_barrier((go, out_a, out_b))
+    in_a = [row_swap(out_a[0], 1), row_swap(out_a[1], 2)]
+    dq, pair, other = attend_back(
+        meta, doc_line, q_ext, jnp.concatenate(go, axis=1), mixed, lse, k_ext, k_t, v_ext, heads, block, scale
+    )
+    dq, pair, other, in_a, out_b = lax.optimization_barrier((dq, pair, other, in_a, out_b))
+    in_b = [row_swap(out_b[0], 1), row_swap(out_b[1], 2)]
+    grads = join_parts(place, dq, pair, seq_swap(other, 1), chips)
+    home = [grads[0]] + [chip_shift(grads[step], -step) for step in range(1, chips)]
+    grads, keep_a, other_a, keep_b, other_b = lax.optimization_barrier(
+        (grads, keep_a, other_a, keep_b, other_b)
+    )
+    kept_a = outgoing(place, keep_a, other_a, True)
+    kept_b = outgoing(place, keep_b, other_b, True)
+    in_a, in_b, kept_a, kept_b, home[1] = lax.optimization_barrier(
+        (in_a, in_b, kept_a, kept_b, home[1])
+    )
+    sums = halfway(place, [(*kept_a, *in_a), (*kept_b, *in_b)])
+    sums, grads = lax.optimization_barrier((sums, grads))
+    low_keep, low_send, high_keep, high_send = sums
+    low_in, high_in = row_swap(low_send, 2), row_swap(high_send, 1)
+    grads_t = jnp.concatenate(grads, axis=1)
     own_grad = nt_dot(normed_p, grads_t)
     dattend = jnp.sum(own_grad * wide(weights_p), axis=1).reshape(2, parts // 2, 1, per)
     dattend = jnp.where(core == 0, dattend, dattend[::-1])
@@ -1468,54 +1647,38 @@
     packed = sent(jnp.concatenate([own_grad, gap, gains_all], axis=1))
     half = model_width // 2
     mine_grad = packed[:half].reshape(parts // 2, per, model_width)
-    other_grad = seq_swap(packed[half:].reshape(parts // 2, per, model_width), 1)
-    low_a, high_a, low_b, high_b, mine_grad, other_grad, home[1] = lax.optimization_barrier(
-        (low_a, high_a, low_b, high_b, mine_grad, other_grad, home[1])
-    )
-    heads_terms = [gridded(mine_grad), gridded(other_grad)]
-    first, second = row_middle(terms_b, low_b, high_b, row)
-    stage_a = row_second(*row_middle(terms_a, low_a, high_a, row), row)
-    heads_first, heads_second = row_middle(heads_terms, *row_first(heads_terms, row), row)
-    home, stage_a, first, second, heads_first, heads_second = lax.optimization_barrier(
-        (home, stage_a, first, second, heads_first, heads_second)
-    )
+    send_grad = packed[half:].reshape(parts // 2, per, model_width)
+    home, low_in, high_in, mine_grad, send_grad = lax.optimization_barrier(
+        (home, low_in, high_in, mine_grad, send_grad)
+    )
+    stage = split(place, [(low_keep, low_in, high_keep, high_in)], chips)
+    arrived = [stage[0]] + [chip_shift(stage[step], step) for step in range(1, chips)]
     grad_input = final(
         place, home, tokens, grad_middle, w_query, w_key, w_value, gain_first
     )
-    stage_b = row_second(
-        jnp.concatenate([first, heads_first], axis=2),
-        jnp.concatenate([second, heads_second], axis=2),
-        row,
-    )
-
-    def from_chips(stage):
-        return [pick(stage, chip, 0)] + [
-            chip_shift(pick(stage, (chip + step) % chips, 0), step) for step in range(1, chips)
-        ]
-
-    total_a = sum(wide(part) for part in from_chips(stage_a)) * factor
-    arrived = from_chips(stage_b)
-    ends = stage_b.shape[1] - per
-    total_b = sum(wide(part[:ends]) for part in arrived) * factor
-    gains_part = sum(wide(part[ends : ends + gains_rows, -128:]) for part in arrived) * factor
-    gains_part = gains_part.reshape(-1)[:gains_share]
-    home = jnp.stack([part[ends:, : 3 * share] for part in arrived[::-1]])
-    home = rolled(home, (chips - 1 - chip) % chips)
-    home = wide(home.reshape(chips, per, 3, share)).transpose(2, 1, 0, 3)
-    home = home.reshape(3, per * model_width) * factor
-
-    tiles = hidden // model_width
-    done_up = total_b[: per * tiles].reshape(tiles, per, model_width)
+    mine_grad, other_grad = gridded(mine_grad), gridded(seq_swap(send_grad, 1))
+    low, high = outgoing(place, mine_grad, other_grad)
+    low_keep, low_send, high_keep, high_send = halfway(
+        place,
+        [(*outgoing(place, mine_grad, other_grad, True), row_swap(low, 1), row_swap(high, 2))],
+    )
+    stage = split(
+        place, [(low_keep, row_swap(low_send, 2), high_keep, row_swap(high_send, 1))], chips
+    )
+    arrived += [stage[0]] + [chip_shift(stage[step], step) for step in range(1, chips)]
+    down, up, out, query, key, value, gains_part = finish(
+        place, arrived, hidden, parts, per, share, factor
+    )
     return (
         result,
         grad_input,
-        home[0],
-        home[1],
-        home[2],
-        total_b[per * tiles :].reshape(-1),
-        done_up.transpose(1, 0, 2).reshape(-1),
-        total_a.reshape(-1),
-        gains_part,
+        query.reshape(-1),
+        key.reshape(-1),
+        value.reshape(-1),
+        out.reshape(-1),
+        up.reshape(-1),
+        down.reshape(-1),
+        gains_part.reshape(-1)[:gains_share],
     )
 
 

time: 232 us -> 215 us (0.927)
  other arithmetic: 31.7 us -> 5.15 us
  Pallas kernels: 60.7 us -> 76.7 us
  local copies, waits for them, and re-layouts: 23.5 us -> 15.4 us
    ppermute x18 -> x17, waiting for transfers between devices: 36.4 us -> 15.1 us  [chip_shift(): lax.ppermute(value, 'seq', [(i, (i + 2 * steps) % count) for i in range(c...]
    convert_element_type x15 -> x0, other arithmetic: 20.8 us -> none  [the longest x14 19.5 us: sent(): return array.astype(jnp.bfloat16)]
    pallas_call x3 -> x16, Pallas kernels: 12 us -> 29.5 us  [call_whole(): pl.pallas_call(kernel, grid_spec=pltpu.PrefetchScalarGridSpec(num_scalar_...]
    ppermute x10, waiting for transfers between devices: 14.3 us -> 23.6 us  [row_swap(): lax.ppermute(value, 'row', [(i, i ^ bit) for i in range(lax.axis_size('ro...]
    ppermute x0 -> x2, waiting for transfers between devices: none -> 7.34 us  [the longest x1 7.34 us: gathered(): lax.ppermute(ahead, 'seq', down)]
    ppermute x8, waiting for transfers between devices: 0.02 us -> 6.11 us  [seq_swap(): lax.ppermute(value, 'seq', [(i, i ^ bit) for i in range(lax.axis_size('se...]
    squeeze x8 -> x0, local copies, waits for them, and re-layouts: 5 us -> none  [the longest x5 2.73 us: pick(): return lax.dynamic_index_in_dim(array, index, axis, keepdims=False)]
    ppermute x18 -> x17, starting transfers between devices: 33.6 us -> 29.5 us  [chip_shift(): lax.ppermute(value, 'seq', [(i, (i + 2 * steps) % count) for i in range(c...]
  transfers between devices with their start and end apart: 36 -> 37, of which waited for: 12 -> 16; matrix products, arithmetic and copies ran while one was open for 21% -> 13% of each run, Pallas kernels for 8% -> 16%
where the time goes in v2:
time: 215 us
  Pallas kernels  76.7 us (36%)
  waiting for transfers between devices  52.2 us (24%)
  starting transfers between devices  46.2 us (21%)
  matrix products  17.5 us (8%)
  local copies, waits for them, and re-layouts  15.4 us (7%)
  other arithmetic  5.15 us (2%)
    ppermute x17, starting transfers between devices, chip_shift(): lax.ppermute(value, 'seq', [(i, (i + 2 * steps) % count) for i in range(c...  29.5 us
    pallas_call x16, Pallas kernels, call_whole(): pl.pallas_call(kernel, grid_spec=pltpu.PrefetchScalarGridSpec(num_scalar_...  29.5 us
    pallas_call x1, Pallas kernels, middle(): pl.pallas_call(partial(middle_kernel, chips, tiles, per), grid_spec=pltpu...  24.4 us
    ppermute x10, waiting for transfers between devices, row_swap(): lax.ppermute(value, 'row', [(i, i ^ bit) for i in range(lax.axis_size('ro...  23.6 us
    ppermute x17, waiting for transfers between devices, chip_shift(): lax.ppermute(value, 'seq', [(i, (i + 2 * steps) % count) for i in range(c...  15.1 us
    ppermute x10, starting transfers between devices, row_swap(): lax.ppermute(value, 'row', [(i, i ^ bit) for i in range(lax.axis_size('ro...  12.9 us
    pallas_call x1, Pallas kernels, attend_back(): pl.pallas_call(partial(attend_back_kernel, heads, block, key_blocks, scal...  11.9 us
    pallas_call x1, Pallas kernels, attend(): pl.pallas_call(partial(attend_kernel, heads, block, key_blocks), grid_spe...  10.9 us
  transfers between devices with their start and end apart: 37, of which 16 were waited for; matrix products, arithmetic and copies ran while one was open for 13% of the time, Pallas kernels for 16%

profile of v2, /device:TPU:0, one launch (start us, length us, event | category | flops | bytes accessed | tf_op | source)
XLA Modules:
  0.0 214.5 jit_solution(2620724844661415415)
XLA Ops:
  2.6 3.1 %collective-permute-start = (bf16[256,768]{1,0:T(8,128)(2,1)S(1)}, bf16[256,768]{1,0:T(8,128)(2,1)}, u32[]{:S(2)}, u32[]{:S(2)}) collective-permute-start(bf16[256,768]{1,0:T(8,128)(2,1)S(1)} %norm.1.refs_0_), channel_id=1, source_target_pairs={{0,2},{1,3},{2,4},{3,5},{4,6},{5,7},{6,0},{7,1},{8,10},{9,11},{10,... | collective-permute-start | bytes 1179656 | tf_op jit(solution)/shard_map/ppermute | solution.py:1285
  5.7 2.1 collective-permute-start.1
  9.1 1.9 convolution_convert_fusion.6.refs_8_
  17.6 7.2 %collective-permute-done.1.refs_3_ = bf16[256,768]{1,0:T(8,128)(2,1)} collective-permute-done((bf16[256,768]{1,0:T(8,128)(2,1)S(1)}, bf16[256,768]{1,0:T(8,128)(2,1)}, u32[]{:S(2)}, u32[]{:S(2)}) %collective-permute-start.1) | collective-permute-done | bytes 393248 | tf_op jit(solution)/shard_map/ppermute | solution.py:1285
  30.0 7.3 %collective-permute-done.2 = bf16[256,768]{1,0:T(8,128)(2,1)S(1)} collective-permute-done((bf16[256,768]{1,0:T(8,128)(2,1)}, bf16[256,768]{1,0:T(8,128)(2,1)S(1)}, u32[]{:S(2)}, u32[]{:S(2)}) %collective-permute-start.2) | collective-permute-done | bytes 393248 | tf_op jit(solution)/shard_map/ppermute | solution.py:1452
  39.3 5.2 %project.1 = (bf16[384,1024]{1,0:T(8,128)(2,1)S(1)}, bf16[2048,384]{1,0:T(8,128)(2,1)S(1)}, bf16[192,2048]{1,0:T(8,128)(2,1)S(1)}) custom-call(s32[12]{0:T(128)S(1)} %pad_add_fusion.1.meta, bf16[256,768]{1,0:T(8,128)(2,1)S(1)} %norm.1.refs_0_, bf16[256,768]{1,0:T(8,128)(2,1)} %collective-permute-done.refs_1_, ...), custom_call_target="tpu_custom_call" | custom-call | tf_op jit(solution)/shard_map/project/pallas_call | solution.py:577
  44.5 10.9 %attend.1 = (f32[192,1024]{1,0:T(8,128)S(1)}, bf16[4,192,256]{2,1,0:T(8,128)(2,1)S(1)}, f32[3,1,1024]{2,1,0:T(1,128)S(1)}) custom-call(s32[16]{0:T(128)S(1)} %pad_add_fusion.2.meta, s32[1,1024]{1,0:T(1,128)S(1)} %bitcast.88, bf16[384,1024]{1,0:T(8,128)(2,1)S(1)} %get-tuple-element.163.q_ref, bf16[2048,384]{1,0:T(8,128)(2,1)S(1)} %get-tuple-element.164.k_ref, ...), custom_call_target="tpu_custom_call" | custom-call | flops 8000000000 | bytes 8388608 | tf_op jit(solution)/shard_map/attend/pallas_call | solution.py:809
  55.4 3.1 %collective-permute-start.10 = (bf16[192,256]{1,0:T(8,128)(2,1)S(1)}, bf16[192,256]{1,0:T(8,128)(2,1)S(1)}, u32[]{:S(2)}, u32[]{:S(2)}) collective-permute-start(bf16[192,256]{1,0:T(8,128)(2,1)S(1)} %get-tuple-element.299), channel_id=1, source_target_pairs={{0,2},{1,3},{2,4},{3,5},{4,6},{5,7},{6,0},{7,1},{8,10},{9,11},{10,... | collective-permute-start | bytes 294920 | tf_op jit(solution)/shard_map/ppermute | solution.py:1285
  58.6 1.8 collective-permute-start.8
  60.4 2.0 collective-permute-start.9
  64.3 3.9 %convolution_convert_fusion = bf16[768,1024]{1,0:T(8,128)(2,1)} fusion(bf16[768,768]{1,0:T(8,128)(2,1)S(1)} %copy-done.16, bf16[256,768]{1,0:T(8,128)(2,1)} %collective-permute-done.1.refs_3_, bf16[256,768]{1,0:T(8,128)(2,1)S(1)} %broadcast_select_fusion.refs_2_, bf16[256,768]{1,0:T(8,128)(2,1)} %collective-permute-done.refs_1_, ...), kind=kOutput, calls=%fused_computation.3 | convolution fusion | flops 1215037440 | bytes 4325376 | tf_op jit(solution)/shard_map/dot_general | solution.py:567
  68.2 4.6 %project_back.1 = (bf16[192,2048]{1,0:T(8,128)(2,1)S(1)}, bf16[2048,384]{1,0:T(8,128)(2,1)S(1)}) custom-call(s32[4]{0:T(128)S(1)} %pad_add_fusion.3.unused.position.scalars, bf16[256,768]{1,0:T(8,128)(2,1)S(1)} %norm.1.refs_0_, bf16[256,768]{1,0:T(8,128)(2,1)} %collective-permute-done.refs_1_, bf16[256,768]{1,0:T(8,128)(2,1)S(1)} %broadcast_select_fusion.refs_2_, ...), custom_call_target="tpu_custom_call" | custom-call | flops 3000000000 | bytes 6291456 | tf_op jit(solution)/shard_map/project_back/pallas_call | solution.py:577
  72.8 24.4 %middle.1 = (bf16[256,768]{1,0:T(8,128)(2,1)}, f32[256,768]{1,0:T(8,128)S(1)}, bf16[192,256]{1,0:T(8,128)(2,1)S(1)}, bf16[192,256]{1,0:T(8,128)(2,1)S(1)}, bf16[...) custom-call(s32[4]{0:T(128)S(1)} %pad_add_fusion.3.unused.position.s, ...), custom_call_target="tpu_custom_call" | custom-call | flops 16000000000 | bytes 41943040 | tf_op jit(solution)/shard_map/middle/pallas_call | solution.py:1170
  100.3 2.4 %collective-permute-start.13 = (bf16[192,256]{1,0:T(8,128)(2,1)S(1)}, bf16[192,256]{1,0:T(8,128)(2,1)S(1)}, u32[]{:S(2)}, u32[]{:S(2)}) collective-permute-start(bf16[192,256]{1,0:T(8,128)(2,1)S(1)} %get-tuple-element.189), channel_id=1, source_target_pairs={{0,6},{1,7},{2,0},{3,1},{4,2},{5,3},{6,4},{7,5},{8,14},{9,15},{10,... | collective-permute-start | bytes 294920 | tf_op jit(solution)/shard_map/ppermute | solution.py:1285
  102.6 4.1 %collective-permute-done.14 = bf16[16,96,768]{2,1,0:T(8,128)(2,1)S(1)} collective-permute-done((bf16[16,96,768]{2,1,0:T(8,128)(2,1)S(1)}, bf16[16,96,768]{2,1,0:T(8,128)(2,1)S(1)}, u32[]{:S(2)}, u32[]{:S(2)}) %collective-permute-start.14) | collective-permute-done | bytes 2359328 | tf_op jit(solution)/shard_map/ppermute | solution.py:1289
  108.1 2.1 copy-done
  110.2 2.0 outgoing.4
  112.3 2.5 %collective-permute-start.16 = (bf16[2,2,96,768]{3,2,1,0:T(8,128)(2,1)S(1)}, bf16[2,2,96,768]{3,2,1,0:T(8,128)(2,1)S(1)}, u32[]{:S(2)}, u32[]{:S(2)}) collective-permute-start(bf16[2,2,96,768]{3,2,1,0:T(8,128)(2,1)S(1)} %get-tuple-element.209), channel_id=1, source_target_pairs={{0,8},{8,0},{16,24},{24,16},{1,9},{9,1},{17,25},{25,17},{2,10},{10... | collective-permute-start | bytes 1769480 | tf_op jit(solution)/shard_map/ppermute | solution.py:1293
  116.3 11.9 %attend_back.1 = (bf16[192,1024]{1,0:T(8,128)(2,1)S(1)}, f32[384,1024]{1,0:T(8,128)S(1)}, bf16[384,1024]{1,0:T(8,128)(2,1)S(1)}) custom-call(s32[16]{0:T(128)S(1)} %pad_add_fusion.2.meta, s32[1,1024]{1,0:T(1,128)S(1)} %bitcast.89, bf16[384,1024]{1,0:T(8,128)(2,1)S(1)} %get-tuple-element.163.q_ref, bf16[192,1024]{1,0:T(8,128)(2,1)S(1)} %pad_maximum_fusion.2.g_ref, ...), custom_call_target="tpu_custom_call" | custom-call | flops 1000000 | bytes 1024 | tf_op jit(solution)/shard_map/attend_back/pallas_call | solution.py:845
  143.6 5.7 %collective-permute-done.19.refs_6_ = bf16[2,2,120,768]{3,2,1,0:T(8,128)(2,1)} collective-permute-done((bf16[2,2,120,768]{3,2,1,0:T(8,128)(2,1)}, bf16[2,2,120,768]{3,2,1,0:T(8,128)(2,1)}, u32[]{:S(2)}, u32[]{:S(2)}) %collective-permute-start.19) | collective-permute-done | bytes 737312 | tf_op jit(solution)/shard_map/ppermute | solution.py:1293
  149.8 2.8 %halfway.2 = (bf16[2,216,768]{2,1,0:T(8,128)(2,1)S(1)}, bf16[2,216,768]{2,1,0:T(8,128)(2,1)S(1)}, bf16[2,216,768]{2,1,0:T(8,128)(2,1)S(1)}, bf16[2,216,768]{2,1,0:T(8,128)(2,1)S(1)}) custom-call(s32[4]{0:T(128)S(1)} %pad_add_fusion.3.unused.position.scalars, bf16[2,2,96,768]{3,2,1,0:T(8,128)(2,1)S(1)} %get-tuple-element.233.refs_0_, ...), custom_call_target="tpu_custom_call" | custom-call | tf_op jit(solution)/shard_map/halfway/pallas_call | solution.py:577
  152.7 3.2 %fusion.68 = (bf16[768,576]{0,1:T(8,128)(2,1)}, f32[768]{0:T(1024)S(1)}) fusion(bf16[768,576]{0,1:T(8,128)(2,1)S(1)} %copy-done.50, bf16[768,1024]{1,0:T(8,128)(2,1)S(1)} %copy-done.51, bf16[576,256]{1,0:T(8,128)(2,1)S(1)} %copy-done.39, bf16[576,256]{1,0:T(8,128)(2,1)S(1)} %copy-done.41, bf16[576,256]{1,0:T(8,128)(2,1)} %get-tuple-element.253, ...), kind=kOutput, calls=%fused_computation.112 | convolution fusion | flops 912456960 | bytes 4525056 | tf_op jit(solution)/shard_map/dot_general | solution.py:567
  163.4 2.1 copy.58
  165.5 7.2 %collective-permute-done.24.refs_1_ = bf16[2,216,768]{2,1,0:T(8,128)(2,1)S(1)} collective-permute-done((bf16[2,216,768]{2,1,0:T(8,128)(2,1)}, bf16[2,216,768]{2,1,0:T(8,128)(2,1)S(1)}, u32[]{:S(2)}, u32[]{:S(2)}) %collective-permute-start.24) | collective-permute-done | bytes 663584 | tf_op jit(solution)/shard_map/ppermute | solution.py:1293
  174.1 2.4 %split.2 = (bf16[216,768]{1,0:T(8,128)(2,1)S(1)}, bf16[216,768]{1,0:T(8,128)(2,1)S(1)}, bf16[216,768]{1,0:T(8,128)(2,1)S(1)}, bf16[216,768]{1,0:T(8,128)(2,1)S(1)}) custom-call(s32[4]{0:T(128)S(1)} %pad_add_fusion.3.unused.position.scalars, bf16[2,216,768]{2,1,0:T(8,128)(2,1)S(1)} %get-tuple-element.266.refs_0_, ...), custom_call_target="tpu_custom_call" | custom-call | tf_op jit(solution)/shard_map/split/pallas_call | solution.py:577
  176.5 3.8 %collective-permute-start.26 = (bf16[216,768]{1,0:T(8,128)(2,1)S(1)}, bf16[216,768]{1,0:T(8,128)(2,1)S(1)}, u32[]{:S(2)}, u32[]{:S(2)}) collective-permute-start(bf16[216,768]{1,0:T(8,128)(2,1)S(1)} %get-tuple-element.271), channel_id=1, source_target_pairs={{0,2},{1,3},{2,4},{3,5},{4,6},{5,7},{6,0},{7,1},{8,10},{9,11},{10,... | collective-permute-start | bytes 995336 | tf_op jit(solution)/shard_map/ppermute | solution.py:1285
  180.2 2.4 %collective-permute-start.28 = (bf16[216,768]{1,0:T(8,128)(2,1)S(1)}, bf16[216,768]{1,0:T(8,128)(2,1)S(1)}, u32[]{:S(2)}, u32[]{:S(2)}) collective-permute-start(bf16[216,768]{1,0:T(8,128)(2,1)S(1)} %get-tuple-element.273), channel_id=1, source_target_pairs={{0,6},{1,7},{2,0},{3,1},{4,2},{5,3},{6,4},{7,5},{8,14},{9,15},{10,... | collective-permute-start | bytes 995336 | tf_op jit(solution)/shard_map/ppermute | solution.py:1285
  185.8 3.3 %collective-permute-done.30.refs_2_ = bf16[2,2,24,768]{3,2,1,0:T(8,128)(2,1)S(1)} collective-permute-done((bf16[2,2,24,768]{3,2,1,0:T(8,128)(2,1)S(1)}, bf16[2,2,24,768]{3,2,1,0:T(8,128)(2,1)S(1)}, u32[]{:S(2)}, u32[]{:S(2)}) %collective-permute-start.30) | collective-permute-done | bytes 147488 | tf_op jit(solution)/shard_map/ppermute | solution.py:1293
  192.0 2.2 %collective-permute-done.32.refs_1_ = bf16[2,24,768]{2,1,0:T(8,128)(2,1)S(1)} collective-permute-done((bf16[2,24,768]{2,1,0:T(8,128)(2,1)S(1)}, bf16[2,24,768]{2,1,0:T(8,128)(2,1)S(1)}, u32[]{:S(2)}, u32[]{:S(2)}) %collective-permute-start.32) | collective-permute-done | bytes 73760 | tf_op jit(solution)/shard_map/ppermute | solution.py:1293
  196.3 2.2 %collective-permute-start.35 = (bf16[24,768]{1,0:T(8,128)(2,1)S(1)}, bf16[24,768]{1,0:T(8,128)(2,1)S(1)}, u32[]{:S(2)}, u32[]{:S(2)}) collective-permute-start(bf16[24,768]{1,0:T(8,128)(2,1)S(1)} %get-tuple-element.286), channel_id=1, source_target_pairs={{0,4},{1,5},{2,6},{3,7},{4,0},{5,1},{6,2},{7,3},{8,12},{9,13},{10,... | collective-permute-start | bytes 110600 | tf_op jit(solution)/shard_map/ppermute | solution.py:1285
  200.1 4.3 %final.1 = bf16[256,768]{1,0:T(8,128)(2,1)} custom-call(s32[4]{0:T(128)S(1)} %pad_add_fusion.3.unused.position.scalars, bf16[576,256]{1,0:T(8,128)(2,1)S(1)} %copy-done.29, bf16[576,256]{1,0:T(8,128)(2,1)} %collective-permute-done.21.refs_1_, bf16[576,256]{1,0:T(8,128)(2,1)} %collective-permute-done.22.refs_2_, ...), custom_call_target="tpu_custom_call" | custom-call | tf_op jit(solution)/shard_map/final/pallas_call | solution.py:577
  204.5 7.9 %collective-permute-done.35.refs_6_ = bf16[24,768]{1,0:T(8,128)(2,1)S(1)} collective-permute-done((bf16[24,768]{1,0:T(8,128)(2,1)S(1)}, bf16[24,768]{1,0:T(8,128)(2,1)S(1)}, u32[]{:S(2)}, u32[]{:S(2)}) %collective-permute-start.35) | collective-permute-done | bytes 36896 | tf_op jit(solution)/shard_map/ppermute | solution.py:1285
  (222 shorter events, 61.1 us)
Async XLA Ops:
  2.6 23.5 %collective-permute-start = (bf16[256,768]{1,0:T(8,128)(2,1)S(1)}, bf16[256,768]{1,0:T(8,128)(2,1)}, u32[]{:S(2)}, u32[]{:S(2)}) collective-permute-start(bf16[256,768]{1,0:T(8,128)(2,1)S(1)} %norm.1.refs_0_), channel_id=1, source_target_pairs={{0,2},{1,3},{2,4},{3,5},{4,6},{5,7},{6,0},{7,1},{8,10},{9,11},{10,... | collective-permute-start | bytes 1179656 | tf_op jit(solution)/shard_map/ppermute | solution.py:1285
  5.7 19.1 %collective-permute-start.1 = (bf16[256,768]{1,0:T(8,128)(2,1)S(1)}, bf16[256,768]{1,0:T(8,128)(2,1)}, u32[]{:S(2)}, u32[]{:S(2)}) collective-permute-start(bf16[256,768]{1,0:T(8,128)(2,1)S(1)} %norm.1.refs_0_), channel_id=1, source_target_pairs={{0,6},{1,7},{2,0},{3,1},{4,2},{5,3},{6,4},{7,5},{8,14},{9,15},{10,... | collective-permute-start | bytes 1179656 | tf_op jit(solution)/shard_map/ppermute | solution.py:1285
  7.8 29.8 %collective-permute-start.4 = (bf16[256,768]{1,0:T(8,128)(2,1)S(1)}, bf16[256,768]{1,0:T(8,128)(2,1)}, u32[]{:S(2)}, u32[]{:S(2)}) collective-permute-start(bf16[256,768]{1,0:T(8,128)(2,1)S(1)} %norm.1.refs_0_), channel_id=1, source_target_pairs={{0,1},{1,0},{2,3},{3,2},{4,5},{5,4},{6,7},{7,6},{8,9},{9,8},{10,11... | collective-permute-start | bytes 1179656 | tf_op jit(solution)/shard_map/ppermute | solution.py:1289
  24.8 12.5 %collective-permute-start.2 = (bf16[256,768]{1,0:T(8,128)(2,1)}, bf16[256,768]{1,0:T(8,128)(2,1)S(1)}, u32[]{:S(2)}, u32[]{:S(2)}) collective-permute-start(bf16[256,768]{1,0:T(8,128)(2,1)} %collective-permute-done.1.refs_3_), channel_id=1, source_target_pairs={{2,0},{3,1},{4,2},{5,3},{10,8},{11,9},{12,10},{13,11},{18,16},{19,... | collective-permute-start | bytes 1179656 | tf_op jit(solution)/shard_map/ppermute | solution.py:1452
  26.1 11.2 %collective-permute-start.3 = (bf16[256,768]{1,0:T(8,128)(2,1)}, bf16[256,768]{1,0:T(8,128)(2,1)S(1)}, u32[]{:S(2)}, u32[]{:S(2)}) collective-permute-start(bf16[256,768]{1,0:T(8,128)(2,1)} %collective-permute-done.refs_1_), channel_id=1, source_target_pairs={{2,4},{3,5},{4,6},{5,7},{10,12},{11,13},{12,14},{13,15},{18,20},{1... | collective-permute-start | bytes 1179656 | tf_op jit(solution)/shard_map/ppermute | solution.py:1452
  29.5 8.1 %collective-permute-start.5 = (bf16[256,768]{1,0:T(8,128)(2,1)}, bf16[256,768]{1,0:T(8,128)(2,1)S(1)}, u32[]{:S(2)}, u32[]{:S(2)}) collective-permute-start(bf16[256,768]{1,0:T(8,128)(2,1)} %collective-permute-done.refs_1_), channel_id=1, source_target_pairs={{0,1},{1,0},{2,3},{3,2},{4,5},{5,4},{6,7},{7,6},{8,9},{9,8},{10,11... | collective-permute-start | bytes 1179656 | tf_op jit(solution)/shard_map/ppermute | solution.py:1289
  29.5 8.1 %collective-permute-start.7 = (bf16[256,768]{1,0:T(8,128)(2,1)}, bf16[256,768]{1,0:T(8,128)(2,1)S(1)}, u32[]{:S(2)}, u32[]{:S(2)}) collective-permute-start(bf16[256,768]{1,0:T(8,128)(2,1)} %collective-permute-done.1.refs_3_), channel_id=1, source_target_pairs={{0,1},{1,0},{2,3},{3,2},{4,5},{5,4},{6,7},{7,6},{8,9},{9,8},{10,11... | collective-permute-start | bytes 1179656 | tf_op jit(solution)/shard_map/ppermute | solution.py:1289
  55.4 17.3 %collective-permute-start.10 = (bf16[192,256]{1,0:T(8,128)(2,1)S(1)}, bf16[192,256]{1,0:T(8,128)(2,1)S(1)}, u32[]{:S(2)}, u32[]{:S(2)}) collective-permute-start(bf16[192,256]{1,0:T(8,128)(2,1)S(1)} %get-tuple-element.299), channel_id=1, source_target_pairs={{0,2},{1,3},{2,4},{3,5},{4,6},{5,7},{6,0},{7,1},{8,10},{9,11},{10,... | collective-permute-start | bytes 294920 | tf_op jit(solution)/shard_map/ppermute | solution.py:1285
  58.6 14.2 %collective-permute-start.8 = (bf16[192,256]{1,0:T(8,128)(2,1)S(1)}, bf16[192,256]{1,0:T(8,128)(2,1)S(1)}, u32[]{:S(2)}, u32[]{:S(2)}) collective-permute-start(bf16[192,256]{1,0:T(8,128)(2,1)S(1)} %get-tuple-element.301), channel_id=1, source_target_pairs={{0,6},{1,7},{2,0},{3,1},{4,2},{5,3},{6,4},{7,5},{8,14},{9,15},{10,... | collective-permute-start | bytes 294920 | tf_op jit(solution)/shard_map/ppermute | solution.py:1285
  60.4 12.4 %collective-permute-start.9 = (bf16[192,256]{1,0:T(8,128)(2,1)S(1)}, bf16[192,256]{1,0:T(8,128)(2,1)S(1)}, u32[]{:S(2)}, u32[]{:S(2)}) collective-permute-start(bf16[192,256]{1,0:T(8,128)(2,1)S(1)} %get-tuple-element.300), channel_id=1, source_target_pairs={{0,4},{1,5},{2,6},{3,7},{4,0},{5,1},{6,2},{7,3},{8,12},{9,13},{10,... | collective-permute-start | bytes 294920 | tf_op jit(solution)/shard_map/ppermute | solution.py:1285
  97.3 10.9 %collective-permute-start.15 = (bf16[16,120,768]{2,1,0:T(8,128)(2,1)}, bf16[16,120,768]{2,1,0:T(8,128)(2,1)S(1)}, u32[]{:S(2)}, u32[]{:S(2)}) collective-permute-start(bf16[16,120,768]{2,1,0:T(8,128)(2,1)} %get-tuple-element.195), channel_id=1, source_target_pairs={{0,1},{1,0},{2,3},{3,2},{4,5},{5,4},{6,7},{7,6},{8,9},{9,8},{10,11... | collective-permute-start | bytes 8847368 | tf_op jit(solution)/shard_map/ppermute | solution.py:1289
  98.4 8.3 %collective-permute-start.14 = (bf16[16,96,768]{2,1,0:T(8,128)(2,1)S(1)}, bf16[16,96,768]{2,1,0:T(8,128)(2,1)S(1)}, u32[]{:S(2)}, u32[]{:S(2)}) collective-permute-start(bf16[16,96,768]{2,1,0:T(8,128)(2,1)S(1)} %get-tuple-element.191), channel_id=1, source_target_pairs={{0,1},{1,0},{2,3},{3,2},{4,5},{5,4},{6,7},{7,6},{8,9},{9,8},{10,11... | collective-permute-start | bytes 7077896 | tf_op jit(solution)/shard_map/ppermute | solution.py:1289
  98.5 13.7 %collective-permute-start.11 = (bf16[192,256]{1,0:T(8,128)(2,1)S(1)}, bf16[192,256]{1,0:T(8,128)(2,1)S(1)}, u32[]{:S(2)}, u32[]{:S(2)}) collective-permute-start(bf16[192,256]{1,0:T(8,128)(2,1)S(1)} %get-tuple-element.187), channel_id=1, source_target_pairs={{0,2},{1,3},{2,4},{3,5},{4,6},{5,7},{6,0},{7,1},{8,10},{9,11},{10,... | collective-permute-start | bytes 294920 | tf_op jit(solution)/shard_map/ppermute | solution.py:1285
  99.0 13.2 %collective-permute-start.12 = (bf16[192,256]{1,0:T(8,128)(2,1)S(1)}, bf16[192,256]{1,0:T(8,128)(2,1)S(1)}, u32[]{:S(2)}, u32[]{:S(2)}) collective-permute-start(bf16[192,256]{1,0:T(8,128)(2,1)S(1)} %get-tuple-element.188), channel_id=1, source_target_pairs={{0,4},{1,5},{2,6},{3,7},{4,0},{5,1},{6,2},{7,3},{8,12},{9,13},{10,... | collective-permute-start | bytes 294920 | tf_op jit(solution)/shard_map/ppermute | solution.py:1285
  100.3 12.0 %collective-permute-start.13 = (bf16[192,256]{1,0:T(8,128)(2,1)S(1)}, bf16[192,256]{1,0:T(8,128)(2,1)S(1)}, u32[]{:S(2)}, u32[]{:S(2)}) collective-permute-start(bf16[192,256]{1,0:T(8,128)(2,1)S(1)} %get-tuple-element.189), channel_id=1, source_target_pairs={{0,6},{1,7},{2,0},{3,1},{4,2},{5,3},{6,4},{7,5},{8,14},{9,15},{10,... | collective-permute-start | bytes 294920 | tf_op jit(solution)/shard_map/ppermute | solution.py:1285
  112.3 16.3 %collective-permute-start.16 = (bf16[2,2,96,768]{3,2,1,0:T(8,128)(2,1)S(1)}, bf16[2,2,96,768]{3,2,1,0:T(8,128)(2,1)S(1)}, u32[]{:S(2)}, u32[]{:S(2)}) collective-permute-start(bf16[2,2,96,768]{3,2,1,0:T(8,128)(2,1)S(1)} %get-tuple-element.209), channel_id=1, source_target_pairs={{0,8},{8,0},{16,24},{24,16},{1,9},{9,1},{17,25},{25,17},{2,10},{10... | collective-permute-start | bytes 1769480 | tf_op jit(solution)/shard_map/ppermute | solution.py:1293
  114.7 15.3 %collective-permute-start.17 = (bf16[2,2,96,768]{3,2,1,0:T(8,128)(2,1)S(1)}, bf16[2,2,96,768]{3,2,1,0:T(8,128)(2,1)S(1)}, u32[]{:S(2)}, u32[]{:S(2)}) collective-permute-start(bf16[2,2,96,768]{3,2,1,0:T(8,128)(2,1)S(1)} %get-tuple-element.210), channel_id=1, source_target_pairs={{0,16},{8,24},{16,0},{24,8},{1,17},{9,25},{17,1},{25,9},{2,18},{10... | collective-permute-start | bytes 1769480 | tf_op jit(solution)/shard_map/ppermute | solution.py:1293
  130.0 19.2 %collective-permute-start.19 = (bf16[2,2,120,768]{3,2,1,0:T(8,128)(2,1)}, bf16[2,2,120,768]{3,2,1,0:T(8,128)(2,1)}, u32[]{:S(2)}, u32[]{:S(2)}) collective-permute-start(bf16[2,2,120,768]{3,2,1,0:T(8,128)(2,1)} %get-tuple-element.219), channel_id=1, source_target_pairs={{0,8},{8,0},{16,24},{24,16},{1,9},{9,1},{17,25},{25,17},{2,10},{10... | collective-permute-start | bytes 2211848 | tf_op jit(solution)/shard_map/ppermute | solution.py:1293
  131.2 18.5 %collective-permute-start.20 = (bf16[2,2,120,768]{3,2,1,0:T(8,128)(2,1)}, bf16[2,2,120,768]{3,2,1,0:T(8,128)(2,1)}, u32[]{:S(2)}, u32[]{:S(2)}) collective-permute-start(bf16[2,2,120,768]{3,2,1,0:T(8,128)(2,1)} %get-tuple-element.220), channel_id=1, source_target_pairs={{0,16},{8,24},{16,0},{24,8},{1,17},{9,25},{17,1},{25,9},{2,18},{10... | collective-permute-start | bytes 2211848 | tf_op jit(solution)/shard_map/ppermute | solution.py:1293
  135.3 14.5 %collective-permute-start.21 = (bf16[576,256]{1,0:T(8,128)(2,1)}, bf16[576,256]{1,0:T(8,128)(2,1)}, u32[]{:S(2)}, u32[]{:S(2)}) collective-permute-start(bf16[576,256]{1,0:T(8,128)(2,1)} %get-tuple-element.253), channel_id=1, source_target_pairs={{0,6},{1,7},{2,0},{3,1},{4,2},{5,3},{6,4},{7,5},{8,14},{9,15},{10,... | collective-permute-start | bytes 884744 | tf_op jit(solution)/shard_map/ppermute | solution.py:1285
  136.5 29.0 %collective-permute-start.22 = (bf16[576,256]{1,0:T(8,128)(2,1)}, bf16[576,256]{1,0:T(8,128)(2,1)}, u32[]{:S(2)}, u32[]{:S(2)}) collective-permute-start(bf16[576,256]{1,0:T(8,128)(2,1)} %copy-done.40), channel_id=1, source_target_pairs={{0,4},{1,5},{2,6},{3,7},{4,0},{5,1},{6,2},{7,3},{8,12},{9,13},{10,... | collective-permute-start | bytes 884744 | tf_op jit(solution)/shard_map/ppermute | solution.py:1285
  137.3 28.2 %collective-permute-start.23 = (bf16[576,256]{1,0:T(8,128)(2,1)}, bf16[576,256]{1,0:T(8,128)(2,1)}, u32[]{:S(2)}, u32[]{:S(2)}) collective-permute-start(bf16[576,256]{1,0:T(8,128)(2,1)} %copy-done.38), channel_id=1, source_target_pairs={{0,2},{1,3},{2,4},{3,5},{4,6},{5,7},{6,0},{7,1},{8,10},{9,11},{10,... | collective-permute-start | bytes 884744 | tf_op jit(solution)/shard_map/ppermute | solution.py:1285
  156.4 16.3 %collective-permute-start.24 = (bf16[2,216,768]{2,1,0:T(8,128)(2,1)}, bf16[2,216,768]{2,1,0:T(8,128)(2,1)S(1)}, u32[]{:S(2)}, u32[]{:S(2)}) collective-permute-start(bf16[2,216,768]{2,1,0:T(8,128)(2,1)} %copy-done.36), channel_id=1, source_target_pairs={{0,16},{8,24},{16,0},{24,8},{1,17},{9,25},{17,1},{25,9},{2,18},{10... | collective-permute-start | bytes 1990664 | tf_op jit(solution)/shard_map/ppermute | solution.py:1293
  157.6 16.4 %collective-permute-start.25 = (bf16[2,216,768]{2,1,0:T(8,128)(2,1)}, bf16[2,216,768]{2,1,0:T(8,128)(2,1)}, u32[]{:S(2)}, u32[]{:S(2)}) collective-permute-start(bf16[2,216,768]{2,1,0:T(8,128)(2,1)} %copy-done.35), channel_id=1, source_target_pairs={{0,8},{8,0},{16,24},{24,16},{1,9},{9,1},{17,25},{25,17},{2,10},{10... | collective-permute-start | bytes 1990664 | tf_op jit(solution)/shard_map/ppermute | solution.py:1293
  174.1 8.6 %collective-permute-start.29 = (bf16[16,24,768]{2,1,0:T(8,128)(2,1)}, bf16[16,24,768]{2,1,0:T(8,128)(2,1)S(1)}, u32[]{:S(2)}, u32[]{:S(2)}) collective-permute-start(bf16[16,24,768]{2,1,0:T(8,128)(2,1)} %bitcast.93), channel_id=1, source_target_pairs={{0,1},{1,0},{2,3},{3,2},{4,5},{5,4},{6,7},{7,6},{8,9},{9,8},{10,11... | collective-permute-start | bytes 1769480 | tf_op jit(solution)/shard_map/ppermute | solution.py:1289
  176.5 22.1 %collective-permute-start.26 = (bf16[216,768]{1,0:T(8,128)(2,1)S(1)}, bf16[216,768]{1,0:T(8,128)(2,1)S(1)}, u32[]{:S(2)}, u32[]{:S(2)}) collective-permute-start(bf16[216,768]{1,0:T(8,128)(2,1)S(1)} %get-tuple-element.271), channel_id=1, source_target_pairs={{0,2},{1,3},{2,4},{3,5},{4,6},{5,7},{6,0},{7,1},{8,10},{9,11},{10,... | collective-permute-start | bytes 995336 | tf_op jit(solution)/shard_map/ppermute | solution.py:1285
  180.2 24.2 %collective-permute-start.27 = (bf16[216,768]{1,0:T(8,128)(2,1)S(1)}, bf16[216,768]{1,0:T(8,128)(2,1)S(1)}, u32[]{:S(2)}, u32[]{:S(2)}) collective-permute-start(bf16[216,768]{1,0:T(8,128)(2,1)S(1)} %get-tuple-element.272), channel_id=1, source_target_pairs={{0,4},{1,5},{2,6},{3,7},{4,0},{5,1},{6,2},{7,3},{8,12},{9,13},{10,... | collective-permute-start | bytes 995336 | tf_op jit(solution)/shard_map/ppermute | solution.py:1285
  180.2 24.2 %collective-permute-start.28 = (bf16[216,768]{1,0:T(8,128)(2,1)S(1)}, bf16[216,768]{1,0:T(8,128)(2,1)S(1)}, u32[]{:S(2)}, u32[]{:S(2)}) collective-permute-start(bf16[216,768]{1,0:T(8,128)(2,1)S(1)} %get-tuple-element.273), channel_id=1, source_target_pairs={{0,6},{1,7},{2,0},{3,1},{4,2},{5,3},{6,4},{7,5},{8,14},{9,15},{10,... | collective-permute-start | bytes 995336 | tf_op jit(solution)/shard_map/ppermute | solution.py:1285
  183.3 5.8 %collective-permute-start.30 = (bf16[2,2,24,768]{3,2,1,0:T(8,128)(2,1)S(1)}, bf16[2,2,24,768]{3,2,1,0:T(8,128)(2,1)S(1)}, u32[]{:S(2)}, u32[]{:S(2)}) collective-permute-start(bf16[2,2,24,768]{3,2,1,0:T(8,128)(2,1)S(1)} %get-tuple-element.278), channel_id=1, source_target_pairs={{0,8},{8,0},{16,24},{24,16},{1,9},{9,1},{17,25},{25,17},{2,10},{10... | collective-permute-start | bytes 442376 | tf_op jit(solution)/shard_map/ppermute | solution.py:1293
  196.2 8.2 %collective-permute-start.34 = (bf16[24,768]{1,0:T(8,128)(2,1)S(1)}, bf16[24,768]{1,0:T(8,128)(2,1)S(1)}, u32[]{:S(2)}, u32[]{:S(2)}) collective-permute-start(bf16[24,768]{1,0:T(8,128)(2,1)S(1)} %get-tuple-element.285), channel_id=1, source_target_pairs={{0,2},{1,3},{2,4},{3,5},{4,6},{5,7},{6,0},{7,1},{8,10},{9,11},{10,... | collective-permute-start | bytes 110600 | tf_op jit(solution)/shard_map/ppermute | solution.py:1285
  196.3 16.1 %collective-permute-start.35 = (bf16[24,768]{1,0:T(8,128)(2,1)S(1)}, bf16[24,768]{1,0:T(8,128)(2,1)S(1)}, u32[]{:S(2)}, u32[]{:S(2)}) collective-permute-start(bf16[24,768]{1,0:T(8,128)(2,1)S(1)} %get-tuple-element.286), channel_id=1, source_target_pairs={{0,4},{1,5},{2,6},{3,7},{4,0},{5,1},{6,2},{7,3},{8,12},{9,13},{10,... | collective-permute-start | bytes 110600 | tf_op jit(solution)/shard_map/ppermute | solution.py:1285
  198.5 13.9 %collective-permute-start.36 = (bf16[24,768]{1,0:T(8,128)(2,1)S(1)}, bf16[24,768]{1,0:T(8,128)(2,1)S(1)}, u32[]{:S(2)}, u32[]{:S(2)}) collective-permute-start(bf16[24,768]{1,0:T(8,128)(2,1)S(1)} %get-tuple-element.287), channel_id=1, source_target_pairs={{0,6},{1,7},{2,0},{3,1},{4,2},{5,3},{6,4},{7,5},{8,14},{9,15},{10,... | collective-permute-start | bytes 110600 | tf_op jit(solution)/shard_map/ppermute | solution.py:1285
  (57 other events, 361.1 us)

commit v3 on v2

--- a/solution.py
+++ b/solution.py
@@ -535,6 +535,9 @@
     return (result, grad_input) + tuple((summed_part * factor for summed_part in summed))
 
 
+NO_COST = pl.CostEstimate(flops=1000, bytes_accessed=1000, transcendentals=0)
+
+
 def split_log(level):
     remaining = math.log((level + 1) / level)
     pieces = []
@@ -545,22 +548,14 @@
     return pieces
 
 
-def extra_features(heads, size, lanes):
-    masks, owners, query_values, key_values = [], [], [], []
-    for head in range(heads):
-        for lane in range(lanes):
-            level, piece = divmod(lane - size, 3)
-            used = size <= lane < size + 3 * (PATTERNS - 1)
-            masks.append(2 ** (level + 1) - 1 if used else 0)
-            owners.append(head)
-            query_values.append(split_log(level + 1)[piece] if used else 0.0)
-            key_values.append(1.0 if used else 0.0)
-    return (
-        np.array(masks, np.int32),
-        np.array(owners, np.int32),
-        np.array(query_values, np.float32),
-        np.array(key_values, np.float32),
-    )
+def extra_values(places, features, head, size, per_piece):
+    masks, values = jnp.zeros_like(features), jnp.zeros(features.shape, jnp.float32)
+    for level in range(1, PATTERNS):
+        for piece, value in enumerate(split_log(level)):
+            here = features == size + 3 * (level - 1) + piece
+            masks = jnp.where(here, 2**level - 1, masks)
+            values = jnp.where(here, value if per_piece else 1.0, values)
+    return jnp.where(((places - head) & masks) == 0, values, 0.0)
 
 
 def nt_dot(left, right):
@@ -573,7 +568,7 @@
     return jnp.dot(left, right, preferred_element_type=jnp.float32)
 
 
-def call_whole(kernel, out_shape, name, scalars, *arrays, in_specs=None, scratch=(), cost=None, limit=12):
+def call_whole(kernel, out_shape, name, scalars, *arrays, in_specs=None, scratch=(), limit=12):
     return pl.pallas_call(
         kernel,
         grid_spec=pltpu.PrefetchScalarGridSpec(
@@ -585,7 +580,7 @@
         ),
         out_shape=list(out_shape),
         compiler_params=pltpu.CompilerParams(vmem_limit_bytes=limit << 20),
-        cost_estimate=cost,
+        cost_estimate=NO_COST,
         name=name,
     )(scalars, *arrays)
 
@@ -596,37 +591,40 @@
     )
 
 
-def project_kernel(
-    blocks, own, scale, meta, *refs
-):
+def project_kernel(blocks, own, heads, scale, meta, *refs):
     normed = refs[:blocks]
-    wq_ref, wk_ref, wv_ref, row_ref, col_ref, row_value, col_value = refs[blocks : blocks + 7]
-    q_ref, k_ref, vt_ref = refs[blocks + 7 :]
+    wq_ref, wk_ref, wv_ref, q_ref, k_ref, vt_ref = refs[blocks:]
     length = normed[0].shape[0]
+    lanes = wk_ref.shape[1] // heads
+    size = lanes // 2
+    first_head = meta[blocks]
     for index in range(blocks):
         rows = normed[index][...]
-        start = meta[own + index]
+        start = meta[index]
         span = slice(index * length, (index + 1) * length)
-        place = start + lax.broadcasted_iota(jnp.int32, (length, 1), 0)
-        extra = jnp.where(
-            ((place - col_ref[1:2]) & col_ref[0:1]) == 0, col_value[...], 0.0
-        )
-        k_ref[span, :] = (nn_dot(rows, wk_ref[...]) + extra).astype(jnp.bfloat16)
+        keys = nn_dot(rows, wk_ref[...])
         vt_ref[:, span] = nt_dot(wv_ref[...], rows).astype(jnp.bfloat16)
+        places = start + lax.broadcasted_iota(jnp.int32, (length, 1), 0)
+        features = lax.broadcasted_iota(jnp.int32, (1, lanes), 1)
+        for head in range(heads):
+            wide_rows = slice(head * lanes, (head + 1) * lanes)
+            extra = extra_values(places, features, first_head + head, size, False)
+            k_ref[span, wide_rows] = (keys[:, wide_rows] + extra).astype(jnp.bfloat16)
         if index < own:
-            place = start + lax.broadcasted_iota(jnp.int32, (1, length), 1)
-            extra = jnp.where(
-                ((place - row_ref[:, 1:2]) & row_ref[:, 0:1]) == 0, row_value[...], 0.0
-            )
-            query = nt_dot(wq_ref[...], rows).astype(jnp.bfloat16).astype(jnp.float32)
-            q_ref[:, span] = (query * scale + extra).astype(jnp.bfloat16)
-
-
-def project(meta, normed, wq, wk, wv, row_info, col_info, row_value, col_value, own, scale):
+            queries = nt_dot(wq_ref[...], rows).astype(jnp.bfloat16).astype(jnp.float32) * scale
+            places = start + lax.broadcasted_iota(jnp.int32, (1, length), 1)
+            features = lax.broadcasted_iota(jnp.int32, (lanes, 1), 0)
+            for head in range(heads):
+                wide_rows = slice(head * lanes, (head + 1) * lanes)
+                extra = extra_values(places, features, first_head + head, size, True)
+                q_ref[wide_rows, span] = (queries[wide_rows] + extra).astype(jnp.bfloat16)
+
+
+def project(meta, normed, wq, wk, wv, own, heads, scale):
     blocks, length = len(normed), normed[0].shape[0]
     wide, share = wk.shape[1], wv.shape[0]
     return call_whole(
-        partial(project_kernel, blocks, own, scale),
+        partial(project_kernel, blocks, own, heads, scale),
         [
             jax.ShapeDtypeStruct((wide, own * length), jnp.bfloat16),
             jax.ShapeDtypeStruct((blocks * length, wide), jnp.bfloat16),
@@ -638,10 +636,6 @@
         wq,
         wk,
         wv,
-        row_info,
-        col_info,
-        row_value,
-        col_value,
         limit=20,
     )
 
@@ -670,7 +664,6 @@
         *normed,
         wk,
         wv,
-        cost=pl.CostEstimate(flops=3 * 10**9, bytes_accessed=6 << 20, transcendentals=0),
     )
 
 
@@ -686,7 +679,7 @@
     step = pl.program_id(0)
     steps = pl.num_programs(0)
     query_start = meta[step]
-    doc_first = meta[steps + key_blocks + step]
+    doc_first, doc_last = meta[steps + key_blocks + step], meta[2 * steps + key_blocks + step]
     doc_line = doc_ref[...]
     size = o_ref.shape[0] // heads
     lanes = q_ref.shape[0] // heads
@@ -694,27 +687,41 @@
     l_ref[...] = jnp.zeros_like(l_ref)
     o_ref[...] = jnp.zeros_like(o_ref)
 
+    def fold(slot, allowed):
+        span = pl.ds(pl.multiple_of(slot * block, block), block)
+        scores = [
+            nn_dot(
+                k_ref[span, head * lanes : (head + 1) * lanes],
+                q_ref[head * lanes : (head + 1) * lanes, :],
+            )
+            for head in range(heads)
+        ]
+        if allowed is not None:
+            scores = [jnp.where(allowed, part, big_negative) for part in scores]
+        for head in range(heads):
+            rows = slice(head * size, (head + 1) * size)
+            old_peak = m_ref[head]
+            new_peak = jnp.maximum(old_peak, jnp.max(scores[head], axis=0, keepdims=True))
+            weights = jnp.exp(scores[head] - new_peak)
+            fade = jnp.exp(old_peak - new_peak)
+            m_ref[head] = new_peak
+            l_ref[head] = l_ref[head] * fade + jnp.sum(weights, axis=0, keepdims=True)
+            o_ref[rows, :] = o_ref[rows, :] * fade + nn_dot(
+                vt_ref[rows, span], weights.astype(jnp.bfloat16)
+            )
+
     def body(slot, carry):
         key_start = meta[steps + slot]
-
-        @pl.when((key_start <= query_start) & (key_start + block > doc_first))
+        live = (key_start <= query_start) & (key_start + block > doc_first)
+        full = (key_start < query_start) & (key_start >= doc_last)
+
+        @pl.when(full)
         def _():
-            span = pl.ds(pl.multiple_of(slot * block, block), block)
-            allowed = pair_mask(query_start, key_start, doc_line, block)
-            for head in range(heads):
-                wide = slice(head * lanes, (head + 1) * lanes)
-                rows = slice(head * size, (head + 1) * size)
-                scores = nn_dot(k_ref[span, wide], q_ref[wide, :])
-                scores = jnp.where(allowed, scores, big_negative)
-                old_peak = m_ref[head]
-                new_peak = jnp.maximum(old_peak, jnp.max(scores, axis=0, keepdims=True))
-                weights = jnp.exp(scores - new_peak)
-                fade = jnp.exp(old_peak - new_peak)
-                m_ref[head] = new_peak
-                l_ref[head] = l_ref[head] * fade + jnp.sum(weights, axis=0, keepdims=True)
-                o_ref[rows, :] = o_ref[rows, :] * fade + nn_dot(
-                    vt_ref[rows, span], weights.astype(jnp.bfloat16)
-                )
+            fold(slot, None)
+
+        @pl.when(live & jnp.logical_not(full))
+        def _():
+            fold(slot, pair_mask(query_start, key_start, doc_line, block))
 
         return carry
 
@@ -747,15 +754,15 @@
     other_ref,
     acc_ref,
     pair_ref,
+    delta_ref,
 ):
     step = pl.program_id(0)
     steps = pl.num_programs(0)
     query_start = meta[step]
-    doc_first = meta[steps + key_blocks + step]
+    doc_first, doc_last = meta[steps + key_blocks + step], meta[2 * steps + key_blocks + step]
     doc_line = doc_ref[...]
     size = g_ref.shape[0] // heads
     lanes = q_ref.shape[0] // heads
-
     share = g_ref.shape[0]
 
     @pl.when(step == 0)
@@ -763,28 +770,48 @@
         pair_ref[...] = jnp.zeros_like(pair_ref)
 
     acc_ref[...] = jnp.zeros_like(acc_ref)
+    for head in range(heads):
+        rows = slice(head * size, (head + 1) * size)
+        delta_ref[head] = jnp.sum(
+            g_ref[rows, :].astype(jnp.float32) * o_ref[rows, :], axis=0, keepdims=True
+        )
+
+    def fold(slot, allowed):
+        span = pl.ds(pl.multiple_of(slot * block, block), block)
+        probs, grad_scores = [], []
+        for head in range(heads):
+            wide_rows = slice(head * lanes, (head + 1) * lanes)
+            rows = slice(head * size, (head + 1) * size)
+            probs.append(nn_dot(k_ref[span, wide_rows], q_ref[wide_rows, :]))
+            grad_scores.append(
+                nn_dot(v_ref[span, head * lanes : head * lanes + size], g_ref[rows, :])
+            )
+        for head in range(heads):
+            part = jnp.exp(probs[head] - lse_ref[head])
+            if allowed is not None:
+                part = jnp.where(allowed, part, 0.0)
+            grad_scores[head] = (part * (grad_scores[head] - delta_ref[head])).astype(jnp.bfloat16)
+            probs[head] = part.astype(jnp.bfloat16)
+        for head in range(heads):
+            rows = slice(head * size, (head + 1) * size)
+            value_rows = slice(share + head * size, share + (head + 1) * size)
+            query_rows = slice(head * lanes, head * lanes + size)
+            pair_ref[value_rows, span] += nt_dot(g_ref[rows, :], probs[head])
+            pair_ref[rows, span] += nt_dot(q_ref[query_rows, :], grad_scores[head])
+            acc_ref[rows, :] += nn_dot(kt_ref[rows, span], grad_scores[head])
 
     def body(slot, carry):
         key_start = meta[steps + slot]
-
-        @pl.when((key_start <= query_start) & (key_start + block > doc_first))
+        live = (key_start <= query_start) & (key_start + block > doc_first)
+        full = (key_start < query_start) & (key_start >= doc_last)
+
+        @pl.when(full)
         def _():
-            span = pl.ds(pl.multiple_of(slot * block, block), block)
-            allowed = pair_mask(query_start, key_start, doc_line, block)
-            for head in range(heads):
-                wide = slice(head * lanes, (head + 1) * lanes)
-                rows = slice(head * size, (head + 1) * size)
-                grad = g_ref[rows, :]
-                delta = jnp.sum(grad.astype(jnp.float32) * o_ref[rows, :], axis=0, keepdims=True)
-                scores = nn_dot(k_ref[span, wide], q_ref[wide, :])
-                probs = jnp.where(allowed, jnp.exp(scores - lse_ref[head]), 0.0)
-                dots = nn_dot(v_ref[span, head * lanes : head * lanes + size], grad)
-                grad_scores = (probs * (dots - delta)).astype(jnp.bfloat16)
-                value_rows = slice(share + head * size, share + (head + 1) * size)
-                pair_ref[value_rows, span] += nt_dot(grad, probs.astype(jnp.bfloat16))
-                query = q_ref[head * lanes : head * lanes + size, :]
-                pair_ref[rows, span] += nt_dot(query, grad_scores)
-                acc_ref[rows, :] += nn_dot(kt_ref[rows, span], grad_scores)
+            fold(slot, None)
+
+        @pl.when(live & jnp.logical_not(full))
+        def _():
+            fold(slot, pair_mask(query_start, key_start, doc_line, block))
 
         return carry
 
@@ -833,7 +860,7 @@
             jax.ShapeDtypeStruct((heads, 1, queries), jnp.float32),
         ],
         compiler_params=pltpu.CompilerParams(vmem_limit_bytes=12 << 20),
-        cost_estimate=pl.CostEstimate(flops=8 * 10**9, bytes_accessed=8 << 20, transcendentals=0),
+        cost_estimate=NO_COST,
         name="attend",
     )(meta, doc_line, q_ext, k_ext, v_t)
 
@@ -865,6 +892,7 @@
             scratch_shapes=[
                 pltpu.VMEM((share, block), jnp.float32),
                 pltpu.VMEM((2 * share, keys), jnp.float32),
+                pltpu.VMEM((heads, 1, block), jnp.float32),
             ],
         ),
         out_shape=[
@@ -873,7 +901,7 @@
             jax.ShapeDtypeStruct((2 * share, keys // 2), jnp.bfloat16),
         ],
         compiler_params=pltpu.CompilerParams(vmem_limit_bytes=20 << 20),
-        cost_estimate=pl.CostEstimate(flops=10**6, bytes_accessed=1 << 10, transcendentals=0),
+        cost_estimate=NO_COST,
         name="attend_back",
     )(meta, doc_line, q_ext, grad_t, mixed, lse, k_ext, k_t, v_ext)
 
@@ -901,6 +929,48 @@
     )
 
 
+def head_grads_kernel(chips, per, unused, normed_ref, *refs):
+    grads = refs[:chips]
+    weights_ref, gain_ref, row_ref, lane_ref, late_ref, keep_ref, send_ref = refs[chips:]
+    block = normed_ref.shape[1] // chips
+    own = nt_dot(normed_ref[:, :block], grads[0][...])
+    for step in range(1, chips):
+        own = own + nt_dot(normed_ref[:, step * block : (step + 1) * block], grads[step][...])
+    gains = jnp.sum(own * weights_ref[...].astype(jnp.float32), axis=1, keepdims=True)
+    gains = (gains * gain_ref[...] * lane_ref[...]).astype(jnp.bfloat16)
+    gains = nn_dot(row_ref[...], gains) + late_ref[...]
+    chunks, _, width = keep_ref.shape
+    columns = own.shape[1]
+    for which, target in enumerate((keep_ref, send_ref)):
+        for chunk in range(chunks):
+            first = (which * chunks + chunk) * per
+            rows = slice(first, first + per)
+            target[chunk, :, :columns] = own[rows].astype(jnp.bfloat16)
+            target[chunk, :, columns : width - 128] = jnp.zeros(
+                (per, width - 128 - columns), jnp.bfloat16
+            )
+            target[chunk, :, width - 128 :] = gains[rows].astype(jnp.bfloat16)
+
+
+def head_grads(scalars, normed_p, grads, weights_p, gain_rows, where_row, where_lane, late, per):
+    width = normed_p.shape[0]
+    out = jax.ShapeDtypeStruct((width // (2 * per), per, width), jnp.bfloat16)
+    return call_whole(
+        partial(head_grads_kernel, len(grads), per),
+        [out, out],
+        "head_grads",
+        scalars,
+        normed_p,
+        *grads,
+        weights_p,
+        gain_rows,
+        where_row,
+        where_lane,
+        late,
+        limit=24,
+    )
+
+
 def norm_parts(values):
     shifted = values - jnp.mean(values, axis=-1, keepdims=True)
     rate = lax.rsqrt(jnp.mean(shifted * shifted, axis=-1, keepdims=True) + 1e-05)
@@ -917,238 +987,226 @@
     )
 
 
-def middle_kernel(
-    chips,
-    tiles,
-    per,
-    position,
-    *refs,
-):
+def middle_kernel(chips, tiles, position, *refs):
     mixed = refs[:chips]
-    (
-        tokens_ref,
-        cot_ref,
-        wout_ref,
-        wup_ref,
-        wdown_ref,
-        perm_ref,
-        ginner_ref,
-        gfeed_ref,
-        ghidden_ref,
-        result_ref,
-        gmid_ref,
-    ) = refs[chips : chips + 11]
+    tokens_ref, cot_ref, wout_ref, wup_ref, wdown_ref, ginner_ref, gfeed_ref, ghidden_ref = refs[
+        chips : chips + 8
+    ]
+    result_ref, gmid_ref, gmid_b_ref = refs[chips + 8 : chips + 11]
     go_refs = refs[chips + 11 : 2 * chips + 11]
     (
-        down_keep,
-        down_send,
-        flat_keep,
-        flat_send,
+        z_ref,
+        h2_ref,
+        bent_out,
+        pre_out,
         dinner_ref,
         dfeed_ref,
         dhidden_ref,
         swap_ref,
-        mid_ref,
-        z_ref,
+        work_ref,
+        column_ref,
         zhat_ref,
-        h2_ref,
         hat_ref,
-        h2p_ref,
         act_ref,
         slope_ref,
         dact_ref,
         acc_ref,
         stat_ref,
-        down_tile,
-        flat_tile,
-        down_sem,
-        flat_sem,
     ) = refs[2 * chips + 11 :]
     step = pl.program_id(0)
-    chip, core = position[0], position[1]
+    chip = position[0]
     block, model_width = tokens_ref.shape
     share = model_width // chips
     tile = wdown_ref.shape[0]
     hidden = tile * tiles
     root = math.sqrt(2.0 / math.pi)
     phase, index = step // tiles, step % tiles
-    slot = lax.rem(index, 2)
-    chunks = down_keep.shape[0]
-    group = down_tile.shape[1]
-    flat = model_width // (2 * chunks)
-
-    def down_copies(where, tile_index):
-        area = pl.ds(group * tile_index, group)
-        return [
-            pltpu.make_async_copy(
-                down_tile.at[where, :, side], target.at[area], down_sem.at[where, which]
-            )
-            for which, (side, target) in enumerate(((core, down_keep), (1 - core, down_send)))
-        ]
-
-    def flat_copies(where, first_row):
-        area = (slice(None), pl.ds(first_row, flat))
-        return [
-            pltpu.make_async_copy(
-                flat_tile.at[where, which], target.at[area], flat_sem.at[where, which]
-            )
-            for which, target in enumerate((flat_keep, flat_send))
-        ]
-
-    def fill_flat(where, grad):
-        for which in range(2):
-            for chunk in range(chunks):
-                first = (which * chunks + chunk) * flat
-                flat_tile[where, which, chunk] = grad[first : first + flat].astype(jnp.bfloat16)
+    lanes = stat_ref.shape[2]
+    groups = tile // lanes
+
+    def by_rows(body):
+        body(slice(None))
+
+    def spread(stat):
+        return jnp.concatenate([stat] * groups, axis=1)
+
+    def gathered_lanes(values):
+        total = values[:, :lanes]
+        for group in range(1, groups):
+            total = total + values[:, group * lanes : (group + 1) * lanes]
+        return total
+
+    def lane_sum(values):
+        return jnp.broadcast_to(jnp.sum(values, axis=-1, keepdims=True), values.shape)
+
+    def column_sums(values):
+        total = values[:8]
+        for first in range(8, values.shape[0], 8):
+            total = total + values[first : first + 8]
+        return total
+
+    def norm_rows(values):
+        shifted = values - spread(lane_sum(gathered_lanes(values)) / tile)
+        rate = lax.rsqrt(lane_sum(gathered_lanes(shifted * shifted)) / tile + 1e-05)
+        return shifted * spread(rate), rate
+
+    def norm_rows_back(grad, hat, rate, gain):
+        scaled = grad * gain
+        mean_scaled = lane_sum(gathered_lanes(scaled)) / tile
+        mean_product = lane_sum(gathered_lanes(scaled * hat)) / tile
+        return spread(rate) * (scaled - spread(mean_scaled) - hat * spread(mean_product))
 
     @pl.when(step == 0)
     def _():
         for near in range(chips):
             start = pl.multiple_of(share * lax.rem(chip + near, chips), share)
             swap_ref[pl.ds(start, share), :] = mixed[near][...].astype(jnp.float32)
-        zhat, zrate = norm_parts(swap_ref[...].T)
-        zhat_ref[...] = zhat
-        stat_ref[0] = jnp.broadcast_to(zrate, stat_ref.shape[1:])
-        z = (zhat * ginner_ref[...]).astype(jnp.bfloat16)
-        z_ref[...] = z
-        mid = tokens_ref[...].astype(jnp.float32) + nn_dot(z, wout_ref[...])
-        mid_ref[...] = mid
-        hat, rate = norm_parts(mid)
-        hat_ref[...] = hat
-        stat_ref[1] = jnp.broadcast_to(rate, stat_ref.shape[1:])
-        h2 = (hat * gfeed_ref[...]).astype(jnp.bfloat16)
-        h2_ref[...] = h2
-        h2p_ref[...] = nt_dot(perm_ref[...], h2).astype(jnp.bfloat16)
+        work_ref[...] = swap_ref[...].T
+
+        def first_norm(rows):
+            zhat, zrate = norm_rows(work_ref[rows, :])
+            zhat_ref[rows, :] = zhat
+            stat_ref[0, rows, :] = zrate
+            z_ref[rows, :] = (zhat * ginner_ref[...]).astype(jnp.bfloat16)
+
+        by_rows(first_norm)
+        work_ref[...] = nn_dot(z_ref[...], wout_ref[...])
+
+        def second_norm(rows):
+            mid = tokens_ref[rows, :].astype(jnp.float32) + work_ref[rows, :]
+            acc_ref[rows, :] = mid
+            hat, rate = norm_rows(mid)
+            hat_ref[rows, :] = hat
+            stat_ref[1, rows, :] = rate
+            h2_ref[rows, :] = (hat * gfeed_ref[...]).astype(jnp.bfloat16)
+
+        by_rows(second_norm)
+        for stat in range(3, 7):
+            stat_ref[stat] = jnp.zeros_like(stat_ref[stat])
 
     @pl.when(phase == 0)
     def _():
-        u = nn_dot(h2_ref[...], wup_ref[...])
-        squared = u * u
-        bend = jnp.tanh(root * (u + 0.044715 * u * squared))
-        value = 0.5 * u * (1.0 + bend)
-        slope_ref[index] = 0.5 * (1.0 + bend) + 0.5 * u * (1.0 - bend * bend) * root * (
-            1.0 + 3.0 * 0.044715 * squared
-        )
-        act_ref[index] = value
+        work_ref[...] = nn_dot(h2_ref[...], wup_ref[...])
+
+        def bend_rows(rows):
+            u = work_ref[rows, :]
+            squared = u * u
+            bend = jnp.tanh(root * (u + 0.044715 * u * squared))
+            act_ref[index, rows, :] = 0.5 * u * (1.0 + bend)
+            slope_ref[index, rows, :] = 0.5 * (1.0 + bend) + 0.5 * u * (1.0 - bend * bend) * root * (
+                1.0 + 3.0 * 0.044715 * squared
+            )
+
+        by_rows(bend_rows)
 
         @pl.when(index == 0)
         def _():
-            stat_ref[2] = jnp.broadcast_to(
-                jnp.mean(value, axis=-1, keepdims=True), stat_ref.shape[1:]
-            )
-            stat_ref[3] = jnp.zeros_like(stat_ref[3])
-            stat_ref[4] = jnp.zeros_like(stat_ref[4])
-
-        off = value - stat_ref[2][:, :1]
-        stat_ref[3] += jnp.broadcast_to(
-            jnp.sum(off, axis=-1, keepdims=True), stat_ref.shape[1:]
-        )
-        stat_ref[4] += jnp.broadcast_to(
-            jnp.sum(off * off, axis=-1, keepdims=True), stat_ref.shape[1:]
-        )
+            def pivot(rows):
+                stat_ref[2, rows, :] = lane_sum(gathered_lanes(act_ref[0, rows, :])) / tile
+
+            by_rows(pivot)
+
+        def sums(rows):
+            off = act_ref[index, rows, :] - spread(stat_ref[2, rows, :])
+            stat_ref[3, rows, :] += gathered_lanes(off)
+            stat_ref[4, rows, :] += gathered_lanes(off * off)
+
+        by_rows(sums)
 
     @pl.when(step == tiles)
     def _():
-        drift = stat_ref[3] / hidden
+        drift = lane_sum(stat_ref[3]) / hidden
         stat_ref[2] = stat_ref[2] + drift
-        stat_ref[4] = lax.rsqrt(jnp.maximum(stat_ref[4] / hidden - drift * drift, 0.0) + 1e-05)
-        stat_ref[5] = jnp.zeros_like(stat_ref[5])
-        stat_ref[6] = jnp.zeros_like(stat_ref[6])
-        acc_ref[...] = mid_ref[...]
+        stat_ref[4] = lax.rsqrt(
+            jnp.maximum(lane_sum(stat_ref[4]) / hidden - drift * drift, 0.0) + 1e-05
+        )
 
     @pl.when(phase == 1)
     def _():
-        gain = ghidden_ref[...]
-        hat = (act_ref[index] - stat_ref[2][:, :1]) * stat_ref[4][:, :1]
-        act_ref[index] = hat
-        act = (hat * gain).astype(jnp.bfloat16)
-        cot = cot_ref[...]
-        acc_ref[...] += nn_dot(act, wdown_ref[...])
-        grad = nt_dot(cot, wdown_ref[...])
-        dhidden_ref[...] = jnp.sum(grad * hat, axis=0, keepdims=True)
-        scaled = grad * gain
-        dact_ref[index] = scaled
-        stat_ref[5] += jnp.broadcast_to(
-            jnp.sum(scaled, axis=-1, keepdims=True), stat_ref.shape[1:]
-        )
-        stat_ref[6] += jnp.broadcast_to(
-            jnp.sum(scaled * hat, axis=-1, keepdims=True), stat_ref.shape[1:]
-        )
-        grad = lax.dot_general(
-            act, cot, (((0,), (0,)), ((), ())), preferred_element_type=jnp.float32
-        )
-
-        @pl.when(index >= 2)
-        def _():
-            for copy in down_copies(slot, index - 2):
-                copy.wait()
-
-        for part in range(group):
-            for side in range(2):
-                first = (2 * part + side) * per
-                down_tile[slot, part, side] = grad[first : first + per].astype(jnp.bfloat16)
-        for copy in down_copies(slot, index):
-            copy.start()
+        def hidden_rows(rows):
+            hat = (act_ref[index, rows, :] - spread(stat_ref[2, rows, :])) * spread(
+                stat_ref[4, rows, :]
+            )
+            act_ref[index, rows, :] = hat
+            bent_out[rows, :] = (hat * ghidden_ref[...]).astype(jnp.bfloat16)
+
+        by_rows(hidden_rows)
+        work_ref[...] = nt_dot(cot_ref[...], wdown_ref[...])
+        acc_ref[...] += nn_dot(bent_out[...], wdown_ref[...])
+        column_ref[...] = jnp.zeros_like(column_ref)
+
+        def grad_rows(rows):
+            hat, grad = act_ref[index, rows, :], work_ref[rows, :]
+            column_ref[...] += column_sums(grad * hat)
+            scaled = grad * ghidden_ref[...]
+            dact_ref[index, rows, :] = scaled
+            stat_ref[5, rows, :] += gathered_lanes(scaled)
+            stat_ref[6, rows, :] += gathered_lanes(scaled * hat)
+
+        by_rows(grad_rows)
+        dhidden_ref[...] = jnp.sum(column_ref[...], axis=0, keepdims=True)
 
     @pl.when(step == 2 * tiles)
     def _():
         result_ref[...] = acc_ref[...].astype(jnp.bfloat16)
         acc_ref[...] = jnp.zeros_like(acc_ref)
+        stat_ref[5] = lane_sum(stat_ref[5]) / hidden
+        stat_ref[6] = lane_sum(stat_ref[6]) / hidden
 
     @pl.when(phase == 2)
     def _():
-        inner = dact_ref[index] - (stat_ref[5][:, :1] + act_ref[index] * stat_ref[6][:, :1]) / hidden
-        pre = (stat_ref[4][:, :1] * inner * slope_ref[index]).astype(jnp.bfloat16)
-        grad = nn_dot(h2p_ref[...], pre)
-
-        @pl.when(index >= 2)
-        def _():
-            for copy in flat_copies(slot, flat * (index - 2)):
-                copy.wait()
-
-        fill_flat(slot, grad)
-        for copy in flat_copies(slot, flat * index):
-            copy.start()
-
-        acc_ref[...] += nt_dot(pre, wup_ref[...])
+        def pre_rows(rows):
+            inner = (
+                dact_ref[index, rows, :]
+                - spread(stat_ref[5, rows, :])
+                - act_ref[index, rows, :] * spread(stat_ref[6, rows, :])
+            )
+            pre_out[rows, :] = (
+                spread(stat_ref[4, rows, :]) * inner * slope_ref[index, rows, :]
+            ).astype(jnp.bfloat16)
+
+        by_rows(pre_rows)
+        acc_ref[...] += nt_dot(pre_out[...], wup_ref[...])
 
     @pl.when(step == 3 * tiles - 1)
     def _():
-        back, dfeed = norm_back(acc_ref[...], hat_ref[...], stat_ref[1][:, :1], gfeed_ref[...])
-        dfeed_ref[...] = dfeed
-        gmid = cot_ref[...].astype(jnp.float32) + back
-        gmid_ref[...] = gmid
-        gmid_b = gmid.astype(jnp.bfloat16)
-        zp = nt_dot(perm_ref[...], z_ref[...]).astype(jnp.bfloat16)
-        fill_flat(2, nn_dot(zp, gmid_b))
-        for copy in flat_copies(2, flat * tiles):
-            copy.start()
-        go, dinner = norm_back(
-            nt_dot(gmid_b, wout_ref[...]), zhat_ref[...], stat_ref[0][:, :1], ginner_ref[...]
-        )
-        dinner_ref[...] = dinner
-        swap_ref[...] = go.T
+        column_ref[...] = jnp.zeros_like(column_ref)
+
+        def middle_rows(rows):
+            grad, hat = acc_ref[rows, :], hat_ref[rows, :]
+            column_ref[...] += column_sums(grad * hat)
+            gmid = cot_ref[rows, :].astype(jnp.float32) + norm_rows_back(
+                grad, hat, stat_ref[1, rows, :], gfeed_ref[...]
+            )
+            gmid_ref[rows, :] = gmid
+            gmid_b_ref[rows, :] = gmid.astype(jnp.bfloat16)
+
+        by_rows(middle_rows)
+        dfeed_ref[...] = jnp.sum(column_ref[...], axis=0, keepdims=True)
+        work_ref[...] = nt_dot(gmid_b_ref[...], wout_ref[...])
+        column_ref[...] = jnp.zeros_like(column_ref)
+
+        def inner_rows(rows):
+            grad, hat = work_ref[rows, :], zhat_ref[rows, :]
+            column_ref[...] += column_sums(grad * hat)
+            work_ref[rows, :] = norm_rows_back(grad, hat, stat_ref[0, rows, :], ginner_ref[...])
+
+        by_rows(inner_rows)
+        dinner_ref[...] = jnp.sum(column_ref[...], axis=0, keepdims=True)
+        swap_ref[...] = work_ref[...].T
         for near in range(chips):
             start = pl.multiple_of(share * lax.rem(chip + near, chips), share)
             go_refs[near][...] = swap_ref[pl.ds(start, share), :].astype(jnp.bfloat16)
-        for late in range(tiles - min(tiles, 2), tiles):
-            for copy in down_copies(late % 2, late) + flat_copies(late % 2, flat * late):
-                copy.wait()
-        for copy in flat_copies(2, flat * tiles):
-            copy.wait()
-
-
-def middle(position, mixed, tokens, cotangent, w_out, w_up, w_down, perm, gains, per):
+
+
+def middle(position, mixed, tokens, cotangent, w_out, w_up, w_down, gains):
     chips = len(mixed)
     block, model_width = tokens.shape
     hidden = w_up.shape[1]
     tile = model_width
     tiles = hidden // tile
     share = model_width // chips
-    chunks, last = hidden // (2 * per), tiles - 1
-    flat, group = model_width // (2 * chunks), chunks // tiles
-    down_out = jax.ShapeDtypeStruct((chunks, per, model_width), jnp.bfloat16)
-    flat_out = jax.ShapeDtypeStruct((chunks, flat * (tiles + 1), model_width), jnp.bfloat16)
+    last = tiles - 1
 
     def up_index(i, pos):
         return (0, jnp.where(i < tiles, i, jnp.where(i < 2 * tiles, last, i - 2 * tiles)))
@@ -1159,79 +1217,156 @@
     def hidden_index(i, pos):
         return (0, jnp.clip(i - tiles, 0, last))
 
+    def pre_index(i, pos):
+        return (0, jnp.clip(i - 2 * tiles, 0, last))
+
     def f32(*shape):
         return pltpu.VMEM(shape, jnp.float32)
 
-    def b16(*shape):
-        return pltpu.VMEM(shape, jnp.bfloat16)
-
-    square = (model_width, model_width)
-    row = (1, model_width)
+    row, rows = (1, model_width), (block, model_width)
+    narrow = jax.ShapeDtypeStruct(rows, jnp.bfloat16)
     return pl.pallas_call(
-        partial(middle_kernel, chips, tiles, per),
+        partial(middle_kernel, chips, tiles),
         grid_spec=pltpu.PrefetchScalarGridSpec(
             num_scalar_prefetch=1,
             grid=(3 * tiles,),
             in_specs=[whole((share, block))] * chips
             + [
-                whole((block, model_width)),
-                whole((block, model_width)),
-                whole(square),
+                whole(rows),
+                whole(rows),
+                whole((model_width, model_width)),
                 pl.BlockSpec((model_width, tile), up_index),
                 pl.BlockSpec((tile, model_width), down_index),
-                whole(square),
                 whole(row),
                 whole(row),
                 pl.BlockSpec((1, tile), hidden_index),
             ],
-            out_specs=[whole((block, model_width)), whole((block, model_width))]
+            out_specs=[whole(rows)] * 3
             + [whole((share, block))] * chips
             + [
-                pl.BlockSpec(memory_space=pl.ANY),
-                pl.BlockSpec(memory_space=pl.ANY),
-                pl.BlockSpec(memory_space=pl.ANY),
-                pl.BlockSpec(memory_space=pl.ANY),
+                whole(rows),
+                whole(rows),
+                pl.BlockSpec((block, tile), hidden_index),
+                pl.BlockSpec((block, tile), pre_index),
                 whole(row),
                 whole(row),
                 pl.BlockSpec((1, tile), hidden_index),
             ],
             scratch_shapes=[
                 f32(model_width, block),
+                f32(block, tile),
+                f32(8, tile),
                 f32(block, model_width),
-                b16(block, model_width),
                 f32(block, model_width),
-                b16(block, model_width),
-                f32(block, model_width),
-                b16(model_width, block),
                 f32(tiles, block, tile),
                 f32(tiles, block, tile),
                 f32(tiles, block, tile),
                 f32(block, model_width),
                 f32(7, block, 128),
-                b16(2, group, 2, per, model_width),
-                b16(3, 2, chunks, flat, model_width),
-                pltpu.SemaphoreType.DMA((2, 2)),
-                pltpu.SemaphoreType.DMA((3, 2)),
             ],
         ),
-        out_shape=[
-            jax.ShapeDtypeStruct((block, model_width), jnp.bfloat16),
-            jax.ShapeDtypeStruct((block, model_width), jnp.float32),
-        ]
+        out_shape=[narrow, jax.ShapeDtypeStruct(rows, jnp.float32), narrow]
         + [jax.ShapeDtypeStruct((share, block), jnp.bfloat16)] * chips
         + [
-            down_out,
-            down_out,
-            flat_out,
-            flat_out,
+            narrow,
+            narrow,
+            jax.ShapeDtypeStruct((block, hidden), jnp.bfloat16),
+            jax.ShapeDtypeStruct((block, hidden), jnp.bfloat16),
             jax.ShapeDtypeStruct(row, jnp.float32),
             jax.ShapeDtypeStruct(row, jnp.float32),
             jax.ShapeDtypeStruct((1, hidden), jnp.float32),
         ],
-        compiler_params=pltpu.CompilerParams(vmem_limit_bytes=44 << 20),
-        cost_estimate=pl.CostEstimate(flops=16 * 10**9, bytes_accessed=40 << 20, transcendentals=0),
+        compiler_params=pltpu.CompilerParams(vmem_limit_bytes=36 << 20),
+        cost_estimate=NO_COST,
         name="middle",
-    )(position, *mixed, tokens, cotangent, w_out, w_up, w_down, perm, *gains)
+    )(position, *mixed, tokens, cotangent, w_out, w_up, w_down, *gains)
+
+
+def down_kernel(per, position, bent_ref, cot_ref, keep_ref, send_ref):
+    first_core = position[1] == 0
+    grad = lax.dot_general(
+        bent_ref[...], cot_ref[...], (((0,), (0,)), ((), ())), preferred_element_type=jnp.float32
+    ).astype(jnp.bfloat16)
+    for part in range(keep_ref.shape[0]):
+        even = grad[2 * per * part : 2 * per * part + per]
+        odd = grad[2 * per * part + per : 2 * per * (part + 1)]
+        keep_ref[part] = jnp.where(first_core, even, odd)
+        send_ref[part] = jnp.where(first_core, odd, even)
+
+
+def down_grad(position, bent, cotangent, per):
+    (block, hidden), model_width = bent.shape, cotangent.shape[1]
+    tiles, chunks = hidden // model_width, hidden // (2 * per)
+    out = jax.ShapeDtypeStruct((chunks, per, model_width), jnp.bfloat16)
+    out_spec = pl.BlockSpec((chunks // tiles, per, model_width), lambda i, pos: (i, 0, 0))
+    return pl.pallas_call(
+        partial(down_kernel, per),
+        grid_spec=pltpu.PrefetchScalarGridSpec(
+            num_scalar_prefetch=1,
+            grid=(tiles,),
+            in_specs=[
+                pl.BlockSpec((block, model_width), lambda i, pos: (0, i)),
+                whole(cotangent.shape),
+            ],
+            out_specs=[out_spec, out_spec],
+        ),
+        out_shape=[out, out],
+        compiler_params=pltpu.CompilerParams(vmem_limit_bytes=20 << 20),
+        cost_estimate=NO_COST,
+        name="down_grad",
+    )(position, bent, cotangent)
+
+
+def up_out_kernel(tiles, position, h2_ref, pre_ref, z_ref, gmid_ref, perm_ref, keep_ref, send_ref, left_ref):
+    step = pl.program_id(0)
+    chunks, per = keep_ref.shape[:2]
+
+    @pl.when(step == 0)
+    def _():
+        left_ref[...] = nt_dot(perm_ref[...], h2_ref[...]).astype(jnp.bfloat16)
+
+    def store(right):
+        grad = nn_dot(left_ref[...], right)
+        for chunk in range(chunks):
+            keep_ref[chunk] = grad[chunk * per : (chunk + 1) * per].astype(jnp.bfloat16)
+            first = (chunks + chunk) * per
+            send_ref[chunk] = grad[first : first + per].astype(jnp.bfloat16)
+
+    @pl.when(step < tiles)
+    def _():
+        store(pre_ref[...])
+
+    @pl.when(step == tiles)
+    def _():
+        left_ref[...] = nt_dot(perm_ref[...], z_ref[...]).astype(jnp.bfloat16)
+        store(gmid_ref[...])
+
+
+def up_out_grad(position, h2, pre, z, gmid, perm, per):
+    (block, hidden), model_width = pre.shape, h2.shape[1]
+    tiles, chunks = hidden // model_width, model_width // (2 * per)
+    out = jax.ShapeDtypeStruct((chunks, per * (tiles + 1), model_width), jnp.bfloat16)
+    out_spec = pl.BlockSpec((chunks, per, model_width), lambda i, pos: (0, i, 0))
+    return pl.pallas_call(
+        partial(up_out_kernel, tiles),
+        grid_spec=pltpu.PrefetchScalarGridSpec(
+            num_scalar_prefetch=1,
+            grid=(tiles + 1,),
+            in_specs=[
+                whole(h2.shape),
+                pl.BlockSpec((block, model_width), lambda i, pos: (0, jnp.minimum(i, tiles - 1))),
+                whole(z.shape),
+                whole(gmid.shape),
+                whole(perm.shape),
+            ],
+            out_specs=[out_spec, out_spec],
+            scratch_shapes=[pltpu.VMEM((model_width, block), jnp.bfloat16)],
+        ),
+        out_shape=[out, out],
+        compiler_params=pltpu.CompilerParams(vmem_limit_bytes=20 << 20),
+        cost_estimate=NO_COST,
+        name="up_out_grad",
+    )(position, h2, pre, z, gmid, perm)
 
 
 def final_kernel(chips, position, *refs):
@@ -1502,7 +1637,9 @@
     in_block = jnp.arange(block, dtype=jnp.int32)[None, :]
     query_places = (query_starts[:, None] + in_block).reshape(-1)
     doc_line = jnp.max(jnp.where(bounds[:, None] <= query_places[None, :], bounds[:, None], 0), axis=0)
-    meta = jnp.concatenate([query_starts, key_starts, doc_line.reshape(chips, block)[:, 0]])
+    meta = jnp.concatenate(
+        [query_starts, key_starts, doc_line.reshape(chips, block)[:, 0], doc_line.reshape(chips, block)[:, -1]]
+    )
     doc_line = doc_line[None, :]
 
     feature = jnp.arange(model_width, dtype=jnp.int32)
@@ -1532,11 +1669,24 @@
     wanted = (2 * (chunk % chunks) + parity) * per + inside
     perm = (wanted[:, None] == feature[None, :]).astype(jnp.bfloat16)
 
-    masks, owners, query_values, key_values = extra_features(heads, size, lanes)
-    head_ids = heads * chip + jnp.asarray(owners)
-    info = jnp.stack([jnp.asarray(masks), head_ids])
+    gains_share = (3 * model_width + hidden) // parts
+    gains_rows = -(-gains_share // 128)
+    owner = 2 * (chunk % chunks) + parity
+    first_gain = owner * gains_share + 128 * inside
+    end_gain = jnp.minimum(first_gain + 128, (owner + 1) * gains_share)
+    where_row = (
+        (inside < gains_rows)[:, None]
+        & (wanted[None, :] >= first_gain[:, None])
+        & (wanted[None, :] < end_gain[:, None])
+    ).astype(jnp.bfloat16)
+    where_lane = (
+        (wanted % gains_share % 128)[:, None] == jnp.arange(128, dtype=jnp.int32)[None, :]
+    ).astype(jnp.float32)
+    gain_rows = (1.0 / gain_attend).reshape(parts // 2, 2, per)
+    gain_rows = jnp.where(core == 0, gain_rows, gain_rows[:, ::-1]).transpose(1, 0, 2)
+    gain_rows = gain_rows.reshape(model_width, 1)
     early = (
-        jnp.concatenate([query_starts, key_starts]),
+        jnp.concatenate([query_starts, 2 * block * chip_ids + block * (1 - core), heads * chip[None]]),
         meta,
         doc_line,
         perm,
@@ -1546,17 +1696,19 @@
         picked_rows(w_key, pick_narrow),
         picked(w_value, pick_wide),
         jnp.concatenate([picked(weight, pick_narrow) for weight in (w_query, w_key, w_value)], axis=1),
-        info,
-        info.T,
         gain_attend[None, :],
         gain_inner[None, :],
         gain_feed[None, :],
         gain_hidden[None, :],
         place,
+        where_row,
+        where_lane,
+        gain_rows,
     )
     own[1], early = lax.optimization_barrier((own[1], early))
     starts, meta, doc_line, perm, wq_wide, wk_wide, wv_rows, wk_rows, wv_wide, w_own = early[:10]
-    info, info_t, gain_first, gain_inner, gain_feed, gain_hidden, place = early[10:]
+    gain_first, gain_inner, gain_feed, gain_hidden, place = early[10:15]
+    where_row, where_lane, gain_rows = early[15:]
     sibling = [seq_swap(rows, 1) for rows in own]
     q_ext, k_ext, v_t = project(
         starts,
@@ -1564,11 +1716,8 @@
         wq_wide,
         wk_wide,
         wv_rows,
-        info_t,
-        info,
-        jnp.asarray(query_values)[:, None],
-        jnp.asarray(key_values)[None, :],
         chips,
+        heads,
         scale,
     )
     mixed, mixed_b, lse = attend(meta, doc_line, q_ext, k_ext, v_t, heads, block)
@@ -1584,79 +1733,65 @@
     )
 
     outs = middle(
-        place,
-        back,
-        tokens,
-        cotangent,
-        w_out,
-        w_up,
-        w_down,
-        perm,
-        (gain_inner, gain_feed, gain_hidden),
-        hidden // parts,
-    )
-    result, grad_middle = outs[:2]
-    go = outs[2 : 2 + chips]
-    keep_a, send_a, keep_b, send_b, dinner, dfeed, dhidden = outs[2 + chips :]
+        place, back, tokens, cotangent, w_out, w_up, w_down, (gain_inner, gain_feed, gain_hidden)
+    )
+    result, grad_middle, gmid_b = outs[:3]
+    go = outs[3 : 3 + chips]
+    z, h2, bent, pre, dinner, dfeed, dhidden = outs[3 + chips :]
+    go = [go[0]] + [chip_shift(go[step], step) for step in range(1, chips)]
+    go[1], bent, pre = lax.optimization_barrier((go[1], bent, pre))
+    keep_a, send_a = down_grad(place, bent, cotangent, hidden // parts)
+    keep_b, send_b = up_out_grad(place, h2, pre, z, gmid_b, perm, per)
+
+    gains_late = jnp.concatenate([jnp.zeros_like(dinner), dinner, dfeed, dhidden], axis=1)
+    gains_late = gains_late.reshape(parts // 2, 2, gains_share)
+    gains_late = jnp.where(core == 0, gains_late, gains_late[:, ::-1]).transpose(1, 0, 2)
+    gains_late = jnp.pad(gains_late, ((0, 0), (0, 0), (0, gains_rows * 128 - gains_share)))
+    gains_late = jnp.pad(
+        gains_late.reshape(parts, gains_rows, 128), ((0, 0), (0, per - gains_rows), (0, 0))
+    ).reshape(model_width, 128)
 
     def gridded(array):
         return array.reshape((2, 2, chips) + array.shape[1:])
 
     keep_a, other_a = gridded(keep_a), gridded(seq_swap(send_a, 1))
-    keep_b, other_b = gridded(keep_b), gridded(seq_swap(send_b, 1))
-    out_a, out_b = outgoing(place, keep_a, other_a), outgoing(place, keep_b, other_b)
-    go = [go[0]] + [chip_shift(go[step], step) for step in range(1, chips)]
-    go, out_a, out_b = lax.optimization_barrier((go, out_a, out_b))
+    out_a = outgoing(place, keep_a, other_a)
+    kept_a = outgoing(place, keep_a, other_a, True)
+    other_b = seq_swap(send_b, 1)
+    go, out_a, kept_a, keep_b, send_b = lax.optimization_barrier(
+        (go, out_a, kept_a, keep_b, send_b)
+    )
     in_a = [row_swap(out_a[0], 1), row_swap(out_a[1], 2)]
     dq, pair, other = attend_back(
         meta, doc_line, q_ext, jnp.concatenate(go, axis=1), mixed, lse, k_ext, k_t, v_ext, heads, block, scale
     )
-    dq, pair, other, in_a, out_b = lax.optimization_barrier((dq, pair, other, in_a, out_b))
+    dq, pair, other, in_a, keep_b, other_b = lax.optimization_barrier(
+        (dq, pair, other, in_a, keep_b, other_b)
+    )
+    keep_b, other_b = gridded(keep_b), gridded(other_b)
+    out_b = outgoing(place, keep_b, other_b)
     in_b = [row_swap(out_b[0], 1), row_swap(out_b[1], 2)]
     grads = join_parts(place, dq, pair, seq_swap(other, 1), chips)
     home = [grads[0]] + [chip_shift(grads[step], -step) for step in range(1, chips)]
-    grads, keep_a, other_a, keep_b, other_b = lax.optimization_barrier(
-        (grads, keep_a, other_a, keep_b, other_b)
-    )
-    kept_a = outgoing(place, keep_a, other_a, True)
+    grads, keep_b, other_b = lax.optimization_barrier((grads, keep_b, other_b))
     kept_b = outgoing(place, keep_b, other_b, True)
-    in_a, in_b, kept_a, kept_b, home[1] = lax.optimization_barrier(
-        (in_a, in_b, kept_a, kept_b, home[1])
-    )
-    sums = halfway(place, [(*kept_a, *in_a), (*kept_b, *in_b)])
-    sums, grads = lax.optimization_barrier((sums, grads))
-    low_keep, low_send, high_keep, high_send = sums
+    mine_grad, send_grad = head_grads(
+        place, normed_p, grads, weights_p, gain_rows, where_row, where_lane, gains_late, per
+    )
+    in_a, in_b, kept_a, kept_b, home[1], mine_grad, send_grad = lax.optimization_barrier(
+        (in_a, in_b, kept_a, kept_b, home[1], mine_grad, send_grad)
+    )
+    low_keep, low_send, high_keep, high_send = halfway(place, [(*kept_a, *in_a), (*kept_b, *in_b)])
     low_in, high_in = row_swap(low_send, 2), row_swap(high_send, 1)
-    grads_t = jnp.concatenate(grads, axis=1)
-    own_grad = nt_dot(normed_p, grads_t)
-    dattend = jnp.sum(own_grad * wide(weights_p), axis=1).reshape(2, parts // 2, 1, per)
-    dattend = jnp.where(core == 0, dattend, dattend[::-1])
-    dattend = jnp.concatenate([dattend[0], dattend[1]], axis=1).reshape(1, model_width)
-    dattend = dattend / gain_first
-    gains_all = jnp.concatenate([dattend, dinner, dfeed, dhidden], axis=1)
-
-    gains_share = gains_all.shape[1] // parts
-    gains_rows = -(-gains_share // 128)
-    gains_all = gains_all.reshape(parts // 2, 2, gains_share)
-    gains_all = jnp.where(core == 0, gains_all, gains_all[:, ::-1]).transpose(1, 0, 2)
-    gains_all = jnp.pad(gains_all, ((0, 0), (0, 0), (0, gains_rows * 128 - gains_share)))
-    gains_all = jnp.pad(
-        gains_all.reshape(parts, gains_rows, 128), ((0, 0), (0, per - gains_rows), (0, 0))
-    ).reshape(model_width, 128)
-    gap = jnp.zeros((model_width, model_width - 128 - 3 * share), jnp.float32)
-    packed = sent(jnp.concatenate([own_grad, gap, gains_all], axis=1))
-    half = model_width // 2
-    mine_grad = packed[:half].reshape(parts // 2, per, model_width)
-    send_grad = packed[half:].reshape(parts // 2, per, model_width)
     home, low_in, high_in, mine_grad, send_grad = lax.optimization_barrier(
         (home, low_in, high_in, mine_grad, send_grad)
     )
+    mine_grad, other_grad = gridded(mine_grad), gridded(seq_swap(send_grad, 1))
     stage = split(place, [(low_keep, low_in, high_keep, high_in)], chips)
     arrived = [stage[0]] + [chip_shift(stage[step], step) for step in range(1, chips)]
     grad_input = final(
         place, home, tokens, grad_middle, w_query, w_key, w_value, gain_first
     )
-    mine_grad, other_grad = gridded(mine_grad), gridded(seq_swap(send_grad, 1))
     low, high = outgoing(place, mine_grad, other_grad)
     low_keep, low_send, high_keep, high_send = halfway(
         place,

time: 215 us -> 207 us (0.963)
  waiting for transfers between devices: 52.2 us -> 64.2 us
  Pallas kernels: 76.7 us -> 69.3 us
  matrix products: 17.5 us -> 12.5 us
  local copies, waits for them, and re-layouts: 15.4 us -> 10.4 us
    ppermute x17, waiting for transfers between devices: 15.1 us -> 42.5 us  [chip_shift(): lax.ppermute(value, 'seq', [(i, (i + 2 * steps) % count) for i in range(c...]
    ppermute x10, waiting for transfers between devices: 23.6 us -> 12.1 us  [row_swap(): lax.ppermute(value, 'row', [(i, i ^ bit) for i in range(lax.axis_size('ro...]
    slice x5 -> x1, local copies, waits for them, and re-layouts: 4.74 us -> 0.18 us  [fast_local(): doc_line.reshape(chips, block)[:, -1]]
    dot_general x2 -> x1, matrix products: 7.1 us -> 2.61 us  [nt_dot(): lax.dot_general(left, right, (((1,), (1,)), ((), ())), preferred_element_...]
    ppermute x8, waiting for transfers between devices: 6.11 us -> 1.7 us  [seq_swap(): lax.ppermute(value, 'seq', [(i, i ^ bit) for i in range(lax.axis_size('se...]
    pallas_call x1, Pallas kernels: 10.9 us -> 7.5 us  [attend(): pl.pallas_call(partial(attend_kernel, heads, block, key_blocks), grid_spe...]
    pallas_call x1, Pallas kernels: 11.9 us -> 9.15 us  [attend_back(): pl.pallas_call(partial(attend_back_kernel, heads, block, key_blocks, scal...]
    unnamed x105 -> x94, local copies, waits for them, and re-layouts: 8.64 us -> 7.33 us
  transfers between devices with their start and end apart: 37 -> 37, of which waited for: 16 -> 18; matrix products, arithmetic and copies ran while one was open for 13% -> 9% of each run, Pallas kernels for 16% -> 17%
where the time goes in v3:
time: 207 us
  Pallas kernels  69.3 us (33%)
  waiting for transfers between devices  64.2 us (31%)
  starting transfers between devices  44.9 us (22%)
  matrix products  12.5 us (6%)
  local copies, waits for them, and re-layouts  10.4 us (5%)
  other arithmetic  4.56 us (2%)
    ppermute x17, waiting for transfers between devices, chip_shift(): lax.ppermute(value, 'seq', [(i, (i + 2 * steps) % count) for i in range(c...  42.5 us
    pallas_call x17, Pallas kernels, call_whole(): pl.pallas_call(kernel, grid_spec=pltpu.PrefetchScalarGridSpec(num_scalar_...  29.5 us
    ppermute x17, starting transfers between devices, chip_shift(): lax.ppermute(value, 'seq', [(i, (i + 2 * steps) % count) for i in range(c...  28.8 us
    pallas_call x1, Pallas kernels, middle(): pl.pallas_call(partial(middle_kernel, chips, tiles), grid_spec=pltpu.Pref...  15.4 us
    ppermute x10, starting transfers between devices, row_swap(): lax.ppermute(value, 'row', [(i, i ^ bit) for i in range(lax.axis_size('ro...  12.7 us
    ppermute x10, waiting for transfers between devices, row_swap(): lax.ppermute(value, 'row', [(i, i ^ bit) for i in range(lax.axis_size('ro...  12.1 us
    pallas_call x1, Pallas kernels, attend_back(): pl.pallas_call(partial(attend_back_kernel, heads, block, key_blocks, scal...  9.15 us
    ppermute x1, waiting for transfers between devices, gathered(): lax.ppermute(ahead, 'seq', down)  7.92 us
  transfers between devices with their start and end apart: 37, of which 18 were waited for; matrix products, arithmetic and copies ran while one was open for 9% of the time, Pallas kernels for 17%

profile of v3, /device:TPU:0, one launch (start us, length us, event | category | flops | bytes accessed | tf_op | source)
XLA Modules:
  0.0 207.2 jit_solution(53145276465040944)
XLA Ops:
  2.6 3.1 %collective-permute-start = (bf16[256,768]{1,0:T(8,128)(2,1)S(1)}, bf16[256,768]{1,0:T(8,128)(2,1)S(1)}, u32[]{:S(2)}, u32[]{:S(2)}) collective-permute-start(bf16[256,768]{1,0:T(8,128)(2,1)S(1)} %norm.1.refs_0_), channel_id=1, source_target_pairs={{0,2},{1,3},{2,4},{3,5},{4,6},{5,7},{6,0},{7,1},{8,10},{9,11},{10,... | collective-permute-start | bytes 1179656 | tf_op jit(solution)/shard_map/ppermute | solution.py:1420
  5.7 2.1 %collective-permute-start.1 = (bf16[256,768]{1,0:T(8,128)(2,1)S(1)}, bf16[256,768]{1,0:T(8,128)(2,1)S(1)}, u32[]{:S(2)}, u32[]{:S(2)}) collective-permute-start(bf16[256,768]{1,0:T(8,128)(2,1)S(1)} %norm.1.refs_0_), channel_id=1, source_target_pairs={{0,6},{1,7},{2,0},{3,1},{4,2},{5,3},{6,4},{7,5},{8,14},{9,15},{10,... | collective-permute-start | bytes 1179656 | tf_op jit(solution)/shard_map/ppermute | solution.py:1420
  7.9 2.9 %convolution_convert_fusion.2.refs_8_ = bf16[384,768]{1,0:T(8,128)(2,1)} fusion(bf16[768,768]{1,0:T(8,128)(2,1)} %refs_6_.3, s32[384]{0:T(512)S(1)} %fusion.55, pred[384]{0:T(512)(128)(4,1)S(1)} %fusion.59), kind=kOutput, calls=%fused_computation.12 | convolution fusion | flops 454164480 | bytes 1771392 | tf_op jit(solution)/shard_map/dot_general | solution.py:1659
  19.5 5.2 %collective-permute-done.1.refs_3_ = bf16[256,768]{1,0:T(8,128)(2,1)S(1)} collective-permute-done((bf16[256,768]{1,0:T(8,128)(2,1)S(1)}, bf16[256,768]{1,0:T(8,128)(2,1)S(1)}, u32[]{:S(2)}, u32[]{:S(2)}) %collective-permute-start.1) | collective-permute-done | bytes 393248 | tf_op jit(solution)/shard_map/ppermute | solution.py:1420
  29.1 7.9 %collective-permute-done.2 = bf16[256,768]{1,0:T(8,128)(2,1)S(1)} collective-permute-done((bf16[256,768]{1,0:T(8,128)(2,1)S(1)}, bf16[256,768]{1,0:T(8,128)(2,1)S(1)}, u32[]{:S(2)}, u32[]{:S(2)}) %collective-permute-start.2) | collective-permute-done | bytes 393248 | tf_op jit(solution)/shard_map/ppermute | solution.py:1587
  38.9 3.8 %project.1 = (bf16[384,1024]{1,0:T(8,128)(2,1)S(1)}, bf16[2048,384]{1,0:T(8,128)(2,1)S(1)}, bf16[192,2048]{1,0:T(8,128)(2,1)S(1)}) custom-call(s32[9]{0:T(128)S(1)} %pad_add_fusion.meta, bf16[256,768]{1,0:T(8,128)(2,1)S(1)} %norm.1.refs_0_, bf16[256,768]{1,0:T(8,128)(2,1)S(1)} %collective-permute-done.refs_1_, ...), custom_call_target="tpu_custom_call" | custom-call | flops 1000 | bytes 1000 | tf_op jit(solution)/shard_map/project/pallas_call | solution.py:572
  42.7 7.5 %attend.1 = (f32[192,1024]{1,0:T(8,128)S(1)}, bf16[4,192,256]{2,1,0:T(8,128)(2,1)S(1)}, f32[3,1,1024]{2,1,0:T(1,128)S(1)}) custom-call(s32[20]{0:T(128)S(1)} %concatenate.19.meta, s32[1,1024]{1,0:T(1,128)S(1)} %bitcast.86, bf16[384,1024]{1,0:T(8,128)(2,1)S(1)} %get-tuple-element.165.q_ref, bf16[2048,384]{1,0:T(8,128)(2,1)S(1)} %get-tuple-element.166.k_ref, ...), custom_call_target="tpu_custom_call" | custom-call | flops 1000 | bytes 1000 | tf_op jit(solution)/shard_map/attend/pallas_call | solution.py:836
  50.2 4.7 %collective-permute-start.8 = (bf16[192,256]{1,0:T(8,128)(2,1)S(1)}, bf16[192,256]{1,0:T(8,128)(2,1)S(1)}, u32[]{:S(2)}, u32[]{:S(2)}) collective-permute-start(bf16[192,256]{1,0:T(8,128)(2,1)S(1)} %get-tuple-element.307), channel_id=1, source_target_pairs={{0,6},{1,7},{2,0},{3,1},{4,2},{5,3},{6,4},{7,5},{8,14},{9,15},{10,... | collective-permute-start | bytes 294920 | tf_op jit(solution)/shard_map/ppermute | solution.py:1420
  55.2 2.2 %collective-permute-start.10 = (bf16[192,256]{1,0:T(8,128)(2,1)S(1)}, bf16[192,256]{1,0:T(8,128)(2,1)S(1)}, u32[]{:S(2)}, u32[]{:S(2)}) collective-permute-start(bf16[192,256]{1,0:T(8,128)(2,1)S(1)} %get-tuple-element.305), channel_id=1, source_target_pairs={{0,2},{1,3},{2,4},{3,5},{4,6},{5,7},{6,0},{7,1},{8,10},{9,11},{10,... | collective-permute-start | bytes 294920 | tf_op jit(solution)/shard_map/ppermute | solution.py:1420
  57.4 2.6 %convolution_convert_fusion.normed_ref = bf16[768,1024]{1,0:T(8,128)(2,1)} fusion(bf16[768,768]{1,0:T(8,128)(2,1)S(1)} %get-tuple-element.178.perm_ref, bf16[256,768]{1,0:T(8,128)(2,1)S(1)} %collective-permute-done.1.refs_3_, bf16[256,768]{1,0:T(8,128)(2,1)S(1)} %broadcast_select_fusion.refs_2_, bf16[256,768]{1,0:T(8,128)(2,1)S(1)} %collective-permute-done.refs_1_, ...), kind=kOutput, calls=%fused_computation.3 | convolution fusion | flops 1215037440 | bytes 4325376 | tf_op jit(solution)/shard_map/dot_general | solution.py:562
  60.0 2.1 convolution_convert_fusion.1.refs_4_
  62.1 3.2 %project_back.1 = (bf16[192,2048]{1,0:T(8,128)(2,1)S(1)}, bf16[2048,384]{1,0:T(8,128)(2,1)S(1)}) custom-call(s32[4]{0:T(128)S(1)} %pad_add_fusion.1.unused.position.scalars, bf16[256,768]{1,0:T(8,128)(2,1)S(1)} %norm.1.refs_0_, bf16[256,768]{1,0:T(8,128)(2,1)S(1)} %collective-permute-done.refs_1_, bf16[256,768]{1,0:T(8,128)(2,1)S(1)} %broadcast_select_fusion.refs_2_, ...), custom_call_target="tpu_custom_call" | custom-call | flops 1000 | bytes 1000 | tf_op jit(solution)/shard_map/project_back/pallas_call | solution.py:572
  65.5 15.4 %middle.1 = (bf16[256,768]{1,0:T(8,128)(2,1)}, f32[256,768]{1,0:T(8,128)S(1)}, bf16[256,768]{1,0:T(8,128)(2,1)S(1)}, bf16[192,256]{1,0:T(8,128)(2,1)S(1)}, bf16[...) custom-call(s32[4]{0:T(128)S(1)} %pad_add_fusion.1.unused.position.s, ...), custom_call_target="tpu_custom_call" | custom-call | flops 1000 | bytes 1000 | tf_op jit(solution)/shard_map/middle/pallas_call | solution.py:1228
  82.1 5.2 %collective-permute-done.11 = bf16[192,256]{1,0:T(8,128)(2,1)S(1)} collective-permute-done((bf16[192,256]{1,0:T(8,128)(2,1)S(1)}, bf16[192,256]{1,0:T(8,128)(2,1)S(1)}, u32[]{:S(2)}, u32[]{:S(2)}) %collective-permute-start.11) | collective-permute-done | bytes 98336 | tf_op jit(solution)/shard_map/ppermute | solution.py:1420
  87.3 2.8 %down_grad.1 = (bf16[16,96,768]{2,1,0:T(8,128)(2,1)S(1)}, bf16[16,96,768]{2,1,0:T(8,128)(2,1)S(1)}) custom-call(s32[4]{0:T(128)S(1)} %pad_add_fusion.1.unused.position.scalars, bf16[256,3072]{1,0:T(8,128)(2,1)S(1)} %get-tuple-element.195.bent_ref, bf16[256,768]{1,0:T(8,128)(2,1)S(1)} %copy-done.5), custom_call_target="tpu_custom_call" | custom-call | flops 1000 | bytes 1000 | tf_op jit(solution)/shard_map/down_grad/pallas_call | solution.py:1302
  90.2 4.9 %up_out_grad.1 = (bf16[16,120,768]{2,1,0:T(8,128)(2,1)S(1)}, bf16[16,120,768]{2,1,0:T(8,128)(2,1)S(1)}) custom-call(s32[4]{0:T(128)S(1)} %pad_add_fusion.1.unused.position.scalars, bf16[256,768]{1,0:T(8,128)(2,1)S(1)} %get-tuple-element.202.h2_ref, bf16[256,3072]{1,0:T(8,128)(2,1)S(1)} %get-tuple-element.203.pre_ref, ...), custom_call_target="tpu_custom_call" | custom-call | flops 1000 | bytes 1000 | tf_op jit(solution)/shard_map/up_out_grad/pallas_call | solution.py:1350
  99.1 3.3 %collective-permute-done.12 = bf16[192,256]{1,0:T(8,128)(2,1)S(1)} collective-permute-done((bf16[192,256]{1,0:T(8,128)(2,1)S(1)}, bf16[192,256]{1,0:T(8,128)(2,1)S(1)}, u32[]{:S(2)}, u32[]{:S(2)}) %collective-permute-start.12) | collective-permute-done | bytes 98336 | tf_op jit(solution)/shard_map/ppermute | solution.py:1420
  104.4 2.6 %collective-permute-start.16 = (bf16[2,2,96,768]{3,2,1,0:T(8,128)(2,1)S(1)}, bf16[2,2,96,768]{3,2,1,0:T(8,128)(2,1)S(1)}, u32[]{:S(2)}, u32[]{:S(2)}) collective-permute-start(bf16[2,2,96,768]{3,2,1,0:T(8,128)(2,1)S(1)} %get-tuple-element.220), channel_id=1, source_target_pairs={{0,16},{8,24},{16,0},{24,8},{1,17},{9,25},{17,1},{25,9},{2,18},{10... | collective-permute-start | bytes 1769480 | tf_op jit(solution)/shard_map/ppermute | solution.py:1428
  107.0 9.2 %attend_back.1 = (bf16[192,1024]{1,0:T(8,128)(2,1)S(1)}, f32[384,1024]{1,0:T(8,128)S(1)}, bf16[384,1024]{1,0:T(8,128)(2,1)S(1)}) custom-call(s32[20]{0:T(128)S(1)} %concatenate.19.meta, s32[1,1024]{1,0:T(1,128)S(1)} %bitcast.87, bf16[384,1024]{1,0:T(8,128)(2,1)S(1)} %get-tuple-element.165.q_ref, bf16[192,1024]{1,0:T(8,128)(2,1)S(1)} %pad_maximum_fusion.1.g_ref, ...), custom_call_target="tpu_custom_call" | custom-call | flops 1000 | bytes 1000 | tf_op jit(solution)/shard_map/attend_back/pallas_call | solution.py:872
  117.6 2.1 collective-permute-done.16.refs_3_
  119.8 2.1 %outgoing.4 = (bf16[2,2,120,768]{3,2,1,0:T(8,128)(2,1)}, bf16[2,2,120,768]{3,2,1,0:T(8,128)(2,1)}) custom-call(s32[4]{0:T(128)S(1)} %pad_add_fusion.1.unused.position.scalars, bf16[2,2,4,120,768]{4,3,2,1,0:T(8,128)(2,1)S(1)} %bitcast.55, bf16[2,2,4,120,768]{4,3,2,1,0:T(8,128)(2,1)S(1)} %bitcast.59, bf16[2,2,4,120,768]{4,3,2,1,0:T(8,128)(2,1)S(1)} %bitcast.56, ...), custom_call_target="tpu_custom_call" | custom-call | flops 1000 | bytes 1000 | tf_op jit(solution)/shard_map/outgoing/pallas_call | solution.py:572
  122.3 1.9 collective-permute-start.20
  127.7 2.0 collective-permute-start.21
  135.5 4.2 %head_grads.1 = (bf16[16,24,768]{2,1,0:T(8,128)(2,1)S(1)}, bf16[16,24,768]{2,1,0:T(8,128)(2,1)S(1)}) custom-call(s32[4]{0:T(128)S(1)} %pad_add_fusion.1.unused.position.scalars, bf16[768,1024]{1,0:T(8,128)(2,1)S(1)} %copy-done.8, bf16[576,256]{1,0:T(8,128)(2,1)S(1)} %copy-done.11, bf16[576,256]{1,0:T(8,128)(2,1)} %get-tuple-element.243.refs_1_, ...), custom_call_target="tpu_custom_call" | custom-call | flops 1000 | bytes 1000 | tf_op jit(solution)/shard_map/head_grads/pallas_call | solution.py:572
  141.1 2.5 %halfway.2 = (bf16[2,216,768]{2,1,0:T(8,128)(2,1)S(1)}, bf16[2,216,768]{2,1,0:T(8,128)(2,1)S(1)}, bf16[2,216,768]{2,1,0:T(8,128)(2,1)S(1)}, bf16[2,216,768]{2,1,0:T(8,128)(2,1)S(1)}) custom-call(s32[4]{0:T(128)S(1)} %pad_add_fusion.1.unused.position.scalars, bf16[2,2,96,768]{3,2,1,0:T(8,128)(2,1)S(1)} %copy-done.26, bf16[2,2,96,768]{3,2,1,0:T(8,128)(2,1)S(1)} %copy-done.28, ...), custom_call_target="tpu_custom_call" | custom-call | flops 1000 | bytes 1000 | tf_op jit(solution)/shard_map/halfway/pallas_call | solution.py:572
  149.8 18.4 %collective-permute-done.22.refs_2_ = bf16[576,256]{1,0:T(8,128)(2,1)S(1)} collective-permute-done((bf16[576,256]{1,0:T(8,128)(2,1)S(1)}, bf16[576,256]{1,0:T(8,128)(2,1)S(1)}, u32[]{:S(2)}, u32[]{:S(2)}) %collective-permute-start.22) | collective-permute-done | bytes 294944 | tf_op jit(solution)/shard_map/ppermute | solution.py:1420
  171.2 2.8 %collective-permute-start.28 = (bf16[216,768]{1,0:T(8,128)(2,1)S(1)}, bf16[216,768]{1,0:T(8,128)(2,1)S(1)}, u32[]{:S(2)}, u32[]{:S(2)}) collective-permute-start(bf16[216,768]{1,0:T(8,128)(2,1)S(1)} %get-tuple-element.281), channel_id=1, source_target_pairs={{0,6},{1,7},{2,0},{3,1},{4,2},{5,3},{6,4},{7,5},{8,14},{9,15},{10,... | collective-permute-start | bytes 995336 | tf_op jit(solution)/shard_map/ppermute | solution.py:1420
  176.3 3.8 %collective-permute-done.30.refs_2_ = bf16[2,2,24,768]{3,2,1,0:T(8,128)(2,1)S(1)} collective-permute-done((bf16[2,2,24,768]{3,2,1,0:T(8,128)(2,1)S(1)}, bf16[2,2,24,768]{3,2,1,0:T(8,128)(2,1)S(1)}, u32[]{:S(2)}, u32[]{:S(2)}) %collective-permute-start.30) | collective-permute-done | bytes 147488 | tf_op jit(solution)/shard_map/ppermute | solution.py:1428
  183.0 2.6 %collective-permute-done.32.refs_1_ = bf16[2,24,768]{2,1,0:T(8,128)(2,1)S(1)} collective-permute-done((bf16[2,24,768]{2,1,0:T(8,128)(2,1)S(1)}, bf16[2,24,768]{2,1,0:T(8,128)(2,1)S(1)}, u32[]{:S(2)}, u32[]{:S(2)}) %collective-permute-start.32) | collective-permute-done | bytes 73760 | tf_op jit(solution)/shard_map/ppermute | solution.py:1428
  188.1 2.8 %collective-permute-start.36 = (bf16[24,768]{1,0:T(8,128)(2,1)S(1)}, bf16[24,768]{1,0:T(8,128)(2,1)S(1)}, u32[]{:S(2)}, u32[]{:S(2)}) collective-permute-start(bf16[24,768]{1,0:T(8,128)(2,1)S(1)} %get-tuple-element.295), channel_id=1, source_target_pairs={{0,6},{1,7},{2,0},{3,1},{4,2},{5,3},{6,4},{7,5},{8,14},{9,15},{10,... | collective-permute-start | bytes 110600 | tf_op jit(solution)/shard_map/ppermute | solution.py:1420
  191.0 4.1 %final.1 = bf16[256,768]{1,0:T(8,128)(2,1)} custom-call(s32[4]{0:T(128)S(1)} %pad_add_fusion.1.unused.position.scalars, bf16[576,256]{1,0:T(8,128)(2,1)S(1)} %copy-done.11, bf16[576,256]{1,0:T(8,128)(2,1)} %collective-permute-done.21.refs_1_, bf16[576,256]{1,0:T(8,128)(2,1)S(1)} %collective-permute-done.22.refs_2_, ...), custom_call_target="tpu_custom_call" | custom-call | flops 1000 | bytes 1000 | tf_op jit(solution)/shard_map/final/pallas_call | solution.py:572
  197.3 7.8 %collective-permute-done.35.refs_6_ = bf16[24,768]{1,0:T(8,128)(2,1)S(1)} collective-permute-done((bf16[24,768]{1,0:T(8,128)(2,1)S(1)}, bf16[24,768]{1,0:T(8,128)(2,1)S(1)}, u32[]{:S(2)}, u32[]{:S(2)}) %collective-permute-start.35) | collective-permute-done | bytes 36896 | tf_op jit(solution)/shard_map/ppermute | solution.py:1420
  (212 shorter events, 57.9 us)
Async XLA Ops:
  2.6 23.4 %collective-permute-start = (bf16[256,768]{1,0:T(8,128)(2,1)S(1)}, bf16[256,768]{1,0:T(8,128)(2,1)S(1)}, u32[]{:S(2)}, u32[]{:S(2)}) collective-permute-start(bf16[256,768]{1,0:T(8,128)(2,1)S(1)} %norm.1.refs_0_), channel_id=1, source_target_pairs={{0,2},{1,3},{2,4},{3,5},{4,6},{5,7},{6,0},{7,1},{8,10},{9,11},{10,... | collective-permute-start | bytes 1179656 | tf_op jit(solution)/shard_map/ppermute | solution.py:1420
  5.7 19.0 %collective-permute-start.1 = (bf16[256,768]{1,0:T(8,128)(2,1)S(1)}, bf16[256,768]{1,0:T(8,128)(2,1)S(1)}, u32[]{:S(2)}, u32[]{:S(2)}) collective-permute-start(bf16[256,768]{1,0:T(8,128)(2,1)S(1)} %norm.1.refs_0_), channel_id=1, source_target_pairs={{0,6},{1,7},{2,0},{3,1},{4,2},{5,3},{6,4},{7,5},{8,14},{9,15},{10,... | collective-permute-start | bytes 1179656 | tf_op jit(solution)/shard_map/ppermute | solution.py:1420
  7.8 29.4 %collective-permute-start.4 = (bf16[256,768]{1,0:T(8,128)(2,1)S(1)}, bf16[256,768]{1,0:T(8,128)(2,1)S(1)}, u32[]{:S(2)}, u32[]{:S(2)}) collective-permute-start(bf16[256,768]{1,0:T(8,128)(2,1)S(1)} %norm.1.refs_0_), channel_id=1, source_target_pairs={{0,1},{1,0},{2,3},{3,2},{4,5},{5,4},{6,7},{7,6},{8,9},{9,8},{10,11... | collective-permute-start | bytes 1179656 | tf_op jit(solution)/shard_map/ppermute | solution.py:1424
  24.7 12.3 %collective-permute-start.2 = (bf16[256,768]{1,0:T(8,128)(2,1)S(1)}, bf16[256,768]{1,0:T(8,128)(2,1)S(1)}, u32[]{:S(2)}, u32[]{:S(2)}) collective-permute-start(bf16[256,768]{1,0:T(8,128)(2,1)S(1)} %collective-permute-done.1.refs_3_), channel_id=1, source_target_pairs={{2,0},{3,1},{4,2},{5,3},{10,8},{11,9},{12,10},{13,11},{18,16},{19,... | collective-permute-start | bytes 1179656 | tf_op jit(solution)/shard_map/ppermute | solution.py:1587
  26.0 11.0 %collective-permute-start.3 = (bf16[256,768]{1,0:T(8,128)(2,1)S(1)}, bf16[256,768]{1,0:T(8,128)(2,1)S(1)}, u32[]{:S(2)}, u32[]{:S(2)}) collective-permute-start(bf16[256,768]{1,0:T(8,128)(2,1)S(1)} %collective-permute-done.refs_1_), channel_id=1, source_target_pairs={{2,4},{3,5},{4,6},{5,7},{10,12},{11,13},{12,14},{13,15},{18,20},{1... | collective-permute-start | bytes 1179656 | tf_op jit(solution)/shard_map/ppermute | solution.py:1587
  28.6 8.6 %collective-permute-start.5 = (bf16[256,768]{1,0:T(8,128)(2,1)S(1)}, bf16[256,768]{1,0:T(8,128)(2,1)S(1)}, u32[]{:S(2)}, u32[]{:S(2)}) collective-permute-start(bf16[256,768]{1,0:T(8,128)(2,1)S(1)} %collective-permute-done.refs_1_), channel_id=1, source_target_pairs={{0,1},{1,0},{2,3},{3,2},{4,5},{5,4},{6,7},{7,6},{8,9},{9,8},{10,11... | collective-permute-start | bytes 1179656 | tf_op jit(solution)/shard_map/ppermute | solution.py:1424
  28.6 8.6 %collective-permute-start.7 = (bf16[256,768]{1,0:T(8,128)(2,1)S(1)}, bf16[256,768]{1,0:T(8,128)(2,1)S(1)}, u32[]{:S(2)}, u32[]{:S(2)}) collective-permute-start(bf16[256,768]{1,0:T(8,128)(2,1)S(1)} %collective-permute-done.1.refs_3_), channel_id=1, source_target_pairs={{0,1},{1,0},{2,3},{3,2},{4,5},{5,4},{6,7},{7,6},{8,9},{9,8},{10,11... | collective-permute-start | bytes 1179656 | tf_op jit(solution)/shard_map/ppermute | solution.py:1424
  50.2 15.1 %collective-permute-start.8 = (bf16[192,256]{1,0:T(8,128)(2,1)S(1)}, bf16[192,256]{1,0:T(8,128)(2,1)S(1)}, u32[]{:S(2)}, u32[]{:S(2)}) collective-permute-start(bf16[192,256]{1,0:T(8,128)(2,1)S(1)} %get-tuple-element.307), channel_id=1, source_target_pairs={{0,6},{1,7},{2,0},{3,1},{4,2},{5,3},{6,4},{7,5},{8,14},{9,15},{10,... | collective-permute-start | bytes 294920 | tf_op jit(solution)/shard_map/ppermute | solution.py:1420
  54.9 10.5 %collective-permute-start.9 = (bf16[192,256]{1,0:T(8,128)(2,1)S(1)}, bf16[192,256]{1,0:T(8,128)(2,1)S(1)}, u32[]{:S(2)}, u32[]{:S(2)}) collective-permute-start(bf16[192,256]{1,0:T(8,128)(2,1)S(1)} %get-tuple-element.306), channel_id=1, source_target_pairs={{0,4},{1,5},{2,6},{3,7},{4,0},{5,1},{6,2},{7,3},{8,12},{9,13},{10,... | collective-permute-start | bytes 294920 | tf_op jit(solution)/shard_map/ppermute | solution.py:1420
  55.2 10.1 %collective-permute-start.10 = (bf16[192,256]{1,0:T(8,128)(2,1)S(1)}, bf16[192,256]{1,0:T(8,128)(2,1)S(1)}, u32[]{:S(2)}, u32[]{:S(2)}) collective-permute-start(bf16[192,256]{1,0:T(8,128)(2,1)S(1)} %get-tuple-element.305), channel_id=1, source_target_pairs={{0,2},{1,3},{2,4},{3,5},{4,6},{5,7},{6,0},{7,1},{8,10},{9,11},{10,... | collective-permute-start | bytes 294920 | tf_op jit(solution)/shard_map/ppermute | solution.py:1420
  80.9 6.4 %collective-permute-start.11 = (bf16[192,256]{1,0:T(8,128)(2,1)S(1)}, bf16[192,256]{1,0:T(8,128)(2,1)S(1)}, u32[]{:S(2)}, u32[]{:S(2)}) collective-permute-start(bf16[192,256]{1,0:T(8,128)(2,1)S(1)} %get-tuple-element.189), channel_id=1, source_target_pairs={{0,2},{1,3},{2,4},{3,5},{4,6},{5,7},{6,0},{7,1},{8,10},{9,11},{10,... | collective-permute-start | bytes 294920 | tf_op jit(solution)/shard_map/ppermute | solution.py:1420
  90.1 7.3 %collective-permute-start.14 = (bf16[16,96,768]{2,1,0:T(8,128)(2,1)S(1)}, bf16[16,96,768]{2,1,0:T(8,128)(2,1)S(1)}, u32[]{:S(2)}, u32[]{:S(2)}) collective-permute-start(bf16[16,96,768]{2,1,0:T(8,128)(2,1)S(1)} %get-tuple-element.197), channel_id=1, source_target_pairs={{0,1},{1,0},{2,3},{3,2},{4,5},{5,4},{6,7},{7,6},{8,9},{9,8},{10,11... | collective-permute-start | bytes 7077896 | tf_op jit(solution)/shard_map/ppermute | solution.py:1424
  95.2 24.6 %collective-permute-start.17 = (bf16[16,120,768]{2,1,0:T(8,128)(2,1)S(1)}, bf16[16,120,768]{2,1,0:T(8,128)(2,1)S(1)}, u32[]{:S(2)}, u32[]{:S(2)}) collective-permute-start(bf16[16,120,768]{2,1,0:T(8,128)(2,1)S(1)} %get-tuple-element.207), channel_id=1, source_target_pairs={{0,1},{1,0},{2,3},{3,2},{4,5},{5,4},{6,7},{7,6},{8,9},{9,8},{10,11... | collective-permute-start | bytes 8847368 | tf_op jit(solution)/shard_map/ppermute | solution.py:1424
  95.7 6.7 %collective-permute-start.12 = (bf16[192,256]{1,0:T(8,128)(2,1)S(1)}, bf16[192,256]{1,0:T(8,128)(2,1)S(1)}, u32[]{:S(2)}, u32[]{:S(2)}) collective-permute-start(bf16[192,256]{1,0:T(8,128)(2,1)S(1)} %get-tuple-element.193), channel_id=1, source_target_pairs={{0,4},{1,5},{2,6},{3,7},{4,0},{5,1},{6,2},{7,3},{8,12},{9,13},{10,... | collective-permute-start | bytes 294920 | tf_op jit(solution)/shard_map/ppermute | solution.py:1420
  95.7 7.2 %collective-permute-start.13 = (bf16[192,256]{1,0:T(8,128)(2,1)S(1)}, bf16[192,256]{1,0:T(8,128)(2,1)S(1)}, u32[]{:S(2)}, u32[]{:S(2)}) collective-permute-start(bf16[192,256]{1,0:T(8,128)(2,1)S(1)} %get-tuple-element.194), channel_id=1, source_target_pairs={{0,6},{1,7},{2,0},{3,1},{4,2},{5,3},{6,4},{7,5},{8,14},{9,15},{10,... | collective-permute-start | bytes 294920 | tf_op jit(solution)/shard_map/ppermute | solution.py:1420
  102.9 14.8 %collective-permute-start.15 = (bf16[2,2,96,768]{3,2,1,0:T(8,128)(2,1)S(1)}, bf16[2,2,96,768]{3,2,1,0:T(8,128)(2,1)S(1)}, u32[]{:S(2)}, u32[]{:S(2)}) collective-permute-start(bf16[2,2,96,768]{3,2,1,0:T(8,128)(2,1)S(1)} %get-tuple-element.219), channel_id=1, source_target_pairs={{0,8},{8,0},{16,24},{24,16},{1,9},{9,1},{17,25},{25,17},{2,10},{10... | collective-permute-start | bytes 1769480 | tf_op jit(solution)/shard_map/ppermute | solution.py:1428
  104.4 15.3 %collective-permute-start.16 = (bf16[2,2,96,768]{3,2,1,0:T(8,128)(2,1)S(1)}, bf16[2,2,96,768]{3,2,1,0:T(8,128)(2,1)S(1)}, u32[]{:S(2)}, u32[]{:S(2)}) collective-permute-start(bf16[2,2,96,768]{3,2,1,0:T(8,128)(2,1)S(1)} %get-tuple-element.220), channel_id=1, source_target_pairs={{0,16},{8,24},{16,0},{24,8},{1,17},{9,25},{17,1},{25,9},{2,18},{10... | collective-permute-start | bytes 1769480 | tf_op jit(solution)/shard_map/ppermute | solution.py:1428
  121.9 19.1 %collective-permute-start.19 = (bf16[2,2,120,768]{3,2,1,0:T(8,128)(2,1)}, bf16[2,2,120,768]{3,2,1,0:T(8,128)(2,1)}, u32[]{:S(2)}, u32[]{:S(2)}) collective-permute-start(bf16[2,2,120,768]{3,2,1,0:T(8,128)(2,1)} %get-tuple-element.230), channel_id=1, source_target_pairs={{0,8},{8,0},{16,24},{24,16},{1,9},{9,1},{17,25},{25,17},{2,10},{10... | collective-permute-start | bytes 2211848 | tf_op jit(solution)/shard_map/ppermute | solution.py:1428
  122.3 18.9 %collective-permute-start.20 = (bf16[2,2,120,768]{3,2,1,0:T(8,128)(2,1)}, bf16[2,2,120,768]{3,2,1,0:T(8,128)(2,1)}, u32[]{:S(2)}, u32[]{:S(2)}) collective-permute-start(bf16[2,2,120,768]{3,2,1,0:T(8,128)(2,1)} %get-tuple-element.231), channel_id=1, source_target_pairs={{0,16},{8,24},{16,0},{24,8},{1,17},{9,25},{17,1},{25,9},{2,18},{10... | collective-permute-start | bytes 2211848 | tf_op jit(solution)/shard_map/ppermute | solution.py:1428
  127.7 13.4 %collective-permute-start.21 = (bf16[576,256]{1,0:T(8,128)(2,1)}, bf16[576,256]{1,0:T(8,128)(2,1)}, u32[]{:S(2)}, u32[]{:S(2)}) collective-permute-start(bf16[576,256]{1,0:T(8,128)(2,1)} %get-tuple-element.243.refs_1_), channel_id=1, source_target_pairs={{0,6},{1,7},{2,0},{3,1},{4,2},{5,3},{6,4},{7,5},{8,14},{9,15},{10,... | collective-permute-start | bytes 884744 | tf_op jit(solution)/shard_map/ppermute | solution.py:1420
  143.6 24.6 %collective-permute-start.24 = (bf16[2,216,768]{2,1,0:T(8,128)(2,1)S(1)}, bf16[2,216,768]{2,1,0:T(8,128)(2,1)S(1)}, u32[]{:S(2)}, u32[]{:S(2)}) collective-permute-start(bf16[2,216,768]{2,1,0:T(8,128)(2,1)S(1)} %get-tuple-element.264), channel_id=1, source_target_pairs={{0,16},{8,24},{16,0},{24,8},{1,17},{9,25},{17,1},{25,9},{2,18},{10... | collective-permute-start | bytes 1990664 | tf_op jit(solution)/shard_map/ppermute | solution.py:1428
  145.4 22.8 %collective-permute-start.25 = (bf16[2,216,768]{2,1,0:T(8,128)(2,1)S(1)}, bf16[2,216,768]{2,1,0:T(8,128)(2,1)S(1)}, u32[]{:S(2)}, u32[]{:S(2)}) collective-permute-start(bf16[2,216,768]{2,1,0:T(8,128)(2,1)S(1)} %get-tuple-element.265), channel_id=1, source_target_pairs={{0,8},{8,0},{16,24},{24,16},{1,9},{9,1},{17,25},{25,17},{2,10},{10... | collective-permute-start | bytes 1990664 | tf_op jit(solution)/shard_map/ppermute | solution.py:1428
  147.1 21.1 %collective-permute-start.22 = (bf16[576,256]{1,0:T(8,128)(2,1)S(1)}, bf16[576,256]{1,0:T(8,128)(2,1)S(1)}, u32[]{:S(2)}, u32[]{:S(2)}) collective-permute-start(bf16[576,256]{1,0:T(8,128)(2,1)S(1)} %copy-done.36), channel_id=1, source_target_pairs={{0,4},{1,5},{2,6},{3,7},{4,0},{5,1},{6,2},{7,3},{8,12},{9,13},{10,... | collective-permute-start | bytes 884744 | tf_op jit(solution)/shard_map/ppermute | solution.py:1420
  148.8 19.5 %collective-permute-start.23 = (bf16[576,256]{1,0:T(8,128)(2,1)S(1)}, bf16[576,256]{1,0:T(8,128)(2,1)S(1)}, u32[]{:S(2)}, u32[]{:S(2)}) collective-permute-start(bf16[576,256]{1,0:T(8,128)(2,1)S(1)} %copy-done.34), channel_id=1, source_target_pairs={{0,2},{1,3},{2,4},{3,5},{4,6},{5,7},{6,0},{7,1},{8,10},{9,11},{10,... | collective-permute-start | bytes 884744 | tf_op jit(solution)/shard_map/ppermute | solution.py:1420
  168.2 5.8 %collective-permute-start.29 = (bf16[16,24,768]{2,1,0:T(8,128)(2,1)S(1)}, bf16[16,24,768]{2,1,0:T(8,128)(2,1)S(1)}, u32[]{:S(2)}, u32[]{:S(2)}) collective-permute-start(bf16[16,24,768]{2,1,0:T(8,128)(2,1)S(1)} %get-tuple-element.283), channel_id=1, source_target_pairs={{0,1},{1,0},{2,3},{3,2},{4,5},{5,4},{6,7},{7,6},{8,9},{9,8},{10,11... | collective-permute-start | bytes 1769480 | tf_op jit(solution)/shard_map/ppermute | solution.py:1424
  169.6 18.5 %collective-permute-start.26 = (bf16[216,768]{1,0:T(8,128)(2,1)S(1)}, bf16[216,768]{1,0:T(8,128)(2,1)S(1)}, u32[]{:S(2)}, u32[]{:S(2)}) collective-permute-start(bf16[216,768]{1,0:T(8,128)(2,1)S(1)} %get-tuple-element.279), channel_id=1, source_target_pairs={{0,2},{1,3},{2,4},{3,5},{4,6},{5,7},{6,0},{7,1},{8,10},{9,11},{10,... | collective-permute-start | bytes 995336 | tf_op jit(solution)/shard_map/ppermute | solution.py:1420
  169.7 25.9 %collective-permute-start.27 = (bf16[216,768]{1,0:T(8,128)(2,1)S(1)}, bf16[216,768]{1,0:T(8,128)(2,1)S(1)}, u32[]{:S(2)}, u32[]{:S(2)}) collective-permute-start(bf16[216,768]{1,0:T(8,128)(2,1)S(1)} %get-tuple-element.280), channel_id=1, source_target_pairs={{0,4},{1,5},{2,6},{3,7},{4,0},{5,1},{6,2},{7,3},{8,12},{9,13},{10,... | collective-permute-start | bytes 995336 | tf_op jit(solution)/shard_map/ppermute | solution.py:1420
  171.2 24.4 %collective-permute-start.28 = (bf16[216,768]{1,0:T(8,128)(2,1)S(1)}, bf16[216,768]{1,0:T(8,128)(2,1)S(1)}, u32[]{:S(2)}, u32[]{:S(2)}) collective-permute-start(bf16[216,768]{1,0:T(8,128)(2,1)S(1)} %get-tuple-element.281), channel_id=1, source_target_pairs={{0,6},{1,7},{2,0},{3,1},{4,2},{5,3},{6,4},{7,5},{8,14},{9,15},{10,... | collective-permute-start | bytes 995336 | tf_op jit(solution)/shard_map/ppermute | solution.py:1420
  174.7 5.5 %collective-permute-start.30 = (bf16[2,2,24,768]{3,2,1,0:T(8,128)(2,1)S(1)}, bf16[2,2,24,768]{3,2,1,0:T(8,128)(2,1)S(1)}, u32[]{:S(2)}, u32[]{:S(2)}) collective-permute-start(bf16[2,2,24,768]{3,2,1,0:T(8,128)(2,1)S(1)} %get-tuple-element.286), channel_id=1, source_target_pairs={{0,8},{8,0},{16,24},{24,16},{1,9},{9,1},{17,25},{25,17},{2,10},{10... | collective-permute-start | bytes 442376 | tf_op jit(solution)/shard_map/ppermute | solution.py:1428
  186.5 10.8 %collective-permute-start.34 = (bf16[24,768]{1,0:T(8,128)(2,1)S(1)}, bf16[24,768]{1,0:T(8,128)(2,1)S(1)}, u32[]{:S(2)}, u32[]{:S(2)}) collective-permute-start(bf16[24,768]{1,0:T(8,128)(2,1)S(1)} %get-tuple-element.293), channel_id=1, source_target_pairs={{0,2},{1,3},{2,4},{3,5},{4,6},{5,7},{6,0},{7,1},{8,10},{9,11},{10,... | collective-permute-start | bytes 110600 | tf_op jit(solution)/shard_map/ppermute | solution.py:1420
  186.8 18.2 %collective-permute-start.35 = (bf16[24,768]{1,0:T(8,128)(2,1)S(1)}, bf16[24,768]{1,0:T(8,128)(2,1)S(1)}, u32[]{:S(2)}, u32[]{:S(2)}) collective-permute-start(bf16[24,768]{1,0:T(8,128)(2,1)S(1)} %get-tuple-element.294), channel_id=1, source_target_pairs={{0,4},{1,5},{2,6},{3,7},{4,0},{5,1},{6,2},{7,3},{8,12},{9,13},{10,... | collective-permute-start | bytes 110600 | tf_op jit(solution)/shard_map/ppermute | solution.py:1420
  188.1 16.9 %collective-permute-start.36 = (bf16[24,768]{1,0:T(8,128)(2,1)S(1)}, bf16[24,768]{1,0:T(8,128)(2,1)S(1)}, u32[]{:S(2)}, u32[]{:S(2)}) collective-permute-start(bf16[24,768]{1,0:T(8,128)(2,1)S(1)} %get-tuple-element.295), channel_id=1, source_target_pairs={{0,6},{1,7},{2,0},{3,1},{4,2},{5,3},{6,4},{7,5},{8,14},{9,15},{10,... | collective-permute-start | bytes 110600 | tf_op jit(solution)/shard_map/ppermute | solution.py:1420
  (51 other events, 275.5 us)

commit v4 on v3

--- a/solution.py
+++ b/solution.py
@@ -536,6 +536,8 @@
 
 
 NO_COST = pl.CostEstimate(flops=1000, bytes_accessed=1000, transcendentals=0)
+SOME_COST = pl.CostEstimate(flops=4 * 10**9, bytes_accessed=1000, transcendentals=0)
+HIGH_COST = pl.CostEstimate(flops=5 * 10**10, bytes_accessed=1000, transcendentals=0)
 
 
 def split_log(level):
@@ -568,7 +570,7 @@
     return jnp.dot(left, right, preferred_element_type=jnp.float32)
 
 
-def call_whole(kernel, out_shape, name, scalars, *arrays, in_specs=None, scratch=(), limit=12):
+def call_whole(kernel, out_shape, name, scalars, *arrays, in_specs=None, scratch=(), limit=12, cost=None):
     return pl.pallas_call(
         kernel,
         grid_spec=pltpu.PrefetchScalarGridSpec(
@@ -580,8 +582,26 @@
         ),
         out_shape=list(out_shape),
         compiler_params=pltpu.CompilerParams(vmem_limit_bytes=limit << 20),
-        cost_estimate=NO_COST,
+        cost_estimate=cost or NO_COST,
         name=name,
+    )(scalars, *arrays)
+
+
+def after_kernel(scalars, *refs):
+    for index in range(scalars.shape[0]):
+        refs[-1][index] = scalars[index]
+
+
+def after(scalars, arrays, cost):
+    return pl.pallas_call(
+        after_kernel,
+        in_specs=[pl.BlockSpec(memory_space=pltpu.SMEM)]
+        + [pl.BlockSpec(memory_space=pl.ANY)] * len(arrays),
+        out_specs=pl.BlockSpec(memory_space=pltpu.SMEM),
+        out_shape=jax.ShapeDtypeStruct(scalars.shape, scalars.dtype),
+        compiler_params=pltpu.CompilerParams(vmem_limit_bytes=1 << 20),
+        cost_estimate=cost,
+        name="after",
     )(scalars, *arrays)
 
 
@@ -674,10 +694,11 @@
 
 
 def attend_kernel(
-    heads, block, key_blocks, meta, doc_ref, q_ref, k_ref, vt_ref, o_ref, ob_ref, lse_ref, m_ref, l_ref
+    heads, block, key_blocks, meta, doc_ref, q_ref, k_ref, vt_ref, o_ref, lse_ref, *refs
 ):
+    ob_refs, (m_ref, l_ref) = refs[:-2], refs[-2:]
     step = pl.program_id(0)
-    steps = pl.num_programs(0)
+    steps = len(ob_refs)
     query_start = meta[step]
     doc_first, doc_last = meta[steps + key_blocks + step], meta[2 * steps + key_blocks + step]
     doc_line = doc_ref[...]
@@ -731,8 +752,12 @@
         total = l_ref[head]
         mixed = o_ref[rows, :] / total
         o_ref[rows, :] = mixed
-        ob_ref[0, rows, :] = mixed.astype(jnp.bfloat16)
         lse_ref[head] = m_ref[head] + jnp.log(total)
+    for index, ob_ref in enumerate(ob_refs):
+
+        @pl.when(step == index)
+        def _(ob_ref=ob_ref):
+            ob_ref[...] = o_ref[...].astype(jnp.bfloat16)
 
 
 def attend_back_kernel(
@@ -743,21 +768,23 @@
     meta,
     doc_ref,
     q_ref,
-    g_ref,
     o_ref,
     lse_ref,
     k_ref,
     kt_ref,
     v_ref,
-    dq_ref,
-    mine_ref,
-    other_ref,
-    acc_ref,
-    pair_ref,
-    delta_ref,
+    *refs,
 ):
+    g_refs = refs[:-7]
+    dq_ref, mine_ref, other_ref, acc_ref, pair_ref, delta_ref, g_ref = refs[-7:]
     step = pl.program_id(0)
-    steps = pl.num_programs(0)
+    steps = len(g_refs)
+    for index, grad_ref in enumerate(g_refs):
+
+        @pl.when(step == index)
+        def _(grad_ref=grad_ref):
+            g_ref[...] = grad_ref[...]
+
     query_start = meta[step]
     doc_first, doc_last = meta[steps + key_blocks + step], meta[2 * steps + key_blocks + step]
     doc_line = doc_ref[...]
@@ -841,14 +868,14 @@
             in_specs=[
                 pl.BlockSpec((1, block), lambda i, meta: (0, i)),
                 pl.BlockSpec((wide, block), lambda i, meta: (0, i)),
-                whole(k_ext.shape),
-                whole(v_t.shape),
+                pl.BlockSpec(memory_space=pltpu.VMEM),
+                pl.BlockSpec(memory_space=pltpu.VMEM),
             ],
             out_specs=[
                 pl.BlockSpec((share, block), lambda i, meta: (0, i)),
-                pl.BlockSpec((1, share, block), lambda i, meta: (i, 0, 0)),
                 pl.BlockSpec((heads, 1, block), lambda i, meta: (0, 0, i)),
-            ],
+            ]
+            + [whole((share, block))] * steps,
             scratch_shapes=[
                 pltpu.VMEM((heads, 1, block), jnp.float32),
                 pltpu.VMEM((heads, 1, block), jnp.float32),
@@ -856,9 +883,9 @@
         ),
         out_shape=[
             jax.ShapeDtypeStruct((share, queries), jnp.float32),
-            jax.ShapeDtypeStruct((steps, share, block), jnp.bfloat16),
             jax.ShapeDtypeStruct((heads, 1, queries), jnp.float32),
-        ],
+        ]
+        + [jax.ShapeDtypeStruct((share, block), jnp.bfloat16)] * steps,
         compiler_params=pltpu.CompilerParams(vmem_limit_bytes=12 << 20),
         cost_estimate=NO_COST,
         name="attend",
@@ -878,12 +905,12 @@
                 pl.BlockSpec((1, block), lambda i, meta: (0, i)),
                 pl.BlockSpec((wide, block), lambda i, meta: (0, i)),
                 pl.BlockSpec((share, block), lambda i, meta: (0, i)),
-                pl.BlockSpec((share, block), lambda i, meta: (0, i)),
                 pl.BlockSpec((heads, 1, block), lambda i, meta: (0, 0, i)),
-                whole(k_ext.shape),
-                whole(k_t.shape),
-                whole(v_ext.shape),
-            ],
+                pl.BlockSpec(memory_space=pltpu.VMEM),
+                pl.BlockSpec(memory_space=pltpu.VMEM),
+                pl.BlockSpec(memory_space=pltpu.VMEM),
+            ]
+            + [whole((share, block))] * steps,
             out_specs=[
                 pl.BlockSpec((share, block), lambda i, meta: (0, i)),
                 whole((2 * share, keys // 2)),
@@ -893,6 +920,7 @@
                 pltpu.VMEM((share, block), jnp.float32),
                 pltpu.VMEM((2 * share, keys), jnp.float32),
                 pltpu.VMEM((heads, 1, block), jnp.float32),
+                pltpu.VMEM((share, block), jnp.bfloat16),
             ],
         ),
         out_shape=[
@@ -903,7 +931,7 @@
         compiler_params=pltpu.CompilerParams(vmem_limit_bytes=20 << 20),
         cost_estimate=NO_COST,
         name="attend_back",
-    )(meta, doc_line, q_ext, grad_t, mixed, lse, k_ext, k_t, v_ext)
+    )(meta, doc_line, q_ext, mixed, lse, k_ext, k_t, v_ext, *grad_t)
 
 
 def join_kernel(chips, unused, dq_ref, mine_ref, other_ref, *out_refs):
@@ -929,44 +957,54 @@
     )
 
 
-def head_grads_kernel(chips, per, unused, normed_ref, *refs):
-    grads = refs[:chips]
-    weights_ref, gain_ref, row_ref, lane_ref, late_ref, keep_ref, send_ref = refs[chips:]
-    block = normed_ref.shape[1] // chips
-    own = nt_dot(normed_ref[:, :block], grads[0][...])
+def head_grads_kernel(chips, per, unused, *refs):
+    normed, grads = refs[:chips], refs[chips : 2 * chips]
+    wq_ref, wk_ref, wv_ref, gain_ref, inner_ref, feed_ref, hidden_ref = refs[2 * chips : 2 * chips + 7]
+    perm_ref, row_ref, lane_ref, keep_ref, send_ref = refs[2 * chips + 7 :]
+    share, model_width = wq_ref.shape
+    own = nn_dot(grads[0][...], normed[0][...])
     for step in range(1, chips):
-        own = own + nt_dot(normed_ref[:, step * block : (step + 1) * block], grads[step][...])
-    gains = jnp.sum(own * weights_ref[...].astype(jnp.float32), axis=1, keepdims=True)
-    gains = (gains * gain_ref[...] * lane_ref[...]).astype(jnp.bfloat16)
-    gains = nn_dot(row_ref[...], gains) + late_ref[...]
+        own = own + nn_dot(grads[step][...], normed[step][...])
+    attend = jnp.zeros((1, model_width), jnp.float32)
+    for index, weight in enumerate((wq_ref, wk_ref, wv_ref)):
+        part = own[index * share : (index + 1) * share] * weight[...].astype(jnp.float32)
+        attend = attend + jnp.sum(part, axis=0, keepdims=True)
+    gains = jnp.concatenate(
+        [attend / gain_ref[...], inner_ref[...], feed_ref[...], hidden_ref[...]], axis=1
+    )
+    gains = (row_ref[...].astype(jnp.float32) * gains).astype(jnp.bfloat16)
+    gains = nn_dot(gains, lane_ref[...]).astype(jnp.bfloat16)
+    own = nt_dot(perm_ref[...], own.astype(jnp.bfloat16))
     chunks, _, width = keep_ref.shape
     columns = own.shape[1]
+    gain_rows = gains.shape[0] // (2 * chunks)
     for which, target in enumerate((keep_ref, send_ref)):
+        target[:, :, columns:] = jnp.zeros((chunks, per, width - columns), jnp.bfloat16)
         for chunk in range(chunks):
-            first = (which * chunks + chunk) * per
-            rows = slice(first, first + per)
+            place = which * chunks + chunk
+            rows = slice(place * per, (place + 1) * per)
             target[chunk, :, :columns] = own[rows].astype(jnp.bfloat16)
-            target[chunk, :, columns : width - 128] = jnp.zeros(
-                (per, width - 128 - columns), jnp.bfloat16
-            )
-            target[chunk, :, width - 128 :] = gains[rows].astype(jnp.bfloat16)
-
-
-def head_grads(scalars, normed_p, grads, weights_p, gain_rows, where_row, where_lane, late, per):
-    width = normed_p.shape[0]
+            target[chunk, :gain_rows, width - 128 :] = gains[
+                place * gain_rows : (place + 1) * gain_rows
+            ]
+
+
+def head_grads(scalars, normed, grads, weights, gain, late_gains, perm, where_row, where_lane, per):
+    width = perm.shape[0]
     out = jax.ShapeDtypeStruct((width // (2 * per), per, width), jnp.bfloat16)
     return call_whole(
         partial(head_grads_kernel, len(grads), per),
         [out, out],
         "head_grads",
         scalars,
-        normed_p,
+        *normed,
         *grads,
-        weights_p,
-        gain_rows,
+        *weights,
+        gain,
+        *late_gains,
+        perm,
         where_row,
         where_lane,
-        late,
         limit=24,
     )
 
@@ -1671,20 +1709,19 @@
 
     gains_share = (3 * model_width + hidden) // parts
     gains_rows = -(-gains_share // 128)
-    owner = 2 * (chunk % chunks) + parity
-    first_gain = owner * gains_share + 128 * inside
+    line = jnp.arange(parts * gains_rows, dtype=jnp.int32)
+    half_lines = parts // 2 * gains_rows
+    line_parity = jnp.where(line < half_lines, core, 1 - core)
+    owner = 2 * (line % half_lines // gains_rows) + line_parity
+    first_gain = owner * gains_share + 128 * (line % gains_rows)
     end_gain = jnp.minimum(first_gain + 128, (owner + 1) * gains_share)
+    gain_index = jnp.arange(gains_share * parts, dtype=jnp.int32)
     where_row = (
-        (inside < gains_rows)[:, None]
-        & (wanted[None, :] >= first_gain[:, None])
-        & (wanted[None, :] < end_gain[:, None])
+        (gain_index[None, :] >= first_gain[:, None]) & (gain_index[None, :] < end_gain[:, None])
     ).astype(jnp.bfloat16)
     where_lane = (
-        (wanted % gains_share % 128)[:, None] == jnp.arange(128, dtype=jnp.int32)[None, :]
-    ).astype(jnp.float32)
-    gain_rows = (1.0 / gain_attend).reshape(parts // 2, 2, per)
-    gain_rows = jnp.where(core == 0, gain_rows, gain_rows[:, ::-1]).transpose(1, 0, 2)
-    gain_rows = gain_rows.reshape(model_width, 1)
+        (gain_index % gains_share % 128)[:, None] == jnp.arange(128, dtype=jnp.int32)[None, :]
+    ).astype(jnp.bfloat16)
     early = (
         jnp.concatenate([query_starts, 2 * block * chip_ids + block * (1 - core), heads * chip[None]]),
         meta,
@@ -1695,7 +1732,7 @@
         picked_rows(w_value, pick_narrow),
         picked_rows(w_key, pick_narrow),
         picked(w_value, pick_wide),
-        jnp.concatenate([picked(weight, pick_narrow) for weight in (w_query, w_key, w_value)], axis=1),
+        picked_rows(w_query, pick_narrow),
         gain_attend[None, :],
         gain_inner[None, :],
         gain_feed[None, :],
@@ -1703,12 +1740,11 @@
         place,
         where_row,
         where_lane,
-        gain_rows,
     )
     own[1], early = lax.optimization_barrier((own[1], early))
-    starts, meta, doc_line, perm, wq_wide, wk_wide, wv_rows, wk_rows, wv_wide, w_own = early[:10]
+    starts, meta, doc_line, perm, wq_wide, wk_wide, wv_rows, wk_rows, wv_wide, wq_rows = early[:10]
     gain_first, gain_inner, gain_feed, gain_hidden, place = early[10:15]
-    where_row, where_lane, gain_rows = early[15:]
+    where_row, where_lane = early[15:]
     sibling = [seq_swap(rows, 1) for rows in own]
     q_ext, k_ext, v_t = project(
         starts,
@@ -1720,18 +1756,11 @@
         heads,
         scale,
     )
-    mixed, mixed_b, lse = attend(meta, doc_line, q_ext, k_ext, v_t, heads, block)
-    own, w_own, mixed_b = lax.optimization_barrier((own, w_own, mixed_b))
+    mixed, lse, *mixed_b = attend(meta, doc_line, q_ext, k_ext, v_t, heads, block)
+    mixed_b, wk_rows = lax.optimization_barrier((mixed_b, wk_rows))
+    k_t, v_ext = project_back(place, own + sibling, wk_rows, wv_wide)
     back = [mixed_b[0]] + [chip_shift(mixed_b[step], -step) for step in range(1, chips)]
-
-    own_normed = jnp.concatenate(own, axis=0)
-    k_t, v_ext = project_back(place, own + sibling, wk_rows, wv_wide)
-    normed_p = sent(nt_dot(perm, own_normed))
-    weights_p = sent(nn_dot(perm, w_own))
-    back, k_t, v_ext, normed_p, weights_p = lax.optimization_barrier(
-        (back, k_t, v_ext, normed_p, weights_p)
-    )
-
+    back, k_t, v_ext = lax.optimization_barrier((back, k_t, v_ext))
     outs = middle(
         place, back, tokens, cotangent, w_out, w_up, w_down, (gain_inner, gain_feed, gain_hidden)
     )
@@ -1739,31 +1768,24 @@
     go = outs[3 : 3 + chips]
     z, h2, bent, pre, dinner, dfeed, dhidden = outs[3 + chips :]
     go = [go[0]] + [chip_shift(go[step], step) for step in range(1, chips)]
-    go[1], bent, pre = lax.optimization_barrier((go[1], bent, pre))
     keep_a, send_a = down_grad(place, bent, cotangent, hidden // parts)
     keep_b, send_b = up_out_grad(place, h2, pre, z, gmid_b, perm, per)
 
-    gains_late = jnp.concatenate([jnp.zeros_like(dinner), dinner, dfeed, dhidden], axis=1)
-    gains_late = gains_late.reshape(parts // 2, 2, gains_share)
-    gains_late = jnp.where(core == 0, gains_late, gains_late[:, ::-1]).transpose(1, 0, 2)
-    gains_late = jnp.pad(gains_late, ((0, 0), (0, 0), (0, gains_rows * 128 - gains_share)))
-    gains_late = jnp.pad(
-        gains_late.reshape(parts, gains_rows, 128), ((0, 0), (0, per - gains_rows), (0, 0))
-    ).reshape(model_width, 128)
 
     def gridded(array):
         return array.reshape((2, 2, chips) + array.shape[1:])
 
     keep_a, other_a = gridded(keep_a), gridded(seq_swap(send_a, 1))
-    out_a = outgoing(place, keep_a, other_a)
-    kept_a = outgoing(place, keep_a, other_a, True)
     other_b = seq_swap(send_b, 1)
+    arrived_place = after(place, [*go, keep_b], HIGH_COST)
+    out_a = outgoing(arrived_place, keep_a, other_a)
+    kept_a = outgoing(arrived_place, keep_a, other_a, True)
     go, out_a, kept_a, keep_b, send_b = lax.optimization_barrier(
         (go, out_a, kept_a, keep_b, send_b)
     )
     in_a = [row_swap(out_a[0], 1), row_swap(out_a[1], 2)]
     dq, pair, other = attend_back(
-        meta, doc_line, q_ext, jnp.concatenate(go, axis=1), mixed, lse, k_ext, k_t, v_ext, heads, block, scale
+        meta, doc_line, q_ext, go, mixed, lse, k_ext, k_t, v_ext, heads, block, scale
     )
     dq, pair, other, in_a, keep_b, other_b = lax.optimization_barrier(
         (dq, pair, other, in_a, keep_b, other_b)
@@ -1776,18 +1798,25 @@
     grads, keep_b, other_b = lax.optimization_barrier((grads, keep_b, other_b))
     kept_b = outgoing(place, keep_b, other_b, True)
     mine_grad, send_grad = head_grads(
-        place, normed_p, grads, weights_p, gain_rows, where_row, where_lane, gains_late, per
-    )
-    in_a, in_b, kept_a, kept_b, home[1], mine_grad, send_grad = lax.optimization_barrier(
-        (in_a, in_b, kept_a, kept_b, home[1], mine_grad, send_grad)
+        place,
+        own,
+        grads,
+        (wq_rows, wk_rows, wv_rows),
+        gain_first,
+        (dinner, dfeed, dhidden),
+        perm,
+        where_row,
+        where_lane,
+        per,
+    )
+    in_a, in_b, kept_a, kept_b, mine_grad, send_grad = lax.optimization_barrier(
+        (in_a, in_b, kept_a, kept_b, mine_grad, send_grad)
     )
     low_keep, low_send, high_keep, high_send = halfway(place, [(*kept_a, *in_a), (*kept_b, *in_b)])
     low_in, high_in = row_swap(low_send, 2), row_swap(high_send, 1)
-    home, low_in, high_in, mine_grad, send_grad = lax.optimization_barrier(
-        (home, low_in, high_in, mine_grad, send_grad)
-    )
+    home, mine_grad, send_grad = lax.optimization_barrier((home, mine_grad, send_grad))
     mine_grad, other_grad = gridded(mine_grad), gridded(seq_swap(send_grad, 1))
-    stage = split(place, [(low_keep, low_in, high_keep, high_in)], chips)
+    stage = split(after(place, home, SOME_COST), [(low_keep, low_in, high_keep, high_in)], chips)
     arrived = [stage[0]] + [chip_shift(stage[step], step) for step in range(1, chips)]
     grad_input = final(
         place, home, tokens, grad_middle, w_query, w_key, w_value, gain_first

time: 207 us -> 192 us (0.928)
  waiting for transfers between devices: 64.2 us -> 56.3 us
  local copies, waits for them, and re-layouts: 10.4 us -> 3.92 us
    ppermute x17, waiting for transfers between devices: 42.5 us -> 20 us  [chip_shift(): lax.ppermute(value, 'seq', [(i, (i + 2 * steps) % count) for i in range(c...]
    ppermute x10, waiting for transfers between devices: 12.1 us -> 27.6 us  [row_swap(): lax.ppermute(value, 'row', [(i, i ^ bit) for i in range(lax.axis_size('ro...]
    unnamed x94 -> x47, local copies, waits for them, and re-layouts: 7.33 us -> 2.38 us
    ppermute x10, starting transfers between devices: 12.7 us -> 9.76 us  [row_swap(): lax.ppermute(value, 'row', [(i, i ^ bit) for i in range(lax.axis_size('ro...]
    dot_general x1 -> x0, matrix products: 2.61 us -> none  [nt_dot(): lax.dot_general(left, right, (((1,), (1,)), ((), ())), preferred_element_...]
    pallas_call x0 -> x2, Pallas kernels: none -> 2.28 us  [after(): pl.pallas_call(after_kernel, in_specs=[pl.BlockSpec(memory_space=pltpu.SM...]
    dot_general x3 -> x4, matrix products: 4 us -> 5.34 us  [picked_rows(): lax.dot_general(choice, weight, (((0,), (1,)), ((), ())), preferred_eleme...]
    dot_general x4 -> x2, matrix products: 5.84 us -> 5.2 us  [nn_dot(): return jnp.dot(left, right, preferred_element_type=jnp.float32)]
  transfers between devices with their start and end apart: 37 -> 37, of which waited for: 18 -> 17; matrix products, arithmetic and copies ran while one was open for 9% -> 9% of each run, Pallas kernels for 17% -> 21%
where the time goes in v4:
time: 192 us
  Pallas kernels  70.3 us (37%)
  waiting for transfers between devices  56.3 us (29%)
  starting transfers between devices  43.4 us (23%)
  matrix products  10.5 us (5%)
  other arithmetic  6.11 us (3%)
  local copies, waits for them, and re-layouts  3.92 us (2%)
    ppermute x17, starting transfers between devices, chip_shift(): lax.ppermute(value, 'seq', [(i, (i + 2 * steps) % count) for i in range(c...  29.6 us
    pallas_call x17, Pallas kernels, call_whole(): pl.pallas_call(kernel, grid_spec=pltpu.PrefetchScalarGridSpec(num_scalar_...  27.9 us
    ppermute x10, waiting for transfers between devices, row_swap(): lax.ppermute(value, 'row', [(i, i ^ bit) for i in range(lax.axis_size('ro...  27.6 us
    ppermute x17, waiting for transfers between devices, chip_shift(): lax.ppermute(value, 'seq', [(i, (i + 2 * steps) % count) for i in range(c...  20 us
    pallas_call x1, Pallas kernels, middle(): pl.pallas_call(partial(middle_kernel, chips, tiles), grid_spec=pltpu.Pref...  15.5 us
    ppermute x10, starting transfers between devices, row_swap(): lax.ppermute(value, 'row', [(i, i ^ bit) for i in range(lax.axis_size('ro...  9.76 us
    pallas_call x1, Pallas kernels, attend_back(): pl.pallas_call(partial(attend_back_kernel, heads, block, key_blocks, scal...  9.3 us
    pallas_call x1, Pallas kernels, attend(): pl.pallas_call(partial(attend_kernel, heads, block, key_blocks), grid_spe...  7.63 us
  transfers between devices with their start and end apart: 37, of which 17 were waited for; matrix products, arithmetic and copies ran while one was open for 9% of the time, Pallas kernels for 21%

profile of v4, /device:TPU:0, one launch (start us, length us, event | category | flops | bytes accessed | tf_op | source)
XLA Modules:
  0.0 191.8 jit_solution(184242821827940812)
XLA Ops:
  2.6 3.1 %collective-permute-start = (bf16[256,768]{1,0:T(8,128)(2,1)S(1)}, bf16[256,768]{1,0:T(8,128)(2,1)S(1)}, u32[]{:S(2)}, u32[]{:S(2)}) collective-permute-start(bf16[256,768]{1,0:T(8,128)(2,1)S(1)} %norm.1.refs_0_), channel_id=1, source_target_pairs={{0,2},{1,3},{2,4},{3,5},{4,6},{5,7},{6,0},{7,1},{8,10},{9,11},{10,... | collective-permute-start | bytes 1179656 | tf_op jit(solution)/shard_map/ppermute | solution.py:1458
  5.7 2.1 %collective-permute-start.1 = (bf16[256,768]{1,0:T(8,128)(2,1)S(1)}, bf16[256,768]{1,0:T(8,128)(2,1)}, u32[]{:S(2)}, u32[]{:S(2)}) collective-permute-start(bf16[256,768]{1,0:T(8,128)(2,1)S(1)} %norm.1.refs_0_), channel_id=1, source_target_pairs={{0,6},{1,7},{2,0},{3,1},{4,2},{5,3},{6,4},{7,5},{8,14},{9,15},{10,... | collective-permute-start | bytes 1179656 | tf_op jit(solution)/shard_map/ppermute | solution.py:1458
  13.9 2.4 %fusion.refs_17_ = bf16[5376,128]{1,0:T(8,128)(2,1)S(1)} fusion(s32[5376]{0:T(1024)S(1)} %add_select_fusion), kind=kLoop, calls=%fused_computation.1 | loop fusion | flops 1376256 | bytes 1397760 | tf_op jit(solution)/shard_map/convert_element_type | solution.py:1724
  19.3 2.9 %fusion.4.refs_9_ = bf16[768,384]{1,0:T(8,128)(2,1)} fusion(bf16[768,768]{1,0:T(8,128)(2,1)} %refs_7_.3, s32[384]{0:T(512)S(1)} %fusion.47, pred[384]{0:T(512)(128)(4,1)S(1)} %fusion.51), kind=kOutput, calls=%fused_computation.11 | convolution fusion | flops 453869568 | bytes 1771392 | tf_op jit(solution)/shard_map/dot_general | solution.py:570
  22.3 2.5 %collective-permute-done.1.refs_3_ = bf16[256,768]{1,0:T(8,128)(2,1)} collective-permute-done((bf16[256,768]{1,0:T(8,128)(2,1)S(1)}, bf16[256,768]{1,0:T(8,128)(2,1)}, u32[]{:S(2)}, u32[]{:S(2)}) %collective-permute-start.1) | collective-permute-done | bytes 393248 | tf_op jit(solution)/shard_map/ppermute | solution.py:1458
  27.8 2.3 %fusion.5.refs_9_ = bf16[768,384]{1,0:T(8,128)(2,1)S(1)} fusion(bf16[768,768]{1,0:T(8,128)(2,1)} %refs_8_.3, s32[384]{0:T(512)S(1)} %fusion.47, pred[384]{0:T(512)(128)(4,1)S(1)} %fusion.51), kind=kOutput, calls=%fused_computation.12 | convolution fusion | flops 453869568 | bytes 1771392 | tf_op jit(solution)/shard_map/dot_general | solution.py:570
  30.6 6.8 %collective-permute-done.2 = bf16[256,768]{1,0:T(8,128)(2,1)} collective-permute-done((bf16[256,768]{1,0:T(8,128)(2,1)}, bf16[256,768]{1,0:T(8,128)(2,1)}, u32[]{:S(2)}, u32[]{:S(2)}) %collective-permute-start.2) | collective-permute-done | bytes 393248 | tf_op jit(solution)/shard_map/ppermute | solution.py:1625
  40.3 5.0 %project.1 = (bf16[384,1024]{1,0:T(8,128)(2,1)S(1)}, bf16[2048,384]{1,0:T(8,128)(2,1)S(1)}, bf16[192,2048]{1,0:T(8,128)(2,1)S(1)}) custom-call(s32[9]{0:T(128)S(1)} %pad_add_fusion.meta, bf16[256,768]{1,0:T(8,128)(2,1)S(1)} %norm.1.refs_0_, bf16[256,768]{1,0:T(8,128)(2,1)S(1)} %collective-permute-done.refs_1_, ...), custom_call_target="tpu_custom_call" | custom-call | flops 1000 | bytes 1000 | tf_op jit(solution)/shard_map/project/pallas_call | solution.py:574
  45.3 7.6 %attend.1 = (f32[192,1024]{1,0:T(8,128)S(1)}, f32[3,1,1024]{2,1,0:T(1,128)S(1)}, bf16[192,256]{1,0:T(8,128)(2,1)S(1)}, bf16[192,256]{1,0:T(8,128)(2,1)S(1)}, bf1...) custom-call(s32[20]{0:T(128)S(1)} %concatenate.7.meta, s32[1,1024]{1,0:T(1,128)S(1)} %bitcast.63, ...), custom_call_target="tpu_custom_call" | custom-call | flops 1000 | bytes 1000 | tf_op jit(solution)/shard_map/attend/pallas_call | solution.py:863
  53.0 5.1 %collective-permute-start.8 = (bf16[192,256]{1,0:T(8,128)(2,1)S(1)}, bf16[192,256]{1,0:T(8,128)(2,1)S(1)}, u32[]{:S(2)}, u32[]{:S(2)}) collective-permute-start(bf16[192,256]{1,0:T(8,128)(2,1)S(1)} %get-tuple-element.166), channel_id=1, source_target_pairs={{0,6},{1,7},{2,0},{3,1},{4,2},{5,3},{6,4},{7,5},{8,14},{9,15},{10,... | collective-permute-start | bytes 294920 | tf_op jit(solution)/shard_map/ppermute | solution.py:1458
  58.5 1.9 %collective-permute-start.10 = (bf16[192,256]{1,0:T(8,128)(2,1)S(1)}, bf16[192,256]{1,0:T(8,128)(2,1)S(1)}, u32[]{:S(2)}, u32[]{:S(2)}) collective-permute-start(bf16[192,256]{1,0:T(8,128)(2,1)S(1)} %get-tuple-element.168), channel_id=1, source_target_pairs={{0,2},{1,3},{2,4},{3,5},{4,6},{5,7},{6,0},{7,1},{8,10},{9,11},{10,... | collective-permute-start | bytes 294920 | tf_op jit(solution)/shard_map/ppermute | solution.py:1458
  60.5 4.3 %project_back.1 = (bf16[192,2048]{1,0:T(8,128)(2,1)S(1)}, bf16[2048,384]{1,0:T(8,128)(2,1)S(1)}) custom-call(s32[4]{0:T(128)S(1)} %pad_add_fusion.1.unused.position.scalars, bf16[256,768]{1,0:T(8,128)(2,1)S(1)} %norm.1.refs_0_, bf16[256,768]{1,0:T(8,128)(2,1)S(1)} %collective-permute-done.refs_1_, bf16[256,768]{1,0:T(8,128)(2,1)S(1)} %broadcast_select_fusion.refs_2_, ...), custom_call_target="tpu_custom_call" | custom-call | flops 1000 | bytes 1000 | tf_op jit(solution)/shard_map/project_back/pallas_call | solution.py:574
  64.8 4.1 %collective-permute-done.9.refs_2_ = bf16[192,256]{1,0:T(8,128)(2,1)S(1)} collective-permute-done((bf16[192,256]{1,0:T(8,128)(2,1)S(1)}, bf16[192,256]{1,0:T(8,128)(2,1)S(1)}, u32[]{:S(2)}, u32[]{:S(2)}) %collective-permute-start.9) | collective-permute-done | bytes 98336 | tf_op jit(solution)/shard_map/ppermute | solution.py:1458
  69.0 15.5 %middle.1 = (bf16[256,768]{1,0:T(8,128)(2,1)}, f32[256,768]{1,0:T(8,128)S(1)}, bf16[256,768]{1,0:T(8,128)(2,1)S(1)}, bf16[192,256]{1,0:T(8,128)(2,1)S(1)}, bf16[...) custom-call(s32[4]{0:T(128)S(1)} %pad_add_fusion.1.unused.position.s, ...), custom_call_target="tpu_custom_call" | custom-call | flops 1000 | bytes 1000 | tf_op jit(solution)/shard_map/middle/pallas_call | solution.py:1266
  84.7 1.9 %collective-permute-start.12 = (bf16[192,256]{1,0:T(8,128)(2,1)S(1)}, bf16[192,256]{1,0:T(8,128)(2,1)S(1)}, u32[]{:S(2)}, u32[]{:S(2)}) collective-permute-start(bf16[192,256]{1,0:T(8,128)(2,1)S(1)} %get-tuple-element.187), channel_id=1, source_target_pairs={{0,4},{1,5},{2,6},{3,7},{4,0},{5,1},{6,2},{7,3},{8,12},{9,13},{10,... | collective-permute-start | bytes 294920 | tf_op jit(solution)/shard_map/ppermute | solution.py:1458
  86.7 2.9 %collective-permute-start.13 = (bf16[192,256]{1,0:T(8,128)(2,1)S(1)}, bf16[192,256]{1,0:T(8,128)(2,1)S(1)}, u32[]{:S(2)}, u32[]{:S(2)}) collective-permute-start(bf16[192,256]{1,0:T(8,128)(2,1)S(1)} %get-tuple-element.188), channel_id=1, source_target_pairs={{0,6},{1,7},{2,0},{3,1},{4,2},{5,3},{6,4},{7,5},{8,14},{9,15},{10,... | collective-permute-start | bytes 294920 | tf_op jit(solution)/shard_map/ppermute | solution.py:1458
  89.6 2.8 %down_grad.1 = (bf16[16,96,768]{2,1,0:T(8,128)(2,1)S(1)}, bf16[16,96,768]{2,1,0:T(8,128)(2,1)S(1)}) custom-call(s32[4]{0:T(128)S(1)} %pad_add_fusion.1.unused.position.scalars, bf16[256,3072]{1,0:T(8,128)(2,1)S(1)} %get-tuple-element.195.bent_ref, bf16[256,768]{1,0:T(8,128)(2,1)S(1)} %copy-done.3), custom_call_target="tpu_custom_call" | custom-call | flops 1000 | bytes 1000 | tf_op jit(solution)/shard_map/down_grad/pallas_call | solution.py:1340
  92.5 4.9 %up_out_grad.1 = (bf16[16,120,768]{2,1,0:T(8,128)(2,1)S(1)}, bf16[16,120,768]{2,1,0:T(8,128)(2,1)S(1)}) custom-call(s32[4]{0:T(128)S(1)} %pad_add_fusion.1.unused.position.scalars, bf16[256,768]{1,0:T(8,128)(2,1)S(1)} %get-tuple-element.189.h2_ref, bf16[256,3072]{1,0:T(8,128)(2,1)S(1)} %get-tuple-element.190.pre_ref, ...), custom_call_target="tpu_custom_call" | custom-call | flops 1000 | bytes 1000 | tf_op jit(solution)/shard_map/up_out_grad/pallas_call | solution.py:1388
  102.2 9.3 %attend_back.1 = (bf16[192,1024]{1,0:T(8,128)(2,1)S(1)}, f32[384,1024]{1,0:T(8,128)S(1)}, bf16[384,1024]{1,0:T(8,128)(2,1)S(1)}) custom-call(s32[20]{0:T(128)S(1)} %concatenate.7.meta, s32[1,1024]{1,0:T(1,128)S(1)} %bitcast.64, bf16[384,1024]{1,0:T(8,128)(2,1)S(1)} %get-tuple-element.157.q_ref, f32[192,1024]{1,0:T(8,128)S(1)} %get-tuple-element.181.o_ref, ...), custom_call_target="tpu_custom_call" | custom-call | flops 1000 | bytes 1000 | tf_op jit(solution)/shard_map/attend_back/pallas_call | solution.py:899
  111.5 4.6 %collective-permute-done.15.refs_2_ = bf16[2,2,96,768]{3,2,1,0:T(8,128)(2,1)S(1)} collective-permute-done((bf16[2,2,96,768]{3,2,1,0:T(8,128)(2,1)S(1)}, bf16[2,2,96,768]{3,2,1,0:T(8,128)(2,1)S(1)}, u32[]{:S(2)}, u32[]{:S(2)}) %collective-permute-start.15) | collective-permute-done | bytes 589856 | tf_op jit(solution)/shard_map/ppermute | solution.py:1466
  120.9 1.9 %collective-permute-start.21 = (bf16[576,256]{1,0:T(8,128)(2,1)S(1)}, bf16[576,256]{1,0:T(8,128)(2,1)S(1)}, u32[]{:S(2)}, u32[]{:S(2)}) collective-permute-start(bf16[576,256]{1,0:T(8,128)(2,1)S(1)} %get-tuple-element.235.refs_7_), channel_id=1, source_target_pairs={{0,2},{1,3},{2,4},{3,5},{4,6},{5,7},{6,0},{7,1},{8,10},{9,11},{10,... | collective-permute-start | bytes 884744 | tf_op jit(solution)/shard_map/ppermute | solution.py:1458
  124.0 4.5 %head_grads.1 = (bf16[16,24,768]{2,1,0:T(8,128)(2,1)S(1)}, bf16[16,24,768]{2,1,0:T(8,128)(2,1)S(1)}) custom-call(s32[4]{0:T(128)S(1)} %pad_add_fusion.1.unused.position.scalars, bf16[256,768]{1,0:T(8,128)(2,1)S(1)} %norm.1.refs_0_, bf16[256,768]{1,0:T(8,128)(2,1)S(1)} %collective-permute-done.refs_1_, bf16[256,768]{1,0:T(8,128)(2,1)S(1)} %broadcast_select_fusion.refs_2_, ...), custom_call_target="tpu_custom_call" | custom-call | flops 1000 | bytes 1000 | tf_op jit(solution)/shard_map/head_grads/pallas_call | solution.py:574
  128.5 8.4 %collective-permute-done.22.refs_6_ = bf16[2,2,120,768]{3,2,1,0:T(8,128)(2,1)S(1)} collective-permute-done((bf16[2,2,120,768]{3,2,1,0:T(8,128)(2,1)S(1)}, bf16[2,2,120,768]{3,2,1,0:T(8,128)(2,1)S(1)}, u32[]{:S(2)}, u32[]{:S(2)}) %collective-permute-start.22) | collective-permute-done | bytes 737312 | tf_op jit(solution)/shard_map/ppermute | solution.py:1466
  140.2 6.9 %collective-permute-done.20.refs_2_ = bf16[576,256]{1,0:T(8,128)(2,1)S(1)} collective-permute-done((bf16[576,256]{1,0:T(8,128)(2,1)S(1)}, bf16[576,256]{1,0:T(8,128)(2,1)S(1)}, u32[]{:S(2)}, u32[]{:S(2)}) %collective-permute-start.20) | collective-permute-done | bytes 294944 | tf_op jit(solution)/shard_map/ppermute | solution.py:1458
  148.2 6.7 %collective-permute-done.24.refs_1_ = bf16[2,216,768]{2,1,0:T(8,128)(2,1)S(1)} collective-permute-done((bf16[2,216,768]{2,1,0:T(8,128)(2,1)S(1)}, bf16[2,216,768]{2,1,0:T(8,128)(2,1)S(1)}, u32[]{:S(2)}, u32[]{:S(2)}) %collective-permute-start.24) | collective-permute-done | bytes 663584 | tf_op jit(solution)/shard_map/ppermute | solution.py:1466
  157.2 3.0 %collective-permute-start.28 = (bf16[216,768]{1,0:T(8,128)(2,1)S(1)}, bf16[216,768]{1,0:T(8,128)(2,1)S(1)}, u32[]{:S(2)}, u32[]{:S(2)}) collective-permute-start(bf16[216,768]{1,0:T(8,128)(2,1)S(1)} %get-tuple-element.267), channel_id=1, source_target_pairs={{0,6},{1,7},{2,0},{3,1},{4,2},{5,3},{6,4},{7,5},{8,14},{9,15},{10,... | collective-permute-start | bytes 995336 | tf_op jit(solution)/shard_map/ppermute | solution.py:1458
  167.8 1.9 collective-permute-start.32
  172.2 1.8 collective-permute-done.33.refs_3_
  175.3 1.9 collective-permute-start.35
  177.1 2.8 %collective-permute-start.36 = (bf16[24,768]{1,0:T(8,128)(2,1)S(1)}, bf16[24,768]{1,0:T(8,128)(2,1)S(1)}, u32[]{:S(2)}, u32[]{:S(2)}) collective-permute-start(bf16[24,768]{1,0:T(8,128)(2,1)S(1)} %get-tuple-element.281), channel_id=1, source_target_pairs={{0,6},{1,7},{2,0},{3,1},{4,2},{5,3},{6,4},{7,5},{8,14},{9,15},{10,... | collective-permute-start | bytes 110600 | tf_op jit(solution)/shard_map/ppermute | solution.py:1458
  180.0 3.2 %final.1 = bf16[256,768]{1,0:T(8,128)(2,1)} custom-call(s32[4]{0:T(128)S(1)} %pad_add_fusion.1.unused.position.scalars, bf16[576,256]{1,0:T(8,128)(2,1)S(1)} %get-tuple-element.247.refs_4_.refs_0_, bf16[576,256]{1,0:T(8,128)(2,1)S(1)} %collective-permute-done.19.refs_1_, bf16[576,256]{1,0:T(8,128)(2,1)S(1)} %collective-permute-done.20.refs_2_, ...), custom_call_target="tpu_custom_call" | custom-call | flops 1000 | bytes 1000 | tf_op jit(solution)/shard_map/final/pallas_call | solution.py:574
  183.2 6.4 %collective-permute-done.35.refs_6_ = bf16[24,768]{1,0:T(8,128)(2,1)S(1)} collective-permute-done((bf16[24,768]{1,0:T(8,128)(2,1)S(1)}, bf16[24,768]{1,0:T(8,128)(2,1)S(1)}, u32[]{:S(2)}, u32[]{:S(2)}) %collective-permute-start.35) | collective-permute-done | bytes 36896 | tf_op jit(solution)/shard_map/ppermute | solution.py:1458
  (146 shorter events, 48.9 us)
Async XLA Ops:
  2.6 23.5 %collective-permute-start = (bf16[256,768]{1,0:T(8,128)(2,1)S(1)}, bf16[256,768]{1,0:T(8,128)(2,1)S(1)}, u32[]{:S(2)}, u32[]{:S(2)}) collective-permute-start(bf16[256,768]{1,0:T(8,128)(2,1)S(1)} %norm.1.refs_0_), channel_id=1, source_target_pairs={{0,2},{1,3},{2,4},{3,5},{4,6},{5,7},{6,0},{7,1},{8,10},{9,11},{10,... | collective-permute-start | bytes 1179656 | tf_op jit(solution)/shard_map/ppermute | solution.py:1458
  5.7 19.1 %collective-permute-start.1 = (bf16[256,768]{1,0:T(8,128)(2,1)S(1)}, bf16[256,768]{1,0:T(8,128)(2,1)}, u32[]{:S(2)}, u32[]{:S(2)}) collective-permute-start(bf16[256,768]{1,0:T(8,128)(2,1)S(1)} %norm.1.refs_0_), channel_id=1, source_target_pairs={{0,6},{1,7},{2,0},{3,1},{4,2},{5,3},{6,4},{7,5},{8,14},{9,15},{10,... | collective-permute-start | bytes 1179656 | tf_op jit(solution)/shard_map/ppermute | solution.py:1458
  7.8 30.8 %collective-permute-start.4 = (bf16[256,768]{1,0:T(8,128)(2,1)S(1)}, bf16[256,768]{1,0:T(8,128)(2,1)}, u32[]{:S(2)}, u32[]{:S(2)}) collective-permute-start(bf16[256,768]{1,0:T(8,128)(2,1)S(1)} %norm.1.refs_0_), channel_id=1, source_target_pairs={{0,1},{1,0},{2,3},{3,2},{4,5},{5,4},{6,7},{7,6},{8,9},{9,8},{10,11... | collective-permute-start | bytes 1179656 | tf_op jit(solution)/shard_map/ppermute | solution.py:1462
  24.8 12.6 %collective-permute-start.2 = (bf16[256,768]{1,0:T(8,128)(2,1)}, bf16[256,768]{1,0:T(8,128)(2,1)}, u32[]{:S(2)}, u32[]{:S(2)}) collective-permute-start(bf16[256,768]{1,0:T(8,128)(2,1)} %collective-permute-done.1.refs_3_), channel_id=1, source_target_pairs={{2,0},{3,1},{4,2},{5,3},{10,8},{11,9},{12,10},{13,11},{18,16},{19,... | collective-permute-start | bytes 1179656 | tf_op jit(solution)/shard_map/ppermute | solution.py:1625
  26.1 11.3 %collective-permute-start.3 = (bf16[256,768]{1,0:T(8,128)(2,1)S(1)}, bf16[256,768]{1,0:T(8,128)(2,1)}, u32[]{:S(2)}, u32[]{:S(2)}) collective-permute-start(bf16[256,768]{1,0:T(8,128)(2,1)S(1)} %collective-permute-done.refs_1_), channel_id=1, source_target_pairs={{2,4},{3,5},{4,6},{5,7},{10,12},{11,13},{12,14},{13,15},{18,20},{1... | collective-permute-start | bytes 1179656 | tf_op jit(solution)/shard_map/ppermute | solution.py:1625
  30.1 8.5 %collective-permute-start.5 = (bf16[256,768]{1,0:T(8,128)(2,1)S(1)}, bf16[256,768]{1,0:T(8,128)(2,1)S(1)}, u32[]{:S(2)}, u32[]{:S(2)}) collective-permute-start(bf16[256,768]{1,0:T(8,128)(2,1)S(1)} %collective-permute-done.refs_1_), channel_id=1, source_target_pairs={{0,1},{1,0},{2,3},{3,2},{4,5},{5,4},{6,7},{7,6},{8,9},{9,8},{10,11... | collective-permute-start | bytes 1179656 | tf_op jit(solution)/shard_map/ppermute | solution.py:1462
  30.2 8.5 %collective-permute-start.7 = (bf16[256,768]{1,0:T(8,128)(2,1)}, bf16[256,768]{1,0:T(8,128)(2,1)S(1)}, u32[]{:S(2)}, u32[]{:S(2)}) collective-permute-start(bf16[256,768]{1,0:T(8,128)(2,1)} %collective-permute-done.1.refs_3_), channel_id=1, source_target_pairs={{0,1},{1,0},{2,3},{3,2},{4,5},{5,4},{6,7},{7,6},{8,9},{9,8},{10,11... | collective-permute-start | bytes 1179656 | tf_op jit(solution)/shard_map/ppermute | solution.py:1462
  53.0 11.8 %collective-permute-start.8 = (bf16[192,256]{1,0:T(8,128)(2,1)S(1)}, bf16[192,256]{1,0:T(8,128)(2,1)S(1)}, u32[]{:S(2)}, u32[]{:S(2)}) collective-permute-start(bf16[192,256]{1,0:T(8,128)(2,1)S(1)} %get-tuple-element.166), channel_id=1, source_target_pairs={{0,6},{1,7},{2,0},{3,1},{4,2},{5,3},{6,4},{7,5},{8,14},{9,15},{10,... | collective-permute-start | bytes 294920 | tf_op jit(solution)/shard_map/ppermute | solution.py:1458
  58.2 10.7 %collective-permute-start.9 = (bf16[192,256]{1,0:T(8,128)(2,1)S(1)}, bf16[192,256]{1,0:T(8,128)(2,1)S(1)}, u32[]{:S(2)}, u32[]{:S(2)}) collective-permute-start(bf16[192,256]{1,0:T(8,128)(2,1)S(1)} %get-tuple-element.167), channel_id=1, source_target_pairs={{0,4},{1,5},{2,6},{3,7},{4,0},{5,1},{6,2},{7,3},{8,12},{9,13},{10,... | collective-permute-start | bytes 294920 | tf_op jit(solution)/shard_map/ppermute | solution.py:1458
  58.5 10.4 %collective-permute-start.10 = (bf16[192,256]{1,0:T(8,128)(2,1)S(1)}, bf16[192,256]{1,0:T(8,128)(2,1)S(1)}, u32[]{:S(2)}, u32[]{:S(2)}) collective-permute-start(bf16[192,256]{1,0:T(8,128)(2,1)S(1)} %get-tuple-element.168), channel_id=1, source_target_pairs={{0,2},{1,3},{2,4},{3,5},{4,6},{5,7},{6,0},{7,1},{8,10},{9,11},{10,... | collective-permute-start | bytes 294920 | tf_op jit(solution)/shard_map/ppermute | solution.py:1458
  84.5 13.5 %collective-permute-start.11 = (bf16[192,256]{1,0:T(8,128)(2,1)S(1)}, bf16[192,256]{1,0:T(8,128)(2,1)S(1)}, u32[]{:S(2)}, u32[]{:S(2)}) collective-permute-start(bf16[192,256]{1,0:T(8,128)(2,1)S(1)} %get-tuple-element.186), channel_id=1, source_target_pairs={{0,2},{1,3},{2,4},{3,5},{4,6},{5,7},{6,0},{7,1},{8,10},{9,11},{10,... | collective-permute-start | bytes 294920 | tf_op jit(solution)/shard_map/ppermute | solution.py:1458
  84.7 13.3 %collective-permute-start.12 = (bf16[192,256]{1,0:T(8,128)(2,1)S(1)}, bf16[192,256]{1,0:T(8,128)(2,1)S(1)}, u32[]{:S(2)}, u32[]{:S(2)}) collective-permute-start(bf16[192,256]{1,0:T(8,128)(2,1)S(1)} %get-tuple-element.187), channel_id=1, source_target_pairs={{0,4},{1,5},{2,6},{3,7},{4,0},{5,1},{6,2},{7,3},{8,12},{9,13},{10,... | collective-permute-start | bytes 294920 | tf_op jit(solution)/shard_map/ppermute | solution.py:1458
  86.7 11.3 %collective-permute-start.13 = (bf16[192,256]{1,0:T(8,128)(2,1)S(1)}, bf16[192,256]{1,0:T(8,128)(2,1)S(1)}, u32[]{:S(2)}, u32[]{:S(2)}) collective-permute-start(bf16[192,256]{1,0:T(8,128)(2,1)S(1)} %get-tuple-element.188), channel_id=1, source_target_pairs={{0,6},{1,7},{2,0},{3,1},{4,2},{5,3},{6,4},{7,5},{8,14},{9,15},{10,... | collective-permute-start | bytes 294920 | tf_op jit(solution)/shard_map/ppermute | solution.py:1458
  92.4 6.7 %collective-permute-start.14 = (bf16[16,96,768]{2,1,0:T(8,128)(2,1)S(1)}, bf16[16,96,768]{2,1,0:T(8,128)(2,1)S(1)}, u32[]{:S(2)}, u32[]{:S(2)}) collective-permute-start(bf16[16,96,768]{2,1,0:T(8,128)(2,1)S(1)} %get-tuple-element.197), channel_id=1, source_target_pairs={{0,1},{1,0},{2,3},{3,2},{4,5},{5,4},{6,7},{7,6},{8,9},{9,8},{10,11... | collective-permute-start | bytes 7077896 | tf_op jit(solution)/shard_map/ppermute | solution.py:1462
  97.4 19.6 %collective-permute-start.17 = (bf16[16,120,768]{2,1,0:T(8,128)(2,1)S(1)}, bf16[16,120,768]{2,1,0:T(8,128)(2,1)S(1)}, u32[]{:S(2)}, u32[]{:S(2)}) collective-permute-start(bf16[16,120,768]{2,1,0:T(8,128)(2,1)S(1)} %get-tuple-element.202), channel_id=1, source_target_pairs={{0,1},{1,0},{2,3},{3,2},{4,5},{5,4},{6,7},{7,6},{8,9},{9,8},{10,11... | collective-permute-start | bytes 8847368 | tf_op jit(solution)/shard_map/ppermute | solution.py:1462
  100.8 15.3 %collective-permute-start.15 = (bf16[2,2,96,768]{3,2,1,0:T(8,128)(2,1)S(1)}, bf16[2,2,96,768]{3,2,1,0:T(8,128)(2,1)S(1)}, u32[]{:S(2)}, u32[]{:S(2)}) collective-permute-start(bf16[2,2,96,768]{3,2,1,0:T(8,128)(2,1)S(1)} %get-tuple-element.210), channel_id=1, source_target_pairs={{0,8},{8,0},{16,24},{24,16},{1,9},{9,1},{17,25},{25,17},{2,10},{10... | collective-permute-start | bytes 1769480 | tf_op jit(solution)/shard_map/ppermute | solution.py:1466
  102.1 15.0 %collective-permute-start.16 = (bf16[2,2,96,768]{3,2,1,0:T(8,128)(2,1)S(1)}, bf16[2,2,96,768]{3,2,1,0:T(8,128)(2,1)S(1)}, u32[]{:S(2)}, u32[]{:S(2)}) collective-permute-start(bf16[2,2,96,768]{3,2,1,0:T(8,128)(2,1)S(1)} %get-tuple-element.211), channel_id=1, source_target_pairs={{0,16},{8,24},{16,0},{24,8},{1,17},{9,25},{17,1},{25,9},{2,18},{10... | collective-permute-start | bytes 1769480 | tf_op jit(solution)/shard_map/ppermute | solution.py:1466
  117.9 19.0 %collective-permute-start.22 = (bf16[2,2,120,768]{3,2,1,0:T(8,128)(2,1)S(1)}, bf16[2,2,120,768]{3,2,1,0:T(8,128)(2,1)S(1)}, u32[]{:S(2)}, u32[]{:S(2)}) collective-permute-start(bf16[2,2,120,768]{3,2,1,0:T(8,128)(2,1)S(1)} %get-tuple-element.224), channel_id=1, source_target_pairs={{0,8},{8,0},{16,24},{24,16},{1,9},{9,1},{17,25},{25,17},{2,10},{10... | collective-permute-start | bytes 2211848 | tf_op jit(solution)/shard_map/ppermute | solution.py:1466
  118.8 18.6 %collective-permute-start.23 = (bf16[2,2,120,768]{3,2,1,0:T(8,128)(2,1)S(1)}, bf16[2,2,120,768]{3,2,1,0:T(8,128)(2,1)S(1)}, u32[]{:S(2)}, u32[]{:S(2)}) collective-permute-start(bf16[2,2,120,768]{3,2,1,0:T(8,128)(2,1)S(1)} %get-tuple-element.225), channel_id=1, source_target_pairs={{0,16},{8,24},{16,0},{24,8},{1,17},{9,25},{17,1},{25,9},{2,18},{10... | collective-permute-start | bytes 2211848 | tf_op jit(solution)/shard_map/ppermute | solution.py:1466
  120.1 20.1 %collective-permute-start.19 = (bf16[576,256]{1,0:T(8,128)(2,1)S(1)}, bf16[576,256]{1,0:T(8,128)(2,1)S(1)}, u32[]{:S(2)}, u32[]{:S(2)}) collective-permute-start(bf16[576,256]{1,0:T(8,128)(2,1)S(1)} %get-tuple-element.233.refs_5_), channel_id=1, source_target_pairs={{0,6},{1,7},{2,0},{3,1},{4,2},{5,3},{6,4},{7,5},{8,14},{9,15},{10,... | collective-permute-start | bytes 884744 | tf_op jit(solution)/shard_map/ppermute | solution.py:1458
  120.1 26.9 %collective-permute-start.20 = (bf16[576,256]{1,0:T(8,128)(2,1)S(1)}, bf16[576,256]{1,0:T(8,128)(2,1)S(1)}, u32[]{:S(2)}, u32[]{:S(2)}) collective-permute-start(bf16[576,256]{1,0:T(8,128)(2,1)S(1)} %get-tuple-element.234.refs_6_), channel_id=1, source_target_pairs={{0,4},{1,5},{2,6},{3,7},{4,0},{5,1},{6,2},{7,3},{8,12},{9,13},{10,... | collective-permute-start | bytes 884744 | tf_op jit(solution)/shard_map/ppermute | solution.py:1458
  120.9 26.2 %collective-permute-start.21 = (bf16[576,256]{1,0:T(8,128)(2,1)S(1)}, bf16[576,256]{1,0:T(8,128)(2,1)S(1)}, u32[]{:S(2)}, u32[]{:S(2)}) collective-permute-start(bf16[576,256]{1,0:T(8,128)(2,1)S(1)} %get-tuple-element.235.refs_7_), channel_id=1, source_target_pairs={{0,2},{1,3},{2,4},{3,5},{4,6},{5,7},{6,0},{7,1},{8,10},{9,11},{10,... | collective-permute-start | bytes 884744 | tf_op jit(solution)/shard_map/ppermute | solution.py:1458
  138.6 16.3 %collective-permute-start.24 = (bf16[2,216,768]{2,1,0:T(8,128)(2,1)S(1)}, bf16[2,216,768]{2,1,0:T(8,128)(2,1)S(1)}, u32[]{:S(2)}, u32[]{:S(2)}) collective-permute-start(bf16[2,216,768]{2,1,0:T(8,128)(2,1)S(1)} %get-tuple-element.261), channel_id=1, source_target_pairs={{0,16},{8,24},{16,0},{24,8},{1,17},{9,25},{17,1},{25,9},{2,18},{10... | collective-permute-start | bytes 1990664 | tf_op jit(solution)/shard_map/ppermute | solution.py:1466
  139.0 16.0 %collective-permute-start.25 = (bf16[2,216,768]{2,1,0:T(8,128)(2,1)S(1)}, bf16[2,216,768]{2,1,0:T(8,128)(2,1)S(1)}, u32[]{:S(2)}, u32[]{:S(2)}) collective-permute-start(bf16[2,216,768]{2,1,0:T(8,128)(2,1)S(1)} %get-tuple-element.263), channel_id=1, source_target_pairs={{0,8},{8,0},{16,24},{24,16},{1,9},{9,1},{17,25},{25,17},{2,10},{10... | collective-permute-start | bytes 1990664 | tf_op jit(solution)/shard_map/ppermute | solution.py:1466
  147.1 13.1 %collective-permute-start.29 = (bf16[16,24,768]{2,1,0:T(8,128)(2,1)S(1)}, bf16[16,24,768]{2,1,0:T(8,128)(2,1)S(1)}, u32[]{:S(2)}, u32[]{:S(2)}) collective-permute-start(bf16[16,24,768]{2,1,0:T(8,128)(2,1)S(1)} %get-tuple-element.269), channel_id=1, source_target_pairs={{0,1},{1,0},{2,3},{3,2},{4,5},{5,4},{6,7},{7,6},{8,9},{9,8},{10,11... | collective-permute-start | bytes 1769480 | tf_op jit(solution)/shard_map/ppermute | solution.py:1462
  156.3 20.9 %collective-permute-start.26 = (bf16[216,768]{1,0:T(8,128)(2,1)S(1)}, bf16[216,768]{1,0:T(8,128)(2,1)S(1)}, u32[]{:S(2)}, u32[]{:S(2)}) collective-permute-start(bf16[216,768]{1,0:T(8,128)(2,1)S(1)} %get-tuple-element.265), channel_id=1, source_target_pairs={{0,2},{1,3},{2,4},{3,5},{4,6},{5,7},{6,0},{7,1},{8,10},{9,11},{10,... | collective-permute-start | bytes 995336 | tf_op jit(solution)/shard_map/ppermute | solution.py:1458
  156.4 26.9 %collective-permute-start.27 = (bf16[216,768]{1,0:T(8,128)(2,1)S(1)}, bf16[216,768]{1,0:T(8,128)(2,1)S(1)}, u32[]{:S(2)}, u32[]{:S(2)}) collective-permute-start(bf16[216,768]{1,0:T(8,128)(2,1)S(1)} %get-tuple-element.266), channel_id=1, source_target_pairs={{0,4},{1,5},{2,6},{3,7},{4,0},{5,1},{6,2},{7,3},{8,12},{9,13},{10,... | collective-permute-start | bytes 995336 | tf_op jit(solution)/shard_map/ppermute | solution.py:1458
  157.2 26.0 %collective-permute-start.28 = (bf16[216,768]{1,0:T(8,128)(2,1)S(1)}, bf16[216,768]{1,0:T(8,128)(2,1)S(1)}, u32[]{:S(2)}, u32[]{:S(2)}) collective-permute-start(bf16[216,768]{1,0:T(8,128)(2,1)S(1)} %get-tuple-element.267), channel_id=1, source_target_pairs={{0,6},{1,7},{2,0},{3,1},{4,2},{5,3},{6,4},{7,5},{8,14},{9,15},{10,... | collective-permute-start | bytes 995336 | tf_op jit(solution)/shard_map/ppermute | solution.py:1458
  160.8 5.2 %collective-permute-start.30 = (bf16[2,2,24,768]{3,2,1,0:T(8,128)(2,1)S(1)}, bf16[2,2,24,768]{3,2,1,0:T(8,128)(2,1)S(1)}, u32[]{:S(2)}, u32[]{:S(2)}) collective-permute-start(bf16[2,2,24,768]{3,2,1,0:T(8,128)(2,1)S(1)} %get-tuple-element.272), channel_id=1, source_target_pairs={{0,8},{8,0},{16,24},{24,16},{1,9},{9,1},{17,25},{25,17},{2,10},{10... | collective-permute-start | bytes 442376 | tf_op jit(solution)/shard_map/ppermute | solution.py:1466
  174.7 8.5 %collective-permute-start.34 = (bf16[24,768]{1,0:T(8,128)(2,1)S(1)}, bf16[24,768]{1,0:T(8,128)(2,1)S(1)}, u32[]{:S(2)}, u32[]{:S(2)}) collective-permute-start(bf16[24,768]{1,0:T(8,128)(2,1)S(1)} %get-tuple-element.279), channel_id=1, source_target_pairs={{0,2},{1,3},{2,4},{3,5},{4,6},{5,7},{6,0},{7,1},{8,10},{9,11},{10,... | collective-permute-start | bytes 110600 | tf_op jit(solution)/shard_map/ppermute | solution.py:1458
  175.3 14.3 %collective-permute-start.35 = (bf16[24,768]{1,0:T(8,128)(2,1)S(1)}, bf16[24,768]{1,0:T(8,128)(2,1)S(1)}, u32[]{:S(2)}, u32[]{:S(2)}) collective-permute-start(bf16[24,768]{1,0:T(8,128)(2,1)S(1)} %get-tuple-element.280), channel_id=1, source_target_pairs={{0,4},{1,5},{2,6},{3,7},{4,0},{5,1},{6,2},{7,3},{8,12},{9,13},{10,... | collective-permute-start | bytes 110600 | tf_op jit(solution)/shard_map/ppermute | solution.py:1458
  177.1 12.5 %collective-permute-start.36 = (bf16[24,768]{1,0:T(8,128)(2,1)S(1)}, bf16[24,768]{1,0:T(8,128)(2,1)S(1)}, u32[]{:S(2)}, u32[]{:S(2)}) collective-permute-start(bf16[24,768]{1,0:T(8,128)(2,1)S(1)} %get-tuple-element.281), channel_id=1, source_target_pairs={{0,6},{1,7},{2,0},{3,1},{4,2},{5,3},{6,4},{7,5},{8,14},{9,15},{10,... | collective-permute-start | bytes 110600 | tf_op jit(solution)/shard_map/ppermute | solution.py:1458
  (28 other events, 358.4 us)

commit v5 on v4

--- a/solution.py
+++ b/solution.py
@@ -929,7 +929,7 @@
             jax.ShapeDtypeStruct((2 * share, keys // 2), jnp.bfloat16),
         ],
         compiler_params=pltpu.CompilerParams(vmem_limit_bytes=20 << 20),
-        cost_estimate=NO_COST,
+        cost_estimate=HIGH_COST,
         name="attend_back",
     )(meta, doc_line, q_ext, mixed, lse, k_ext, k_t, v_ext, *grad_t)
 
@@ -1488,25 +1488,34 @@
     return pl.BlockSpec((1, 2, shape[2] // 2) + shape[3:], index)
 
 
-def outgoing_kernel(scalars, low_a, low_b, high_a, high_b, low_ref, high_ref):
-    low_ref[...] = sent(wide(low_a[:, 0]) + wide(low_b[:, 0]))
-    high_ref[...] = sent(wide(high_a[0]) + wide(high_b[0]))
-
-
-def outgoing(scalars, keep, other, kept=False):
-    shape = keep.shape
-    out = jax.ShapeDtypeStruct((2, shape[2] // 2) + shape[3:], jnp.bfloat16)
-    low, high = low_part(shape, kept), high_part(shape, kept)
+def outgoing_kernel(scalars, *refs):
+    low_ref, high_ref = refs[-2:]
+    first = 0
+    for group in range(len(refs) // 4):
+        low_a, low_b, high_a, high_b = refs[4 * group : 4 * group + 4]
+        rows = slice(first, first + low_a.shape[3])
+        low_ref[:, :, rows] = sent(wide(low_a[:, 0]) + wide(low_b[:, 0]))
+        high_ref[:, :, rows] = sent(wide(high_a[0]) + wide(high_b[0]))
+        first += low_a.shape[3]
+
+
+def outgoing(scalars, groups, kept=False):
+    arrays, specs = [], []
+    for keep, other in groups:
+        low, high = low_part(keep.shape, kept), high_part(keep.shape, kept)
+        arrays += [keep, other, keep, other]
+        specs += [low, low, high, high]
+    shape = groups[0][0].shape
+    rows = sum(keep.shape[3] for keep, _ in groups)
+    out = jax.ShapeDtypeStruct((2, shape[2] // 2, rows, shape[4]), jnp.bfloat16)
     return call_whole(
         outgoing_kernel,
         [out, out],
         "kept" if kept else "outgoing",
         scalars,
-        keep,
-        other,
-        keep,
-        other,
-        in_specs=[low, low, high, high],
+        *arrays,
+        in_specs=specs,
+        limit=20,
     )
 
 
@@ -1767,36 +1776,27 @@
     result, grad_middle, gmid_b = outs[:3]
     go = outs[3 : 3 + chips]
     z, h2, bent, pre, dinner, dfeed, dhidden = outs[3 + chips :]
-    go = [go[0]] + [chip_shift(go[step], step) for step in range(1, chips)]
     keep_a, send_a = down_grad(place, bent, cotangent, hidden // parts)
     keep_b, send_b = up_out_grad(place, h2, pre, z, gmid_b, perm, per)
-
+    go, keep_b, send_b = lax.optimization_barrier((go, keep_b, send_b))
+    go = [go[0]] + [chip_shift(go[step], step) for step in range(1, chips)]
 
     def gridded(array):
         return array.reshape((2, 2, chips) + array.shape[1:])
 
-    keep_a, other_a = gridded(keep_a), gridded(seq_swap(send_a, 1))
-    other_b = seq_swap(send_b, 1)
-    arrived_place = after(place, [*go, keep_b], HIGH_COST)
-    out_a = outgoing(arrived_place, keep_a, other_a)
-    kept_a = outgoing(arrived_place, keep_a, other_a, True)
-    go, out_a, kept_a, keep_b, send_b = lax.optimization_barrier(
-        (go, out_a, kept_a, keep_b, send_b)
-    )
-    in_a = [row_swap(out_a[0], 1), row_swap(out_a[1], 2)]
+    sums = [
+        (gridded(keep), gridded(seq_swap(send, 1)))
+        for keep, send in ((keep_a, send_a), (keep_b, send_b))
+    ]
+    low, high = outgoing(place, sums)
+    arrived_sums = [row_swap(low, 1), row_swap(high, 2)]
     dq, pair, other = attend_back(
         meta, doc_line, q_ext, go, mixed, lse, k_ext, k_t, v_ext, heads, block, scale
     )
-    dq, pair, other, in_a, keep_b, other_b = lax.optimization_barrier(
-        (dq, pair, other, in_a, keep_b, other_b)
-    )
-    keep_b, other_b = gridded(keep_b), gridded(other_b)
-    out_b = outgoing(place, keep_b, other_b)
-    in_b = [row_swap(out_b[0], 1), row_swap(out_b[1], 2)]
     grads = join_parts(place, dq, pair, seq_swap(other, 1), chips)
     home = [grads[0]] + [chip_shift(grads[step], -step) for step in range(1, chips)]
-    grads, keep_b, other_b = lax.optimization_barrier((grads, keep_b, other_b))
-    kept_b = outgoing(place, keep_b, other_b, True)
+    grads, sums = lax.optimization_barrier((grads, sums))
+    kept = outgoing(place, sums, True)
     mine_grad, send_grad = head_grads(
         place,
         own,
@@ -1809,10 +1809,10 @@
         where_lane,
         per,
     )
-    in_a, in_b, kept_a, kept_b, mine_grad, send_grad = lax.optimization_barrier(
-        (in_a, in_b, kept_a, kept_b, mine_grad, send_grad)
-    )
-    low_keep, low_send, high_keep, high_send = halfway(place, [(*kept_a, *in_a), (*kept_b, *in_b)])
+    arrived_sums, kept, mine_grad, send_grad = lax.optimization_barrier(
+        (arrived_sums, kept, mine_grad, send_grad)
+    )
+    low_keep, low_send, high_keep, high_send = halfway(place, [(*kept, *arrived_sums)])
     low_in, high_in = row_swap(low_send, 2), row_swap(high_send, 1)
     home, mine_grad, send_grad = lax.optimization_barrier((home, mine_grad, send_grad))
     mine_grad, other_grad = gridded(mine_grad), gridded(seq_swap(send_grad, 1))
@@ -1821,10 +1821,10 @@
     grad_input = final(
         place, home, tokens, grad_middle, w_query, w_key, w_value, gain_first
     )
-    low, high = outgoing(place, mine_grad, other_grad)
+    low, high = outgoing(place, [(mine_grad, other_grad)])
     low_keep, low_send, high_keep, high_send = halfway(
         place,
-        [(*outgoing(place, mine_grad, other_grad, True), row_swap(low, 1), row_swap(high, 2))],
+        [(*outgoing(place, [(mine_grad, other_grad)], True), row_swap(low, 1), row_swap(high, 2))],
     )
     stage = split(
         place, [(low_keep, row_swap(low_send, 2), high_keep, row_swap(high_send, 1))], chips

time: 192 us -> 187 us (0.974)
  starting transfers between devices: 43.4 us -> 40.8 us
  waiting for transfers between devices: 56.3 us -> 54.1 us
    ppermute x10 -> x8, waiting for transfers between devices: 27.6 us -> 12 us  [row_swap(): lax.ppermute(value, 'row', [(i, i ^ bit) for i in range(lax.axis_size('ro...]
    ppermute x17, waiting for transfers between devices: 20 us -> 31.2 us  [chip_shift(): lax.ppermute(value, 'seq', [(i, (i + 2 * steps) % count) for i in range(c...]
    ppermute x8, waiting for transfers between devices: 1.92 us -> 4.14 us  [seq_swap(): lax.ppermute(value, 'seq', [(i, i ^ bit) for i in range(lax.axis_size('se...]
    ppermute x17, starting transfers between devices: 29.6 us -> 27.6 us  [chip_shift(): lax.ppermute(value, 'seq', [(i, (i + 2 * steps) % count) for i in range(c...]
    pallas_call x17 -> x15, Pallas kernels: 27.9 us -> 26.6 us  [call_whole(): pl.pallas_call(kernel, grid_spec=pltpu.PrefetchScalarGridSpec(num_scalar_...]
    ppermute x10 -> x8, starting transfers between devices: 9.76 us -> 9.15 us  [row_swap(): lax.ppermute(value, 'row', [(i, i ^ bit) for i in range(lax.axis_size('ro...]
  transfers between devices with their start and end apart: 37 -> 35, of which waited for: 17 -> 19; matrix products, arithmetic and copies ran while one was open for 9% -> 9% of each run, Pallas kernels for 21% -> 18%
where the time goes in v5:
time: 187 us
  Pallas kernels  70 us (37%)
  waiting for transfers between devices  54.1 us (29%)
  starting transfers between devices  40.8 us (22%)
  matrix products  10.6 us (6%)
  other arithmetic  6.09 us (3%)
  local copies, waits for them, and re-layouts  4.54 us (2%)
    ppermute x17, waiting for transfers between devices, chip_shift(): lax.ppermute(value, 'seq', [(i, (i + 2 * steps) % count) for i in range(c...  31.2 us
    ppermute x17, starting transfers between devices, chip_shift(): lax.ppermute(value, 'seq', [(i, (i + 2 * steps) % count) for i in range(c...  27.6 us
    pallas_call x15, Pallas kernels, call_whole(): pl.pallas_call(kernel, grid_spec=pltpu.PrefetchScalarGridSpec(num_scalar_...  26.6 us
    pallas_call x1, Pallas kernels, middle(): pl.pallas_call(partial(middle_kernel, chips, tiles), grid_spec=pltpu.Pref...  15.2 us
    ppermute x8, waiting for transfers between devices, row_swap(): lax.ppermute(value, 'row', [(i, i ^ bit) for i in range(lax.axis_size('ro...  12 us
    pallas_call x1, Pallas kernels, attend_back(): pl.pallas_call(partial(attend_back_kernel, heads, block, key_blocks, scal...  10.6 us
    ppermute x8, starting transfers between devices, row_swap(): lax.ppermute(value, 'row', [(i, i ^ bit) for i in range(lax.axis_size('ro...  9.15 us
    pallas_call x1, Pallas kernels, attend(): pl.pallas_call(partial(attend_kernel, heads, block, key_blocks), grid_spe...  8.75 us
  transfers between devices with their start and end apart: 35, of which 19 were waited for; matrix products, arithmetic and copies ran while one was open for 9% of the time, Pallas kernels for 18%

profile of v5, /device:TPU:0, one launch (start us, length us, event | category | flops | bytes accessed | tf_op | source)
XLA Modules:
  0.0 187.3 jit_solution(11669567775788411792)
XLA Ops:
  2.6 3.1 %collective-permute-start = (bf16[256,768]{1,0:T(8,128)(2,1)S(1)}, bf16[256,768]{1,0:T(8,128)(2,1)S(1)}, u32[]{:S(2)}, u32[]{:S(2)}) collective-permute-start(bf16[256,768]{1,0:T(8,128)(2,1)S(1)} %norm.1.refs_0_), channel_id=1, source_target_pairs={{0,2},{1,3},{2,4},{3,5},{4,6},{5,7},{6,0},{7,1},{8,10},{9,11},{10,... | collective-permute-start | bytes 1179656 | tf_op jit(solution)/shard_map/ppermute | solution.py:1458
  5.7 2.1 %collective-permute-start.1 = (bf16[256,768]{1,0:T(8,128)(2,1)S(1)}, bf16[256,768]{1,0:T(8,128)(2,1)}, u32[]{:S(2)}, u32[]{:S(2)}) collective-permute-start(bf16[256,768]{1,0:T(8,128)(2,1)S(1)} %norm.1.refs_0_), channel_id=1, source_target_pairs={{0,6},{1,7},{2,0},{3,1},{4,2},{5,3},{6,4},{7,5},{8,14},{9,15},{10,... | collective-permute-start | bytes 1179656 | tf_op jit(solution)/shard_map/ppermute | solution.py:1458
  13.9 2.4 %fusion.refs_17_ = bf16[5376,128]{1,0:T(8,128)(2,1)S(1)} fusion(s32[5376]{0:T(1024)S(1)} %add_select_fusion), kind=kLoop, calls=%fused_computation.1 | loop fusion | flops 1376256 | bytes 1397760 | tf_op jit(solution)/shard_map/convert_element_type | solution.py:1733
  19.4 3.0 %fusion.4.refs_9_ = bf16[768,384]{1,0:T(8,128)(2,1)} fusion(bf16[768,768]{1,0:T(8,128)(2,1)} %refs_7_.3, s32[384]{0:T(512)S(1)} %fusion.47, pred[384]{0:T(512)(128)(4,1)S(1)} %fusion.51), kind=kOutput, calls=%fused_computation.11 | convolution fusion | flops 453869568 | bytes 1771392 | tf_op jit(solution)/shard_map/dot_general | solution.py:570
  22.3 2.5 %collective-permute-done.1.refs_3_ = bf16[256,768]{1,0:T(8,128)(2,1)} collective-permute-done((bf16[256,768]{1,0:T(8,128)(2,1)S(1)}, bf16[256,768]{1,0:T(8,128)(2,1)}, u32[]{:S(2)}, u32[]{:S(2)}) %collective-permute-start.1) | collective-permute-done | bytes 393248 | tf_op jit(solution)/shard_map/ppermute | solution.py:1458
  27.8 2.2 %fusion.5.refs_9_ = bf16[768,384]{1,0:T(8,128)(2,1)S(1)} fusion(bf16[768,768]{1,0:T(8,128)(2,1)} %refs_8_.3, s32[384]{0:T(512)S(1)} %fusion.47, pred[384]{0:T(512)(128)(4,1)S(1)} %fusion.51), kind=kOutput, calls=%fused_computation.12 | convolution fusion | flops 453869568 | bytes 1771392 | tf_op jit(solution)/shard_map/dot_general | solution.py:570
  30.6 6.8 %collective-permute-done.2 = bf16[256,768]{1,0:T(8,128)(2,1)} collective-permute-done((bf16[256,768]{1,0:T(8,128)(2,1)}, bf16[256,768]{1,0:T(8,128)(2,1)}, u32[]{:S(2)}, u32[]{:S(2)}) %collective-permute-start.2) | collective-permute-done | bytes 393248 | tf_op jit(solution)/shard_map/ppermute | solution.py:1634
  40.3 4.9 %project.1 = (bf16[384,1024]{1,0:T(8,128)(2,1)S(1)}, bf16[2048,384]{1,0:T(8,128)(2,1)S(1)}, bf16[192,2048]{1,0:T(8,128)(2,1)S(1)}) custom-call(s32[9]{0:T(128)S(1)} %pad_add_fusion.meta, bf16[256,768]{1,0:T(8,128)(2,1)S(1)} %norm.1.refs_0_, bf16[256,768]{1,0:T(8,128)(2,1)S(1)} %collective-permute-done.refs_1_, ...), custom_call_target="tpu_custom_call" | custom-call | flops 1000 | bytes 1000 | tf_op jit(solution)/shard_map/project/pallas_call | solution.py:574
  45.3 8.7 %attend.1 = (f32[192,1024]{1,0:T(8,128)S(1)}, f32[3,1,1024]{2,1,0:T(1,128)S(1)}, bf16[192,256]{1,0:T(8,128)(2,1)S(1)}, bf16[192,256]{1,0:T(8,128)(2,1)S(1)}, bf1...) custom-call(s32[20]{0:T(128)S(1)} %concatenate.7.meta, s32[1,1024]{1,0:T(1,128)S(1)} %bitcast.63, ...), custom_call_target="tpu_custom_call" | custom-call | flops 1000 | bytes 1000 | tf_op jit(solution)/shard_map/attend/pallas_call | solution.py:863
  54.1 5.1 %collective-permute-start.8 = (bf16[192,256]{1,0:T(8,128)(2,1)S(1)}, bf16[192,256]{1,0:T(8,128)(2,1)S(1)}, u32[]{:S(2)}, u32[]{:S(2)}) collective-permute-start(bf16[192,256]{1,0:T(8,128)(2,1)S(1)} %get-tuple-element.150), channel_id=1, source_target_pairs={{0,6},{1,7},{2,0},{3,1},{4,2},{5,3},{6,4},{7,5},{8,14},{9,15},{10,... | collective-permute-start | bytes 294920 | tf_op jit(solution)/shard_map/ppermute | solution.py:1458
  59.6 1.9 %collective-permute-start.10 = (bf16[192,256]{1,0:T(8,128)(2,1)S(1)}, bf16[192,256]{1,0:T(8,128)(2,1)S(1)}, u32[]{:S(2)}, u32[]{:S(2)}) collective-permute-start(bf16[192,256]{1,0:T(8,128)(2,1)S(1)} %get-tuple-element.152), channel_id=1, source_target_pairs={{0,2},{1,3},{2,4},{3,5},{4,6},{5,7},{6,0},{7,1},{8,10},{9,11},{10,... | collective-permute-start | bytes 294920 | tf_op jit(solution)/shard_map/ppermute | solution.py:1458
  61.5 4.3 %project_back.1 = (bf16[192,2048]{1,0:T(8,128)(2,1)S(1)}, bf16[2048,384]{1,0:T(8,128)(2,1)S(1)}) custom-call(s32[4]{0:T(128)S(1)} %pad_add_fusion.1.unused.position.scalars, bf16[256,768]{1,0:T(8,128)(2,1)S(1)} %norm.1.refs_0_, bf16[256,768]{1,0:T(8,128)(2,1)S(1)} %collective-permute-done.refs_1_, bf16[256,768]{1,0:T(8,128)(2,1)S(1)} %broadcast_select_fusion.refs_2_, ...), custom_call_target="tpu_custom_call" | custom-call | flops 1000 | bytes 1000 | tf_op jit(solution)/shard_map/project_back/pallas_call | solution.py:574
  68.5 15.2 %middle.1 = (bf16[256,768]{1,0:T(8,128)(2,1)}, f32[256,768]{1,0:T(8,128)S(1)}, bf16[256,768]{1,0:T(8,128)(2,1)S(1)}, bf16[192,256]{1,0:T(8,128)(2,1)S(1)}, bf16[...) custom-call(s32[4]{0:T(128)S(1)} %pad_add_fusion.1.unused.position.s, ...), custom_call_target="tpu_custom_call" | custom-call | flops 1000 | bytes 1000 | tf_op jit(solution)/shard_map/middle/pallas_call | solution.py:1266
  83.7 4.9 %up_out_grad.1 = (bf16[16,120,768]{2,1,0:T(8,128)(2,1)S(1)}, bf16[16,120,768]{2,1,0:T(8,128)(2,1)S(1)}) custom-call(s32[4]{0:T(128)S(1)} %pad_add_fusion.1.unused.position.scalars, bf16[256,768]{1,0:T(8,128)(2,1)S(1)} %get-tuple-element.173.h2_ref, bf16[256,3072]{1,0:T(8,128)(2,1)S(1)} %get-tuple-element.174.pre_ref, ...), custom_call_target="tpu_custom_call" | custom-call | flops 1000 | bytes 1000 | tf_op jit(solution)/shard_map/up_out_grad/pallas_call | solution.py:1388
  88.7 2.8 %down_grad.1 = (bf16[16,96,768]{2,1,0:T(8,128)(2,1)S(1)}, bf16[16,96,768]{2,1,0:T(8,128)(2,1)S(1)}) custom-call(s32[4]{0:T(128)S(1)} %pad_add_fusion.1.unused.position.scalars, bf16[256,3072]{1,0:T(8,128)(2,1)S(1)} %get-tuple-element.191.bent_ref, bf16[256,768]{1,0:T(8,128)(2,1)S(1)} %copy-done.3), custom_call_target="tpu_custom_call" | custom-call | flops 1000 | bytes 1000 | tf_op jit(solution)/shard_map/down_grad/pallas_call | solution.py:1340
  92.4 1.9 %collective-permute-start.12 = (bf16[192,256]{1,0:T(8,128)(2,1)S(1)}, bf16[192,256]{1,0:T(8,128)(2,1)S(1)}, u32[]{:S(2)}, u32[]{:S(2)}) collective-permute-start(bf16[192,256]{1,0:T(8,128)(2,1)S(1)} %get-tuple-element.182), channel_id=1, source_target_pairs={{0,4},{1,5},{2,6},{3,7},{4,0},{5,1},{6,2},{7,3},{8,12},{9,13},{10,... | collective-permute-start | bytes 294920 | tf_op jit(solution)/shard_map/ppermute | solution.py:1458
  94.3 2.9 %collective-permute-start.13 = (bf16[192,256]{1,0:T(8,128)(2,1)S(1)}, bf16[192,256]{1,0:T(8,128)(2,1)S(1)}, u32[]{:S(2)}, u32[]{:S(2)}) collective-permute-start(bf16[192,256]{1,0:T(8,128)(2,1)S(1)} %get-tuple-element.183), channel_id=1, source_target_pairs={{0,6},{1,7},{2,0},{3,1},{4,2},{5,3},{6,4},{7,5},{8,14},{9,15},{10,... | collective-permute-start | bytes 294920 | tf_op jit(solution)/shard_map/ppermute | solution.py:1458
  100.4 2.5 %collective-permute-done.12.refs_2_ = bf16[192,256]{1,0:T(8,128)(2,1)S(1)} collective-permute-done((bf16[192,256]{1,0:T(8,128)(2,1)S(1)}, bf16[192,256]{1,0:T(8,128)(2,1)S(1)}, u32[]{:S(2)}, u32[]{:S(2)}) %collective-permute-start.12) | collective-permute-done | bytes 98336 | tf_op jit(solution)/shard_map/ppermute | solution.py:1458
  102.9 10.6 %attend_back.1 = (bf16[192,1024]{1,0:T(8,128)(2,1)S(1)}, f32[384,1024]{1,0:T(8,128)S(1)}, bf16[384,1024]{1,0:T(8,128)(2,1)S(1)}) custom-call(s32[20]{0:T(128)S(1)} %concatenate.7.meta, s32[1,1024]{1,0:T(1,128)S(1)} %bitcast.64, bf16[384,1024]{1,0:T(8,128)(2,1)S(1)} %get-tuple-element.141.q_ref, f32[192,1024]{1,0:T(8,128)S(1)} %copy-done.18, ...), custom_call_target="tpu_custom_call" | custom-call | flops 49999998976 | bytes 1000 | tf_op jit(solution)/shard_map/attend_back/pallas_call | solution.py:899
  113.7 2.3 %collective-permute-done.14.other_ref = bf16[384,1024]{1,0:T(8,128)(2,1)S(1)} collective-permute-done((bf16[384,1024]{1,0:T(8,128)(2,1)S(1)}, bf16[384,1024]{1,0:T(8,128)(2,1)S(1)}, u32[]{:S(2)}, u32[]{:S(2)}) %collective-permute-start.14) | collective-permute-done | bytes 786464 | tf_op jit(solution)/shard_map/ppermute | solution.py:1462
  116.7 3.4 %collective-permute-start.15 = (bf16[576,256]{1,0:T(8,128)(2,1)S(1)}, bf16[576,256]{1,0:T(8,128)(2,1)S(1)}, u32[]{:S(2)}, u32[]{:S(2)}) collective-permute-start(bf16[576,256]{1,0:T(8,128)(2,1)S(1)} %get-tuple-element.205.refs_5_), channel_id=1, source_target_pairs={{0,6},{1,7},{2,0},{3,1},{4,2},{5,3},{6,4},{7,5},{8,14},{9,15},{10,... | collective-permute-start | bytes 884744 | tf_op jit(solution)/shard_map/ppermute | solution.py:1458
  121.9 4.5 %head_grads.1 = (bf16[16,24,768]{2,1,0:T(8,128)(2,1)S(1)}, bf16[16,24,768]{2,1,0:T(8,128)(2,1)S(1)}) custom-call(s32[4]{0:T(128)S(1)} %pad_add_fusion.1.unused.position.scalars, bf16[256,768]{1,0:T(8,128)(2,1)S(1)} %norm.1.refs_0_, bf16[256,768]{1,0:T(8,128)(2,1)S(1)} %collective-permute-done.refs_1_, bf16[256,768]{1,0:T(8,128)(2,1)S(1)} %broadcast_select_fusion.refs_2_, ...), custom_call_target="tpu_custom_call" | custom-call | flops 1000 | bytes 1000 | tf_op jit(solution)/shard_map/head_grads/pallas_call | solution.py:574
  126.4 3.4 %collective-permute-done.20.refs_2_ = bf16[2,2,216,768]{3,2,1,0:T(8,128)(2,1)S(1)} collective-permute-done((bf16[2,2,216,768]{3,2,1,0:T(8,128)(2,1)S(1)}, bf16[2,2,216,768]{3,2,1,0:T(8,128)(2,1)S(1)}, u32[]{:S(2)}, u32[]{:S(2)}) %collective-permute-start.20) | collective-permute-done | bytes 1327136 | tf_op jit(solution)/shard_map/ppermute | solution.py:1466
  133.5 12.4 %collective-permute-done.16.refs_2_ = bf16[576,256]{1,0:T(8,128)(2,1)S(1)} collective-permute-done((bf16[576,256]{1,0:T(8,128)(2,1)S(1)}, bf16[576,256]{1,0:T(8,128)(2,1)S(1)}, u32[]{:S(2)}, u32[]{:S(2)}) %collective-permute-start.16) | collective-permute-done | bytes 294944 | tf_op jit(solution)/shard_map/ppermute | solution.py:1458
  149.4 1.9 %collective-permute-start.25 = (bf16[216,768]{1,0:T(8,128)(2,1)S(1)}, bf16[216,768]{1,0:T(8,128)(2,1)S(1)}, u32[]{:S(2)}, u32[]{:S(2)}) collective-permute-start(bf16[216,768]{1,0:T(8,128)(2,1)S(1)} %get-tuple-element.234), channel_id=1, source_target_pairs={{0,4},{1,5},{2,6},{3,7},{4,0},{5,1},{6,2},{7,3},{8,12},{9,13},{10,... | collective-permute-start | bytes 995336 | tf_op jit(solution)/shard_map/ppermute | solution.py:1458
  151.3 2.8 %collective-permute-start.26 = (bf16[216,768]{1,0:T(8,128)(2,1)S(1)}, bf16[216,768]{1,0:T(8,128)(2,1)S(1)}, u32[]{:S(2)}, u32[]{:S(2)}) collective-permute-start(bf16[216,768]{1,0:T(8,128)(2,1)S(1)} %get-tuple-element.235), channel_id=1, source_target_pairs={{0,6},{1,7},{2,0},{3,1},{4,2},{5,3},{6,4},{7,5},{8,14},{9,15},{10,... | collective-permute-start | bytes 995336 | tf_op jit(solution)/shard_map/ppermute | solution.py:1458
  162.0 2.1 %collective-permute-start.30 = (bf16[2,24,768]{2,1,0:T(8,128)(2,1)S(1)}, bf16[2,24,768]{2,1,0:T(8,128)(2,1)S(1)}, u32[]{:S(2)}, u32[]{:S(2)}) collective-permute-start(bf16[2,24,768]{2,1,0:T(8,128)(2,1)S(1)} %get-tuple-element.243), channel_id=1, source_target_pairs={{0,16},{8,24},{16,0},{24,8},{1,17},{9,25},{17,1},{25,9},{2,18},{10... | collective-permute-start | bytes 221192 | tf_op jit(solution)/shard_map/ppermute | solution.py:1466
  164.1 2.4 %collective-permute-done.30.refs_1_ = bf16[2,24,768]{2,1,0:T(8,128)(2,1)S(1)} collective-permute-done((bf16[2,24,768]{2,1,0:T(8,128)(2,1)S(1)}, bf16[2,24,768]{2,1,0:T(8,128)(2,1)S(1)}, u32[]{:S(2)}, u32[]{:S(2)}) %collective-permute-start.30) | collective-permute-done | bytes 73760 | tf_op jit(solution)/shard_map/ppermute | solution.py:1466
  166.4 2.0 %collective-permute-done.31.refs_3_ = bf16[2,24,768]{2,1,0:T(8,128)(2,1)S(1)} collective-permute-done((bf16[2,24,768]{2,1,0:T(8,128)(2,1)S(1)}, bf16[2,24,768]{2,1,0:T(8,128)(2,1)S(1)}, u32[]{:S(2)}, u32[]{:S(2)}) %collective-permute-start.31) | collective-permute-done | bytes 73760 | tf_op jit(solution)/shard_map/ppermute | solution.py:1466
  169.9 6.2 %collective-permute-done.32.refs_5_ = bf16[24,768]{1,0:T(8,128)(2,1)S(1)} collective-permute-done((bf16[24,768]{1,0:T(8,128)(2,1)S(1)}, bf16[24,768]{1,0:T(8,128)(2,1)S(1)}, u32[]{:S(2)}, u32[]{:S(2)}) %collective-permute-start.32) | collective-permute-done | bytes 36896 | tf_op jit(solution)/shard_map/ppermute | solution.py:1458
  176.1 3.1 %final.1 = bf16[256,768]{1,0:T(8,128)(2,1)} custom-call(s32[4]{0:T(128)S(1)} %pad_add_fusion.1.unused.position.scalars, bf16[576,256]{1,0:T(8,128)(2,1)S(1)} %get-tuple-element.219.refs_4_.refs_0_, bf16[576,256]{1,0:T(8,128)(2,1)S(1)} %collective-permute-done.15.refs_1_, bf16[576,256]{1,0:T(8,128)(2,1)S(1)} %collective-permute-done.16.refs_2_, ...), custom_call_target="tpu_custom_call" | custom-call | flops 1000 | bytes 1000 | tf_op jit(solution)/shard_map/final/pallas_call | solution.py:574
  179.2 4.4 %collective-permute-done.33.refs_6_ = bf16[24,768]{1,0:T(8,128)(2,1)S(1)} collective-permute-done((bf16[24,768]{1,0:T(8,128)(2,1)S(1)}, bf16[24,768]{1,0:T(8,128)(2,1)S(1)}, u32[]{:S(2)}, u32[]{:S(2)}) %collective-permute-start.33) | collective-permute-done | bytes 36896 | tf_op jit(solution)/shard_map/ppermute | solution.py:1458
  (147 shorter events, 47.2 us)
Async XLA Ops:
  2.6 23.5 %collective-permute-start = (bf16[256,768]{1,0:T(8,128)(2,1)S(1)}, bf16[256,768]{1,0:T(8,128)(2,1)S(1)}, u32[]{:S(2)}, u32[]{:S(2)}) collective-permute-start(bf16[256,768]{1,0:T(8,128)(2,1)S(1)} %norm.1.refs_0_), channel_id=1, source_target_pairs={{0,2},{1,3},{2,4},{3,5},{4,6},{5,7},{6,0},{7,1},{8,10},{9,11},{10,... | collective-permute-start | bytes 1179656 | tf_op jit(solution)/shard_map/ppermute | solution.py:1458
  5.7 19.1 %collective-permute-start.1 = (bf16[256,768]{1,0:T(8,128)(2,1)S(1)}, bf16[256,768]{1,0:T(8,128)(2,1)}, u32[]{:S(2)}, u32[]{:S(2)}) collective-permute-start(bf16[256,768]{1,0:T(8,128)(2,1)S(1)} %norm.1.refs_0_), channel_id=1, source_target_pairs={{0,6},{1,7},{2,0},{3,1},{4,2},{5,3},{6,4},{7,5},{8,14},{9,15},{10,... | collective-permute-start | bytes 1179656 | tf_op jit(solution)/shard_map/ppermute | solution.py:1458
  7.8 30.8 %collective-permute-start.4 = (bf16[256,768]{1,0:T(8,128)(2,1)S(1)}, bf16[256,768]{1,0:T(8,128)(2,1)}, u32[]{:S(2)}, u32[]{:S(2)}) collective-permute-start(bf16[256,768]{1,0:T(8,128)(2,1)S(1)} %norm.1.refs_0_), channel_id=1, source_target_pairs={{0,1},{1,0},{2,3},{3,2},{4,5},{5,4},{6,7},{7,6},{8,9},{9,8},{10,11... | collective-permute-start | bytes 1179656 | tf_op jit(solution)/shard_map/ppermute | solution.py:1462
  24.8 12.6 %collective-permute-start.2 = (bf16[256,768]{1,0:T(8,128)(2,1)}, bf16[256,768]{1,0:T(8,128)(2,1)}, u32[]{:S(2)}, u32[]{:S(2)}) collective-permute-start(bf16[256,768]{1,0:T(8,128)(2,1)} %collective-permute-done.1.refs_3_), channel_id=1, source_target_pairs={{2,0},{3,1},{4,2},{5,3},{10,8},{11,9},{12,10},{13,11},{18,16},{19,... | collective-permute-start | bytes 1179656 | tf_op jit(solution)/shard_map/ppermute | solution.py:1634
  26.1 11.3 %collective-permute-start.3 = (bf16[256,768]{1,0:T(8,128)(2,1)S(1)}, bf16[256,768]{1,0:T(8,128)(2,1)}, u32[]{:S(2)}, u32[]{:S(2)}) collective-permute-start(bf16[256,768]{1,0:T(8,128)(2,1)S(1)} %collective-permute-done.refs_1_), channel_id=1, source_target_pairs={{2,4},{3,5},{4,6},{5,7},{10,12},{11,13},{12,14},{13,15},{18,20},{1... | collective-permute-start | bytes 1179656 | tf_op jit(solution)/shard_map/ppermute | solution.py:1634
  30.1 8.5 %collective-permute-start.5 = (bf16[256,768]{1,0:T(8,128)(2,1)S(1)}, bf16[256,768]{1,0:T(8,128)(2,1)S(1)}, u32[]{:S(2)}, u32[]{:S(2)}) collective-permute-start(bf16[256,768]{1,0:T(8,128)(2,1)S(1)} %collective-permute-done.refs_1_), channel_id=1, source_target_pairs={{0,1},{1,0},{2,3},{3,2},{4,5},{5,4},{6,7},{7,6},{8,9},{9,8},{10,11... | collective-permute-start | bytes 1179656 | tf_op jit(solution)/shard_map/ppermute | solution.py:1462
  30.1 8.5 %collective-permute-start.7 = (bf16[256,768]{1,0:T(8,128)(2,1)}, bf16[256,768]{1,0:T(8,128)(2,1)S(1)}, u32[]{:S(2)}, u32[]{:S(2)}) collective-permute-start(bf16[256,768]{1,0:T(8,128)(2,1)} %collective-permute-done.1.refs_3_), channel_id=1, source_target_pairs={{0,1},{1,0},{2,3},{3,2},{4,5},{5,4},{6,7},{7,6},{8,9},{9,8},{10,11... | collective-permute-start | bytes 1179656 | tf_op jit(solution)/shard_map/ppermute | solution.py:1462
  54.1 12.6 %collective-permute-start.8 = (bf16[192,256]{1,0:T(8,128)(2,1)S(1)}, bf16[192,256]{1,0:T(8,128)(2,1)S(1)}, u32[]{:S(2)}, u32[]{:S(2)}) collective-permute-start(bf16[192,256]{1,0:T(8,128)(2,1)S(1)} %get-tuple-element.150), channel_id=1, source_target_pairs={{0,6},{1,7},{2,0},{3,1},{4,2},{5,3},{6,4},{7,5},{8,14},{9,15},{10,... | collective-permute-start | bytes 294920 | tf_op jit(solution)/shard_map/ppermute | solution.py:1458
  59.2 9.2 %collective-permute-start.9 = (bf16[192,256]{1,0:T(8,128)(2,1)S(1)}, bf16[192,256]{1,0:T(8,128)(2,1)S(1)}, u32[]{:S(2)}, u32[]{:S(2)}) collective-permute-start(bf16[192,256]{1,0:T(8,128)(2,1)S(1)} %get-tuple-element.151), channel_id=1, source_target_pairs={{0,4},{1,5},{2,6},{3,7},{4,0},{5,1},{6,2},{7,3},{8,12},{9,13},{10,... | collective-permute-start | bytes 294920 | tf_op jit(solution)/shard_map/ppermute | solution.py:1458
  59.6 8.8 %collective-permute-start.10 = (bf16[192,256]{1,0:T(8,128)(2,1)S(1)}, bf16[192,256]{1,0:T(8,128)(2,1)S(1)}, u32[]{:S(2)}, u32[]{:S(2)}) collective-permute-start(bf16[192,256]{1,0:T(8,128)(2,1)S(1)} %get-tuple-element.152), channel_id=1, source_target_pairs={{0,2},{1,3},{2,4},{3,5},{4,6},{5,7},{6,0},{7,1},{8,10},{9,11},{10,... | collective-permute-start | bytes 294920 | tf_op jit(solution)/shard_map/ppermute | solution.py:1458
  88.6 8.8 %collective-permute-start.19 = (bf16[16,120,768]{2,1,0:T(8,128)(2,1)S(1)}, bf16[16,120,768]{2,1,0:T(8,128)(2,1)S(1)}, u32[]{:S(2)}, u32[]{:S(2)}) collective-permute-start(bf16[16,120,768]{2,1,0:T(8,128)(2,1)S(1)} %get-tuple-element.195), channel_id=1, source_target_pairs={{0,1},{1,0},{2,3},{3,2},{4,5},{5,4},{6,7},{7,6},{8,9},{9,8},{10,11... | collective-permute-start | bytes 8847368 | tf_op jit(solution)/shard_map/ppermute | solution.py:1462
  91.5 5.9 %collective-permute-start.18 = (bf16[16,96,768]{2,1,0:T(8,128)(2,1)S(1)}, bf16[16,96,768]{2,1,0:T(8,128)(2,1)S(1)}, u32[]{:S(2)}, u32[]{:S(2)}) collective-permute-start(bf16[16,96,768]{2,1,0:T(8,128)(2,1)S(1)} %get-tuple-element.193), channel_id=1, source_target_pairs={{0,1},{1,0},{2,3},{3,2},{4,5},{5,4},{6,7},{7,6},{8,9},{9,8},{10,11... | collective-permute-start | bytes 7077896 | tf_op jit(solution)/shard_map/ppermute | solution.py:1462
  92.0 8.4 %collective-permute-start.11 = (bf16[192,256]{1,0:T(8,128)(2,1)S(1)}, bf16[192,256]{1,0:T(8,128)(2,1)S(1)}, u32[]{:S(2)}, u32[]{:S(2)}) collective-permute-start(bf16[192,256]{1,0:T(8,128)(2,1)S(1)} %get-tuple-element.181), channel_id=1, source_target_pairs={{0,2},{1,3},{2,4},{3,5},{4,6},{5,7},{6,0},{7,1},{8,10},{9,11},{10,... | collective-permute-start | bytes 294920 | tf_op jit(solution)/shard_map/ppermute | solution.py:1458
  92.4 10.6 %collective-permute-start.12 = (bf16[192,256]{1,0:T(8,128)(2,1)S(1)}, bf16[192,256]{1,0:T(8,128)(2,1)S(1)}, u32[]{:S(2)}, u32[]{:S(2)}) collective-permute-start(bf16[192,256]{1,0:T(8,128)(2,1)S(1)} %get-tuple-element.182), channel_id=1, source_target_pairs={{0,4},{1,5},{2,6},{3,7},{4,0},{5,1},{6,2},{7,3},{8,12},{9,13},{10,... | collective-permute-start | bytes 294920 | tf_op jit(solution)/shard_map/ppermute | solution.py:1458
  94.3 8.6 %collective-permute-start.13 = (bf16[192,256]{1,0:T(8,128)(2,1)S(1)}, bf16[192,256]{1,0:T(8,128)(2,1)S(1)}, u32[]{:S(2)}, u32[]{:S(2)}) collective-permute-start(bf16[192,256]{1,0:T(8,128)(2,1)S(1)} %get-tuple-element.183), channel_id=1, source_target_pairs={{0,6},{1,7},{2,0},{3,1},{4,2},{5,3},{6,4},{7,5},{8,14},{9,15},{10,... | collective-permute-start | bytes 294920 | tf_op jit(solution)/shard_map/ppermute | solution.py:1458
  98.6 31.2 %collective-permute-start.20 = (bf16[2,2,216,768]{3,2,1,0:T(8,128)(2,1)S(1)}, bf16[2,2,216,768]{3,2,1,0:T(8,128)(2,1)S(1)}, u32[]{:S(2)}, u32[]{:S(2)}) collective-permute-start(bf16[2,2,216,768]{3,2,1,0:T(8,128)(2,1)S(1)} %get-tuple-element.196), channel_id=1, source_target_pairs={{0,8},{8,0},{16,24},{24,16},{1,9},{9,1},{17,25},{25,17},{2,10},{10... | collective-permute-start | bytes 3981320 | tf_op jit(solution)/shard_map/ppermute | solution.py:1466
  98.6 31.2 %collective-permute-start.21 = (bf16[2,2,216,768]{3,2,1,0:T(8,128)(2,1)S(1)}, bf16[2,2,216,768]{3,2,1,0:T(8,128)(2,1)S(1)}, u32[]{:S(2)}, u32[]{:S(2)}) collective-permute-start(bf16[2,2,216,768]{3,2,1,0:T(8,128)(2,1)S(1)} %get-tuple-element.197), channel_id=1, source_target_pairs={{0,16},{8,24},{16,0},{24,8},{1,17},{9,25},{17,1},{25,9},{2,18},{10... | collective-permute-start | bytes 3981320 | tf_op jit(solution)/shard_map/ppermute | solution.py:1466
  116.7 16.9 %collective-permute-start.15 = (bf16[576,256]{1,0:T(8,128)(2,1)S(1)}, bf16[576,256]{1,0:T(8,128)(2,1)S(1)}, u32[]{:S(2)}, u32[]{:S(2)}) collective-permute-start(bf16[576,256]{1,0:T(8,128)(2,1)S(1)} %get-tuple-element.205.refs_5_), channel_id=1, source_target_pairs={{0,6},{1,7},{2,0},{3,1},{4,2},{5,3},{6,4},{7,5},{8,14},{9,15},{10,... | collective-permute-start | bytes 884744 | tf_op jit(solution)/shard_map/ppermute | solution.py:1458
  120.1 25.8 %collective-permute-start.16 = (bf16[576,256]{1,0:T(8,128)(2,1)S(1)}, bf16[576,256]{1,0:T(8,128)(2,1)S(1)}, u32[]{:S(2)}, u32[]{:S(2)}) collective-permute-start(bf16[576,256]{1,0:T(8,128)(2,1)S(1)} %get-tuple-element.206.refs_6_), channel_id=1, source_target_pairs={{0,4},{1,5},{2,6},{3,7},{4,0},{5,1},{6,2},{7,3},{8,12},{9,13},{10,... | collective-permute-start | bytes 884744 | tf_op jit(solution)/shard_map/ppermute | solution.py:1458
  120.1 25.8 %collective-permute-start.17 = (bf16[576,256]{1,0:T(8,128)(2,1)S(1)}, bf16[576,256]{1,0:T(8,128)(2,1)S(1)}, u32[]{:S(2)}, u32[]{:S(2)}) collective-permute-start(bf16[576,256]{1,0:T(8,128)(2,1)S(1)} %get-tuple-element.207.refs_7_), channel_id=1, source_target_pairs={{0,2},{1,3},{2,4},{3,5},{4,6},{5,7},{6,0},{7,1},{8,10},{9,11},{10,... | collective-permute-start | bytes 884744 | tf_op jit(solution)/shard_map/ppermute | solution.py:1458
  131.0 16.2 %collective-permute-start.22 = (bf16[2,216,768]{2,1,0:T(8,128)(2,1)S(1)}, bf16[2,216,768]{2,1,0:T(8,128)(2,1)S(1)}, u32[]{:S(2)}, u32[]{:S(2)}) collective-permute-start(bf16[2,216,768]{2,1,0:T(8,128)(2,1)S(1)} %get-tuple-element.229), channel_id=1, source_target_pairs={{0,16},{8,24},{16,0},{24,8},{1,17},{9,25},{17,1},{25,9},{2,18},{10... | collective-permute-start | bytes 1990664 | tf_op jit(solution)/shard_map/ppermute | solution.py:1466
  132.5 15.5 %collective-permute-start.23 = (bf16[2,216,768]{2,1,0:T(8,128)(2,1)S(1)}, bf16[2,216,768]{2,1,0:T(8,128)(2,1)S(1)}, u32[]{:S(2)}, u32[]{:S(2)}) collective-permute-start(bf16[2,216,768]{2,1,0:T(8,128)(2,1)S(1)} %get-tuple-element.231), channel_id=1, source_target_pairs={{0,8},{8,0},{16,24},{24,16},{1,9},{9,1},{17,25},{25,17},{2,10},{10... | collective-permute-start | bytes 1990664 | tf_op jit(solution)/shard_map/ppermute | solution.py:1466
  145.9 8.3 %collective-permute-start.27 = (bf16[16,24,768]{2,1,0:T(8,128)(2,1)S(1)}, bf16[16,24,768]{2,1,0:T(8,128)(2,1)S(1)}, u32[]{:S(2)}, u32[]{:S(2)}) collective-permute-start(bf16[16,24,768]{2,1,0:T(8,128)(2,1)S(1)} %get-tuple-element.237), channel_id=1, source_target_pairs={{0,1},{1,0},{2,3},{3,2},{4,5},{5,4},{6,7},{7,6},{8,9},{9,8},{10,11... | collective-permute-start | bytes 1769480 | tf_op jit(solution)/shard_map/ppermute | solution.py:1462
  149.3 35.8 %collective-permute-start.24 = (bf16[216,768]{1,0:T(8,128)(2,1)S(1)}, bf16[216,768]{1,0:T(8,128)(2,1)S(1)}, u32[]{:S(2)}, u32[]{:S(2)}) collective-permute-start(bf16[216,768]{1,0:T(8,128)(2,1)S(1)} %get-tuple-element.233), channel_id=1, source_target_pairs={{0,2},{1,3},{2,4},{3,5},{4,6},{5,7},{6,0},{7,1},{8,10},{9,11},{10,... | collective-permute-start | bytes 995336 | tf_op jit(solution)/shard_map/ppermute | solution.py:1458
  149.4 35.7 %collective-permute-start.25 = (bf16[216,768]{1,0:T(8,128)(2,1)S(1)}, bf16[216,768]{1,0:T(8,128)(2,1)S(1)}, u32[]{:S(2)}, u32[]{:S(2)}) collective-permute-start(bf16[216,768]{1,0:T(8,128)(2,1)S(1)} %get-tuple-element.234), channel_id=1, source_target_pairs={{0,4},{1,5},{2,6},{3,7},{4,0},{5,1},{6,2},{7,3},{8,12},{9,13},{10,... | collective-permute-start | bytes 995336 | tf_op jit(solution)/shard_map/ppermute | solution.py:1458
  151.3 33.8 %collective-permute-start.26 = (bf16[216,768]{1,0:T(8,128)(2,1)S(1)}, bf16[216,768]{1,0:T(8,128)(2,1)S(1)}, u32[]{:S(2)}, u32[]{:S(2)}) collective-permute-start(bf16[216,768]{1,0:T(8,128)(2,1)S(1)} %get-tuple-element.235), channel_id=1, source_target_pairs={{0,6},{1,7},{2,0},{3,1},{4,2},{5,3},{6,4},{7,5},{8,14},{9,15},{10,... | collective-permute-start | bytes 995336 | tf_op jit(solution)/shard_map/ppermute | solution.py:1458
  154.8 5.2 %collective-permute-start.28 = (bf16[2,2,24,768]{3,2,1,0:T(8,128)(2,1)S(1)}, bf16[2,2,24,768]{3,2,1,0:T(8,128)(2,1)S(1)}, u32[]{:S(2)}, u32[]{:S(2)}) collective-permute-start(bf16[2,2,24,768]{3,2,1,0:T(8,128)(2,1)S(1)} %get-tuple-element.240), channel_id=1, source_target_pairs={{0,8},{8,0},{16,24},{24,16},{1,9},{9,1},{17,25},{25,17},{2,10},{10... | collective-permute-start | bytes 442376 | tf_op jit(solution)/shard_map/ppermute | solution.py:1466
  156.2 5.1 %collective-permute-start.29 = (bf16[2,2,24,768]{3,2,1,0:T(8,128)(2,1)S(1)}, bf16[2,2,24,768]{3,2,1,0:T(8,128)(2,1)S(1)}, u32[]{:S(2)}, u32[]{:S(2)}) collective-permute-start(bf16[2,2,24,768]{3,2,1,0:T(8,128)(2,1)S(1)} %get-tuple-element.241), channel_id=1, source_target_pairs={{0,16},{8,24},{16,0},{24,8},{1,17},{9,25},{17,1},{25,9},{2,18},{10... | collective-permute-start | bytes 442376 | tf_op jit(solution)/shard_map/ppermute | solution.py:1466
  162.0 4.4 %collective-permute-start.30 = (bf16[2,24,768]{2,1,0:T(8,128)(2,1)S(1)}, bf16[2,24,768]{2,1,0:T(8,128)(2,1)S(1)}, u32[]{:S(2)}, u32[]{:S(2)}) collective-permute-start(bf16[2,24,768]{2,1,0:T(8,128)(2,1)S(1)} %get-tuple-element.243), channel_id=1, source_target_pairs={{0,16},{8,24},{16,0},{24,8},{1,17},{9,25},{17,1},{25,9},{2,18},{10... | collective-permute-start | bytes 221192 | tf_op jit(solution)/shard_map/ppermute | solution.py:1466
  169.0 7.0 %collective-permute-start.32 = (bf16[24,768]{1,0:T(8,128)(2,1)S(1)}, bf16[24,768]{1,0:T(8,128)(2,1)S(1)}, u32[]{:S(2)}, u32[]{:S(2)}) collective-permute-start(bf16[24,768]{1,0:T(8,128)(2,1)S(1)} %get-tuple-element.247), channel_id=1, source_target_pairs={{0,2},{1,3},{2,4},{3,5},{4,6},{5,7},{6,0},{7,1},{8,10},{9,11},{10,... | collective-permute-start | bytes 110600 | tf_op jit(solution)/shard_map/ppermute | solution.py:1458
  169.1 14.5 %collective-permute-start.33 = (bf16[24,768]{1,0:T(8,128)(2,1)S(1)}, bf16[24,768]{1,0:T(8,128)(2,1)S(1)}, u32[]{:S(2)}, u32[]{:S(2)}) collective-permute-start(bf16[24,768]{1,0:T(8,128)(2,1)S(1)} %get-tuple-element.248), channel_id=1, source_target_pairs={{0,4},{1,5},{2,6},{3,7},{4,0},{5,1},{6,2},{7,3},{8,12},{9,13},{10,... | collective-permute-start | bytes 110600 | tf_op jit(solution)/shard_map/ppermute | solution.py:1458
  176.1 9.1 %collective-permute-start.34 = (bf16[24,768]{1,0:T(8,128)(2,1)S(1)}, bf16[24,768]{1,0:T(8,128)(2,1)S(1)}, u32[]{:S(2)}, u32[]{:S(2)}) collective-permute-start(bf16[24,768]{1,0:T(8,128)(2,1)S(1)} %get-tuple-element.249), channel_id=1, source_target_pairs={{0,6},{1,7},{2,0},{3,1},{4,2},{5,3},{6,4},{7,5},{8,14},{9,15},{10,... | collective-permute-start | bytes 110600 | tf_op jit(solution)/shard_map/ppermute | solution.py:1458
  (30 other events, 371.3 us)

commit v6 on v5

--- a/solution.py
+++ b/solution.py
@@ -611,9 +611,56 @@
     )
 
 
+def column_choice(chip, heads, size, lanes, width, transposed):
+    shape, axis = ((lanes, width), 0) if transposed else ((width, lanes), 1)
+    lane = lax.broadcasted_iota(jnp.int32, shape, axis)
+    feature = lax.broadcasted_iota(jnp.int32, shape, 1 - axis)
+    parts = []
+    for head in range(heads):
+        here = (feature == lane + (chip * heads + head) * size) & (lane < size)
+        parts.append(jnp.where(here, 1.0, 0.0).astype(jnp.bfloat16))
+    return jnp.concatenate(parts, axis=axis)
+
+
+def choose_kernel(heads, size, scalars, wq_ref, wk_ref, wv_ref, *refs):
+    query_rows, key_columns, value_rows, key_rows, value_columns, narrow_rows = refs
+    width, chip = wq_ref.shape[0], scalars[0]
+    tall = column_choice(chip, heads, size, 2 * size, width, True)
+    flat = column_choice(chip, heads, size, 2 * size, width, False)
+    narrow = column_choice(chip, heads, size, size, width, True)
+    query_rows[...] = sent(nt_dot(tall, wq_ref[...]))
+    key_columns[...] = sent(nn_dot(wk_ref[...], flat))
+    value_columns[...] = sent(nn_dot(wv_ref[...], flat))
+    for target, weight in ((value_rows, wv_ref), (key_rows, wk_ref), (narrow_rows, wq_ref)):
+        target[...] = sent(nt_dot(narrow, weight[...]))
+
+
+def choose(scalars, w_query, w_key, w_value, heads, size):
+    width = w_query.shape[0]
+    shapes = [
+        (2 * heads * size, width),
+        (width, 2 * heads * size),
+        (heads * size, width),
+        (heads * size, width),
+        (width, 2 * heads * size),
+        (heads * size, width),
+    ]
+    return call_whole(
+        partial(choose_kernel, heads, size),
+        [jax.ShapeDtypeStruct(shape, jnp.bfloat16) for shape in shapes],
+        "choose",
+        scalars,
+        w_query,
+        w_key,
+        w_value,
+        limit=24,
+    )
+
+
 def project_kernel(blocks, own, heads, scale, meta, *refs):
     normed = refs[:blocks]
-    wq_ref, wk_ref, wv_ref, q_ref, k_ref, vt_ref = refs[blocks:]
+    wq_ref, wk_ref, wv_ref = refs[blocks : blocks + 3]
+    q_ref, k_ref, vt_ref = refs[-3:]
     length = normed[0].shape[0]
     lanes = wk_ref.shape[1] // heads
     size = lanes // 2
@@ -640,24 +687,35 @@
                 q_ref[wide_rows, span] = (queries[wide_rows] + extra).astype(jnp.bfloat16)
 
 
-def project(meta, normed, wq, wk, wv, own, heads, scale):
+def project(meta, normed, wq, wk, wv, own, heads, scale, chips, filled=None):
     blocks, length = len(normed), normed[0].shape[0]
-    wide, share = wk.shape[1], wv.shape[0]
-    return call_whole(
+    wide_columns, share = wk.shape[1], wv.shape[0]
+    last = 0 if filled is None else 2 * chips // blocks - 1
+    last_own = 0 if filled is None else chips // own - 1
+    aliases = {} if filled is None else {blocks + 4 + index: index for index in range(3)}
+    return pl.pallas_call(
         partial(project_kernel, blocks, own, heads, scale),
-        [
-            jax.ShapeDtypeStruct((wide, own * length), jnp.bfloat16),
-            jax.ShapeDtypeStruct((blocks * length, wide), jnp.bfloat16),
-            jax.ShapeDtypeStruct((share, blocks * length), jnp.bfloat16),
+        grid_spec=pltpu.PrefetchScalarGridSpec(
+            num_scalar_prefetch=1,
+            grid=(1,),
+            in_specs=[whole(array.shape) for array in (*normed, wq, wk, wv)]
+            + [pl.BlockSpec(memory_space=pl.ANY)] * (0 if filled is None else 3),
+            out_specs=[
+                pl.BlockSpec((wide_columns, own * length), lambda i, meta: (0, last_own)),
+                pl.BlockSpec((blocks * length, wide_columns), lambda i, meta: (last, 0)),
+                pl.BlockSpec((share, blocks * length), lambda i, meta: (0, last)),
+            ],
+        ),
+        out_shape=[
+            jax.ShapeDtypeStruct((wide_columns, chips * length), jnp.bfloat16),
+            jax.ShapeDtypeStruct((2 * chips * length, wide_columns), jnp.bfloat16),
+            jax.ShapeDtypeStruct((share, 2 * chips * length), jnp.bfloat16),
         ],
-        "project",
-        meta,
-        *normed,
-        wq,
-        wk,
-        wv,
-        limit=20,
-    )
+        input_output_aliases=aliases,
+        compiler_params=pltpu.CompilerParams(vmem_limit_bytes=16 << 20),
+        cost_estimate=NO_COST,
+        name="project",
+    )(meta, *normed, wq, wk, wv, *(filled or ()))
 
 
 def project_back_kernel(blocks, unused, *refs):
@@ -847,9 +905,15 @@
 
     @pl.when(step == steps - 1)
     def _():
-        half = mine_ref.shape[1]
-        mine_ref[...] = pair_ref[:, :half]
-        other_ref[...] = pair_ref[:, half:].astype(jnp.bfloat16)
+        for index in range(steps):
+            late = index == steps - 1
+            mine = 2 * index if late else index
+            other = 2 * index + 1 if late else steps - 1 + index
+            span = slice(index * block, (index + 1) * block)
+            mine_ref[:, span] = pair_ref[:, mine * block : (mine + 1) * block]
+            other_ref[:, span] = pair_ref[:, other * block : (other + 1) * block].astype(
+                jnp.bfloat16
+            )
 
 
 def whole(shape):
@@ -957,10 +1021,11 @@
     )
 
 
-def head_grads_kernel(chips, per, unused, *refs):
+def head_grads_kernel(chips, per, scalars, *refs):
     normed, grads = refs[:chips], refs[chips : 2 * chips]
     wq_ref, wk_ref, wv_ref, gain_ref, inner_ref, feed_ref, hidden_ref = refs[2 * chips : 2 * chips + 7]
-    perm_ref, row_ref, lane_ref, keep_ref, send_ref = refs[2 * chips + 7 :]
+    perm_ref, keep_ref, send_ref = refs[2 * chips + 7 :]
+    first_core = scalars[1] == 0
     share, model_width = wq_ref.shape
     own = nn_dot(grads[0][...], normed[0][...])
     for step in range(1, chips):
@@ -969,27 +1034,31 @@
     for index, weight in enumerate((wq_ref, wk_ref, wv_ref)):
         part = own[index * share : (index + 1) * share] * weight[...].astype(jnp.float32)
         attend = attend + jnp.sum(part, axis=0, keepdims=True)
-    gains = jnp.concatenate(
-        [attend / gain_ref[...], inner_ref[...], feed_ref[...], hidden_ref[...]], axis=1
-    )
-    gains = (row_ref[...].astype(jnp.float32) * gains).astype(jnp.bfloat16)
-    gains = nn_dot(gains, lane_ref[...]).astype(jnp.bfloat16)
+    gains = [attend / gain_ref[...], inner_ref[...], feed_ref[...], hidden_ref[...]]
     own = nt_dot(perm_ref[...], own.astype(jnp.bfloat16))
     chunks, _, width = keep_ref.shape
     columns = own.shape[1]
-    gain_rows = gains.shape[0] // (2 * chunks)
-    for which, target in enumerate((keep_ref, send_ref)):
+    part = sum(row.shape[1] for row in gains) // (2 * chunks)
+    lines = -(-part // 128)
+    gains = jnp.concatenate(gains + [jnp.zeros((1, 128), jnp.float32)], axis=1)
+
+    def device_gains(device):
+        starts = [device * part + 128 * line for line in range(lines)]
+        rows = [gains[:, start : start + 128] for start in starts]
+        return jnp.concatenate(rows, axis=0).astype(jnp.bfloat16)
+
+    for target in (keep_ref, send_ref):
         target[:, :, columns:] = jnp.zeros((chunks, per, width - columns), jnp.bfloat16)
-        for chunk in range(chunks):
-            place = which * chunks + chunk
-            rows = slice(place * per, (place + 1) * per)
-            target[chunk, :, :columns] = own[rows].astype(jnp.bfloat16)
-            target[chunk, :gain_rows, width - 128 :] = gains[
-                place * gain_rows : (place + 1) * gain_rows
-            ]
-
-
-def head_grads(scalars, normed, grads, weights, gain, late_gains, perm, where_row, where_lane, per):
+    for chunk in range(chunks):
+        even, odd = device_gains(2 * chunk), device_gains(2 * chunk + 1)
+        keep_ref[chunk, :lines, width - 128 :] = jnp.where(first_core, even, odd)
+        send_ref[chunk, :lines, width - 128 :] = jnp.where(first_core, odd, even)
+        for which, target in enumerate((keep_ref, send_ref)):
+            first = (which * chunks + chunk) * per
+            target[chunk, :, :columns] = own[first : first + per].astype(jnp.bfloat16)
+
+
+def head_grads(scalars, normed, grads, weights, gain, late_gains, perm, per):
     width = perm.shape[0]
     out = jax.ShapeDtypeStruct((width // (2 * per), per, width), jnp.bfloat16)
     return call_whole(
@@ -1003,8 +1072,6 @@
         gain,
         *late_gains,
         perm,
-        where_row,
-        where_lane,
         limit=24,
     )
 
@@ -1624,16 +1691,12 @@
     )
 
 
-def gathered(rows, chips, chip):
-    if chips != 4:
-        return [rows] + [chip_shift(rows, step) for step in range(1, chips)]
+def gathered(rows):
     behind, ahead = chip_shift(rows, 1), chip_shift(rows, -1)
     up = [(2 * i + core, 2 * i + 2 + core) for i in (1, 2) for core in (0, 1)]
     down = [(2 * i + core, 2 * i - 2 + core) for i in (1, 2) for core in (0, 1)]
-    across = jnp.where(
-        chip < 2, lax.ppermute(ahead, "seq", down), lax.ppermute(behind, "seq", up)
-    )
-    return [rows, behind, across, ahead]
+    across = (lax.ppermute(ahead, "seq", down), lax.ppermute(behind, "seq", up))
+    return behind, ahead, across
 
 
 def fast_local(
@@ -1676,11 +1739,16 @@
         tokens,
         gain_attend[None, :],
     )[0]
-    own = gathered(normed_b, chips, chip)
-
-    chip_ids = (chip - jnp.arange(chips, dtype=jnp.int32)) % chips
+    behind, ahead, across = gathered(normed_b)
+
+    order = [step for step in range(chips) if step != chips // 2] + [chips // 2]
+    slots = [order.index(step) for step in range(chips)]
+    chip_ids = (chip - jnp.asarray(order, jnp.int32)) % chips
     query_starts = block * (2 * chip_ids + core)
-    key_starts = jnp.concatenate([query_starts, block * (2 * chip_ids + 1 - core)])
+    other_starts = block * (2 * chip_ids + 1 - core)
+    key_starts = jnp.concatenate(
+        [query_starts[:-1], other_starts[:-1], query_starts[-1:], other_starts[-1:]]
+    )
     in_block = jnp.arange(block, dtype=jnp.int32)[None, :]
     query_places = (query_starts[:, None] + in_block).reshape(-1)
     doc_line = jnp.max(jnp.where(bounds[:, None] <= query_places[None, :], bounds[:, None], 0), axis=0)
@@ -1690,27 +1758,8 @@
     doc_line = doc_line[None, :]
 
     feature = jnp.arange(model_width, dtype=jnp.int32)
-    wide_lane = jnp.arange(spread, dtype=jnp.int32)
-    source = chip * share + wide_lane // lanes * size + wide_lane % lanes
-    pick_wide = ((feature[:, None] == source[None, :]) & (wide_lane % lanes < size)[None, :]).astype(
-        jnp.bfloat16
-    )
-    narrow = chip * share + jnp.arange(share, dtype=jnp.int32)
-    pick_narrow = (feature[:, None] == narrow[None, :]).astype(jnp.bfloat16)
-
-    def picked(weight, choice):
-        return sent(nn_dot(weight, choice))
-
-    def picked_rows(weight, choice):
-        return sent(
-            lax.dot_general(
-                choice, weight, (((0,), (1,)), ((), ())), preferred_element_type=jnp.float32
-            )
-        )
-
     per = model_width // parts
-    order = jnp.arange(model_width, dtype=jnp.int32)
-    chunk, inside = order // per, order % per
+    chunk, inside = feature // per, feature % per
     chunks = parts // 2
     parity = jnp.where(chunk < chunks, core, 1 - core)
     wanted = (2 * (chunk % chunks) + parity) * per + inside
@@ -1718,57 +1767,42 @@
 
     gains_share = (3 * model_width + hidden) // parts
     gains_rows = -(-gains_share // 128)
-    line = jnp.arange(parts * gains_rows, dtype=jnp.int32)
-    half_lines = parts // 2 * gains_rows
-    line_parity = jnp.where(line < half_lines, core, 1 - core)
-    owner = 2 * (line % half_lines // gains_rows) + line_parity
-    first_gain = owner * gains_share + 128 * (line % gains_rows)
-    end_gain = jnp.minimum(first_gain + 128, (owner + 1) * gains_share)
-    gain_index = jnp.arange(gains_share * parts, dtype=jnp.int32)
-    where_row = (
-        (gain_index[None, :] >= first_gain[:, None]) & (gain_index[None, :] < end_gain[:, None])
-    ).astype(jnp.bfloat16)
-    where_lane = (
-        (gain_index % gains_share % 128)[:, None] == jnp.arange(128, dtype=jnp.int32)[None, :]
-    ).astype(jnp.bfloat16)
-    early = (
-        jnp.concatenate([query_starts, 2 * block * chip_ids + block * (1 - core), heads * chip[None]]),
+    first_head = heads * chip[None]
+    small = (
+        jnp.concatenate([query_starts[:-1], other_starts[:-1], first_head]),
+        jnp.concatenate([query_starts[-1:], other_starts[-1:], first_head]),
         meta,
         doc_line,
-        perm,
-        picked_rows(w_query, pick_wide),
-        picked(w_key, pick_wide),
-        picked_rows(w_value, pick_narrow),
-        picked_rows(w_key, pick_narrow),
-        picked(w_value, pick_wide),
-        picked_rows(w_query, pick_narrow),
         gain_attend[None, :],
         gain_inner[None, :],
         gain_feed[None, :],
         gain_hidden[None, :],
         place,
-        where_row,
-        where_lane,
-    )
-    own[1], early = lax.optimization_barrier((own[1], early))
-    starts, meta, doc_line, perm, wq_wide, wk_wide, wv_rows, wk_rows, wv_wide, wq_rows = early[:10]
-    gain_first, gain_inner, gain_feed, gain_hidden, place = early[10:15]
-    where_row, where_lane = early[15:]
-    sibling = [seq_swap(rows, 1) for rows in own]
+        perm,
+    )
+    small = lax.optimization_barrier(small)
+    starts, late_starts, meta, doc_line, gain_first, gain_inner, gain_feed, gain_hidden = small[:8]
+    place, perm = small[8:]
+    early = choose(place, w_query, w_key, w_value, heads, size)
+    behind, early = lax.optimization_barrier((behind, early))
+    wq_wide, wk_wide, wv_rows, wk_rows, wv_wide, wq_rows = early
+    own = [normed_b, behind, ahead]
+    early_blocks = own + [seq_swap(rows, 1) for rows in own]
+    filled = project(
+        starts, early_blocks, wq_wide, wk_wide, wv_rows, chips - 1, heads, scale, chips
+    )
+    filled, across = lax.optimization_barrier((filled, across))
+    own.append(across[0] + across[1])
+    late_blocks = [own[-1], seq_swap(own[-1], 1)]
     q_ext, k_ext, v_t = project(
-        starts,
-        own + sibling,
-        wq_wide,
-        wk_wide,
-        wv_rows,
-        chips,
-        heads,
-        scale,
+        late_starts, late_blocks, wq_wide, wk_wide, wv_rows, 1, heads, scale, chips, filled
     )
     mixed, lse, *mixed_b = attend(meta, doc_line, q_ext, k_ext, v_t, heads, block)
     mixed_b, wk_rows = lax.optimization_barrier((mixed_b, wk_rows))
-    k_t, v_ext = project_back(place, own + sibling, wk_rows, wv_wide)
-    back = [mixed_b[0]] + [chip_shift(mixed_b[step], -step) for step in range(1, chips)]
+    k_t, v_ext = project_back(place, early_blocks + late_blocks, wk_rows, wv_wide)
+    back = [mixed_b[slots[0]]] + [
+        chip_shift(mixed_b[slots[step]], -step) for step in range(1, chips)
+    ]
     back, k_t, v_ext = lax.optimization_barrier((back, k_t, v_ext))
     outs = middle(
         place, back, tokens, cotangent, w_out, w_up, w_down, (gain_inner, gain_feed, gain_hidden)
@@ -1791,10 +1825,10 @@
     low, high = outgoing(place, sums)
     arrived_sums = [row_swap(low, 1), row_swap(high, 2)]
     dq, pair, other = attend_back(
-        meta, doc_line, q_ext, go, mixed, lse, k_ext, k_t, v_ext, heads, block, scale
+        meta, doc_line, q_ext, [go[step] for step in order], mixed, lse, k_ext, k_t, v_ext, heads, block, scale
     )
     grads = join_parts(place, dq, pair, seq_swap(other, 1), chips)
-    home = [grads[0]] + [chip_shift(grads[step], -step) for step in range(1, chips)]
+    home = [grads[slots[0]]] + [chip_shift(grads[slots[step]], -step) for step in range(1, chips)]
     grads, sums = lax.optimization_barrier((grads, sums))
     kept = outgoing(place, sums, True)
     mine_grad, send_grad = head_grads(
@@ -1805,8 +1839,6 @@
         gain_first,
         (dinner, dfeed, dhidden),
         perm,
-        where_row,
-        where_lane,
         per,
     )
     arrived_sums, kept, mine_grad, send_grad = lax.optimization_barrier(
@@ -1850,7 +1882,7 @@
     seq_devices, row_devices = lax.axis_size("seq"), lax.axis_size("row")
     block = arrays[0].shape[0]
     one_segment = block * seq_devices <= SEGMENT and block % 2 ** (PATTERNS - 1) == 0
-    if one_segment and seq_devices in (2, 4, 8) and row_devices == 4:
+    if one_segment and seq_devices == 8 and row_devices == 4:
         return fast_local(*arrays)
     return ring_local(*arrays)
 

time: 187 us -> 183 us (0.979)
  matrix products: 10.6 us -> 0 us
  local copies, waits for them, and re-layouts: 4.54 us -> 10.3 us
  waiting for transfers between devices: 54.1 us -> 59.4 us
  starting transfers between devices: 40.8 us -> 36.7 us
  other arithmetic: 6.09 us -> 3.57 us
    dot_general x6 -> x0, matrix products: 10.6 us -> none  [the longest x4 5.39 us: picked_rows(): lax.dot_general(choice, weight, (((0,), (1,)), ((), ())), preferred_eleme...]
    pallas_call x0 -> x2, Pallas kernels: none -> 4.9 us  [project(): pl.pallas_call(partial(project_kernel, blocks, own, heads, scale), grid_s...]
    pallas_call x15, Pallas kernels: 26.6 us -> 22.8 us  [call_whole(): pl.pallas_call(kernel, grid_spec=pltpu.PrefetchScalarGridSpec(num_scalar_...]
    convert_element_type x2 -> x0, other arithmetic: 3.54 us -> none  [the longest x1 2.42 us: fast_local(): where_lane = ((gain_index % gains_share % 128)[:, None] == jnp.arange(128...]
    ppermute x8, starting transfers between devices: 9.15 us -> 7.11 us  [row_swap(): lax.ppermute(value, 'row', [(i, i ^ bit) for i in range(lax.axis_size('ro...]
    unnamed x55 -> x41, local copies, waits for them, and re-layouts: 3.01 us -> 4.8 us
  transfers between devices with their start and end apart: 35 -> 35, of which waited for: 19 -> 19; matrix products, arithmetic and copies ran while one was open for 9% -> 4% of each run, Pallas kernels for 18% -> 21%
where the time goes in v6:
time: 183 us
  Pallas kernels  71.7 us (39%)
  waiting for transfers between devices  59.4 us (32%)
  starting transfers between devices  36.7 us (20%)
  local copies, waits for them, and re-layouts  10.3 us (6%)
  other arithmetic  3.57 us (2%)
    ppermute x17, waiting for transfers between devices, chip_shift(): lax.ppermute(value, 'seq', [(i, (i + 2 * steps) % count) for i in range(c...  32.8 us
    ppermute x17, starting transfers between devices, chip_shift(): lax.ppermute(value, 'seq', [(i, (i + 2 * steps) % count) for i in range(c...  26.3 us
    pallas_call x15, Pallas kernels, call_whole(): pl.pallas_call(kernel, grid_spec=pltpu.PrefetchScalarGridSpec(num_scalar_...  22.8 us
    pallas_call x1, Pallas kernels, middle(): pl.pallas_call(partial(middle_kernel, chips, tiles), grid_spec=pltpu.Pref...  15.5 us
    ppermute x8, waiting for transfers between devices, row_swap(): lax.ppermute(value, 'row', [(i, i ^ bit) for i in range(lax.axis_size('ro...  13.2 us
    pallas_call x1, Pallas kernels, attend_back(): pl.pallas_call(partial(attend_back_kernel, heads, block, key_blocks, scal...  10.8 us
    pallas_call x1, Pallas kernels, attend(): pl.pallas_call(partial(attend_kernel, heads, block, key_blocks), grid_spe...  8.79 us
    ppermute x2, waiting for transfers between devices, gathered(): across = (lax.ppermute(ahead, 'seq', down), lax.ppermute(behind, 'seq', up))  7.95 us
  transfers between devices with their start and end apart: 35, of which 19 were waited for; matrix products, arithmetic and copies ran while one was open for 4% of the time, Pallas kernels for 21%

profile of v6, /device:TPU:0, one launch (start us, length us, event | category | flops | bytes accessed | tf_op | source)
XLA Modules:
  0.0 182.8 jit_solution(17355100018367725707)
XLA Ops:
  2.7 3.1 %collective-permute-start = (bf16[256,768]{1,0:T(8,128)(2,1)S(1)}, bf16[256,768]{1,0:T(8,128)(2,1)S(1)}, u32[]{:S(2)}, u32[]{:S(2)}) collective-permute-start(bf16[256,768]{1,0:T(8,128)(2,1)S(1)} %norm.1.refs_0_), channel_id=1, source_target_pairs={{0,2},{1,3},{2,4},{3,5},{4,6},{5,7},{6,0},{7,1},{8,10},{9,11},{10,... | collective-permute-start | bytes 1179656 | tf_op jit(solution)/shard_map/ppermute | solution.py:1525
  5.8 2.1 %collective-permute-start.1 = (bf16[256,768]{1,0:T(8,128)(2,1)S(1)}, bf16[256,768]{1,0:T(8,128)(2,1)S(1)}, u32[]{:S(2)}, u32[]{:S(2)}) collective-permute-start(bf16[256,768]{1,0:T(8,128)(2,1)S(1)} %norm.1.refs_0_), channel_id=1, source_target_pairs={{0,6},{1,7},{2,0},{3,1},{4,2},{5,3},{6,4},{7,5},{8,14},{9,15},{10,... | collective-permute-start | bytes 1179656 | tf_op jit(solution)/shard_map/ppermute | solution.py:1525
  18.1 3.5 %choose.1 = (bf16[384,768]{1,0:T(8,128)(2,1)S(1)}, bf16[768,384]{1,0:T(8,128)(2,1)S(1)}, bf16[192,768]{1,0:T(8,128)(2,1)S(1)}, bf16[192,768]{1,0:T(8,128)(2,1)S(...) custom-call(s32[4]{0:T(128)S(1)} %pad_add_fusion.2.scalars.unused.position, bf16[768,768]{1,0:T(8,128)(2,1)S(1)} %copy-done, ...), custom_call_target="tpu_custom_call" | custom-call | flops 1000 | bytes 1000 | tf_op jit(solution)/shard_map/choose/pallas_call | solution.py:574
  22.2 2.6 %collective-permute-done.1.refs_2_ = bf16[256,768]{1,0:T(8,128)(2,1)S(1)} collective-permute-done((bf16[256,768]{1,0:T(8,128)(2,1)S(1)}, bf16[256,768]{1,0:T(8,128)(2,1)S(1)}, u32[]{:S(2)}, u32[]{:S(2)}) %collective-permute-start.1) | collective-permute-done | bytes 393248 | tf_op jit(solution)/shard_map/ppermute | solution.py:1525
  26.9 3.4 %project.2 = (bf16[384,1024]{1,0:T(8,128)(2,1)S(1)}, bf16[2048,384]{1,0:T(8,128)(2,1)S(1)}, bf16[192,2048]{1,0:T(8,128)(2,1)S(1)}) custom-call(s32[7]{0:T(128)S(1)} %pad_add_fusion.meta, bf16[256,768]{1,0:T(8,128)(2,1)S(1)} %norm.1.refs_0_, bf16[256,768]{1,0:T(8,128)(2,1)S(1)} %collective-permute-done.refs_1_, ...), custom_call_target="tpu_custom_call" | custom-call | flops 1000 | bytes 1000 | tf_op jit(solution)/shard_map/project/pallas_call | solution.py:696
  30.3 7.9 %collective-permute-done.5 = bf16[256,768]{1,0:T(8,128)(2,1)S(1)} collective-permute-done((bf16[256,768]{1,0:T(8,128)(2,1)S(1)}, bf16[256,768]{1,0:T(8,128)(2,1)S(1)}, u32[]{:S(2)}, u32[]{:S(2)}) %collective-permute-start.5) | collective-permute-done | bytes 393248 | tf_op jit(solution)/shard_map/ppermute | solution.py:1698
  41.6 8.8 %attend.1 = (f32[192,1024]{1,0:T(8,128)S(1)}, f32[3,1,1024]{2,1,0:T(1,128)S(1)}, bf16[192,256]{1,0:T(8,128)(2,1)S(1)}, bf16[192,256]{1,0:T(8,128)(2,1)S(1)}, bf1...) custom-call(s32[20]{0:T(128)S(1)} %concatenate.11.meta, s32[1,1024]{1,0:T(1,128)S(1)} %bitcast.55, ...), custom_call_target="tpu_custom_call" | custom-call | flops 1000 | bytes 1000 | tf_op jit(solution)/shard_map/attend/pallas_call | solution.py:927
  50.5 2.4 %collective-permute-start.10 = (bf16[192,256]{1,0:T(8,128)(2,1)S(1)}, bf16[192,256]{1,0:T(8,128)(2,1)S(1)}, u32[]{:S(2)}, u32[]{:S(2)}) collective-permute-start(bf16[192,256]{1,0:T(8,128)(2,1)S(1)} %get-tuple-element.180), channel_id=1, source_target_pairs={{0,2},{1,3},{2,4},{3,5},{4,6},{5,7},{6,0},{7,1},{8,10},{9,11},{10,... | collective-permute-start | bytes 294920 | tf_op jit(solution)/shard_map/ppermute | solution.py:1525
  52.9 1.9 %collective-permute-start.8 = (bf16[192,256]{1,0:T(8,128)(2,1)S(1)}, bf16[192,256]{1,0:T(8,128)(2,1)S(1)}, u32[]{:S(2)}, u32[]{:S(2)}) collective-permute-start(bf16[192,256]{1,0:T(8,128)(2,1)S(1)} %get-tuple-element.178), channel_id=1, source_target_pairs={{0,6},{1,7},{2,0},{3,1},{4,2},{5,3},{6,4},{7,5},{8,14},{9,15},{10,... | collective-permute-start | bytes 294920 | tf_op jit(solution)/shard_map/ppermute | solution.py:1525
  54.8 2.0 %collective-permute-start.9 = (bf16[192,256]{1,0:T(8,128)(2,1)S(1)}, bf16[192,256]{1,0:T(8,128)(2,1)S(1)}, u32[]{:S(2)}, u32[]{:S(2)}) collective-permute-start(bf16[192,256]{1,0:T(8,128)(2,1)S(1)} %get-tuple-element.179), channel_id=1, source_target_pairs={{0,4},{1,5},{2,6},{3,7},{4,0},{5,1},{6,2},{7,3},{8,12},{9,13},{10,... | collective-permute-start | bytes 294920 | tf_op jit(solution)/shard_map/ppermute | solution.py:1525
  56.8 3.2 %project_back.1 = (bf16[192,2048]{1,0:T(8,128)(2,1)S(1)}, bf16[2048,384]{1,0:T(8,128)(2,1)S(1)}) custom-call(s32[4]{0:T(128)S(1)} %pad_add_fusion.2.scalars.unused.position, bf16[256,768]{1,0:T(8,128)(2,1)S(1)} %norm.1.refs_0_, bf16[256,768]{1,0:T(8,128)(2,1)S(1)} %collective-permute-done.refs_1_, bf16[256,768]{1,0:T(8,128)(2,1)S(1)} %collective-permute-done.1.refs_2_, ...), custom_call_target="tpu_custom_call" | custom-call | flops 1000 | bytes 1000 | tf_op jit(solution)/shard_map/project_back/pallas_call | solution.py:574
  61.2 2.2 %collective-permute-done.9.refs_2_ = bf16[192,256]{1,0:T(8,128)(2,1)S(1)} collective-permute-done((bf16[192,256]{1,0:T(8,128)(2,1)S(1)}, bf16[192,256]{1,0:T(8,128)(2,1)S(1)}, u32[]{:S(2)}, u32[]{:S(2)}) %collective-permute-start.9) | collective-permute-done | bytes 98336 | tf_op jit(solution)/shard_map/ppermute | solution.py:1525
  63.6 15.5 %middle.1 = (bf16[256,768]{1,0:T(8,128)(2,1)}, f32[256,768]{1,0:T(8,128)S(1)}, bf16[256,768]{1,0:T(8,128)(2,1)S(1)}, bf16[192,256]{1,0:T(8,128)(2,1)S(1)}, bf16[...) custom-call(s32[4]{0:T(128)S(1)} %pad_add_fusion.2.scalars.unused.po, ...), custom_call_target="tpu_custom_call" | custom-call | flops 1000 | bytes 1000 | tf_op jit(solution)/shard_map/middle/pallas_call | solution.py:1333
  79.1 4.9 %up_out_grad.1 = (bf16[16,120,768]{2,1,0:T(8,128)(2,1)S(1)}, bf16[16,120,768]{2,1,0:T(8,128)(2,1)S(1)}) custom-call(s32[4]{0:T(128)S(1)} %pad_add_fusion.2.scalars.unused.position, bf16[256,768]{1,0:T(8,128)(2,1)S(1)} %get-tuple-element.201.h2_ref, bf16[256,3072]{1,0:T(8,128)(2,1)S(1)} %get-tuple-element.202.pre_ref, ...), custom_call_target="tpu_custom_call" | custom-call | flops 1000 | bytes 1000 | tf_op jit(solution)/shard_map/up_out_grad/pallas_call | solution.py:1455
  84.1 2.8 %down_grad.1 = (bf16[16,96,768]{2,1,0:T(8,128)(2,1)S(1)}, bf16[16,96,768]{2,1,0:T(8,128)(2,1)S(1)}) custom-call(s32[4]{0:T(128)S(1)} %pad_add_fusion.2.scalars.unused.position, bf16[256,3072]{1,0:T(8,128)(2,1)S(1)} %get-tuple-element.219.bent_ref, bf16[256,768]{1,0:T(8,128)(2,1)S(1)} %copy-done.7), custom_call_target="tpu_custom_call" | custom-call | flops 1000 | bytes 1000 | tf_op jit(solution)/shard_map/down_grad/pallas_call | solution.py:1407
  87.5 3.8 %collective-permute-start.12 = (bf16[192,256]{1,0:T(8,128)(2,1)S(1)}, bf16[192,256]{1,0:T(8,128)(2,1)S(1)}, u32[]{:S(2)}, u32[]{:S(2)}) collective-permute-start(bf16[192,256]{1,0:T(8,128)(2,1)S(1)} %get-tuple-element.210), channel_id=1, source_target_pairs={{0,6},{1,7},{2,0},{3,1},{4,2},{5,3},{6,4},{7,5},{8,14},{9,15},{10,... | collective-permute-start | bytes 294920 | tf_op jit(solution)/shard_map/ppermute | solution.py:1525
  95.4 4.5 %collective-permute-done.13.refs_3_ = bf16[192,256]{1,0:T(8,128)(2,1)S(1)} collective-permute-done((bf16[192,256]{1,0:T(8,128)(2,1)S(1)}, bf16[192,256]{1,0:T(8,128)(2,1)S(1)}, u32[]{:S(2)}, u32[]{:S(2)}) %collective-permute-start.13) | collective-permute-done | bytes 98336 | tf_op jit(solution)/shard_map/ppermute | solution.py:1525
  99.9 10.8 %attend_back.1 = (bf16[192,1024]{1,0:T(8,128)(2,1)S(1)}, f32[384,1024]{1,0:T(8,128)S(1)}, bf16[384,1024]{1,0:T(8,128)(2,1)S(1)}) custom-call(s32[20]{0:T(128)S(1)} %concatenate.11.meta, s32[1,1024]{1,0:T(1,128)S(1)} %bitcast.56, bf16[384,1024]{1,0:T(8,128)(2,1)S(1)} %get-tuple-element.169.q_ref, f32[192,1024]{1,0:T(8,128)S(1)} %copy-done.13, ...), custom_call_target="tpu_custom_call" | custom-call | flops 49999998976 | bytes 1000 | tf_op jit(solution)/shard_map/attend_back/pallas_call | solution.py:963
  110.8 2.3 %collective-permute-done.14.other_ref = bf16[384,1024]{1,0:T(8,128)(2,1)S(1)} collective-permute-done((bf16[384,1024]{1,0:T(8,128)(2,1)S(1)}, bf16[384,1024]{1,0:T(8,128)(2,1)S(1)}, u32[]{:S(2)}, u32[]{:S(2)}) %collective-permute-start.14) | collective-permute-done | bytes 786464 | tf_op jit(solution)/shard_map/ppermute | solution.py:1529
  113.9 1.8 collective-permute-start.15
  117.5 3.1 %head_grads.1 = (bf16[16,24,768]{2,1,0:T(8,128)(2,1)S(1)}, bf16[16,24,768]{2,1,0:T(8,128)(2,1)S(1)}) custom-call(s32[4]{0:T(128)S(1)} %pad_add_fusion.2.scalars.unused.position, bf16[256,768]{1,0:T(8,128)(2,1)S(1)} %norm.1.refs_0_, bf16[256,768]{1,0:T(8,128)(2,1)S(1)} %collective-permute-done.refs_1_, bf16[256,768]{1,0:T(8,128)(2,1)S(1)} %collective-permute-done.1.refs_2_, ...), custom_call_target="tpu_custom_call" | custom-call | flops 1000 | bytes 1000 | tf_op jit(solution)/shard_map/head_grads/pallas_call | solution.py:574
  120.6 4.7 %collective-permute-done.20.refs_2_ = bf16[2,2,216,768]{3,2,1,0:T(8,128)(2,1)S(1)} collective-permute-done((bf16[2,2,216,768]{3,2,1,0:T(8,128)(2,1)S(1)}, bf16[2,2,216,768]{3,2,1,0:T(8,128)(2,1)S(1)}, u32[]{:S(2)}, u32[]{:S(2)}) %collective-permute-start.20) | collective-permute-done | bytes 1327136 | tf_op jit(solution)/shard_map/ppermute | solution.py:1533
  128.5 11.9 %collective-permute-done.16.refs_2_ = bf16[576,256]{1,0:T(8,128)(2,1)S(1)} collective-permute-done((bf16[576,256]{1,0:T(8,128)(2,1)S(1)}, bf16[576,256]{1,0:T(8,128)(2,1)S(1)}, u32[]{:S(2)}, u32[]{:S(2)}) %collective-permute-start.16) | collective-permute-done | bytes 294944 | tf_op jit(solution)/shard_map/ppermute | solution.py:1525
  144.4 3.0 %collective-permute-start.25 = (bf16[216,768]{1,0:T(8,128)(2,1)S(1)}, bf16[216,768]{1,0:T(8,128)(2,1)S(1)}, u32[]{:S(2)}, u32[]{:S(2)}) collective-permute-start(bf16[216,768]{1,0:T(8,128)(2,1)S(1)} %get-tuple-element.260), channel_id=1, source_target_pairs={{0,4},{1,5},{2,6},{3,7},{4,0},{5,1},{6,2},{7,3},{8,12},{9,13},{10,... | collective-permute-start | bytes 995336 | tf_op jit(solution)/shard_map/ppermute | solution.py:1525
  147.5 1.8 collective-permute-start.26
  152.3 3.1 %collective-permute-done.28.refs_2_ = bf16[2,2,24,768]{3,2,1,0:T(8,128)(2,1)S(1)} collective-permute-done((bf16[2,2,24,768]{3,2,1,0:T(8,128)(2,1)S(1)}, bf16[2,2,24,768]{3,2,1,0:T(8,128)(2,1)S(1)}, u32[]{:S(2)}, u32[]{:S(2)}) %collective-permute-start.28) | collective-permute-done | bytes 147488 | tf_op jit(solution)/shard_map/ppermute | solution.py:1533
  158.1 2.4 %collective-permute-done.30.refs_1_ = bf16[2,24,768]{2,1,0:T(8,128)(2,1)S(1)} collective-permute-done((bf16[2,24,768]{2,1,0:T(8,128)(2,1)S(1)}, bf16[2,24,768]{2,1,0:T(8,128)(2,1)S(1)}, u32[]{:S(2)}, u32[]{:S(2)}) %collective-permute-start.30) | collective-permute-done | bytes 73760 | tf_op jit(solution)/shard_map/ppermute | solution.py:1533
  162.4 2.4 %collective-permute-start.32 = (bf16[24,768]{1,0:T(8,128)(2,1)S(1)}, bf16[24,768]{1,0:T(8,128)(2,1)S(1)}, u32[]{:S(2)}, u32[]{:S(2)}) collective-permute-start(bf16[24,768]{1,0:T(8,128)(2,1)S(1)} %get-tuple-element.273), channel_id=1, source_target_pairs={{0,2},{1,3},{2,4},{3,5},{4,6},{5,7},{6,0},{7,1},{8,10},{9,11},{10,... | collective-permute-start | bytes 110600 | tf_op jit(solution)/shard_map/ppermute | solution.py:1525
  165.4 5.2 %collective-permute-done.32.refs_5_ = bf16[24,768]{1,0:T(8,128)(2,1)S(1)} collective-permute-done((bf16[24,768]{1,0:T(8,128)(2,1)S(1)}, bf16[24,768]{1,0:T(8,128)(2,1)S(1)}, u32[]{:S(2)}, u32[]{:S(2)}) %collective-permute-start.32) | collective-permute-done | bytes 36896 | tf_op jit(solution)/shard_map/ppermute | solution.py:1525
  171.2 3.2 %final.1 = bf16[256,768]{1,0:T(8,128)(2,1)} custom-call(s32[4]{0:T(128)S(1)} %pad_add_fusion.2.scalars.unused.position, bf16[576,256]{1,0:T(8,128)(2,1)S(1)} %get-tuple-element.245.refs_4_.refs_0_, bf16[576,256]{1,0:T(8,128)(2,1)S(1)} %collective-permute-done.15.refs_1_, bf16[576,256]{1,0:T(8,128)(2,1)S(1)} %collective-permute-done.16.refs_2_, ...), custom_call_target="tpu_custom_call" | custom-call | flops 1000 | bytes 1000 | tf_op jit(solution)/shard_map/final/pallas_call | solution.py:574
  174.4 4.3 %collective-permute-done.33.refs_6_ = bf16[24,768]{1,0:T(8,128)(2,1)S(1)} collective-permute-done((bf16[24,768]{1,0:T(8,128)(2,1)S(1)}, bf16[24,768]{1,0:T(8,128)(2,1)S(1)}, u32[]{:S(2)}, u32[]{:S(2)}) %collective-permute-start.33) | collective-permute-done | bytes 36896 | tf_op jit(solution)/shard_map/ppermute | solution.py:1525
  178.7 2.0 %collective-permute-done.34.refs_7_ = bf16[24,768]{1,0:T(8,128)(2,1)S(1)} collective-permute-done((bf16[24,768]{1,0:T(8,128)(2,1)S(1)}, bf16[24,768]{1,0:T(8,128)(2,1)S(1)}, u32[]{:S(2)}, u32[]{:S(2)}) %collective-permute-start.34) | collective-permute-done | bytes 36896 | tf_op jit(solution)/shard_map/ppermute | solution.py:1525
  (125 shorter events, 44.9 us)
Async XLA Ops:
  2.7 18.9 %collective-permute-start = (bf16[256,768]{1,0:T(8,128)(2,1)S(1)}, bf16[256,768]{1,0:T(8,128)(2,1)S(1)}, u32[]{:S(2)}, u32[]{:S(2)}) collective-permute-start(bf16[256,768]{1,0:T(8,128)(2,1)S(1)} %norm.1.refs_0_), channel_id=1, source_target_pairs={{0,2},{1,3},{2,4},{3,5},{4,6},{5,7},{6,0},{7,1},{8,10},{9,11},{10,... | collective-permute-start | bytes 1179656 | tf_op jit(solution)/shard_map/ppermute | solution.py:1525
  5.8 19.0 %collective-permute-start.1 = (bf16[256,768]{1,0:T(8,128)(2,1)S(1)}, bf16[256,768]{1,0:T(8,128)(2,1)S(1)}, u32[]{:S(2)}, u32[]{:S(2)}) collective-permute-start(bf16[256,768]{1,0:T(8,128)(2,1)S(1)} %norm.1.refs_0_), channel_id=1, source_target_pairs={{0,6},{1,7},{2,0},{3,1},{4,2},{5,3},{6,4},{7,5},{8,14},{9,15},{10,... | collective-permute-start | bytes 1179656 | tf_op jit(solution)/shard_map/ppermute | solution.py:1525
  7.9 18.9 %collective-permute-start.2 = (bf16[256,768]{1,0:T(8,128)(2,1)S(1)}, bf16[256,768]{1,0:T(8,128)(2,1)S(1)}, u32[]{:S(2)}, u32[]{:S(2)}) collective-permute-start(bf16[256,768]{1,0:T(8,128)(2,1)S(1)} %norm.1.refs_0_), channel_id=1, source_target_pairs={{0,1},{1,0},{2,3},{3,2},{4,5},{5,4},{6,7},{7,6},{8,9},{9,8},{10,11... | collective-permute-start | bytes 1179656 | tf_op jit(solution)/shard_map/ppermute | solution.py:1529
  21.6 5.2 %collective-permute-start.3 = (bf16[256,768]{1,0:T(8,128)(2,1)S(1)}, bf16[256,768]{1,0:T(8,128)(2,1)S(1)}, u32[]{:S(2)}, u32[]{:S(2)}) collective-permute-start(bf16[256,768]{1,0:T(8,128)(2,1)S(1)} %collective-permute-done.refs_1_), channel_id=1, source_target_pairs={{0,1},{1,0},{2,3},{3,2},{4,5},{5,4},{6,7},{7,6},{8,9},{9,8},{10,11... | collective-permute-start | bytes 1179656 | tf_op jit(solution)/shard_map/ppermute | solution.py:1529
  24.8 13.4 %collective-permute-start.5 = (bf16[256,768]{1,0:T(8,128)(2,1)S(1)}, bf16[256,768]{1,0:T(8,128)(2,1)S(1)}, u32[]{:S(2)}, u32[]{:S(2)}) collective-permute-start(bf16[256,768]{1,0:T(8,128)(2,1)S(1)} %collective-permute-done.1.refs_2_), channel_id=1, source_target_pairs={{2,0},{3,1},{4,2},{5,3},{10,8},{11,9},{12,10},{13,11},{18,16},{19,... | collective-permute-start | bytes 1179656 | tf_op jit(solution)/shard_map/ppermute | solution.py:1698
  26.1 12.1 %collective-permute-start.6 = (bf16[256,768]{1,0:T(8,128)(2,1)S(1)}, bf16[256,768]{1,0:T(8,128)(2,1)S(1)}, u32[]{:S(2)}, u32[]{:S(2)}) collective-permute-start(bf16[256,768]{1,0:T(8,128)(2,1)S(1)} %collective-permute-done.refs_1_), channel_id=1, source_target_pairs={{2,4},{3,5},{4,6},{5,7},{10,12},{11,13},{12,14},{13,15},{18,20},{1... | collective-permute-start | bytes 1179656 | tf_op jit(solution)/shard_map/ppermute | solution.py:1698
  50.5 10.7 %collective-permute-start.10 = (bf16[192,256]{1,0:T(8,128)(2,1)S(1)}, bf16[192,256]{1,0:T(8,128)(2,1)S(1)}, u32[]{:S(2)}, u32[]{:S(2)}) collective-permute-start(bf16[192,256]{1,0:T(8,128)(2,1)S(1)} %get-tuple-element.180), channel_id=1, source_target_pairs={{0,2},{1,3},{2,4},{3,5},{4,6},{5,7},{6,0},{7,1},{8,10},{9,11},{10,... | collective-permute-start | bytes 294920 | tf_op jit(solution)/shard_map/ppermute | solution.py:1525
  52.9 8.4 %collective-permute-start.8 = (bf16[192,256]{1,0:T(8,128)(2,1)S(1)}, bf16[192,256]{1,0:T(8,128)(2,1)S(1)}, u32[]{:S(2)}, u32[]{:S(2)}) collective-permute-start(bf16[192,256]{1,0:T(8,128)(2,1)S(1)} %get-tuple-element.178), channel_id=1, source_target_pairs={{0,6},{1,7},{2,0},{3,1},{4,2},{5,3},{6,4},{7,5},{8,14},{9,15},{10,... | collective-permute-start | bytes 294920 | tf_op jit(solution)/shard_map/ppermute | solution.py:1525
  54.8 8.7 %collective-permute-start.9 = (bf16[192,256]{1,0:T(8,128)(2,1)S(1)}, bf16[192,256]{1,0:T(8,128)(2,1)S(1)}, u32[]{:S(2)}, u32[]{:S(2)}) collective-permute-start(bf16[192,256]{1,0:T(8,128)(2,1)S(1)} %get-tuple-element.179), channel_id=1, source_target_pairs={{0,4},{1,5},{2,6},{3,7},{4,0},{5,1},{6,2},{7,3},{8,12},{9,13},{10,... | collective-permute-start | bytes 294920 | tf_op jit(solution)/shard_map/ppermute | solution.py:1525
  84.0 8.8 %collective-permute-start.19 = (bf16[16,120,768]{2,1,0:T(8,128)(2,1)S(1)}, bf16[16,120,768]{2,1,0:T(8,128)(2,1)S(1)}, u32[]{:S(2)}, u32[]{:S(2)}) collective-permute-start(bf16[16,120,768]{2,1,0:T(8,128)(2,1)S(1)} %get-tuple-element.223), channel_id=1, source_target_pairs={{0,1},{1,0},{2,3},{3,2},{4,5},{5,4},{6,7},{7,6},{8,9},{9,8},{10,11... | collective-permute-start | bytes 8847368 | tf_op jit(solution)/shard_map/ppermute | solution.py:1529
  86.9 5.9 %collective-permute-start.18 = (bf16[16,96,768]{2,1,0:T(8,128)(2,1)S(1)}, bf16[16,96,768]{2,1,0:T(8,128)(2,1)S(1)}, u32[]{:S(2)}, u32[]{:S(2)}) collective-permute-start(bf16[16,96,768]{2,1,0:T(8,128)(2,1)S(1)} %get-tuple-element.221), channel_id=1, source_target_pairs={{0,1},{1,0},{2,3},{3,2},{4,5},{5,4},{6,7},{7,6},{8,9},{9,8},{10,11... | collective-permute-start | bytes 7077896 | tf_op jit(solution)/shard_map/ppermute | solution.py:1529
  87.5 7.9 %collective-permute-start.11 = (bf16[192,256]{1,0:T(8,128)(2,1)S(1)}, bf16[192,256]{1,0:T(8,128)(2,1)S(1)}, u32[]{:S(2)}, u32[]{:S(2)}) collective-permute-start(bf16[192,256]{1,0:T(8,128)(2,1)S(1)} %get-tuple-element.209), channel_id=1, source_target_pairs={{0,2},{1,3},{2,4},{3,5},{4,6},{5,7},{6,0},{7,1},{8,10},{9,11},{10,... | collective-permute-start | bytes 294920 | tf_op jit(solution)/shard_map/ppermute | solution.py:1525
  87.5 7.9 %collective-permute-start.12 = (bf16[192,256]{1,0:T(8,128)(2,1)S(1)}, bf16[192,256]{1,0:T(8,128)(2,1)S(1)}, u32[]{:S(2)}, u32[]{:S(2)}) collective-permute-start(bf16[192,256]{1,0:T(8,128)(2,1)S(1)} %get-tuple-element.210), channel_id=1, source_target_pairs={{0,6},{1,7},{2,0},{3,1},{4,2},{5,3},{6,4},{7,5},{8,14},{9,15},{10,... | collective-permute-start | bytes 294920 | tf_op jit(solution)/shard_map/ppermute | solution.py:1525
  91.3 8.6 %collective-permute-start.13 = (bf16[192,256]{1,0:T(8,128)(2,1)S(1)}, bf16[192,256]{1,0:T(8,128)(2,1)S(1)}, u32[]{:S(2)}, u32[]{:S(2)}) collective-permute-start(bf16[192,256]{1,0:T(8,128)(2,1)S(1)} %get-tuple-element.211), channel_id=1, source_target_pairs={{0,4},{1,5},{2,6},{3,7},{4,0},{5,1},{6,2},{7,3},{8,12},{9,13},{10,... | collective-permute-start | bytes 294920 | tf_op jit(solution)/shard_map/ppermute | solution.py:1525
  94.0 31.2 %collective-permute-start.20 = (bf16[2,2,216,768]{3,2,1,0:T(8,128)(2,1)S(1)}, bf16[2,2,216,768]{3,2,1,0:T(8,128)(2,1)S(1)}, u32[]{:S(2)}, u32[]{:S(2)}) collective-permute-start(bf16[2,2,216,768]{3,2,1,0:T(8,128)(2,1)S(1)} %get-tuple-element.224), channel_id=1, source_target_pairs={{0,8},{8,0},{16,24},{24,16},{1,9},{9,1},{17,25},{25,17},{2,10},{10... | collective-permute-start | bytes 3981320 | tf_op jit(solution)/shard_map/ppermute | solution.py:1533
  94.3 31.0 %collective-permute-start.21 = (bf16[2,2,216,768]{3,2,1,0:T(8,128)(2,1)S(1)}, bf16[2,2,216,768]{3,2,1,0:T(8,128)(2,1)S(1)}, u32[]{:S(2)}, u32[]{:S(2)}) collective-permute-start(bf16[2,2,216,768]{3,2,1,0:T(8,128)(2,1)S(1)} %get-tuple-element.225), channel_id=1, source_target_pairs={{0,16},{8,24},{16,0},{24,8},{1,17},{9,25},{17,1},{25,9},{2,18},{10... | collective-permute-start | bytes 3981320 | tf_op jit(solution)/shard_map/ppermute | solution.py:1533
  113.9 14.6 %collective-permute-start.15 = (bf16[576,256]{1,0:T(8,128)(2,1)S(1)}, bf16[576,256]{1,0:T(8,128)(2,1)S(1)}, u32[]{:S(2)}, u32[]{:S(2)}) collective-permute-start(bf16[576,256]{1,0:T(8,128)(2,1)S(1)} %get-tuple-element.233.refs_5_), channel_id=1, source_target_pairs={{0,6},{1,7},{2,0},{3,1},{4,2},{5,3},{6,4},{7,5},{8,14},{9,15},{10,... | collective-permute-start | bytes 884744 | tf_op jit(solution)/shard_map/ppermute | solution.py:1525
  115.7 24.7 %collective-permute-start.16 = (bf16[576,256]{1,0:T(8,128)(2,1)S(1)}, bf16[576,256]{1,0:T(8,128)(2,1)S(1)}, u32[]{:S(2)}, u32[]{:S(2)}) collective-permute-start(bf16[576,256]{1,0:T(8,128)(2,1)S(1)} %get-tuple-element.235.refs_7_), channel_id=1, source_target_pairs={{0,4},{1,5},{2,6},{3,7},{4,0},{5,1},{6,2},{7,3},{8,12},{9,13},{10,... | collective-permute-start | bytes 884744 | tf_op jit(solution)/shard_map/ppermute | solution.py:1525
  115.7 24.7 %collective-permute-start.17 = (bf16[576,256]{1,0:T(8,128)(2,1)S(1)}, bf16[576,256]{1,0:T(8,128)(2,1)S(1)}, u32[]{:S(2)}, u32[]{:S(2)}) collective-permute-start(bf16[576,256]{1,0:T(8,128)(2,1)S(1)} %get-tuple-element.234.refs_6_), channel_id=1, source_target_pairs={{0,2},{1,3},{2,4},{3,5},{4,6},{5,7},{6,0},{7,1},{8,10},{9,11},{10,... | collective-permute-start | bytes 884744 | tf_op jit(solution)/shard_map/ppermute | solution.py:1525
  126.5 16.1 %collective-permute-start.22 = (bf16[2,216,768]{2,1,0:T(8,128)(2,1)S(1)}, bf16[2,216,768]{2,1,0:T(8,128)(2,1)S(1)}, u32[]{:S(2)}, u32[]{:S(2)}) collective-permute-start(bf16[2,216,768]{2,1,0:T(8,128)(2,1)S(1)} %get-tuple-element.255), channel_id=1, source_target_pairs={{0,16},{8,24},{16,0},{24,8},{1,17},{9,25},{17,1},{25,9},{2,18},{10... | collective-permute-start | bytes 1990664 | tf_op jit(solution)/shard_map/ppermute | solution.py:1533
  127.5 15.5 %collective-permute-start.23 = (bf16[2,216,768]{2,1,0:T(8,128)(2,1)S(1)}, bf16[2,216,768]{2,1,0:T(8,128)(2,1)S(1)}, u32[]{:S(2)}, u32[]{:S(2)}) collective-permute-start(bf16[2,216,768]{2,1,0:T(8,128)(2,1)S(1)} %get-tuple-element.257), channel_id=1, source_target_pairs={{0,8},{8,0},{16,24},{24,16},{1,9},{9,1},{17,25},{25,17},{2,10},{10... | collective-permute-start | bytes 1990664 | tf_op jit(solution)/shard_map/ppermute | solution.py:1533
  140.4 8.9 %collective-permute-start.27 = (bf16[16,24,768]{2,1,0:T(8,128)(2,1)S(1)}, bf16[16,24,768]{2,1,0:T(8,128)(2,1)S(1)}, u32[]{:S(2)}, u32[]{:S(2)}) collective-permute-start(bf16[16,24,768]{2,1,0:T(8,128)(2,1)S(1)} %get-tuple-element.263), channel_id=1, source_target_pairs={{0,1},{1,0},{2,3},{3,2},{4,5},{5,4},{6,7},{7,6},{8,9},{9,8},{10,11... | collective-permute-start | bytes 1769480 | tf_op jit(solution)/shard_map/ppermute | solution.py:1529
  144.4 36.3 %collective-permute-start.24 = (bf16[216,768]{1,0:T(8,128)(2,1)S(1)}, bf16[216,768]{1,0:T(8,128)(2,1)S(1)}, u32[]{:S(2)}, u32[]{:S(2)}) collective-permute-start(bf16[216,768]{1,0:T(8,128)(2,1)S(1)} %get-tuple-element.259), channel_id=1, source_target_pairs={{0,2},{1,3},{2,4},{3,5},{4,6},{5,7},{6,0},{7,1},{8,10},{9,11},{10,... | collective-permute-start | bytes 995336 | tf_op jit(solution)/shard_map/ppermute | solution.py:1525
  144.4 36.2 %collective-permute-start.25 = (bf16[216,768]{1,0:T(8,128)(2,1)S(1)}, bf16[216,768]{1,0:T(8,128)(2,1)S(1)}, u32[]{:S(2)}, u32[]{:S(2)}) collective-permute-start(bf16[216,768]{1,0:T(8,128)(2,1)S(1)} %get-tuple-element.260), channel_id=1, source_target_pairs={{0,4},{1,5},{2,6},{3,7},{4,0},{5,1},{6,2},{7,3},{8,12},{9,13},{10,... | collective-permute-start | bytes 995336 | tf_op jit(solution)/shard_map/ppermute | solution.py:1525
  147.5 33.2 %collective-permute-start.26 = (bf16[216,768]{1,0:T(8,128)(2,1)S(1)}, bf16[216,768]{1,0:T(8,128)(2,1)S(1)}, u32[]{:S(2)}, u32[]{:S(2)}) collective-permute-start(bf16[216,768]{1,0:T(8,128)(2,1)S(1)} %get-tuple-element.261), channel_id=1, source_target_pairs={{0,6},{1,7},{2,0},{3,1},{4,2},{5,3},{6,4},{7,5},{8,14},{9,15},{10,... | collective-permute-start | bytes 995336 | tf_op jit(solution)/shard_map/ppermute | solution.py:1525
  149.9 5.5 %collective-permute-start.28 = (bf16[2,2,24,768]{3,2,1,0:T(8,128)(2,1)S(1)}, bf16[2,2,24,768]{3,2,1,0:T(8,128)(2,1)S(1)}, u32[]{:S(2)}, u32[]{:S(2)}) collective-permute-start(bf16[2,2,24,768]{3,2,1,0:T(8,128)(2,1)S(1)} %get-tuple-element.266), channel_id=1, source_target_pairs={{0,8},{8,0},{16,24},{24,16},{1,9},{9,1},{17,25},{25,17},{2,10},{10... | collective-permute-start | bytes 442376 | tf_op jit(solution)/shard_map/ppermute | solution.py:1533
  150.0 5.5 %collective-permute-start.29 = (bf16[2,2,24,768]{3,2,1,0:T(8,128)(2,1)S(1)}, bf16[2,2,24,768]{3,2,1,0:T(8,128)(2,1)S(1)}, u32[]{:S(2)}, u32[]{:S(2)}) collective-permute-start(bf16[2,2,24,768]{3,2,1,0:T(8,128)(2,1)S(1)} %get-tuple-element.267), channel_id=1, source_target_pairs={{0,16},{8,24},{16,0},{24,8},{1,17},{9,25},{17,1},{25,9},{2,18},{10... | collective-permute-start | bytes 442376 | tf_op jit(solution)/shard_map/ppermute | solution.py:1533
  156.1 4.4 %collective-permute-start.30 = (bf16[2,24,768]{2,1,0:T(8,128)(2,1)S(1)}, bf16[2,24,768]{2,1,0:T(8,128)(2,1)S(1)}, u32[]{:S(2)}, u32[]{:S(2)}) collective-permute-start(bf16[2,24,768]{2,1,0:T(8,128)(2,1)S(1)} %get-tuple-element.269), channel_id=1, source_target_pairs={{0,16},{8,24},{16,0},{24,8},{1,17},{9,25},{17,1},{25,9},{2,18},{10... | collective-permute-start | bytes 221192 | tf_op jit(solution)/shard_map/ppermute | solution.py:1533
  157.5 4.4 %collective-permute-start.31 = (bf16[2,24,768]{2,1,0:T(8,128)(2,1)S(1)}, bf16[2,24,768]{2,1,0:T(8,128)(2,1)S(1)}, u32[]{:S(2)}, u32[]{:S(2)}) collective-permute-start(bf16[2,24,768]{2,1,0:T(8,128)(2,1)S(1)} %get-tuple-element.271), channel_id=1, source_target_pairs={{0,8},{8,0},{16,24},{24,16},{1,9},{9,1},{17,25},{25,17},{2,10},{10... | collective-permute-start | bytes 221192 | tf_op jit(solution)/shard_map/ppermute | solution.py:1533
  162.4 8.1 %collective-permute-start.32 = (bf16[24,768]{1,0:T(8,128)(2,1)S(1)}, bf16[24,768]{1,0:T(8,128)(2,1)S(1)}, u32[]{:S(2)}, u32[]{:S(2)}) collective-permute-start(bf16[24,768]{1,0:T(8,128)(2,1)S(1)} %get-tuple-element.273), channel_id=1, source_target_pairs={{0,2},{1,3},{2,4},{3,5},{4,6},{5,7},{6,0},{7,1},{8,10},{9,11},{10,... | collective-permute-start | bytes 110600 | tf_op jit(solution)/shard_map/ppermute | solution.py:1525
  164.8 13.8 %collective-permute-start.33 = (bf16[24,768]{1,0:T(8,128)(2,1)S(1)}, bf16[24,768]{1,0:T(8,128)(2,1)S(1)}, u32[]{:S(2)}, u32[]{:S(2)}) collective-permute-start(bf16[24,768]{1,0:T(8,128)(2,1)S(1)} %get-tuple-element.274), channel_id=1, source_target_pairs={{0,4},{1,5},{2,6},{3,7},{4,0},{5,1},{6,2},{7,3},{8,12},{9,13},{10,... | collective-permute-start | bytes 110600 | tf_op jit(solution)/shard_map/ppermute | solution.py:1525
  170.5 10.2 %collective-permute-start.34 = (bf16[24,768]{1,0:T(8,128)(2,1)S(1)}, bf16[24,768]{1,0:T(8,128)(2,1)S(1)}, u32[]{:S(2)}, u32[]{:S(2)}) collective-permute-start(bf16[24,768]{1,0:T(8,128)(2,1)S(1)} %get-tuple-element.275), channel_id=1, source_target_pairs={{0,6},{1,7},{2,0},{3,1},{4,2},{5,3},{6,4},{7,5},{8,14},{9,15},{10,... | collective-permute-start | bytes 110600 | tf_op jit(solution)/shard_map/ppermute | solution.py:1525
  (23 other events, 292.5 us)

commit v7 on v6

--- a/solution.py
+++ b/solution.py
@@ -570,19 +570,20 @@
     return jnp.dot(left, right, preferred_element_type=jnp.float32)
 
 
-def call_whole(kernel, out_shape, name, scalars, *arrays, in_specs=None, scratch=(), limit=12, cost=None):
+def call_whole(kernel, out_shape, name, scalars, *arrays, scratch=(), limit=12, ins=True, outs=True):
+    direct = pl.BlockSpec(memory_space=pltpu.VMEM)
     return pl.pallas_call(
         kernel,
         grid_spec=pltpu.PrefetchScalarGridSpec(
             num_scalar_prefetch=1,
             grid=(1,),
-            in_specs=in_specs or [whole(array.shape) for array in arrays],
-            out_specs=[whole(out.shape) for out in out_shape],
+            in_specs=[direct if ins else whole(array.shape) for array in arrays],
+            out_specs=[direct if outs else whole(out.shape) for out in out_shape],
             scratch_shapes=list(scratch),
         ),
         out_shape=list(out_shape),
         compiler_params=pltpu.CompilerParams(vmem_limit_bytes=limit << 20),
-        cost_estimate=cost or NO_COST,
+        cost_estimate=NO_COST,
         name=name,
     )(scalars, *arrays)
 
@@ -654,6 +655,7 @@
         w_key,
         w_value,
         limit=24,
+        ins=False,
     )
 
 
@@ -751,12 +753,11 @@
     return (key_place <= query_place) & (key_place >= doc_line)
 
 
-def attend_kernel(
-    heads, block, key_blocks, meta, doc_ref, q_ref, k_ref, vt_ref, o_ref, lse_ref, *refs
-):
-    ob_refs, (m_ref, l_ref) = refs[:-2], refs[-2:]
-    step = pl.program_id(0)
-    steps = len(ob_refs)
+def attend_kernel(heads, block, first, steps, key_blocks, meta, doc_ref, q_ref, k_ref, vt_ref, *refs):
+    o_ref, m_ref, l_ref = refs[-3:]
+    count = (len(refs) - 3) // 3
+    mixed_refs, lse_refs, ob_refs = (refs[count * part : count * (part + 1)] for part in range(3))
+    step = first + pl.program_id(0)
     query_start = meta[step]
     doc_first, doc_last = meta[steps + key_blocks + step], meta[2 * steps + key_blocks + step]
     doc_line = doc_ref[...]
@@ -805,44 +806,23 @@
         return carry
 
     lax.fori_loop(0, key_blocks, body, 0)
-    for head in range(heads):
-        rows = slice(head * size, (head + 1) * size)
-        total = l_ref[head]
-        mixed = o_ref[rows, :] / total
-        o_ref[rows, :] = mixed
-        lse_ref[head] = m_ref[head] + jnp.log(total)
-    for index, ob_ref in enumerate(ob_refs):
-
-        @pl.when(step == index)
-        def _(ob_ref=ob_ref):
-            ob_ref[...] = o_ref[...].astype(jnp.bfloat16)
-
-
-def attend_back_kernel(
-    heads,
-    block,
-    key_blocks,
-    scale,
-    meta,
-    doc_ref,
-    q_ref,
-    o_ref,
-    lse_ref,
-    k_ref,
-    kt_ref,
-    v_ref,
-    *refs,
-):
-    g_refs = refs[:-7]
-    dq_ref, mine_ref, other_ref, acc_ref, pair_ref, delta_ref, g_ref = refs[-7:]
+    for index in range(count):
+
+        @pl.when(step == first + index)
+        def _(index=index):
+            for head in range(heads):
+                rows = slice(head * size, (head + 1) * size)
+                total = l_ref[head]
+                mixed = o_ref[rows, :] / total
+                mixed_refs[index][rows, :] = mixed
+                ob_refs[index][rows, :] = mixed.astype(jnp.bfloat16)
+                lse_refs[index][head] = m_ref[head] + jnp.log(total)
+
+
+def attend_back_kernel(heads, block, steps, key_blocks, scale, meta, doc_ref, q_ref, k_ref, kt_ref, v_ref, *refs):
+    o_refs, lse_refs, g_refs = (refs[steps * part : steps * (part + 1)] for part in range(3))
+    dq_ref, mine_ref, other_ref, acc_ref, pair_ref, delta_ref, g_ref, lse_ref = refs[3 * steps :]
     step = pl.program_id(0)
-    steps = len(g_refs)
-    for index, grad_ref in enumerate(g_refs):
-
-        @pl.when(step == index)
-        def _(grad_ref=grad_ref):
-            g_ref[...] = grad_ref[...]
-
     query_start = meta[step]
     doc_first, doc_last = meta[steps + key_blocks + step], meta[2 * steps + key_blocks + step]
     doc_line = doc_ref[...]
@@ -855,11 +835,19 @@
         pair_ref[...] = jnp.zeros_like(pair_ref)
 
     acc_ref[...] = jnp.zeros_like(acc_ref)
-    for head in range(heads):
-        rows = slice(head * size, (head + 1) * size)
-        delta_ref[head] = jnp.sum(
-            g_ref[rows, :].astype(jnp.float32) * o_ref[rows, :], axis=0, keepdims=True
-        )
+    for index in range(steps):
+
+        @pl.when(step == index)
+        def _(index=index):
+            g_ref[...] = g_refs[index][...]
+            lse_ref[...] = lse_refs[index][...]
+            for head in range(heads):
+                rows = slice(head * size, (head + 1) * size)
+                delta_ref[head] = jnp.sum(
+                    g_refs[index][rows, :].astype(jnp.float32) * o_refs[index][rows, :],
+                    axis=0,
+                    keepdims=True,
+                )
 
     def fold(slot, allowed):
         span = pl.ds(pl.multiple_of(slot * block, block), block)
@@ -920,71 +908,61 @@
     return pl.BlockSpec(shape, lambda *index: (0,) * len(shape))
 
 
-def attend(meta, doc_line, q_ext, k_ext, v_t, heads, block):
-    wide, queries = q_ext.shape
+def attend(meta, doc_line, q_ext, k_ext, v_t, heads, block, first, last):
+    wide_rows, queries = q_ext.shape
     share, keys = v_t.shape
+    steps, key_blocks, count = queries // block, keys // block, last - first
+    direct = pl.BlockSpec(memory_space=pltpu.VMEM)
+    outs = pl.pallas_call(
+        partial(attend_kernel, heads, block, first, steps, key_blocks),
+        grid_spec=pltpu.PrefetchScalarGridSpec(
+            num_scalar_prefetch=1,
+            grid=(count,),
+            in_specs=[
+                pl.BlockSpec((1, block), lambda i, meta: (0, first + i)),
+                pl.BlockSpec((wide_rows, block), lambda i, meta: (0, first + i)),
+                direct,
+                direct,
+            ],
+            out_specs=[direct] * (3 * count),
+            scratch_shapes=[
+                pltpu.VMEM((share, block), jnp.float32),
+                pltpu.VMEM((heads, 1, block), jnp.float32),
+                pltpu.VMEM((heads, 1, block), jnp.float32),
+            ],
+        ),
+        out_shape=[jax.ShapeDtypeStruct((share, block), jnp.float32)] * count
+        + [jax.ShapeDtypeStruct((heads, 1, block), jnp.float32)] * count
+        + [jax.ShapeDtypeStruct((share, block), jnp.bfloat16)] * count,
+        compiler_params=pltpu.CompilerParams(vmem_limit_bytes=12 << 20),
+        cost_estimate=NO_COST,
+        name="attend",
+    )(meta, doc_line, q_ext, k_ext, v_t)
+    return outs[:count], outs[count : 2 * count], outs[2 * count :]
+
+
+def attend_back(meta, doc_line, q_ext, grads, mixed, lse, k_ext, k_t, v_ext, heads, block, scale):
+    wide_rows, queries = q_ext.shape
+    share, keys = k_t.shape
     steps, key_blocks = queries // block, keys // block
+    direct = pl.BlockSpec(memory_space=pltpu.VMEM)
     return pl.pallas_call(
-        partial(attend_kernel, heads, block, key_blocks),
+        partial(attend_back_kernel, heads, block, steps, key_blocks, scale),
         grid_spec=pltpu.PrefetchScalarGridSpec(
             num_scalar_prefetch=1,
             grid=(steps,),
             in_specs=[
                 pl.BlockSpec((1, block), lambda i, meta: (0, i)),
-                pl.BlockSpec((wide, block), lambda i, meta: (0, i)),
-                pl.BlockSpec(memory_space=pltpu.VMEM),
-                pl.BlockSpec(memory_space=pltpu.VMEM),
-            ],
-            out_specs=[
-                pl.BlockSpec((share, block), lambda i, meta: (0, i)),
-                pl.BlockSpec((heads, 1, block), lambda i, meta: (0, 0, i)),
+                pl.BlockSpec((wide_rows, block), lambda i, meta: (0, i)),
             ]
-            + [whole((share, block))] * steps,
-            scratch_shapes=[
-                pltpu.VMEM((heads, 1, block), jnp.float32),
-                pltpu.VMEM((heads, 1, block), jnp.float32),
-            ],
-        ),
-        out_shape=[
-            jax.ShapeDtypeStruct((share, queries), jnp.float32),
-            jax.ShapeDtypeStruct((heads, 1, queries), jnp.float32),
-        ]
-        + [jax.ShapeDtypeStruct((share, block), jnp.bfloat16)] * steps,
-        compiler_params=pltpu.CompilerParams(vmem_limit_bytes=12 << 20),
-        cost_estimate=NO_COST,
-        name="attend",
-    )(meta, doc_line, q_ext, k_ext, v_t)
-
-
-def attend_back(meta, doc_line, q_ext, grad_t, mixed, lse, k_ext, k_t, v_ext, heads, block, scale):
-    wide, queries = q_ext.shape
-    share, keys = k_t.shape
-    steps, key_blocks = queries // block, keys // block
-    return pl.pallas_call(
-        partial(attend_back_kernel, heads, block, key_blocks, scale),
-        grid_spec=pltpu.PrefetchScalarGridSpec(
-            num_scalar_prefetch=1,
-            grid=(steps,),
-            in_specs=[
-                pl.BlockSpec((1, block), lambda i, meta: (0, i)),
-                pl.BlockSpec((wide, block), lambda i, meta: (0, i)),
-                pl.BlockSpec((share, block), lambda i, meta: (0, i)),
-                pl.BlockSpec((heads, 1, block), lambda i, meta: (0, 0, i)),
-                pl.BlockSpec(memory_space=pltpu.VMEM),
-                pl.BlockSpec(memory_space=pltpu.VMEM),
-                pl.BlockSpec(memory_space=pltpu.VMEM),
-            ]
-            + [whole((share, block))] * steps,
-            out_specs=[
-                pl.BlockSpec((share, block), lambda i, meta: (0, i)),
-                whole((2 * share, keys // 2)),
-                whole((2 * share, keys // 2)),
-            ],
+            + [direct] * (3 + 3 * steps),
+            out_specs=[pl.BlockSpec((share, block), lambda i, meta: (0, i)), direct, direct],
             scratch_shapes=[
                 pltpu.VMEM((share, block), jnp.float32),
                 pltpu.VMEM((2 * share, keys), jnp.float32),
                 pltpu.VMEM((heads, 1, block), jnp.float32),
                 pltpu.VMEM((share, block), jnp.bfloat16),
+                pltpu.VMEM((heads, 1, block), jnp.float32),
             ],
         ),
         out_shape=[
@@ -995,7 +973,7 @@
         compiler_params=pltpu.CompilerParams(vmem_limit_bytes=20 << 20),
         cost_estimate=HIGH_COST,
         name="attend_back",
-    )(meta, doc_line, q_ext, mixed, lse, k_ext, k_t, v_ext, *grad_t)
+    )(meta, doc_line, q_ext, k_ext, k_t, v_ext, *mixed, *lse, *grads)
 
 
 def join_kernel(chips, unused, dq_ref, mine_ref, other_ref, *out_refs):
@@ -1381,7 +1359,7 @@
             jax.ShapeDtypeStruct(row, jnp.float32),
             jax.ShapeDtypeStruct((1, hidden), jnp.float32),
         ],
-        compiler_params=pltpu.CompilerParams(vmem_limit_bytes=36 << 20),
+        compiler_params=pltpu.CompilerParams(vmem_limit_bytes=26 << 20),
         cost_estimate=NO_COST,
         name="middle",
     )(position, *mixed, tokens, cotangent, w_out, w_up, w_down, *gains)
@@ -1389,21 +1367,23 @@
 
 def down_kernel(per, position, bent_ref, cot_ref, keep_ref, send_ref):
     first_core = position[1] == 0
+    parts = bent_ref.shape[1] // (2 * per)
+    first = pl.program_id(0) * parts
     grad = lax.dot_general(
         bent_ref[...], cot_ref[...], (((0,), (0,)), ((), ())), preferred_element_type=jnp.float32
     ).astype(jnp.bfloat16)
-    for part in range(keep_ref.shape[0]):
+    for part in range(parts):
         even = grad[2 * per * part : 2 * per * part + per]
         odd = grad[2 * per * part + per : 2 * per * (part + 1)]
-        keep_ref[part] = jnp.where(first_core, even, odd)
-        send_ref[part] = jnp.where(first_core, odd, even)
+        keep_ref[first + part] = jnp.where(first_core, even, odd)
+        send_ref[first + part] = jnp.where(first_core, odd, even)
 
 
 def down_grad(position, bent, cotangent, per):
     (block, hidden), model_width = bent.shape, cotangent.shape[1]
     tiles, chunks = hidden // model_width, hidden // (2 * per)
     out = jax.ShapeDtypeStruct((chunks, per, model_width), jnp.bfloat16)
-    out_spec = pl.BlockSpec((chunks // tiles, per, model_width), lambda i, pos: (i, 0, 0))
+    out_spec = pl.BlockSpec(memory_space=pltpu.VMEM)
     return pl.pallas_call(
         partial(down_kernel, per),
         grid_spec=pltpu.PrefetchScalarGridSpec(
@@ -1411,7 +1391,7 @@
             grid=(tiles,),
             in_specs=[
                 pl.BlockSpec((block, model_width), lambda i, pos: (0, i)),
-                whole(cotangent.shape),
+                pl.BlockSpec(memory_space=pltpu.VMEM),
             ],
             out_specs=[out_spec, out_spec],
         ),
@@ -1424,7 +1404,9 @@
 
 def up_out_kernel(tiles, position, h2_ref, pre_ref, z_ref, gmid_ref, perm_ref, keep_ref, send_ref, left_ref):
     step = pl.program_id(0)
-    chunks, per = keep_ref.shape[:2]
+    chunks = keep_ref.shape[0]
+    per = perm_ref.shape[0] // (2 * chunks)
+    place = pl.ds(pl.multiple_of(step * per, per), per)
 
     @pl.when(step == 0)
     def _():
@@ -1433,9 +1415,9 @@
     def store(right):
         grad = nn_dot(left_ref[...], right)
         for chunk in range(chunks):
-            keep_ref[chunk] = grad[chunk * per : (chunk + 1) * per].astype(jnp.bfloat16)
+            keep_ref[chunk, place] = grad[chunk * per : (chunk + 1) * per].astype(jnp.bfloat16)
             first = (chunks + chunk) * per
-            send_ref[chunk] = grad[first : first + per].astype(jnp.bfloat16)
+            send_ref[chunk, place] = grad[first : first + per].astype(jnp.bfloat16)
 
     @pl.when(step < tiles)
     def _():
@@ -1451,19 +1433,17 @@
     (block, hidden), model_width = pre.shape, h2.shape[1]
     tiles, chunks = hidden // model_width, model_width // (2 * per)
     out = jax.ShapeDtypeStruct((chunks, per * (tiles + 1), model_width), jnp.bfloat16)
-    out_spec = pl.BlockSpec((chunks, per, model_width), lambda i, pos: (0, i, 0))
+    out_spec = pl.BlockSpec(memory_space=pltpu.VMEM)
     return pl.pallas_call(
         partial(up_out_kernel, tiles),
         grid_spec=pltpu.PrefetchScalarGridSpec(
             num_scalar_prefetch=1,
             grid=(tiles + 1,),
             in_specs=[
-                whole(h2.shape),
+                pl.BlockSpec(memory_space=pltpu.VMEM),
                 pl.BlockSpec((block, model_width), lambda i, pos: (0, jnp.minimum(i, tiles - 1))),
-                whole(z.shape),
-                whole(gmid.shape),
-                whole(perm.shape),
-            ],
+            ]
+            + [pl.BlockSpec(memory_space=pltpu.VMEM)] * 3,
             out_specs=[out_spec, out_spec],
             scratch_shapes=[pltpu.VMEM((model_width, block), jnp.bfloat16)],
         ),
@@ -1517,6 +1497,7 @@
         w_value,
         gain,
         scratch=[pltpu.VMEM((model_width, block), jnp.float32)],
+        outs=False,
     )[0]
 
 
@@ -1541,48 +1522,37 @@
     return array.astype(jnp.float32)
 
 
-def low_part(shape, keep):
-    def index(i, bits):
-        return (0, bits[2] if keep else 1 - bits[2], 0, 0, 0)
-
-    return pl.BlockSpec((2, 1, shape[2] // 2) + shape[3:], index)
-
-
-def high_part(shape, keep):
-    def index(i, bits):
-        return (bits[3] if keep else 1 - bits[3], 0, 1, 0, 0)
-
-    return pl.BlockSpec((1, 2, shape[2] // 2) + shape[3:], index)
-
-
-def outgoing_kernel(scalars, *refs):
+def outgoing_kernel(kept, scalars, *refs):
     low_ref, high_ref = refs[-2:]
+    low_bit, high_bit = scalars[2], scalars[3]
+    if not kept:
+        low_bit, high_bit = 1 - low_bit, 1 - high_bit
+    half = refs[0].shape[2] // 2
     first = 0
-    for group in range(len(refs) // 4):
-        low_a, low_b, high_a, high_b = refs[4 * group : 4 * group + 4]
-        rows = slice(first, first + low_a.shape[3])
-        low_ref[:, :, rows] = sent(wide(low_a[:, 0]) + wide(low_b[:, 0]))
-        high_ref[:, :, rows] = sent(wide(high_a[0]) + wide(high_b[0]))
-        first += low_a.shape[3]
+    for group in range(len(refs) // 2 - 1):
+        keep, other = refs[2 * group : 2 * group + 2]
+        rows = slice(first, first + keep.shape[3])
+        for side in range(2):
+            low_ref[side, :, rows] = sent(
+                wide(keep[side, low_bit, :half]) + wide(other[side, low_bit, :half])
+            )
+            high_ref[side, :, rows] = sent(
+                wide(keep[high_bit, side, half:]) + wide(other[high_bit, side, half:])
+            )
+        first += keep.shape[3]
 
 
 def outgoing(scalars, groups, kept=False):
-    arrays, specs = [], []
-    for keep, other in groups:
-        low, high = low_part(keep.shape, kept), high_part(keep.shape, kept)
-        arrays += [keep, other, keep, other]
-        specs += [low, low, high, high]
+    arrays = [array for group in groups for array in group]
     shape = groups[0][0].shape
     rows = sum(keep.shape[3] for keep, _ in groups)
     out = jax.ShapeDtypeStruct((2, shape[2] // 2, rows, shape[4]), jnp.bfloat16)
     return call_whole(
-        outgoing_kernel,
+        partial(outgoing_kernel, kept),
         [out, out],
         "kept" if kept else "outgoing",
         scalars,
         *arrays,
-        in_specs=specs,
-        limit=20,
     )
 
 
@@ -1606,7 +1576,7 @@
     rows = sum(group[0].shape[2] for group in groups)
     out = jax.ShapeDtypeStruct((arrays[0].shape[1], rows, arrays[0].shape[3]), jnp.bfloat16)
     return call_whole(
-        partial(halfway_kernel, len(groups)), [out] * 4, "halfway", scalars, *arrays, limit=24
+        partial(halfway_kernel, len(groups)), [out] * 4, "halfway", scalars, *arrays, limit=12
     )
 
 
@@ -1688,6 +1658,7 @@
         scalars,
         *arrived,
         scratch=[pltpu.VMEM((chips, per, 3 * share), jnp.float32)],
+        outs=False,
     )
 
 
@@ -1738,6 +1709,7 @@
         jnp.zeros((1,), jnp.int32),
         tokens,
         gain_attend[None, :],
+        ins=False,
     )[0]
     behind, ahead, across = gathered(normed_b)
 
@@ -1797,8 +1769,13 @@
     q_ext, k_ext, v_t = project(
         late_starts, late_blocks, wq_wide, wk_wide, wv_rows, 1, heads, scale, chips, filled
     )
-    mixed, lse, *mixed_b = attend(meta, doc_line, q_ext, k_ext, v_t, heads, block)
-    mixed_b, wk_rows = lax.optimization_barrier((mixed_b, wk_rows))
+    parts_of = [
+        attend(meta, doc_line, q_ext, k_ext, v_t, heads, block, *span) for span in ((0, 1), (1, chips))
+    ]
+    mixed, lse, mixed_b = (
+        list(parts_of[0][item]) + list(parts_of[1][item]) for item in range(3)
+    )
+    mixed_b[1:], wk_rows = lax.optimization_barrier((mixed_b[1:], wk_rows))
     k_t, v_ext = project_back(place, early_blocks + late_blocks, wk_rows, wv_wide)
     back = [mixed_b[slots[0]]] + [
         chip_shift(mixed_b[slots[step]], -step) for step in range(1, chips)

time: 183 us -> 181 us (0.989); the launches traced: 183 us -> 179 us
  Pallas kernels: 71.7 us -> 67.7 us
    ppermute x8, waiting for transfers between devices: 13.2 us -> 22.3 us  [row_swap(): lax.ppermute(value, 'row', [(i, i ^ bit) for i in range(lax.axis_size('ro...]
    ppermute x17, waiting for transfers between devices: 32.8 us -> 24.2 us  [chip_shift(): lax.ppermute(value, 'seq', [(i, (i + 2 * steps) % count) for i in range(c...]
    pallas_call x2 -> x3, Pallas kernels: 19.6 us -> 15.9 us  [the longest x1 8.53 us: attend_back(): pl.pallas_call(partial(attend_back_kernel, heads, block, steps, key_block...]
    ppermute x8, starting transfers between devices: 7.11 us -> 10.1 us  [row_swap(): lax.ppermute(value, 'row', [(i, i ^ bit) for i in range(lax.axis_size('ro...]
    ppermute x17, starting transfers between devices: 26.3 us -> 23.9 us  [chip_shift(): lax.ppermute(value, 'seq', [(i, (i + 2 * steps) % count) for i in range(c...]
    unnamed x41 -> x29, local copies, waits for them, and re-layouts: 4.8 us -> 3.59 us
where the time goes in v7:
time: 181 us; the launch traced here: 179 us
  Pallas kernels  67.7 us (37%)
  waiting for transfers between devices  60 us (33%)
  starting transfers between devices  37.2 us (21%)
  local copies, waits for them, and re-layouts  9.06 us (5%)
  other arithmetic  3.56 us (2%)
    ppermute x17, waiting for transfers between devices, chip_shift(): lax.ppermute(value, 'seq', [(i, (i + 2 * steps) % count) for i in range(c...  24.2 us
    ppermute x17, starting transfers between devices, chip_shift(): lax.ppermute(value, 'seq', [(i, (i + 2 * steps) % count) for i in range(c...  23.9 us
    pallas_call x15, Pallas kernels, call_whole(): pl.pallas_call(kernel, grid_spec=pltpu.PrefetchScalarGridSpec(num_scalar_...  22.8 us
    ppermute x8, waiting for transfers between devices, row_swap(): lax.ppermute(value, 'row', [(i, i ^ bit) for i in range(lax.axis_size('ro...  22.3 us
    pallas_call x1, Pallas kernels, middle(): pl.pallas_call(partial(middle_kernel, chips, tiles), grid_spec=pltpu.Pref...  15.5 us
    ppermute x8, starting transfers between devices, row_swap(): lax.ppermute(value, 'row', [(i, i ^ bit) for i in range(lax.axis_size('ro...  10.1 us
    pallas_call x1, Pallas kernels, attend_back(): pl.pallas_call(partial(attend_back_kernel, heads, block, steps, key_block...  8.53 us
    ppermute x2, waiting for transfers between devices, gathered(): across = (lax.ppermute(ahead, 'seq', down), lax.ppermute(behind, 'seq', up))  7.98 us
  transfers between devices with their start and end apart: 35, of which 19 were waited for; matrix products, arithmetic and copies ran while one was open for 4% of the time, Pallas kernels for 21%

profile of v7, /device:TPU:0, one launch (start us, length us, event | category | flops | bytes accessed | tf_op | source)
XLA Modules:
  0.0 178.6 jit_solution(14682841296215132562)
XLA Ops:
  2.7 3.1 %collective-permute-start = (bf16[256,768]{1,0:T(8,128)(2,1)S(1)}, bf16[256,768]{1,0:T(8,128)(2,1)S(1)}, u32[]{:S(2)}, u32[]{:S(2)}) collective-permute-start(bf16[256,768]{1,0:T(8,128)(2,1)S(1)} %norm.1.refs_0_), channel_id=1, source_target_pairs={{0,2},{1,3},{2,4},{3,5},{4,6},{5,7},{6,0},{7,1},{8,10},{9,11},{10,... | collective-permute-start | bytes 1179656 | tf_op jit(solution)/shard_map/ppermute | solution.py:1506
  5.8 2.1 %collective-permute-start.1 = (bf16[256,768]{1,0:T(8,128)(2,1)S(1)}, bf16[256,768]{1,0:T(8,128)(2,1)S(1)}, u32[]{:S(2)}, u32[]{:S(2)}) collective-permute-start(bf16[256,768]{1,0:T(8,128)(2,1)S(1)} %norm.1.refs_0_), channel_id=1, source_target_pairs={{0,6},{1,7},{2,0},{3,1},{4,2},{5,3},{6,4},{7,5},{8,14},{9,15},{10,... | collective-permute-start | bytes 1179656 | tf_op jit(solution)/shard_map/ppermute | solution.py:1506
  18.1 3.5 %choose.1 = (bf16[384,768]{1,0:T(8,128)(2,1)S(1)}, bf16[768,384]{1,0:T(8,128)(2,1)S(1)}, bf16[192,768]{1,0:T(8,128)(2,1)S(1)}, bf16[192,768]{1,0:T(8,128)(2,1)S(...) custom-call(s32[4]{0:T(128)S(1)} %pad_add_fusion.2.scalars.unused.position, bf16[768,768]{1,0:T(8,128)(2,1)S(1)} %copy-done, ...), custom_call_target="tpu_custom_call" | custom-call | flops 1000 | bytes 1000 | tf_op jit(solution)/shard_map/choose/pallas_call | solution.py:575
  22.2 2.6 %collective-permute-done.1.refs_2_ = bf16[256,768]{1,0:T(8,128)(2,1)S(1)} collective-permute-done((bf16[256,768]{1,0:T(8,128)(2,1)S(1)}, bf16[256,768]{1,0:T(8,128)(2,1)S(1)}, u32[]{:S(2)}, u32[]{:S(2)}) %collective-permute-start.1) | collective-permute-done | bytes 393248 | tf_op jit(solution)/shard_map/ppermute | solution.py:1506
  26.8 3.4 %project.2 = (bf16[384,1024]{1,0:T(8,128)(2,1)S(1)}, bf16[2048,384]{1,0:T(8,128)(2,1)S(1)}, bf16[192,2048]{1,0:T(8,128)(2,1)S(1)}) custom-call(s32[7]{0:T(128)S(1)} %pad_add_fusion.meta, bf16[256,768]{1,0:T(8,128)(2,1)S(1)} %norm.1.refs_0_, bf16[256,768]{1,0:T(8,128)(2,1)S(1)} %collective-permute-done.refs_1_, ...), custom_call_target="tpu_custom_call" | custom-call | flops 1000 | bytes 1000 | tf_op jit(solution)/shard_map/project/pallas_call | solution.py:698
  30.2 8.0 %collective-permute-done.5 = bf16[256,768]{1,0:T(8,128)(2,1)S(1)} collective-permute-done((bf16[256,768]{1,0:T(8,128)(2,1)S(1)}, bf16[256,768]{1,0:T(8,128)(2,1)S(1)}, u32[]{:S(2)}, u32[]{:S(2)}) %collective-permute-start.5) | collective-permute-done | bytes 393248 | tf_op jit(solution)/shard_map/ppermute | solution.py:1669
  38.4 1.7 collective-permute-done.7.refs_1_.refs_7_
  41.6 6.1 %attend.3 = (f32[192,256]{1,0:T(8,128)S(1)}, f32[192,256]{1,0:T(8,128)S(1)}, f32[192,256]{1,0:T(8,128)S(1)}, f32[3,1,256]{2,1,0:T(1,128)S(1)}, f32[3,1,256]{2,1,...) custom-call(s32[20]{0:T(128)S(1)} %concatenate.11.meta, ...), custom_call_target="tpu_custom_call" | custom-call | flops 1000 | bytes 1000 | tf_op jit(solution)/shard_map/attend/pallas_call | solution.py:916
  47.7 2.4 %collective-permute-start.10 = (bf16[192,256]{1,0:T(8,128)(2,1)S(1)}, bf16[192,256]{1,0:T(8,128)(2,1)S(1)}, u32[]{:S(2)}, u32[]{:S(2)}) collective-permute-start(bf16[192,256]{1,0:T(8,128)(2,1)S(1)} %get-tuple-element.184), channel_id=1, source_target_pairs={{0,2},{1,3},{2,4},{3,5},{4,6},{5,7},{6,0},{7,1},{8,10},{9,11},{10,... | collective-permute-start | bytes 294920 | tf_op jit(solution)/shard_map/ppermute | solution.py:1506
  54.4 3.2 %project_back.1 = (bf16[192,2048]{1,0:T(8,128)(2,1)S(1)}, bf16[2048,384]{1,0:T(8,128)(2,1)S(1)}) custom-call(s32[4]{0:T(128)S(1)} %pad_add_fusion.2.scalars.unused.position, bf16[256,768]{1,0:T(8,128)(2,1)S(1)} %norm.1.refs_0_, bf16[256,768]{1,0:T(8,128)(2,1)S(1)} %collective-permute-done.refs_1_, bf16[256,768]{1,0:T(8,128)(2,1)S(1)} %collective-permute-done.1.refs_2_, ...), custom_call_target="tpu_custom_call" | custom-call | flops 1000 | bytes 1000 | tf_op jit(solution)/shard_map/project_back/pallas_call | solution.py:575
  57.7 3.0 %collective-permute-done.9.refs_2_ = bf16[192,256]{1,0:T(8,128)(2,1)S(1)} collective-permute-done((bf16[192,256]{1,0:T(8,128)(2,1)S(1)}, bf16[192,256]{1,0:T(8,128)(2,1)S(1)}, u32[]{:S(2)}, u32[]{:S(2)}) %collective-permute-start.9) | collective-permute-done | bytes 98336 | tf_op jit(solution)/shard_map/ppermute | solution.py:1506
  60.8 15.5 %middle.1 = (bf16[256,768]{1,0:T(8,128)(2,1)}, f32[256,768]{1,0:T(8,128)S(1)}, bf16[256,768]{1,0:T(8,128)(2,1)S(1)}, bf16[192,256]{1,0:T(8,128)(2,1)S(1)}, bf16[...) custom-call(s32[4]{0:T(128)S(1)} %pad_add_fusion.2.scalars.unused.po, ...), custom_call_target="tpu_custom_call" | custom-call | flops 1000 | bytes 1000 | tf_op jit(solution)/shard_map/middle/pallas_call | solution.py:1311
  76.3 4.5 %up_out_grad.1 = (bf16[16,120,768]{2,1,0:T(8,128)(2,1)S(1)}, bf16[16,120,768]{2,1,0:T(8,128)(2,1)S(1)}) custom-call(s32[4]{0:T(128)S(1)} %pad_add_fusion.2.scalars.unused.position, bf16[256,768]{1,0:T(8,128)(2,1)S(1)} %get-tuple-element.211.h2_ref, bf16[256,3072]{1,0:T(8,128)(2,1)S(1)} %get-tuple-element.212.pre_ref, ...), custom_call_target="tpu_custom_call" | custom-call | flops 1000 | bytes 1000 | tf_op jit(solution)/shard_map/up_out_grad/pallas_call | solution.py:1437
  80.9 2.8 %down_grad.1 = (bf16[16,96,768]{2,1,0:T(8,128)(2,1)S(1)}, bf16[16,96,768]{2,1,0:T(8,128)(2,1)S(1)}) custom-call(s32[4]{0:T(128)S(1)} %pad_add_fusion.2.scalars.unused.position, bf16[256,3072]{1,0:T(8,128)(2,1)S(1)} %get-tuple-element.229.bent_ref, bf16[256,768]{1,0:T(8,128)(2,1)S(1)} %copy-done.7), custom_call_target="tpu_custom_call" | custom-call | flops 1000 | bytes 1000 | tf_op jit(solution)/shard_map/down_grad/pallas_call | solution.py:1387
  84.3 3.8 %collective-permute-start.12 = (bf16[192,256]{1,0:T(8,128)(2,1)S(1)}, bf16[192,256]{1,0:T(8,128)(2,1)S(1)}, u32[]{:S(2)}, u32[]{:S(2)}) collective-permute-start(bf16[192,256]{1,0:T(8,128)(2,1)S(1)} %get-tuple-element.220), channel_id=1, source_target_pairs={{0,6},{1,7},{2,0},{3,1},{4,2},{5,3},{6,4},{7,5},{8,14},{9,15},{10,... | collective-permute-start | bytes 294920 | tf_op jit(solution)/shard_map/ppermute | solution.py:1506
  90.8 3.0 %collective-permute-start.20 = (bf16[2,2,216,768]{3,2,1,0:T(8,128)(2,1)S(1)}, bf16[2,2,216,768]{3,2,1,0:T(8,128)(2,1)S(1)}, u32[]{:S(2)}, u32[]{:S(2)}) collective-permute-start(bf16[2,2,216,768]{3,2,1,0:T(8,128)(2,1)S(1)} %get-tuple-element.234), channel_id=1, source_target_pairs={{0,8},{8,0},{16,24},{24,16},{1,9},{9,1},{17,25},{25,17},{2,10},{10... | collective-permute-start | bytes 3981320 | tf_op jit(solution)/shard_map/ppermute | solution.py:1514
  93.9 2.1 %collective-permute-done.13.refs_11_ = bf16[192,256]{1,0:T(8,128)(2,1)S(1)} collective-permute-done((bf16[192,256]{1,0:T(8,128)(2,1)S(1)}, bf16[192,256]{1,0:T(8,128)(2,1)S(1)}, u32[]{:S(2)}, u32[]{:S(2)}) %collective-permute-start.13) | collective-permute-done | bytes 98336 | tf_op jit(solution)/shard_map/ppermute | solution.py:1506
  96.1 8.5 %attend_back.1 = (bf16[192,1024]{1,0:T(8,128)(2,1)S(1)}, f32[384,1024]{1,0:T(8,128)S(1)}, bf16[384,1024]{1,0:T(8,128)(2,1)S(1)}) custom-call(s32[20]{0:T(128)S(1)} %concatenate.11.meta, s32[1,1024]{1,0:T(1,128)S(1)} %bitcast.45, bf16[384,1024]{1,0:T(8,128)(2,1)S(1)} %get-tuple-element.174.q_ref, bf16[2048,384]{1,0:T(8,128)(2,1)S(1)} %get-tuple-element.175.k_ref, ...), custom_call_target="tpu_custom_call" | custom-call | flops 49999998976 | bytes 1000 | tf_op jit(solution)/shard_map/attend_back/pallas_call | solution.py:949
  104.7 2.3 %collective-permute-done.14.other_ref = bf16[384,1024]{1,0:T(8,128)(2,1)S(1)} collective-permute-done((bf16[384,1024]{1,0:T(8,128)(2,1)S(1)}, bf16[384,1024]{1,0:T(8,128)(2,1)S(1)}, u32[]{:S(2)}, u32[]{:S(2)}) %collective-permute-start.14) | collective-permute-done | bytes 786464 | tf_op jit(solution)/shard_map/ppermute | solution.py:1510
  107.7 1.8 collective-permute-start.15
  111.3 3.1 %head_grads.1 = (bf16[16,24,768]{2,1,0:T(8,128)(2,1)S(1)}, bf16[16,24,768]{2,1,0:T(8,128)(2,1)S(1)}) custom-call(s32[4]{0:T(128)S(1)} %pad_add_fusion.2.scalars.unused.position, bf16[256,768]{1,0:T(8,128)(2,1)S(1)} %norm.1.refs_0_, bf16[256,768]{1,0:T(8,128)(2,1)S(1)} %collective-permute-done.refs_1_, bf16[256,768]{1,0:T(8,128)(2,1)S(1)} %collective-permute-done.1.refs_2_, ...), custom_call_target="tpu_custom_call" | custom-call | flops 1000 | bytes 1000 | tf_op jit(solution)/shard_map/head_grads/pallas_call | solution.py:575
  114.4 8.8 %collective-permute-done.20.refs_2_ = bf16[2,2,216,768]{3,2,1,0:T(8,128)(2,1)S(1)} collective-permute-done((bf16[2,2,216,768]{3,2,1,0:T(8,128)(2,1)S(1)}, bf16[2,2,216,768]{3,2,1,0:T(8,128)(2,1)S(1)}, u32[]{:S(2)}, u32[]{:S(2)}) %collective-permute-start.20) | collective-permute-done | bytes 1327136 | tf_op jit(solution)/shard_map/ppermute | solution.py:1514
  127.6 7.2 %collective-permute-done.16.refs_2_ = bf16[576,256]{1,0:T(8,128)(2,1)S(1)} collective-permute-done((bf16[576,256]{1,0:T(8,128)(2,1)S(1)}, bf16[576,256]{1,0:T(8,128)(2,1)S(1)}, u32[]{:S(2)}, u32[]{:S(2)}) %collective-permute-start.16) | collective-permute-done | bytes 294944 | tf_op jit(solution)/shard_map/ppermute | solution.py:1506
  136.0 5.7 %collective-permute-done.22.refs_1_ = bf16[2,216,768]{2,1,0:T(8,128)(2,1)S(1)} collective-permute-done((bf16[2,216,768]{2,1,0:T(8,128)(2,1)S(1)}, bf16[2,216,768]{2,1,0:T(8,128)(2,1)S(1)}, u32[]{:S(2)}, u32[]{:S(2)}) %collective-permute-start.22) | collective-permute-done | bytes 663584 | tf_op jit(solution)/shard_map/ppermute | solution.py:1514
  143.2 3.1 %collective-permute-start.25 = (bf16[216,768]{1,0:T(8,128)(2,1)S(1)}, bf16[216,768]{1,0:T(8,128)(2,1)S(1)}, u32[]{:S(2)}, u32[]{:S(2)}) collective-permute-start(bf16[216,768]{1,0:T(8,128)(2,1)S(1)} %get-tuple-element.270), channel_id=1, source_target_pairs={{0,4},{1,5},{2,6},{3,7},{4,0},{5,1},{6,2},{7,3},{8,12},{9,13},{10,... | collective-permute-start | bytes 995336 | tf_op jit(solution)/shard_map/ppermute | solution.py:1506
  151.2 2.3 %collective-permute-done.28.refs_2_ = bf16[2,2,24,768]{3,2,1,0:T(8,128)(2,1)S(1)} collective-permute-done((bf16[2,2,24,768]{3,2,1,0:T(8,128)(2,1)S(1)}, bf16[2,2,24,768]{3,2,1,0:T(8,128)(2,1)S(1)}, u32[]{:S(2)}, u32[]{:S(2)}) %collective-permute-start.28) | collective-permute-done | bytes 147488 | tf_op jit(solution)/shard_map/ppermute | solution.py:1514
  157.7 1.6 collective-permute-done.30.refs_1_
  161.5 2.0 %collective-permute-start.33 = (bf16[24,768]{1,0:T(8,128)(2,1)S(1)}, bf16[24,768]{1,0:T(8,128)(2,1)S(1)}, u32[]{:S(2)}, u32[]{:S(2)}) collective-permute-start(bf16[24,768]{1,0:T(8,128)(2,1)S(1)} %get-tuple-element.284), channel_id=1, source_target_pairs={{0,4},{1,5},{2,6},{3,7},{4,0},{5,1},{6,2},{7,3},{8,12},{9,13},{10,... | collective-permute-start | bytes 110600 | tf_op jit(solution)/shard_map/ppermute | solution.py:1506
  163.5 4.7 %collective-permute-done.32.refs_5_ = bf16[24,768]{1,0:T(8,128)(2,1)S(1)} collective-permute-done((bf16[24,768]{1,0:T(8,128)(2,1)S(1)}, bf16[24,768]{1,0:T(8,128)(2,1)S(1)}, u32[]{:S(2)}, u32[]{:S(2)}) %collective-permute-start.32) | collective-permute-done | bytes 36896 | tf_op jit(solution)/shard_map/ppermute | solution.py:1506
  168.8 3.2 %final.1 = bf16[256,768]{1,0:T(8,128)(2,1)} custom-call(s32[4]{0:T(128)S(1)} %pad_add_fusion.2.scalars.unused.position, bf16[576,256]{1,0:T(8,128)(2,1)S(1)} %get-tuple-element.255.refs_4_.refs_0_, bf16[576,256]{1,0:T(8,128)(2,1)S(1)} %collective-permute-done.15.refs_1_, bf16[576,256]{1,0:T(8,128)(2,1)S(1)} %collective-permute-done.16.refs_2_, ...), custom_call_target="tpu_custom_call" | custom-call | flops 1000 | bytes 1000 | tf_op jit(solution)/shard_map/final/pallas_call | solution.py:575
  172.0 4.0 %collective-permute-done.33.refs_6_ = bf16[24,768]{1,0:T(8,128)(2,1)S(1)} collective-permute-done((bf16[24,768]{1,0:T(8,128)(2,1)S(1)}, bf16[24,768]{1,0:T(8,128)(2,1)S(1)}, u32[]{:S(2)}, u32[]{:S(2)}) %collective-permute-start.33) | collective-permute-done | bytes 36896 | tf_op jit(solution)/shard_map/ppermute | solution.py:1506
  176.5 1.6 finish.1
  (114 shorter events, 46.7 us)
Async XLA Ops:
  2.7 18.9 %collective-permute-start = (bf16[256,768]{1,0:T(8,128)(2,1)S(1)}, bf16[256,768]{1,0:T(8,128)(2,1)S(1)}, u32[]{:S(2)}, u32[]{:S(2)}) collective-permute-start(bf16[256,768]{1,0:T(8,128)(2,1)S(1)} %norm.1.refs_0_), channel_id=1, source_target_pairs={{0,2},{1,3},{2,4},{3,5},{4,6},{5,7},{6,0},{7,1},{8,10},{9,11},{10,... | collective-permute-start | bytes 1179656 | tf_op jit(solution)/shard_map/ppermute | solution.py:1506
  5.8 19.0 %collective-permute-start.1 = (bf16[256,768]{1,0:T(8,128)(2,1)S(1)}, bf16[256,768]{1,0:T(8,128)(2,1)S(1)}, u32[]{:S(2)}, u32[]{:S(2)}) collective-permute-start(bf16[256,768]{1,0:T(8,128)(2,1)S(1)} %norm.1.refs_0_), channel_id=1, source_target_pairs={{0,6},{1,7},{2,0},{3,1},{4,2},{5,3},{6,4},{7,5},{8,14},{9,15},{10,... | collective-permute-start | bytes 1179656 | tf_op jit(solution)/shard_map/ppermute | solution.py:1506
  7.9 18.9 %collective-permute-start.2 = (bf16[256,768]{1,0:T(8,128)(2,1)S(1)}, bf16[256,768]{1,0:T(8,128)(2,1)S(1)}, u32[]{:S(2)}, u32[]{:S(2)}) collective-permute-start(bf16[256,768]{1,0:T(8,128)(2,1)S(1)} %norm.1.refs_0_), channel_id=1, source_target_pairs={{0,1},{1,0},{2,3},{3,2},{4,5},{5,4},{6,7},{7,6},{8,9},{9,8},{10,11... | collective-permute-start | bytes 1179656 | tf_op jit(solution)/shard_map/ppermute | solution.py:1510
  21.6 5.2 %collective-permute-start.3 = (bf16[256,768]{1,0:T(8,128)(2,1)S(1)}, bf16[256,768]{1,0:T(8,128)(2,1)S(1)}, u32[]{:S(2)}, u32[]{:S(2)}) collective-permute-start(bf16[256,768]{1,0:T(8,128)(2,1)S(1)} %collective-permute-done.refs_1_), channel_id=1, source_target_pairs={{0,1},{1,0},{2,3},{3,2},{4,5},{5,4},{6,7},{7,6},{8,9},{9,8},{10,11... | collective-permute-start | bytes 1179656 | tf_op jit(solution)/shard_map/ppermute | solution.py:1510
  24.8 13.4 %collective-permute-start.5 = (bf16[256,768]{1,0:T(8,128)(2,1)S(1)}, bf16[256,768]{1,0:T(8,128)(2,1)S(1)}, u32[]{:S(2)}, u32[]{:S(2)}) collective-permute-start(bf16[256,768]{1,0:T(8,128)(2,1)S(1)} %collective-permute-done.1.refs_2_), channel_id=1, source_target_pairs={{2,0},{3,1},{4,2},{5,3},{10,8},{11,9},{12,10},{13,11},{18,16},{19,... | collective-permute-start | bytes 1179656 | tf_op jit(solution)/shard_map/ppermute | solution.py:1669
  26.1 12.1 %collective-permute-start.6 = (bf16[256,768]{1,0:T(8,128)(2,1)S(1)}, bf16[256,768]{1,0:T(8,128)(2,1)S(1)}, u32[]{:S(2)}, u32[]{:S(2)}) collective-permute-start(bf16[256,768]{1,0:T(8,128)(2,1)S(1)} %collective-permute-done.refs_1_), channel_id=1, source_target_pairs={{2,4},{3,5},{4,6},{5,7},{10,12},{11,13},{12,14},{13,15},{18,20},{1... | collective-permute-start | bytes 1179656 | tf_op jit(solution)/shard_map/ppermute | solution.py:1669
  47.7 9.9 %collective-permute-start.10 = (bf16[192,256]{1,0:T(8,128)(2,1)S(1)}, bf16[192,256]{1,0:T(8,128)(2,1)S(1)}, u32[]{:S(2)}, u32[]{:S(2)}) collective-permute-start(bf16[192,256]{1,0:T(8,128)(2,1)S(1)} %get-tuple-element.184), channel_id=1, source_target_pairs={{0,2},{1,3},{2,4},{3,5},{4,6},{5,7},{6,0},{7,1},{8,10},{9,11},{10,... | collective-permute-start | bytes 294920 | tf_op jit(solution)/shard_map/ppermute | solution.py:1506
  50.1 7.5 %collective-permute-start.8 = (bf16[192,256]{1,0:T(8,128)(2,1)S(1)}, bf16[192,256]{1,0:T(8,128)(2,1)S(1)}, u32[]{:S(2)}, u32[]{:S(2)}) collective-permute-start(bf16[192,256]{1,0:T(8,128)(2,1)S(1)} %get-tuple-element.182), channel_id=1, source_target_pairs={{0,6},{1,7},{2,0},{3,1},{4,2},{5,3},{6,4},{7,5},{8,14},{9,15},{10,... | collective-permute-start | bytes 294920 | tf_op jit(solution)/shard_map/ppermute | solution.py:1506
  51.6 9.1 %collective-permute-start.9 = (bf16[192,256]{1,0:T(8,128)(2,1)S(1)}, bf16[192,256]{1,0:T(8,128)(2,1)S(1)}, u32[]{:S(2)}, u32[]{:S(2)}) collective-permute-start(bf16[192,256]{1,0:T(8,128)(2,1)S(1)} %get-tuple-element.183), channel_id=1, source_target_pairs={{0,4},{1,5},{2,6},{3,7},{4,0},{5,1},{6,2},{7,3},{8,12},{9,13},{10,... | collective-permute-start | bytes 294920 | tf_op jit(solution)/shard_map/ppermute | solution.py:1506
  80.8 8.8 %collective-permute-start.19 = (bf16[16,120,768]{2,1,0:T(8,128)(2,1)S(1)}, bf16[16,120,768]{2,1,0:T(8,128)(2,1)S(1)}, u32[]{:S(2)}, u32[]{:S(2)}) collective-permute-start(bf16[16,120,768]{2,1,0:T(8,128)(2,1)S(1)} %get-tuple-element.233), channel_id=1, source_target_pairs={{0,1},{1,0},{2,3},{3,2},{4,5},{5,4},{6,7},{7,6},{8,9},{9,8},{10,11... | collective-permute-start | bytes 8847368 | tf_op jit(solution)/shard_map/ppermute | solution.py:1510
  83.7 5.9 %collective-permute-start.18 = (bf16[16,96,768]{2,1,0:T(8,128)(2,1)S(1)}, bf16[16,96,768]{2,1,0:T(8,128)(2,1)S(1)}, u32[]{:S(2)}, u32[]{:S(2)}) collective-permute-start(bf16[16,96,768]{2,1,0:T(8,128)(2,1)S(1)} %get-tuple-element.231), channel_id=1, source_target_pairs={{0,1},{1,0},{2,3},{3,2},{4,5},{5,4},{6,7},{7,6},{8,9},{9,8},{10,11... | collective-permute-start | bytes 7077896 | tf_op jit(solution)/shard_map/ppermute | solution.py:1510
  84.3 9.6 %collective-permute-start.11 = (bf16[192,256]{1,0:T(8,128)(2,1)S(1)}, bf16[192,256]{1,0:T(8,128)(2,1)S(1)}, u32[]{:S(2)}, u32[]{:S(2)}) collective-permute-start(bf16[192,256]{1,0:T(8,128)(2,1)S(1)} %get-tuple-element.219), channel_id=1, source_target_pairs={{0,2},{1,3},{2,4},{3,5},{4,6},{5,7},{6,0},{7,1},{8,10},{9,11},{10,... | collective-permute-start | bytes 294920 | tf_op jit(solution)/shard_map/ppermute | solution.py:1506
  84.3 9.6 %collective-permute-start.12 = (bf16[192,256]{1,0:T(8,128)(2,1)S(1)}, bf16[192,256]{1,0:T(8,128)(2,1)S(1)}, u32[]{:S(2)}, u32[]{:S(2)}) collective-permute-start(bf16[192,256]{1,0:T(8,128)(2,1)S(1)} %get-tuple-element.220), channel_id=1, source_target_pairs={{0,6},{1,7},{2,0},{3,1},{4,2},{5,3},{6,4},{7,5},{8,14},{9,15},{10,... | collective-permute-start | bytes 294920 | tf_op jit(solution)/shard_map/ppermute | solution.py:1506
  88.1 7.9 %collective-permute-start.13 = (bf16[192,256]{1,0:T(8,128)(2,1)S(1)}, bf16[192,256]{1,0:T(8,128)(2,1)S(1)}, u32[]{:S(2)}, u32[]{:S(2)}) collective-permute-start(bf16[192,256]{1,0:T(8,128)(2,1)S(1)} %get-tuple-element.221), channel_id=1, source_target_pairs={{0,4},{1,5},{2,6},{3,7},{4,0},{5,1},{6,2},{7,3},{8,12},{9,13},{10,... | collective-permute-start | bytes 294920 | tf_op jit(solution)/shard_map/ppermute | solution.py:1506
  90.8 32.4 %collective-permute-start.20 = (bf16[2,2,216,768]{3,2,1,0:T(8,128)(2,1)S(1)}, bf16[2,2,216,768]{3,2,1,0:T(8,128)(2,1)S(1)}, u32[]{:S(2)}, u32[]{:S(2)}) collective-permute-start(bf16[2,2,216,768]{3,2,1,0:T(8,128)(2,1)S(1)} %get-tuple-element.234), channel_id=1, source_target_pairs={{0,8},{8,0},{16,24},{24,16},{1,9},{9,1},{17,25},{25,17},{2,10},{10... | collective-permute-start | bytes 3981320 | tf_op jit(solution)/shard_map/ppermute | solution.py:1514
  93.8 30.9 %collective-permute-start.21 = (bf16[2,2,216,768]{3,2,1,0:T(8,128)(2,1)S(1)}, bf16[2,2,216,768]{3,2,1,0:T(8,128)(2,1)S(1)}, u32[]{:S(2)}, u32[]{:S(2)}) collective-permute-start(bf16[2,2,216,768]{3,2,1,0:T(8,128)(2,1)S(1)} %get-tuple-element.235), channel_id=1, source_target_pairs={{0,16},{8,24},{16,0},{24,8},{1,17},{9,25},{17,1},{25,9},{2,18},{10... | collective-permute-start | bytes 3981320 | tf_op jit(solution)/shard_map/ppermute | solution.py:1514
  107.7 19.9 %collective-permute-start.15 = (bf16[576,256]{1,0:T(8,128)(2,1)S(1)}, bf16[576,256]{1,0:T(8,128)(2,1)S(1)}, u32[]{:S(2)}, u32[]{:S(2)}) collective-permute-start(bf16[576,256]{1,0:T(8,128)(2,1)S(1)} %get-tuple-element.243.refs_5_), channel_id=1, source_target_pairs={{0,6},{1,7},{2,0},{3,1},{4,2},{5,3},{6,4},{7,5},{8,14},{9,15},{10,... | collective-permute-start | bytes 884744 | tf_op jit(solution)/shard_map/ppermute | solution.py:1506
  109.5 25.4 %collective-permute-start.16 = (bf16[576,256]{1,0:T(8,128)(2,1)S(1)}, bf16[576,256]{1,0:T(8,128)(2,1)S(1)}, u32[]{:S(2)}, u32[]{:S(2)}) collective-permute-start(bf16[576,256]{1,0:T(8,128)(2,1)S(1)} %get-tuple-element.245.refs_7_), channel_id=1, source_target_pairs={{0,4},{1,5},{2,6},{3,7},{4,0},{5,1},{6,2},{7,3},{8,12},{9,13},{10,... | collective-permute-start | bytes 884744 | tf_op jit(solution)/shard_map/ppermute | solution.py:1506
  109.5 25.4 %collective-permute-start.17 = (bf16[576,256]{1,0:T(8,128)(2,1)S(1)}, bf16[576,256]{1,0:T(8,128)(2,1)S(1)}, u32[]{:S(2)}, u32[]{:S(2)}) collective-permute-start(bf16[576,256]{1,0:T(8,128)(2,1)S(1)} %get-tuple-element.244.refs_6_), channel_id=1, source_target_pairs={{0,2},{1,3},{2,4},{3,5},{4,6},{5,7},{6,0},{7,1},{8,10},{9,11},{10,... | collective-permute-start | bytes 884744 | tf_op jit(solution)/shard_map/ppermute | solution.py:1506
  125.8 15.9 %collective-permute-start.22 = (bf16[2,216,768]{2,1,0:T(8,128)(2,1)S(1)}, bf16[2,216,768]{2,1,0:T(8,128)(2,1)S(1)}, u32[]{:S(2)}, u32[]{:S(2)}) collective-permute-start(bf16[2,216,768]{2,1,0:T(8,128)(2,1)S(1)} %get-tuple-element.265), channel_id=1, source_target_pairs={{0,16},{8,24},{16,0},{24,8},{1,17},{9,25},{17,1},{25,9},{2,18},{10... | collective-permute-start | bytes 1990664 | tf_op jit(solution)/shard_map/ppermute | solution.py:1514
  126.2 15.7 %collective-permute-start.23 = (bf16[2,216,768]{2,1,0:T(8,128)(2,1)S(1)}, bf16[2,216,768]{2,1,0:T(8,128)(2,1)S(1)}, u32[]{:S(2)}, u32[]{:S(2)}) collective-permute-start(bf16[2,216,768]{2,1,0:T(8,128)(2,1)S(1)} %get-tuple-element.267), channel_id=1, source_target_pairs={{0,8},{8,0},{16,24},{24,16},{1,9},{9,1},{17,25},{25,17},{2,10},{10... | collective-permute-start | bytes 1990664 | tf_op jit(solution)/shard_map/ppermute | solution.py:1514
  134.8 12.8 %collective-permute-start.27 = (bf16[16,24,768]{2,1,0:T(8,128)(2,1)S(1)}, bf16[16,24,768]{2,1,0:T(8,128)(2,1)S(1)}, u32[]{:S(2)}, u32[]{:S(2)}) collective-permute-start(bf16[16,24,768]{2,1,0:T(8,128)(2,1)S(1)} %get-tuple-element.273), channel_id=1, source_target_pairs={{0,1},{1,0},{2,3},{3,2},{4,5},{5,4},{6,7},{7,6},{8,9},{9,8},{10,11... | collective-permute-start | bytes 1769480 | tf_op jit(solution)/shard_map/ppermute | solution.py:1510
  143.2 33.3 %collective-permute-start.24 = (bf16[216,768]{1,0:T(8,128)(2,1)S(1)}, bf16[216,768]{1,0:T(8,128)(2,1)S(1)}, u32[]{:S(2)}, u32[]{:S(2)}) collective-permute-start(bf16[216,768]{1,0:T(8,128)(2,1)S(1)} %get-tuple-element.269), channel_id=1, source_target_pairs={{0,2},{1,3},{2,4},{3,5},{4,6},{5,7},{6,0},{7,1},{8,10},{9,11},{10,... | collective-permute-start | bytes 995336 | tf_op jit(solution)/shard_map/ppermute | solution.py:1506
  143.2 33.2 %collective-permute-start.25 = (bf16[216,768]{1,0:T(8,128)(2,1)S(1)}, bf16[216,768]{1,0:T(8,128)(2,1)S(1)}, u32[]{:S(2)}, u32[]{:S(2)}) collective-permute-start(bf16[216,768]{1,0:T(8,128)(2,1)S(1)} %get-tuple-element.270), channel_id=1, source_target_pairs={{0,4},{1,5},{2,6},{3,7},{4,0},{5,1},{6,2},{7,3},{8,12},{9,13},{10,... | collective-permute-start | bytes 995336 | tf_op jit(solution)/shard_map/ppermute | solution.py:1506
  146.3 30.1 %collective-permute-start.26 = (bf16[216,768]{1,0:T(8,128)(2,1)S(1)}, bf16[216,768]{1,0:T(8,128)(2,1)S(1)}, u32[]{:S(2)}, u32[]{:S(2)}) collective-permute-start(bf16[216,768]{1,0:T(8,128)(2,1)S(1)} %get-tuple-element.271), channel_id=1, source_target_pairs={{0,6},{1,7},{2,0},{3,1},{4,2},{5,3},{6,4},{7,5},{8,14},{9,15},{10,... | collective-permute-start | bytes 995336 | tf_op jit(solution)/shard_map/ppermute | solution.py:1506
  148.2 5.2 %collective-permute-start.28 = (bf16[2,2,24,768]{3,2,1,0:T(8,128)(2,1)S(1)}, bf16[2,2,24,768]{3,2,1,0:T(8,128)(2,1)S(1)}, u32[]{:S(2)}, u32[]{:S(2)}) collective-permute-start(bf16[2,2,24,768]{3,2,1,0:T(8,128)(2,1)S(1)} %get-tuple-element.276), channel_id=1, source_target_pairs={{0,8},{8,0},{16,24},{24,16},{1,9},{9,1},{17,25},{25,17},{2,10},{10... | collective-permute-start | bytes 442376 | tf_op jit(solution)/shard_map/ppermute | solution.py:1514
  149.1 5.1 %collective-permute-start.29 = (bf16[2,2,24,768]{3,2,1,0:T(8,128)(2,1)S(1)}, bf16[2,2,24,768]{3,2,1,0:T(8,128)(2,1)S(1)}, u32[]{:S(2)}, u32[]{:S(2)}) collective-permute-start(bf16[2,2,24,768]{3,2,1,0:T(8,128)(2,1)S(1)} %get-tuple-element.277), channel_id=1, source_target_pairs={{0,16},{8,24},{16,0},{24,8},{1,17},{9,25},{17,1},{25,9},{2,18},{10... | collective-permute-start | bytes 442376 | tf_op jit(solution)/shard_map/ppermute | solution.py:1514
  154.9 4.4 %collective-permute-start.30 = (bf16[2,24,768]{2,1,0:T(8,128)(2,1)S(1)}, bf16[2,24,768]{2,1,0:T(8,128)(2,1)S(1)}, u32[]{:S(2)}, u32[]{:S(2)}) collective-permute-start(bf16[2,24,768]{2,1,0:T(8,128)(2,1)S(1)} %get-tuple-element.279), channel_id=1, source_target_pairs={{0,16},{8,24},{16,0},{24,8},{1,17},{9,25},{17,1},{25,9},{2,18},{10... | collective-permute-start | bytes 221192 | tf_op jit(solution)/shard_map/ppermute | solution.py:1514
  156.4 4.4 %collective-permute-start.31 = (bf16[2,24,768]{2,1,0:T(8,128)(2,1)S(1)}, bf16[2,24,768]{2,1,0:T(8,128)(2,1)S(1)}, u32[]{:S(2)}, u32[]{:S(2)}) collective-permute-start(bf16[2,24,768]{2,1,0:T(8,128)(2,1)S(1)} %get-tuple-element.281), channel_id=1, source_target_pairs={{0,8},{8,0},{16,24},{24,16},{1,9},{9,1},{17,25},{25,17},{2,10},{10... | collective-permute-start | bytes 221192 | tf_op jit(solution)/shard_map/ppermute | solution.py:1514
  161.3 6.9 %collective-permute-start.32 = (bf16[24,768]{1,0:T(8,128)(2,1)S(1)}, bf16[24,768]{1,0:T(8,128)(2,1)S(1)}, u32[]{:S(2)}, u32[]{:S(2)}) collective-permute-start(bf16[24,768]{1,0:T(8,128)(2,1)S(1)} %get-tuple-element.283), channel_id=1, source_target_pairs={{0,2},{1,3},{2,4},{3,5},{4,6},{5,7},{6,0},{7,1},{8,10},{9,11},{10,... | collective-permute-start | bytes 110600 | tf_op jit(solution)/shard_map/ppermute | solution.py:1506
  161.5 14.5 %collective-permute-start.33 = (bf16[24,768]{1,0:T(8,128)(2,1)S(1)}, bf16[24,768]{1,0:T(8,128)(2,1)S(1)}, u32[]{:S(2)}, u32[]{:S(2)}) collective-permute-start(bf16[24,768]{1,0:T(8,128)(2,1)S(1)} %get-tuple-element.284), channel_id=1, source_target_pairs={{0,4},{1,5},{2,6},{3,7},{4,0},{5,1},{6,2},{7,3},{8,12},{9,13},{10,... | collective-permute-start | bytes 110600 | tf_op jit(solution)/shard_map/ppermute | solution.py:1506
  168.3 8.2 %collective-permute-start.34 = (bf16[24,768]{1,0:T(8,128)(2,1)S(1)}, bf16[24,768]{1,0:T(8,128)(2,1)S(1)}, u32[]{:S(2)}, u32[]{:S(2)}) collective-permute-start(bf16[24,768]{1,0:T(8,128)(2,1)S(1)} %get-tuple-element.285), channel_id=1, source_target_pairs={{0,6},{1,7},{2,0},{3,1},{4,2},{5,3},{6,4},{7,5},{8,14},{9,15},{10,... | collective-permute-start | bytes 110600 | tf_op jit(solution)/shard_map/ppermute | solution.py:1506
  (17 other events, 171.8 us)

commit v8 on v7

--- a/solution.py
+++ b/solution.py
@@ -607,9 +607,8 @@
 
 
 def norm_kernel(unused, rows_ref, gain_ref, out_ref):
-    out_ref[...] = (norm_parts(rows_ref[...].astype(jnp.float32))[0] * gain_ref[...]).astype(
-        jnp.bfloat16
-    )
+    hat = norm_parts(rows_ref[...].astype(jnp.float32))[0]
+    out_ref[...] = (hat * gain_ref[...].reshape(1, -1)).astype(jnp.bfloat16)
 
 
 def column_choice(chip, heads, size, lanes, width, transposed):
@@ -1637,7 +1636,11 @@
     gains = wide(heads_in[0][:8, -128:])
     for part in heads_in[1:]:
         gains = gains + wide(part[:8, -128:])
-    gains_ref[...] = gains * factor
+    gains = gains * factor
+    part = gains_ref.shape[0]
+    for line in range(-(-part // 128)):
+        stop = min(part, 128 * (line + 1))
+        gains_ref[128 * line : stop] = gains[line, : stop - 128 * line]
     for step in range(chips):
         heads_ref[lax.rem(chip - step + chips, chips)] = wide(heads_in[step][:, : 3 * share])
     for index, target in enumerate((query_ref, key_ref, value_ref)):
@@ -1647,13 +1650,13 @@
         lay_flat(target, values * factor, 0, pieces)
 
 
-def finish(scalars, arrived, hidden, parts, per, share, factor):
+def finish(scalars, arrived, hidden, gains_part, per, share, factor):
     chips, width = len(arrived) // 2, arrived[0].shape[1]
     square = jax.ShapeDtypeStruct((per * width // 128, 128), jnp.float32)
     large = jax.ShapeDtypeStruct((per * hidden // 128, 128), jnp.float32)
     return call_whole(
         partial(finish_kernel, chips, per, share, factor),
-        [large, large, square, square, square, square, jax.ShapeDtypeStruct((8, 128), jnp.float32)],
+        [large, large, square, square, square, square, jax.ShapeDtypeStruct((gains_part,), jnp.float32)],
         "finish",
         scalars,
         *arrived,
@@ -1708,7 +1711,7 @@
         "norm",
         jnp.zeros((1,), jnp.int32),
         tokens,
-        gain_attend[None, :],
+        gain_attend,
         ins=False,
     )[0]
     behind, ahead, across = gathered(normed_b)
@@ -1840,7 +1843,7 @@
     )
     arrived += [stage[0]] + [chip_shift(stage[step], step) for step in range(1, chips)]
     down, up, out, query, key, value, gains_part = finish(
-        place, arrived, hidden, parts, per, share, factor
+        place, arrived, hidden, gains_share, per, share, factor
     )
     return (
         result,
@@ -1851,7 +1854,7 @@
         out.reshape(-1),
         up.reshape(-1),
         down.reshape(-1),
-        gains_part.reshape(-1)[:gains_share],
+        gains_part,
     )
 
 

time: 181 us -> 180 us (level)
  starting transfers between devices: 37.2 us -> 35.1 us
  waiting for transfers between devices: 60 us -> 62.1 us
    ppermute x17, waiting for transfers between devices: 24.2 us -> 34 us  [chip_shift(): lax.ppermute(value, 'seq', [(i, (i + 2 * steps) % count) for i in range(c...]
    ppermute x8, waiting for transfers between devices: 22.3 us -> 14.8 us  [row_swap(): lax.ppermute(value, 'row', [(i, i ^ bit) for i in range(lax.axis_size('ro...]
    ppermute x17, starting transfers between devices: 23.9 us -> 21.6 us  [chip_shift(): lax.ppermute(value, 'seq', [(i, (i + 2 * steps) % count) for i in range(c...]
    unnamed x29 -> x31, local copies, waits for them, and re-layouts: 3.59 us -> 4.37 us
  transfers between devices with their start and end apart: 35 -> 35, of which waited for: 19 -> 20; matrix products, arithmetic and copies ran while one was open for 4% -> 5% of each run, Pallas kernels for 21% -> 22%
where the time goes in v8:
time: 180 us; the launch traced here: 179 us
  Pallas kernels  68.3 us (38%)
  waiting for transfers between devices  62.1 us (34%)
  starting transfers between devices  35.1 us (20%)
  local copies, waits for them, and re-layouts  9.18 us (5%)
  other arithmetic  3.56 us (2%)
    ppermute x17, waiting for transfers between devices, chip_shift(): lax.ppermute(value, 'seq', [(i, (i + 2 * steps) % count) for i in range(c...  34 us
    pallas_call x15, Pallas kernels, call_whole(): pl.pallas_call(kernel, grid_spec=pltpu.PrefetchScalarGridSpec(num_scalar_...  22.6 us
    ppermute x17, starting transfers between devices, chip_shift(): lax.ppermute(value, 'seq', [(i, (i + 2 * steps) % count) for i in range(c...  21.6 us
    pallas_call x1, Pallas kernels, middle(): pl.pallas_call(partial(middle_kernel, chips, tiles), grid_spec=pltpu.Pref...  15.2 us
    ppermute x8, waiting for transfers between devices, row_swap(): lax.ppermute(value, 'row', [(i, i ^ bit) for i in range(lax.axis_size('ro...  14.8 us
    pallas_call x1, Pallas kernels, attend_back(): pl.pallas_call(partial(attend_back_kernel, heads, block, steps, key_block...  9.33 us
    ppermute x8, starting transfers between devices, row_swap(): lax.ppermute(value, 'row', [(i, i ^ bit) for i in range(lax.axis_size('ro...  8.73 us
    ppermute x2, waiting for transfers between devices, gathered(): across = (lax.ppermute(ahead, 'seq', down), lax.ppermute(behind, 'seq', up))  8.11 us
  transfers between devices with their start and end apart: 35, of which 20 were waited for; matrix products, arithmetic and copies ran while one was open for 5% of the time, Pallas kernels for 22%

profile of v8, /device:TPU:0, one launch (start us, length us, event | category | flops | bytes accessed | tf_op | source)
XLA Modules:
  0.0 179.3 jit_solution(2071059821958911003)
XLA Ops:
  2.7 3.1 %collective-permute-start = (bf16[256,768]{1,0:T(8,128)(2,1)S(1)}, bf16[256,768]{1,0:T(8,128)(2,1)S(1)}, u32[]{:S(2)}, u32[]{:S(2)}) collective-permute-start(bf16[256,768]{1,0:T(8,128)(2,1)S(1)} %norm.1.refs_0_), channel_id=1, source_target_pairs={{0,2},{1,3},{2,4},{3,5},{4,6},{5,7},{6,0},{7,1},{8,10},{9,11},{10,... | collective-permute-start | bytes 1179656 | tf_op jit(solution)/shard_map/ppermute | solution.py:1505
  5.8 2.1 %collective-permute-start.1 = (bf16[256,768]{1,0:T(8,128)(2,1)S(1)}, bf16[256,768]{1,0:T(8,128)(2,1)S(1)}, u32[]{:S(2)}, u32[]{:S(2)}) collective-permute-start(bf16[256,768]{1,0:T(8,128)(2,1)S(1)} %norm.1.refs_0_), channel_id=1, source_target_pairs={{0,6},{1,7},{2,0},{3,1},{4,2},{5,3},{6,4},{7,5},{8,14},{9,15},{10,... | collective-permute-start | bytes 1179656 | tf_op jit(solution)/shard_map/ppermute | solution.py:1505
  18.8 3.5 %choose.1 = (bf16[384,768]{1,0:T(8,128)(2,1)S(1)}, bf16[768,384]{1,0:T(8,128)(2,1)S(1)}, bf16[192,768]{1,0:T(8,128)(2,1)S(1)}, bf16[192,768]{1,0:T(8,128)(2,1)S(...) custom-call(s32[4]{0:T(128)S(1)} %pad_add_fusion.2.scalars.unused.position, bf16[768,768]{1,0:T(8,128)(2,1)S(1)} %copy-done, ...), custom_call_target="tpu_custom_call" | custom-call | flops 1000 | bytes 1000 | tf_op jit(solution)/shard_map/choose/pallas_call | solution.py:575
  22.9 2.0 %collective-permute-done.1.refs_2_ = bf16[256,768]{1,0:T(8,128)(2,1)S(1)} collective-permute-done((bf16[256,768]{1,0:T(8,128)(2,1)S(1)}, bf16[256,768]{1,0:T(8,128)(2,1)S(1)}, u32[]{:S(2)}, u32[]{:S(2)}) %collective-permute-start.1) | collective-permute-done | bytes 393248 | tf_op jit(solution)/shard_map/ppermute | solution.py:1505
  26.8 3.3 %project.2 = (bf16[384,1024]{1,0:T(8,128)(2,1)S(1)}, bf16[2048,384]{1,0:T(8,128)(2,1)S(1)}, bf16[192,2048]{1,0:T(8,128)(2,1)S(1)}) custom-call(s32[7]{0:T(128)S(1)} %pad_add_fusion.meta, bf16[256,768]{1,0:T(8,128)(2,1)S(1)} %norm.1.refs_0_, bf16[256,768]{1,0:T(8,128)(2,1)S(1)} %collective-permute-done.refs_1_, ...), custom_call_target="tpu_custom_call" | custom-call | flops 1000 | bytes 1000 | tf_op jit(solution)/shard_map/project/pallas_call | solution.py:697
  30.1 8.1 %collective-permute-done.5 = bf16[256,768]{1,0:T(8,128)(2,1)S(1)} collective-permute-done((bf16[256,768]{1,0:T(8,128)(2,1)S(1)}, bf16[256,768]{1,0:T(8,128)(2,1)S(1)}, u32[]{:S(2)}, u32[]{:S(2)}) %collective-permute-start.5) | collective-permute-done | bytes 393248 | tf_op jit(solution)/shard_map/ppermute | solution.py:1672
  38.4 1.7 collective-permute-done.7.refs_1_.refs_7_
  41.6 6.7 %attend.3 = (f32[192,256]{1,0:T(8,128)S(1)}, f32[192,256]{1,0:T(8,128)S(1)}, f32[192,256]{1,0:T(8,128)S(1)}, f32[3,1,256]{2,1,0:T(1,128)S(1)}, f32[3,1,256]{2,1,...) custom-call(s32[20]{0:T(128)S(1)} %concatenate.11.meta, ...), custom_call_target="tpu_custom_call" | custom-call | flops 1000 | bytes 1000 | tf_op jit(solution)/shard_map/attend/pallas_call | solution.py:915
  49.6 2.6 %collective-permute-start.8 = (bf16[192,256]{1,0:T(8,128)(2,1)S(1)}, bf16[192,256]{1,0:T(8,128)(2,1)S(1)}, u32[]{:S(2)}, u32[]{:S(2)}) collective-permute-start(bf16[192,256]{1,0:T(8,128)(2,1)S(1)} %get-tuple-element.182), channel_id=1, source_target_pairs={{0,6},{1,7},{2,0},{3,1},{4,2},{5,3},{6,4},{7,5},{8,14},{9,15},{10,... | collective-permute-start | bytes 294920 | tf_op jit(solution)/shard_map/ppermute | solution.py:1505
  53.9 3.2 %project_back.1 = (bf16[192,2048]{1,0:T(8,128)(2,1)S(1)}, bf16[2048,384]{1,0:T(8,128)(2,1)S(1)}) custom-call(s32[4]{0:T(128)S(1)} %pad_add_fusion.2.scalars.unused.position, bf16[256,768]{1,0:T(8,128)(2,1)S(1)} %norm.1.refs_0_, bf16[256,768]{1,0:T(8,128)(2,1)S(1)} %collective-permute-done.refs_1_, bf16[256,768]{1,0:T(8,128)(2,1)S(1)} %collective-permute-done.1.refs_2_, ...), custom_call_target="tpu_custom_call" | custom-call | flops 1000 | bytes 1000 | tf_op jit(solution)/shard_map/project_back/pallas_call | solution.py:575
  57.3 4.8 %collective-permute-done.9.refs_2_ = bf16[192,256]{1,0:T(8,128)(2,1)S(1)} collective-permute-done((bf16[192,256]{1,0:T(8,128)(2,1)S(1)}, bf16[192,256]{1,0:T(8,128)(2,1)S(1)}, u32[]{:S(2)}, u32[]{:S(2)}) %collective-permute-start.9) | collective-permute-done | bytes 98336 | tf_op jit(solution)/shard_map/ppermute | solution.py:1505
  62.2 15.2 %middle.1 = (bf16[256,768]{1,0:T(8,128)(2,1)}, f32[256,768]{1,0:T(8,128)S(1)}, bf16[256,768]{1,0:T(8,128)(2,1)S(1)}, bf16[192,256]{1,0:T(8,128)(2,1)S(1)}, bf16[...) custom-call(s32[4]{0:T(128)S(1)} %pad_add_fusion.2.scalars.unused.po, ...), custom_call_target="tpu_custom_call" | custom-call | flops 1000 | bytes 1000 | tf_op jit(solution)/shard_map/middle/pallas_call | solution.py:1310
  77.3 4.5 %up_out_grad.1 = (bf16[16,120,768]{2,1,0:T(8,128)(2,1)S(1)}, bf16[16,120,768]{2,1,0:T(8,128)(2,1)S(1)}) custom-call(s32[4]{0:T(128)S(1)} %pad_add_fusion.2.scalars.unused.position, bf16[256,768]{1,0:T(8,128)(2,1)S(1)} %get-tuple-element.211.h2_ref, bf16[256,3072]{1,0:T(8,128)(2,1)S(1)} %get-tuple-element.212.pre_ref, ...), custom_call_target="tpu_custom_call" | custom-call | flops 1000 | bytes 1000 | tf_op jit(solution)/shard_map/up_out_grad/pallas_call | solution.py:1436
  82.0 2.8 %down_grad.1 = (bf16[16,96,768]{2,1,0:T(8,128)(2,1)S(1)}, bf16[16,96,768]{2,1,0:T(8,128)(2,1)S(1)}) custom-call(s32[4]{0:T(128)S(1)} %pad_add_fusion.2.scalars.unused.position, bf16[256,3072]{1,0:T(8,128)(2,1)S(1)} %get-tuple-element.229.bent_ref, bf16[256,768]{1,0:T(8,128)(2,1)S(1)} %copy-done.7), custom_call_target="tpu_custom_call" | custom-call | flops 1000 | bytes 1000 | tf_op jit(solution)/shard_map/down_grad/pallas_call | solution.py:1386
  85.3 3.8 %collective-permute-start.12 = (bf16[192,256]{1,0:T(8,128)(2,1)S(1)}, bf16[192,256]{1,0:T(8,128)(2,1)S(1)}, u32[]{:S(2)}, u32[]{:S(2)}) collective-permute-start(bf16[192,256]{1,0:T(8,128)(2,1)S(1)} %get-tuple-element.220), channel_id=1, source_target_pairs={{0,6},{1,7},{2,0},{3,1},{4,2},{5,3},{6,4},{7,5},{8,14},{9,15},{10,... | collective-permute-start | bytes 294920 | tf_op jit(solution)/shard_map/ppermute | solution.py:1505
  93.4 4.1 %collective-permute-done.13.refs_11_ = bf16[192,256]{1,0:T(8,128)(2,1)S(1)} collective-permute-done((bf16[192,256]{1,0:T(8,128)(2,1)S(1)}, bf16[192,256]{1,0:T(8,128)(2,1)S(1)}, u32[]{:S(2)}, u32[]{:S(2)}) %collective-permute-start.13) | collective-permute-done | bytes 98336 | tf_op jit(solution)/shard_map/ppermute | solution.py:1505
  97.5 9.3 %attend_back.1 = (bf16[192,1024]{1,0:T(8,128)(2,1)S(1)}, f32[384,1024]{1,0:T(8,128)S(1)}, bf16[384,1024]{1,0:T(8,128)(2,1)S(1)}) custom-call(s32[20]{0:T(128)S(1)} %concatenate.11.meta, s32[1,1024]{1,0:T(1,128)S(1)} %bitcast.44, bf16[384,1024]{1,0:T(8,128)(2,1)S(1)} %get-tuple-element.174.q_ref, bf16[2048,384]{1,0:T(8,128)(2,1)S(1)} %get-tuple-element.175.k_ref, ...), custom_call_target="tpu_custom_call" | custom-call | flops 49999998976 | bytes 1000 | tf_op jit(solution)/shard_map/attend_back/pallas_call | solution.py:948
  108.4 1.9 %collective-permute-done.14.other_ref = bf16[384,1024]{1,0:T(8,128)(2,1)S(1)} collective-permute-done((bf16[384,1024]{1,0:T(8,128)(2,1)S(1)}, bf16[384,1024]{1,0:T(8,128)(2,1)S(1)}, u32[]{:S(2)}, u32[]{:S(2)}) %collective-permute-start.14) | collective-permute-done | bytes 786464 | tf_op jit(solution)/shard_map/ppermute | solution.py:1509
  114.3 3.1 %head_grads.1 = (bf16[16,24,768]{2,1,0:T(8,128)(2,1)S(1)}, bf16[16,24,768]{2,1,0:T(8,128)(2,1)S(1)}) custom-call(s32[4]{0:T(128)S(1)} %pad_add_fusion.2.scalars.unused.position, bf16[256,768]{1,0:T(8,128)(2,1)S(1)} %norm.1.refs_0_, bf16[256,768]{1,0:T(8,128)(2,1)S(1)} %collective-permute-done.refs_1_, bf16[256,768]{1,0:T(8,128)(2,1)S(1)} %collective-permute-done.1.refs_2_, ...), custom_call_target="tpu_custom_call" | custom-call | flops 1000 | bytes 1000 | tf_op jit(solution)/shard_map/head_grads/pallas_call | solution.py:575
  117.3 5.7 %collective-permute-done.20.refs_2_ = bf16[2,2,216,768]{3,2,1,0:T(8,128)(2,1)S(1)} collective-permute-done((bf16[2,2,216,768]{3,2,1,0:T(8,128)(2,1)S(1)}, bf16[2,2,216,768]{3,2,1,0:T(8,128)(2,1)S(1)}, u32[]{:S(2)}, u32[]{:S(2)}) %collective-permute-start.20) | collective-permute-done | bytes 1327136 | tf_op jit(solution)/shard_map/ppermute | solution.py:1513
  126.3 11.6 %collective-permute-done.16.refs_2_ = bf16[576,256]{1,0:T(8,128)(2,1)S(1)} collective-permute-done((bf16[576,256]{1,0:T(8,128)(2,1)S(1)}, bf16[576,256]{1,0:T(8,128)(2,1)S(1)}, u32[]{:S(2)}, u32[]{:S(2)}) %collective-permute-start.16) | collective-permute-done | bytes 294944 | tf_op jit(solution)/shard_map/ppermute | solution.py:1505
  142.4 2.7 %collective-permute-start.25 = (bf16[216,768]{1,0:T(8,128)(2,1)S(1)}, bf16[216,768]{1,0:T(8,128)(2,1)S(1)}, u32[]{:S(2)}, u32[]{:S(2)}) collective-permute-start(bf16[216,768]{1,0:T(8,128)(2,1)S(1)} %get-tuple-element.270), channel_id=1, source_target_pairs={{0,4},{1,5},{2,6},{3,7},{4,0},{5,1},{6,2},{7,3},{8,12},{9,13},{10,... | collective-permute-start | bytes 995336 | tf_op jit(solution)/shard_map/ppermute | solution.py:1505
  150.5 1.9 %collective-permute-done.28.refs_2_ = bf16[2,2,24,768]{3,2,1,0:T(8,128)(2,1)S(1)} collective-permute-done((bf16[2,2,24,768]{3,2,1,0:T(8,128)(2,1)S(1)}, bf16[2,2,24,768]{3,2,1,0:T(8,128)(2,1)S(1)}, u32[]{:S(2)}, u32[]{:S(2)}) %collective-permute-start.28) | collective-permute-done | bytes 147488 | tf_op jit(solution)/shard_map/ppermute | solution.py:1513
  154.1 1.8 collective-permute-start.30
  156.3 2.2 %collective-permute-done.30.refs_1_ = bf16[2,24,768]{2,1,0:T(8,128)(2,1)S(1)} collective-permute-done((bf16[2,24,768]{2,1,0:T(8,128)(2,1)S(1)}, bf16[2,24,768]{2,1,0:T(8,128)(2,1)S(1)}, u32[]{:S(2)}, u32[]{:S(2)}) %collective-permute-start.30) | collective-permute-done | bytes 73760 | tf_op jit(solution)/shard_map/ppermute | solution.py:1513
  158.5 1.7 collective-permute-done.31.refs_3_
  161.5 1.7 collective-permute-start.33
  163.2 4.9 %collective-permute-done.32.refs_5_ = bf16[24,768]{1,0:T(8,128)(2,1)S(1)} collective-permute-done((bf16[24,768]{1,0:T(8,128)(2,1)S(1)}, bf16[24,768]{1,0:T(8,128)(2,1)S(1)}, u32[]{:S(2)}, u32[]{:S(2)}) %collective-permute-start.32) | collective-permute-done | bytes 36896 | tf_op jit(solution)/shard_map/ppermute | solution.py:1505
  168.1 3.1 %final.1 = bf16[256,768]{1,0:T(8,128)(2,1)} custom-call(s32[4]{0:T(128)S(1)} %pad_add_fusion.2.scalars.unused.position, bf16[576,256]{1,0:T(8,128)(2,1)S(1)} %get-tuple-element.255.refs_4_.refs_0_, bf16[576,256]{1,0:T(8,128)(2,1)S(1)} %collective-permute-done.15.refs_1_, bf16[576,256]{1,0:T(8,128)(2,1)S(1)} %collective-permute-done.16.refs_2_, ...), custom_call_target="tpu_custom_call" | custom-call | flops 1000 | bytes 1000 | tf_op jit(solution)/shard_map/final/pallas_call | solution.py:575
  171.2 4.9 %collective-permute-done.33.refs_6_ = bf16[24,768]{1,0:T(8,128)(2,1)S(1)} collective-permute-done((bf16[24,768]{1,0:T(8,128)(2,1)S(1)}, bf16[24,768]{1,0:T(8,128)(2,1)S(1)}, u32[]{:S(2)}, u32[]{:S(2)}) %collective-permute-start.33) | collective-permute-done | bytes 36896 | tf_op jit(solution)/shard_map/ppermute | solution.py:1505
  176.0 1.7 collective-permute-done.34.refs_7_
  177.7 1.6 finish.1
  (115 shorter events, 47.2 us)
Async XLA Ops:
  2.7 19.5 %collective-permute-start = (bf16[256,768]{1,0:T(8,128)(2,1)S(1)}, bf16[256,768]{1,0:T(8,128)(2,1)S(1)}, u32[]{:S(2)}, u32[]{:S(2)}) collective-permute-start(bf16[256,768]{1,0:T(8,128)(2,1)S(1)} %norm.1.refs_0_), channel_id=1, source_target_pairs={{0,2},{1,3},{2,4},{3,5},{4,6},{5,7},{6,0},{7,1},{8,10},{9,11},{10,... | collective-permute-start | bytes 1179656 | tf_op jit(solution)/shard_map/ppermute | solution.py:1505
  5.8 19.0 %collective-permute-start.1 = (bf16[256,768]{1,0:T(8,128)(2,1)S(1)}, bf16[256,768]{1,0:T(8,128)(2,1)S(1)}, u32[]{:S(2)}, u32[]{:S(2)}) collective-permute-start(bf16[256,768]{1,0:T(8,128)(2,1)S(1)} %norm.1.refs_0_), channel_id=1, source_target_pairs={{0,6},{1,7},{2,0},{3,1},{4,2},{5,3},{6,4},{7,5},{8,14},{9,15},{10,... | collective-permute-start | bytes 1179656 | tf_op jit(solution)/shard_map/ppermute | solution.py:1505
  7.9 18.9 %collective-permute-start.2 = (bf16[256,768]{1,0:T(8,128)(2,1)S(1)}, bf16[256,768]{1,0:T(8,128)(2,1)S(1)}, u32[]{:S(2)}, u32[]{:S(2)}) collective-permute-start(bf16[256,768]{1,0:T(8,128)(2,1)S(1)} %norm.1.refs_0_), channel_id=1, source_target_pairs={{0,1},{1,0},{2,3},{3,2},{4,5},{5,4},{6,7},{7,6},{8,9},{9,8},{10,11... | collective-permute-start | bytes 1179656 | tf_op jit(solution)/shard_map/ppermute | solution.py:1509
  22.3 4.5 %collective-permute-start.3 = (bf16[256,768]{1,0:T(8,128)(2,1)S(1)}, bf16[256,768]{1,0:T(8,128)(2,1)S(1)}, u32[]{:S(2)}, u32[]{:S(2)}) collective-permute-start(bf16[256,768]{1,0:T(8,128)(2,1)S(1)} %collective-permute-done.refs_1_), channel_id=1, source_target_pairs={{0,1},{1,0},{2,3},{3,2},{4,5},{5,4},{6,7},{7,6},{8,9},{9,8},{10,11... | collective-permute-start | bytes 1179656 | tf_op jit(solution)/shard_map/ppermute | solution.py:1509
  24.8 13.4 %collective-permute-start.5 = (bf16[256,768]{1,0:T(8,128)(2,1)S(1)}, bf16[256,768]{1,0:T(8,128)(2,1)S(1)}, u32[]{:S(2)}, u32[]{:S(2)}) collective-permute-start(bf16[256,768]{1,0:T(8,128)(2,1)S(1)} %collective-permute-done.1.refs_2_), channel_id=1, source_target_pairs={{2,0},{3,1},{4,2},{5,3},{10,8},{11,9},{12,10},{13,11},{18,16},{19,... | collective-permute-start | bytes 1179656 | tf_op jit(solution)/shard_map/ppermute | solution.py:1672
  26.1 12.1 %collective-permute-start.6 = (bf16[256,768]{1,0:T(8,128)(2,1)S(1)}, bf16[256,768]{1,0:T(8,128)(2,1)S(1)}, u32[]{:S(2)}, u32[]{:S(2)}) collective-permute-start(bf16[256,768]{1,0:T(8,128)(2,1)S(1)} %collective-permute-done.refs_1_), channel_id=1, source_target_pairs={{2,4},{3,5},{4,6},{5,7},{10,12},{11,13},{12,14},{13,15},{18,20},{1... | collective-permute-start | bytes 1179656 | tf_op jit(solution)/shard_map/ppermute | solution.py:1672
  48.3 8.8 %collective-permute-start.10 = (bf16[192,256]{1,0:T(8,128)(2,1)S(1)}, bf16[192,256]{1,0:T(8,128)(2,1)S(1)}, u32[]{:S(2)}, u32[]{:S(2)}) collective-permute-start(bf16[192,256]{1,0:T(8,128)(2,1)S(1)} %get-tuple-element.184), channel_id=1, source_target_pairs={{0,2},{1,3},{2,4},{3,5},{4,6},{5,7},{6,0},{7,1},{8,10},{9,11},{10,... | collective-permute-start | bytes 294920 | tf_op jit(solution)/shard_map/ppermute | solution.py:1505
  49.6 7.7 %collective-permute-start.8 = (bf16[192,256]{1,0:T(8,128)(2,1)S(1)}, bf16[192,256]{1,0:T(8,128)(2,1)S(1)}, u32[]{:S(2)}, u32[]{:S(2)}) collective-permute-start(bf16[192,256]{1,0:T(8,128)(2,1)S(1)} %get-tuple-element.182), channel_id=1, source_target_pairs={{0,6},{1,7},{2,0},{3,1},{4,2},{5,3},{6,4},{7,5},{8,14},{9,15},{10,... | collective-permute-start | bytes 294920 | tf_op jit(solution)/shard_map/ppermute | solution.py:1505
  52.2 9.9 %collective-permute-start.9 = (bf16[192,256]{1,0:T(8,128)(2,1)S(1)}, bf16[192,256]{1,0:T(8,128)(2,1)S(1)}, u32[]{:S(2)}, u32[]{:S(2)}) collective-permute-start(bf16[192,256]{1,0:T(8,128)(2,1)S(1)} %get-tuple-element.183), channel_id=1, source_target_pairs={{0,4},{1,5},{2,6},{3,7},{4,0},{5,1},{6,2},{7,3},{8,12},{9,13},{10,... | collective-permute-start | bytes 294920 | tf_op jit(solution)/shard_map/ppermute | solution.py:1505
  81.9 8.8 %collective-permute-start.19 = (bf16[16,120,768]{2,1,0:T(8,128)(2,1)S(1)}, bf16[16,120,768]{2,1,0:T(8,128)(2,1)S(1)}, u32[]{:S(2)}, u32[]{:S(2)}) collective-permute-start(bf16[16,120,768]{2,1,0:T(8,128)(2,1)S(1)} %get-tuple-element.233), channel_id=1, source_target_pairs={{0,1},{1,0},{2,3},{3,2},{4,5},{5,4},{6,7},{7,6},{8,9},{9,8},{10,11... | collective-permute-start | bytes 8847368 | tf_op jit(solution)/shard_map/ppermute | solution.py:1509
  84.8 5.8 %collective-permute-start.18 = (bf16[16,96,768]{2,1,0:T(8,128)(2,1)S(1)}, bf16[16,96,768]{2,1,0:T(8,128)(2,1)S(1)}, u32[]{:S(2)}, u32[]{:S(2)}) collective-permute-start(bf16[16,96,768]{2,1,0:T(8,128)(2,1)S(1)} %get-tuple-element.231), channel_id=1, source_target_pairs={{0,1},{1,0},{2,3},{3,2},{4,5},{5,4},{6,7},{7,6},{8,9},{9,8},{10,11... | collective-permute-start | bytes 7077896 | tf_op jit(solution)/shard_map/ppermute | solution.py:1509
  85.3 8.1 %collective-permute-start.11 = (bf16[192,256]{1,0:T(8,128)(2,1)S(1)}, bf16[192,256]{1,0:T(8,128)(2,1)S(1)}, u32[]{:S(2)}, u32[]{:S(2)}) collective-permute-start(bf16[192,256]{1,0:T(8,128)(2,1)S(1)} %get-tuple-element.219), channel_id=1, source_target_pairs={{0,2},{1,3},{2,4},{3,5},{4,6},{5,7},{6,0},{7,1},{8,10},{9,11},{10,... | collective-permute-start | bytes 294920 | tf_op jit(solution)/shard_map/ppermute | solution.py:1505
  85.3 8.1 %collective-permute-start.12 = (bf16[192,256]{1,0:T(8,128)(2,1)S(1)}, bf16[192,256]{1,0:T(8,128)(2,1)S(1)}, u32[]{:S(2)}, u32[]{:S(2)}) collective-permute-start(bf16[192,256]{1,0:T(8,128)(2,1)S(1)} %get-tuple-element.220), channel_id=1, source_target_pairs={{0,6},{1,7},{2,0},{3,1},{4,2},{5,3},{6,4},{7,5},{8,14},{9,15},{10,... | collective-permute-start | bytes 294920 | tf_op jit(solution)/shard_map/ppermute | solution.py:1505
  89.1 8.4 %collective-permute-start.13 = (bf16[192,256]{1,0:T(8,128)(2,1)S(1)}, bf16[192,256]{1,0:T(8,128)(2,1)S(1)}, u32[]{:S(2)}, u32[]{:S(2)}) collective-permute-start(bf16[192,256]{1,0:T(8,128)(2,1)S(1)} %get-tuple-element.221), channel_id=1, source_target_pairs={{0,4},{1,5},{2,6},{3,7},{4,0},{5,1},{6,2},{7,3},{8,12},{9,13},{10,... | collective-permute-start | bytes 294920 | tf_op jit(solution)/shard_map/ppermute | solution.py:1505
  91.8 31.2 %collective-permute-start.20 = (bf16[2,2,216,768]{3,2,1,0:T(8,128)(2,1)S(1)}, bf16[2,2,216,768]{3,2,1,0:T(8,128)(2,1)S(1)}, u32[]{:S(2)}, u32[]{:S(2)}) collective-permute-start(bf16[2,2,216,768]{3,2,1,0:T(8,128)(2,1)S(1)} %get-tuple-element.234), channel_id=1, source_target_pairs={{0,8},{8,0},{16,24},{24,16},{1,9},{9,1},{17,25},{25,17},{2,10},{10... | collective-permute-start | bytes 3981320 | tf_op jit(solution)/shard_map/ppermute | solution.py:1513
  92.1 31.1 %collective-permute-start.21 = (bf16[2,2,216,768]{3,2,1,0:T(8,128)(2,1)S(1)}, bf16[2,2,216,768]{3,2,1,0:T(8,128)(2,1)S(1)}, u32[]{:S(2)}, u32[]{:S(2)}) collective-permute-start(bf16[2,2,216,768]{3,2,1,0:T(8,128)(2,1)S(1)} %get-tuple-element.235), channel_id=1, source_target_pairs={{0,16},{8,24},{16,0},{24,8},{1,17},{9,25},{17,1},{25,9},{2,18},{10... | collective-permute-start | bytes 3981320 | tf_op jit(solution)/shard_map/ppermute | solution.py:1513
  111.0 15.3 %collective-permute-start.15 = (bf16[576,256]{1,0:T(8,128)(2,1)S(1)}, bf16[576,256]{1,0:T(8,128)(2,1)S(1)}, u32[]{:S(2)}, u32[]{:S(2)}) collective-permute-start(bf16[576,256]{1,0:T(8,128)(2,1)S(1)} %get-tuple-element.243.refs_5_), channel_id=1, source_target_pairs={{0,6},{1,7},{2,0},{3,1},{4,2},{5,3},{6,4},{7,5},{8,14},{9,15},{10,... | collective-permute-start | bytes 884744 | tf_op jit(solution)/shard_map/ppermute | solution.py:1505
  112.1 25.8 %collective-permute-start.16 = (bf16[576,256]{1,0:T(8,128)(2,1)S(1)}, bf16[576,256]{1,0:T(8,128)(2,1)S(1)}, u32[]{:S(2)}, u32[]{:S(2)}) collective-permute-start(bf16[576,256]{1,0:T(8,128)(2,1)S(1)} %get-tuple-element.245.refs_7_), channel_id=1, source_target_pairs={{0,4},{1,5},{2,6},{3,7},{4,0},{5,1},{6,2},{7,3},{8,12},{9,13},{10,... | collective-permute-start | bytes 884744 | tf_op jit(solution)/shard_map/ppermute | solution.py:1505
  112.1 25.8 %collective-permute-start.17 = (bf16[576,256]{1,0:T(8,128)(2,1)S(1)}, bf16[576,256]{1,0:T(8,128)(2,1)S(1)}, u32[]{:S(2)}, u32[]{:S(2)}) collective-permute-start(bf16[576,256]{1,0:T(8,128)(2,1)S(1)} %get-tuple-element.244.refs_6_), channel_id=1, source_target_pairs={{0,2},{1,3},{2,4},{3,5},{4,6},{5,7},{6,0},{7,1},{8,10},{9,11},{10,... | collective-permute-start | bytes 884744 | tf_op jit(solution)/shard_map/ppermute | solution.py:1505
  124.3 16.1 %collective-permute-start.22 = (bf16[2,216,768]{2,1,0:T(8,128)(2,1)S(1)}, bf16[2,216,768]{2,1,0:T(8,128)(2,1)S(1)}, u32[]{:S(2)}, u32[]{:S(2)}) collective-permute-start(bf16[2,216,768]{2,1,0:T(8,128)(2,1)S(1)} %get-tuple-element.265), channel_id=1, source_target_pairs={{0,16},{8,24},{16,0},{24,8},{1,17},{9,25},{17,1},{25,9},{2,18},{10... | collective-permute-start | bytes 1990664 | tf_op jit(solution)/shard_map/ppermute | solution.py:1513
  125.5 15.5 %collective-permute-start.23 = (bf16[2,216,768]{2,1,0:T(8,128)(2,1)S(1)}, bf16[2,216,768]{2,1,0:T(8,128)(2,1)S(1)}, u32[]{:S(2)}, u32[]{:S(2)}) collective-permute-start(bf16[2,216,768]{2,1,0:T(8,128)(2,1)S(1)} %get-tuple-element.267), channel_id=1, source_target_pairs={{0,8},{8,0},{16,24},{24,16},{1,9},{9,1},{17,25},{25,17},{2,10},{10... | collective-permute-start | bytes 1990664 | tf_op jit(solution)/shard_map/ppermute | solution.py:1513
  137.9 8.4 %collective-permute-start.27 = (bf16[16,24,768]{2,1,0:T(8,128)(2,1)S(1)}, bf16[16,24,768]{2,1,0:T(8,128)(2,1)S(1)}, u32[]{:S(2)}, u32[]{:S(2)}) collective-permute-start(bf16[16,24,768]{2,1,0:T(8,128)(2,1)S(1)} %get-tuple-element.273), channel_id=1, source_target_pairs={{0,1},{1,0},{2,3},{3,2},{4,5},{5,4},{6,7},{7,6},{8,9},{9,8},{10,11... | collective-permute-start | bytes 1769480 | tf_op jit(solution)/shard_map/ppermute | solution.py:1509
  142.4 35.3 %collective-permute-start.24 = (bf16[216,768]{1,0:T(8,128)(2,1)S(1)}, bf16[216,768]{1,0:T(8,128)(2,1)S(1)}, u32[]{:S(2)}, u32[]{:S(2)}) collective-permute-start(bf16[216,768]{1,0:T(8,128)(2,1)S(1)} %get-tuple-element.269), channel_id=1, source_target_pairs={{0,2},{1,3},{2,4},{3,5},{4,6},{5,7},{6,0},{7,1},{8,10},{9,11},{10,... | collective-permute-start | bytes 995336 | tf_op jit(solution)/shard_map/ppermute | solution.py:1505
  142.4 35.3 %collective-permute-start.25 = (bf16[216,768]{1,0:T(8,128)(2,1)S(1)}, bf16[216,768]{1,0:T(8,128)(2,1)S(1)}, u32[]{:S(2)}, u32[]{:S(2)}) collective-permute-start(bf16[216,768]{1,0:T(8,128)(2,1)S(1)} %get-tuple-element.270), channel_id=1, source_target_pairs={{0,4},{1,5},{2,6},{3,7},{4,0},{5,1},{6,2},{7,3},{8,12},{9,13},{10,... | collective-permute-start | bytes 995336 | tf_op jit(solution)/shard_map/ppermute | solution.py:1505
  145.1 32.5 %collective-permute-start.26 = (bf16[216,768]{1,0:T(8,128)(2,1)S(1)}, bf16[216,768]{1,0:T(8,128)(2,1)S(1)}, u32[]{:S(2)}, u32[]{:S(2)}) collective-permute-start(bf16[216,768]{1,0:T(8,128)(2,1)S(1)} %get-tuple-element.271), channel_id=1, source_target_pairs={{0,6},{1,7},{2,0},{3,1},{4,2},{5,3},{6,4},{7,5},{8,14},{9,15},{10,... | collective-permute-start | bytes 995336 | tf_op jit(solution)/shard_map/ppermute | solution.py:1505
  146.9 5.5 %collective-permute-start.28 = (bf16[2,2,24,768]{3,2,1,0:T(8,128)(2,1)S(1)}, bf16[2,2,24,768]{3,2,1,0:T(8,128)(2,1)S(1)}, u32[]{:S(2)}, u32[]{:S(2)}) collective-permute-start(bf16[2,2,24,768]{3,2,1,0:T(8,128)(2,1)S(1)} %get-tuple-element.276), channel_id=1, source_target_pairs={{0,8},{8,0},{16,24},{24,16},{1,9},{9,1},{17,25},{25,17},{2,10},{10... | collective-permute-start | bytes 442376 | tf_op jit(solution)/shard_map/ppermute | solution.py:1513
  148.3 5.1 %collective-permute-start.29 = (bf16[2,2,24,768]{3,2,1,0:T(8,128)(2,1)S(1)}, bf16[2,2,24,768]{3,2,1,0:T(8,128)(2,1)S(1)}, u32[]{:S(2)}, u32[]{:S(2)}) collective-permute-start(bf16[2,2,24,768]{3,2,1,0:T(8,128)(2,1)S(1)} %get-tuple-element.277), channel_id=1, source_target_pairs={{0,16},{8,24},{16,0},{24,8},{1,17},{9,25},{17,1},{25,9},{2,18},{10... | collective-permute-start | bytes 442376 | tf_op jit(solution)/shard_map/ppermute | solution.py:1513
  154.1 4.4 %collective-permute-start.30 = (bf16[2,24,768]{2,1,0:T(8,128)(2,1)S(1)}, bf16[2,24,768]{2,1,0:T(8,128)(2,1)S(1)}, u32[]{:S(2)}, u32[]{:S(2)}) collective-permute-start(bf16[2,24,768]{2,1,0:T(8,128)(2,1)S(1)} %get-tuple-element.279), channel_id=1, source_target_pairs={{0,16},{8,24},{16,0},{24,8},{1,17},{9,25},{17,1},{25,9},{2,18},{10... | collective-permute-start | bytes 221192 | tf_op jit(solution)/shard_map/ppermute | solution.py:1513
  155.9 4.4 %collective-permute-start.31 = (bf16[2,24,768]{2,1,0:T(8,128)(2,1)S(1)}, bf16[2,24,768]{2,1,0:T(8,128)(2,1)S(1)}, u32[]{:S(2)}, u32[]{:S(2)}) collective-permute-start(bf16[2,24,768]{2,1,0:T(8,128)(2,1)S(1)} %get-tuple-element.281), channel_id=1, source_target_pairs={{0,8},{8,0},{16,24},{24,16},{1,9},{9,1},{17,25},{25,17},{2,10},{10... | collective-permute-start | bytes 221192 | tf_op jit(solution)/shard_map/ppermute | solution.py:1513
  160.8 7.2 %collective-permute-start.32 = (bf16[24,768]{1,0:T(8,128)(2,1)S(1)}, bf16[24,768]{1,0:T(8,128)(2,1)S(1)}, u32[]{:S(2)}, u32[]{:S(2)}) collective-permute-start(bf16[24,768]{1,0:T(8,128)(2,1)S(1)} %get-tuple-element.283), channel_id=1, source_target_pairs={{0,2},{1,3},{2,4},{3,5},{4,6},{5,7},{6,0},{7,1},{8,10},{9,11},{10,... | collective-permute-start | bytes 110600 | tf_op jit(solution)/shard_map/ppermute | solution.py:1505
  161.5 14.5 %collective-permute-start.33 = (bf16[24,768]{1,0:T(8,128)(2,1)S(1)}, bf16[24,768]{1,0:T(8,128)(2,1)S(1)}, u32[]{:S(2)}, u32[]{:S(2)}) collective-permute-start(bf16[24,768]{1,0:T(8,128)(2,1)S(1)} %get-tuple-element.284), channel_id=1, source_target_pairs={{0,4},{1,5},{2,6},{3,7},{4,0},{5,1},{6,2},{7,3},{8,12},{9,13},{10,... | collective-permute-start | bytes 110600 | tf_op jit(solution)/shard_map/ppermute | solution.py:1505
  168.0 9.6 %collective-permute-start.34 = (bf16[24,768]{1,0:T(8,128)(2,1)S(1)}, bf16[24,768]{1,0:T(8,128)(2,1)S(1)}, u32[]{:S(2)}, u32[]{:S(2)}) collective-permute-start(bf16[24,768]{1,0:T(8,128)(2,1)S(1)} %get-tuple-element.285), channel_id=1, source_target_pairs={{0,6},{1,7},{2,0},{3,1},{4,2},{5,3},{6,4},{7,5},{8,14},{9,15},{10,... | collective-permute-start | bytes 110600 | tf_op jit(solution)/shard_map/ppermute | solution.py:1505
  (18 other events, 188.6 us)

commit v9 on v8

--- a/solution.py
+++ b/solution.py
@@ -1615,11 +1615,11 @@
         ]
 
 
-def finish_kernel(chips, per, share, factor, scalars, *refs):
-    arrived, heads_in, refs = refs[:chips], refs[chips : 2 * chips], refs[chips:]
-    down_ref, up_ref, out_ref, query_ref, key_ref, value_ref, gains_ref, heads_ref = refs[chips:]
+def finish_kernel(chips, per, factor, scalars, *refs):
+    arrived = refs[:chips]
+    down_ref, up_ref, out_ref = refs[chips:]
     width = arrived[0].shape[1]
-    chip, pieces = scalars[0], width // 128
+    pieces = width // 128
     tiles = up_ref.shape[0] * 128 // (per * width)
     down_rows = down_ref.shape[0] * 128 // width
 
@@ -1633,6 +1633,12 @@
     for tile in range(tiles):
         lay_flat(up_ref, total(down_rows + tile * per, per), tile * pieces, tiles * pieces)
     lay_flat(out_ref, total(down_rows + tiles * per, per), 0, pieces)
+
+
+def finish_heads_kernel(chips, share, factor, scalars, *refs):
+    heads_in = refs[:chips]
+    query_ref, key_ref, value_ref, gains_ref, heads_ref = refs[chips:]
+    chip, pieces = scalars[0], heads_in[0].shape[1] // 128
     gains = wide(heads_in[0][:8, -128:])
     for part in heads_in[1:]:
         gains = gains + wide(part[:8, -128:])
@@ -1654,15 +1660,25 @@
     chips, width = len(arrived) // 2, arrived[0].shape[1]
     square = jax.ShapeDtypeStruct((per * width // 128, 128), jnp.float32)
     large = jax.ShapeDtypeStruct((per * hidden // 128, 128), jnp.float32)
-    return call_whole(
-        partial(finish_kernel, chips, per, share, factor),
-        [large, large, square, square, square, square, jax.ShapeDtypeStruct((gains_part,), jnp.float32)],
+    first = call_whole(
+        partial(finish_kernel, chips, per, factor),
+        [large, large, square],
         "finish",
         scalars,
-        *arrived,
+        *arrived[:chips],
+        outs=False,
+    )
+    first, heads_in = lax.optimization_barrier((first, list(arrived[chips:])))
+    last = call_whole(
+        partial(finish_heads_kernel, chips, share, factor),
+        [square, square, square, jax.ShapeDtypeStruct((gains_part,), jnp.float32)],
+        "finish_heads",
+        scalars,
+        *heads_in,
         scratch=[pltpu.VMEM((chips, per, 3 * share), jnp.float32)],
         outs=False,
     )
+    return [*first, *last]
 
 
 def gathered(rows):

time: 180 us -> 177 us (0.983)
  waiting for transfers between devices: 62.1 us -> 53.8 us
  Pallas kernels: 68.3 us -> 72.2 us
  starting transfers between devices: 35.1 us -> 37.6 us
    ppermute x17, waiting for transfers between devices: 34 us -> 24.6 us  [chip_shift(): lax.ppermute(value, 'seq', [(i, (i + 2 * steps) % count) for i in range(c...]
    ppermute x17, starting transfers between devices: 21.6 us -> 25.8 us  [chip_shift(): lax.ppermute(value, 'seq', [(i, (i + 2 * steps) % count) for i in range(c...]
    pallas_call x15 -> x16, Pallas kernels: 22.6 us -> 23.9 us  [call_whole(): pl.pallas_call(kernel, grid_spec=pltpu.PrefetchScalarGridSpec(num_scalar_...]
  transfers between devices with their start and end apart: 35 -> 35, of which waited for: 20 -> 17; matrix products, arithmetic and copies ran while one was open for 5% -> 5% of each run, Pallas kernels for 22% -> 23%
where the time goes in v9:
time: 177 us
  Pallas kernels  72.2 us (41%)
  waiting for transfers between devices  53.8 us (30%)
  starting transfers between devices  37.6 us (21%)
  local copies, waits for them, and re-layouts  9.18 us (5%)
  other arithmetic  3.56 us (2%)
    ppermute x17, starting transfers between devices, chip_shift(): lax.ppermute(value, 'seq', [(i, (i + 2 * steps) % count) for i in range(c...  25.8 us
    ppermute x17, waiting for transfers between devices, chip_shift(): lax.ppermute(value, 'seq', [(i, (i + 2 * steps) % count) for i in range(c...  24.6 us
    pallas_call x16, Pallas kernels, call_whole(): pl.pallas_call(kernel, grid_spec=pltpu.PrefetchScalarGridSpec(num_scalar_...  23.9 us
    ppermute x8, waiting for transfers between devices, row_swap(): lax.ppermute(value, 'row', [(i, i ^ bit) for i in range(lax.axis_size('ro...  15.6 us
    pallas_call x1, Pallas kernels, middle(): pl.pallas_call(partial(middle_kernel, chips, tiles), grid_spec=pltpu.Pref...  15.2 us
    pallas_call x1, Pallas kernels, attend_back(): pl.pallas_call(partial(attend_back_kernel, heads, block, steps, key_block...  10.8 us
    pallas_call x2, Pallas kernels, attend(): pl.pallas_call(partial(attend_kernel, heads, block, first, steps, key_blo...  9.17 us
    ppermute x8, starting transfers between devices, row_swap(): lax.ppermute(value, 'row', [(i, i ^ bit) for i in range(lax.axis_size('ro...  8.44 us
  transfers between devices with their start and end apart: 35, of which 17 were waited for; matrix products, arithmetic and copies ran while one was open for 5% of the time, Pallas kernels for 23%

profile of v9, /device:TPU:0, one launch (start us, length us, event | category | flops | bytes accessed | tf_op | source)
XLA Modules:
  0.0 177.3 jit_solution(510695119790050824)
XLA Ops:
  2.7 3.1 %collective-permute-start = (bf16[256,768]{1,0:T(8,128)(2,1)S(1)}, bf16[256,768]{1,0:T(8,128)(2,1)S(1)}, u32[]{:S(2)}, u32[]{:S(2)}) collective-permute-start(bf16[256,768]{1,0:T(8,128)(2,1)S(1)} %norm.1.refs_0_), channel_id=1, source_target_pairs={{0,2},{1,3},{2,4},{3,5},{4,6},{5,7},{6,0},{7,1},{8,10},{9,11},{10,... | collective-permute-start | bytes 1179656 | tf_op jit(solution)/shard_map/ppermute | solution.py:1505
  5.8 2.1 %collective-permute-start.1 = (bf16[256,768]{1,0:T(8,128)(2,1)S(1)}, bf16[256,768]{1,0:T(8,128)(2,1)S(1)}, u32[]{:S(2)}, u32[]{:S(2)}) collective-permute-start(bf16[256,768]{1,0:T(8,128)(2,1)S(1)} %norm.1.refs_0_), channel_id=1, source_target_pairs={{0,6},{1,7},{2,0},{3,1},{4,2},{5,3},{6,4},{7,5},{8,14},{9,15},{10,... | collective-permute-start | bytes 1179656 | tf_op jit(solution)/shard_map/ppermute | solution.py:1505
  18.8 3.5 %choose.1 = (bf16[384,768]{1,0:T(8,128)(2,1)S(1)}, bf16[768,384]{1,0:T(8,128)(2,1)S(1)}, bf16[192,768]{1,0:T(8,128)(2,1)S(1)}, bf16[192,768]{1,0:T(8,128)(2,1)S(...) custom-call(s32[4]{0:T(128)S(1)} %pad_add_fusion.2.scalars.unused.position, bf16[768,768]{1,0:T(8,128)(2,1)S(1)} %copy-done, ...), custom_call_target="tpu_custom_call" | custom-call | flops 1000 | bytes 1000 | tf_op jit(solution)/shard_map/choose/pallas_call | solution.py:575
  22.9 2.0 %collective-permute-done.1.refs_2_ = bf16[256,768]{1,0:T(8,128)(2,1)S(1)} collective-permute-done((bf16[256,768]{1,0:T(8,128)(2,1)S(1)}, bf16[256,768]{1,0:T(8,128)(2,1)S(1)}, u32[]{:S(2)}, u32[]{:S(2)}) %collective-permute-start.1) | collective-permute-done | bytes 393248 | tf_op jit(solution)/shard_map/ppermute | solution.py:1505
  26.8 3.3 %project.2 = (bf16[384,1024]{1,0:T(8,128)(2,1)S(1)}, bf16[2048,384]{1,0:T(8,128)(2,1)S(1)}, bf16[192,2048]{1,0:T(8,128)(2,1)S(1)}) custom-call(s32[7]{0:T(128)S(1)} %pad_add_fusion.meta, bf16[256,768]{1,0:T(8,128)(2,1)S(1)} %norm.1.refs_0_, bf16[256,768]{1,0:T(8,128)(2,1)S(1)} %collective-permute-done.refs_1_, ...), custom_call_target="tpu_custom_call" | custom-call | flops 1000 | bytes 1000 | tf_op jit(solution)/shard_map/project/pallas_call | solution.py:697
  30.1 8.1 %collective-permute-done.5 = bf16[256,768]{1,0:T(8,128)(2,1)S(1)} collective-permute-done((bf16[256,768]{1,0:T(8,128)(2,1)S(1)}, bf16[256,768]{1,0:T(8,128)(2,1)S(1)}, u32[]{:S(2)}, u32[]{:S(2)}) %collective-permute-start.5) | collective-permute-done | bytes 393248 | tf_op jit(solution)/shard_map/ppermute | solution.py:1688
  41.6 7.9 %attend.3 = (f32[192,256]{1,0:T(8,128)S(1)}, f32[192,256]{1,0:T(8,128)S(1)}, f32[192,256]{1,0:T(8,128)S(1)}, f32[3,1,256]{2,1,0:T(1,128)S(1)}, f32[3,1,256]{2,1,...) custom-call(s32[20]{0:T(128)S(1)} %concatenate.11.meta, ...), custom_call_target="tpu_custom_call" | custom-call | flops 1000 | bytes 1000 | tf_op jit(solution)/shard_map/attend/pallas_call | solution.py:915
  49.5 1.8 %collective-permute-start.10 = (bf16[192,256]{1,0:T(8,128)(2,1)S(1)}, bf16[192,256]{1,0:T(8,128)(2,1)S(1)}, u32[]{:S(2)}, u32[]{:S(2)}) collective-permute-start(bf16[192,256]{1,0:T(8,128)(2,1)S(1)} %get-tuple-element.191), channel_id=1, source_target_pairs={{0,2},{1,3},{2,4},{3,5},{4,6},{5,7},{6,0},{7,1},{8,10},{9,11},{10,... | collective-permute-start | bytes 294920 | tf_op jit(solution)/shard_map/ppermute | solution.py:1505
  51.3 2.1 %collective-permute-start.8 = (bf16[192,256]{1,0:T(8,128)(2,1)S(1)}, bf16[192,256]{1,0:T(8,128)(2,1)S(1)}, u32[]{:S(2)}, u32[]{:S(2)}) collective-permute-start(bf16[192,256]{1,0:T(8,128)(2,1)S(1)} %get-tuple-element.189), channel_id=1, source_target_pairs={{0,6},{1,7},{2,0},{3,1},{4,2},{5,3},{6,4},{7,5},{8,14},{9,15},{10,... | collective-permute-start | bytes 294920 | tf_op jit(solution)/shard_map/ppermute | solution.py:1505
  55.6 3.2 %project_back.1 = (bf16[192,2048]{1,0:T(8,128)(2,1)S(1)}, bf16[2048,384]{1,0:T(8,128)(2,1)S(1)}) custom-call(s32[4]{0:T(128)S(1)} %pad_add_fusion.2.scalars.unused.position, bf16[256,768]{1,0:T(8,128)(2,1)S(1)} %norm.1.refs_0_, bf16[256,768]{1,0:T(8,128)(2,1)S(1)} %collective-permute-done.refs_1_, bf16[256,768]{1,0:T(8,128)(2,1)S(1)} %collective-permute-done.1.refs_2_, ...), custom_call_target="tpu_custom_call" | custom-call | flops 1000 | bytes 1000 | tf_op jit(solution)/shard_map/project_back/pallas_call | solution.py:575
  58.8 2.7 %collective-permute-done.9.refs_2_ = bf16[192,256]{1,0:T(8,128)(2,1)S(1)} collective-permute-done((bf16[192,256]{1,0:T(8,128)(2,1)S(1)}, bf16[192,256]{1,0:T(8,128)(2,1)S(1)}, u32[]{:S(2)}, u32[]{:S(2)}) %collective-permute-start.9) | collective-permute-done | bytes 98336 | tf_op jit(solution)/shard_map/ppermute | solution.py:1505
  61.5 15.2 %middle.1 = (bf16[256,768]{1,0:T(8,128)(2,1)}, f32[256,768]{1,0:T(8,128)S(1)}, bf16[256,768]{1,0:T(8,128)(2,1)S(1)}, bf16[192,256]{1,0:T(8,128)(2,1)S(1)}, bf16[...) custom-call(s32[4]{0:T(128)S(1)} %pad_add_fusion.2.scalars.unused.po, ...), custom_call_target="tpu_custom_call" | custom-call | flops 1000 | bytes 1000 | tf_op jit(solution)/shard_map/middle/pallas_call | solution.py:1310
  76.7 4.5 %up_out_grad.1 = (bf16[16,120,768]{2,1,0:T(8,128)(2,1)S(1)}, bf16[16,120,768]{2,1,0:T(8,128)(2,1)S(1)}) custom-call(s32[4]{0:T(128)S(1)} %pad_add_fusion.2.scalars.unused.position, bf16[256,768]{1,0:T(8,128)(2,1)S(1)} %get-tuple-element.218.h2_ref, bf16[256,3072]{1,0:T(8,128)(2,1)S(1)} %get-tuple-element.219.pre_ref, ...), custom_call_target="tpu_custom_call" | custom-call | flops 1000 | bytes 1000 | tf_op jit(solution)/shard_map/up_out_grad/pallas_call | solution.py:1436
  81.3 2.8 %down_grad.1 = (bf16[16,96,768]{2,1,0:T(8,128)(2,1)S(1)}, bf16[16,96,768]{2,1,0:T(8,128)(2,1)S(1)}) custom-call(s32[4]{0:T(128)S(1)} %pad_add_fusion.2.scalars.unused.position, bf16[256,3072]{1,0:T(8,128)(2,1)S(1)} %get-tuple-element.236.bent_ref, bf16[256,768]{1,0:T(8,128)(2,1)S(1)} %copy-done.7), custom_call_target="tpu_custom_call" | custom-call | flops 1000 | bytes 1000 | tf_op jit(solution)/shard_map/down_grad/pallas_call | solution.py:1386
  84.6 3.8 %collective-permute-start.12 = (bf16[192,256]{1,0:T(8,128)(2,1)S(1)}, bf16[192,256]{1,0:T(8,128)(2,1)S(1)}, u32[]{:S(2)}, u32[]{:S(2)}) collective-permute-start(bf16[192,256]{1,0:T(8,128)(2,1)S(1)} %get-tuple-element.227), channel_id=1, source_target_pairs={{0,6},{1,7},{2,0},{3,1},{4,2},{5,3},{6,4},{7,5},{8,14},{9,15},{10,... | collective-permute-start | bytes 294920 | tf_op jit(solution)/shard_map/ppermute | solution.py:1505
  91.8 2.1 %collective-permute-start.21 = (bf16[2,2,216,768]{3,2,1,0:T(8,128)(2,1)S(1)}, bf16[2,2,216,768]{3,2,1,0:T(8,128)(2,1)S(1)}, u32[]{:S(2)}, u32[]{:S(2)}) collective-permute-start(bf16[2,2,216,768]{3,2,1,0:T(8,128)(2,1)S(1)} %get-tuple-element.242), channel_id=1, source_target_pairs={{0,16},{8,24},{16,0},{24,8},{1,17},{9,25},{17,1},{25,9},{2,18},{10... | collective-permute-start | bytes 3981320 | tf_op jit(solution)/shard_map/ppermute | solution.py:1513
  93.9 2.9 %collective-permute-done.13.refs_11_ = bf16[192,256]{1,0:T(8,128)(2,1)S(1)} collective-permute-done((bf16[192,256]{1,0:T(8,128)(2,1)S(1)}, bf16[192,256]{1,0:T(8,128)(2,1)S(1)}, u32[]{:S(2)}, u32[]{:S(2)}) %collective-permute-start.13) | collective-permute-done | bytes 98336 | tf_op jit(solution)/shard_map/ppermute | solution.py:1505
  96.8 10.8 %attend_back.1 = (bf16[192,1024]{1,0:T(8,128)(2,1)S(1)}, f32[384,1024]{1,0:T(8,128)S(1)}, bf16[384,1024]{1,0:T(8,128)(2,1)S(1)}) custom-call(s32[20]{0:T(128)S(1)} %concatenate.11.meta, s32[1,1024]{1,0:T(1,128)S(1)} %bitcast.44, bf16[384,1024]{1,0:T(8,128)(2,1)S(1)} %get-tuple-element.181.q_ref, bf16[2048,384]{1,0:T(8,128)(2,1)S(1)} %get-tuple-element.182.k_ref, ...), custom_call_target="tpu_custom_call" | custom-call | flops 49999998976 | bytes 1000 | tf_op jit(solution)/shard_map/attend_back/pallas_call | solution.py:948
  107.6 2.3 %collective-permute-done.14.other_ref = bf16[384,1024]{1,0:T(8,128)(2,1)S(1)} collective-permute-done((bf16[384,1024]{1,0:T(8,128)(2,1)S(1)}, bf16[384,1024]{1,0:T(8,128)(2,1)S(1)}, u32[]{:S(2)}, u32[]{:S(2)}) %collective-permute-start.14) | collective-permute-done | bytes 786464 | tf_op jit(solution)/shard_map/ppermute | solution.py:1509
  110.7 1.8 collective-permute-start.15
  114.2 3.1 %head_grads.1 = (bf16[16,24,768]{2,1,0:T(8,128)(2,1)S(1)}, bf16[16,24,768]{2,1,0:T(8,128)(2,1)S(1)}) custom-call(s32[4]{0:T(128)S(1)} %pad_add_fusion.2.scalars.unused.position, bf16[256,768]{1,0:T(8,128)(2,1)S(1)} %norm.1.refs_0_, bf16[256,768]{1,0:T(8,128)(2,1)S(1)} %collective-permute-done.refs_1_, bf16[256,768]{1,0:T(8,128)(2,1)S(1)} %collective-permute-done.1.refs_2_, ...), custom_call_target="tpu_custom_call" | custom-call | flops 1000 | bytes 1000 | tf_op jit(solution)/shard_map/head_grads/pallas_call | solution.py:575
  117.3 5.1 %collective-permute-done.20.refs_2_ = bf16[2,2,216,768]{3,2,1,0:T(8,128)(2,1)S(1)} collective-permute-done((bf16[2,2,216,768]{3,2,1,0:T(8,128)(2,1)S(1)}, bf16[2,2,216,768]{3,2,1,0:T(8,128)(2,1)S(1)}, u32[]{:S(2)}, u32[]{:S(2)}) %collective-permute-start.20) | collective-permute-done | bytes 1327136 | tf_op jit(solution)/shard_map/ppermute | solution.py:1513
  124.2 1.8 %collective-permute-start.22 = (bf16[2,216,768]{2,1,0:T(8,128)(2,1)S(1)}, bf16[2,216,768]{2,1,0:T(8,128)(2,1)S(1)}, u32[]{:S(2)}, u32[]{:S(2)}) collective-permute-start(bf16[2,216,768]{2,1,0:T(8,128)(2,1)S(1)} %get-tuple-element.272), channel_id=1, source_target_pairs={{0,16},{8,24},{16,0},{24,8},{1,17},{9,25},{17,1},{25,9},{2,18},{10... | collective-permute-start | bytes 1990664 | tf_op jit(solution)/shard_map/ppermute | solution.py:1513
  126.3 11.0 %collective-permute-done.16.refs_2_ = bf16[576,256]{1,0:T(8,128)(2,1)S(1)} collective-permute-done((bf16[576,256]{1,0:T(8,128)(2,1)S(1)}, bf16[576,256]{1,0:T(8,128)(2,1)S(1)}, u32[]{:S(2)}, u32[]{:S(2)}) %collective-permute-start.16) | collective-permute-done | bytes 294944 | tf_op jit(solution)/shard_map/ppermute | solution.py:1505
  138.5 1.8 %collective-permute-done.22.refs_1_ = bf16[2,216,768]{2,1,0:T(8,128)(2,1)S(1)} collective-permute-done((bf16[2,216,768]{2,1,0:T(8,128)(2,1)S(1)}, bf16[2,216,768]{2,1,0:T(8,128)(2,1)S(1)}, u32[]{:S(2)}, u32[]{:S(2)}) %collective-permute-start.22) | collective-permute-done | bytes 663584 | tf_op jit(solution)/shard_map/ppermute | solution.py:1513
  142.9 2.7 %collective-permute-start.25 = (bf16[216,768]{1,0:T(8,128)(2,1)S(1)}, bf16[216,768]{1,0:T(8,128)(2,1)S(1)}, u32[]{:S(2)}, u32[]{:S(2)}) collective-permute-start(bf16[216,768]{1,0:T(8,128)(2,1)S(1)} %get-tuple-element.277), channel_id=1, source_target_pairs={{0,4},{1,5},{2,6},{3,7},{4,0},{5,1},{6,2},{7,3},{8,12},{9,13},{10,... | collective-permute-start | bytes 995336 | tf_op jit(solution)/shard_map/ppermute | solution.py:1505
  149.4 3.1 %collective-permute-done.28.refs_2_ = bf16[2,2,24,768]{3,2,1,0:T(8,128)(2,1)S(1)} collective-permute-done((bf16[2,2,24,768]{3,2,1,0:T(8,128)(2,1)S(1)}, bf16[2,2,24,768]{3,2,1,0:T(8,128)(2,1)S(1)}, u32[]{:S(2)}, u32[]{:S(2)}) %collective-permute-start.28) | collective-permute-done | bytes 147488 | tf_op jit(solution)/shard_map/ppermute | solution.py:1513
  155.9 2.3 %collective-permute-done.30.refs_1_ = bf16[2,24,768]{2,1,0:T(8,128)(2,1)S(1)} collective-permute-done((bf16[2,24,768]{2,1,0:T(8,128)(2,1)S(1)}, bf16[2,24,768]{2,1,0:T(8,128)(2,1)S(1)}, u32[]{:S(2)}, u32[]{:S(2)}) %collective-permute-start.30) | collective-permute-done | bytes 73760 | tf_op jit(solution)/shard_map/ppermute | solution.py:1513
  159.6 2.1 %collective-permute-start.32 = (bf16[24,768]{1,0:T(8,128)(2,1)S(1)}, bf16[24,768]{1,0:T(8,128)(2,1)S(1)}, u32[]{:S(2)}, u32[]{:S(2)}) collective-permute-start(bf16[24,768]{1,0:T(8,128)(2,1)S(1)} %get-tuple-element.293), channel_id=1, source_target_pairs={{0,2},{1,3},{2,4},{3,5},{4,6},{5,7},{6,0},{7,1},{8,10},{9,11},{10,... | collective-permute-start | bytes 110600 | tf_op jit(solution)/shard_map/ppermute | solution.py:1505
  162.5 2.8 %collective-permute-start.34 = (bf16[24,768]{1,0:T(8,128)(2,1)S(1)}, bf16[24,768]{1,0:T(8,128)(2,1)S(1)}, u32[]{:S(2)}, u32[]{:S(2)}) collective-permute-start(bf16[24,768]{1,0:T(8,128)(2,1)S(1)} %get-tuple-element.295), channel_id=1, source_target_pairs={{0,6},{1,7},{2,0},{3,1},{4,2},{5,3},{6,4},{7,5},{8,14},{9,15},{10,... | collective-permute-start | bytes 110600 | tf_op jit(solution)/shard_map/ppermute | solution.py:1505
  165.4 3.1 %final.1 = bf16[256,768]{1,0:T(8,128)(2,1)} custom-call(s32[4]{0:T(128)S(1)} %pad_add_fusion.2.scalars.unused.position, bf16[576,256]{1,0:T(8,128)(2,1)S(1)} %get-tuple-element.262.refs_4_.refs_0_, bf16[576,256]{1,0:T(8,128)(2,1)S(1)} %collective-permute-done.15.refs_1_, bf16[576,256]{1,0:T(8,128)(2,1)S(1)} %collective-permute-done.16.refs_2_, ...), custom_call_target="tpu_custom_call" | custom-call | flops 1000 | bytes 1000 | tf_op jit(solution)/shard_map/final/pallas_call | solution.py:575
  170.0 6.0 %collective-permute-done.33.refs_2_ = bf16[24,768]{1,0:T(8,128)(2,1)S(1)} collective-permute-done((bf16[24,768]{1,0:T(8,128)(2,1)S(1)}, bf16[24,768]{1,0:T(8,128)(2,1)S(1)}, u32[]{:S(2)}, u32[]{:S(2)}) %collective-permute-start.33) | collective-permute-done | bytes 36896 | tf_op jit(solution)/shard_map/ppermute | solution.py:1505
  (116 shorter events, 45.6 us)
Async XLA Ops:
  2.7 19.5 %collective-permute-start = (bf16[256,768]{1,0:T(8,128)(2,1)S(1)}, bf16[256,768]{1,0:T(8,128)(2,1)S(1)}, u32[]{:S(2)}, u32[]{:S(2)}) collective-permute-start(bf16[256,768]{1,0:T(8,128)(2,1)S(1)} %norm.1.refs_0_), channel_id=1, source_target_pairs={{0,2},{1,3},{2,4},{3,5},{4,6},{5,7},{6,0},{7,1},{8,10},{9,11},{10,... | collective-permute-start | bytes 1179656 | tf_op jit(solution)/shard_map/ppermute | solution.py:1505
  5.8 19.0 %collective-permute-start.1 = (bf16[256,768]{1,0:T(8,128)(2,1)S(1)}, bf16[256,768]{1,0:T(8,128)(2,1)S(1)}, u32[]{:S(2)}, u32[]{:S(2)}) collective-permute-start(bf16[256,768]{1,0:T(8,128)(2,1)S(1)} %norm.1.refs_0_), channel_id=1, source_target_pairs={{0,6},{1,7},{2,0},{3,1},{4,2},{5,3},{6,4},{7,5},{8,14},{9,15},{10,... | collective-permute-start | bytes 1179656 | tf_op jit(solution)/shard_map/ppermute | solution.py:1505
  7.9 18.9 %collective-permute-start.2 = (bf16[256,768]{1,0:T(8,128)(2,1)S(1)}, bf16[256,768]{1,0:T(8,128)(2,1)S(1)}, u32[]{:S(2)}, u32[]{:S(2)}) collective-permute-start(bf16[256,768]{1,0:T(8,128)(2,1)S(1)} %norm.1.refs_0_), channel_id=1, source_target_pairs={{0,1},{1,0},{2,3},{3,2},{4,5},{5,4},{6,7},{7,6},{8,9},{9,8},{10,11... | collective-permute-start | bytes 1179656 | tf_op jit(solution)/shard_map/ppermute | solution.py:1509
  22.3 4.5 %collective-permute-start.3 = (bf16[256,768]{1,0:T(8,128)(2,1)S(1)}, bf16[256,768]{1,0:T(8,128)(2,1)S(1)}, u32[]{:S(2)}, u32[]{:S(2)}) collective-permute-start(bf16[256,768]{1,0:T(8,128)(2,1)S(1)} %collective-permute-done.refs_1_), channel_id=1, source_target_pairs={{0,1},{1,0},{2,3},{3,2},{4,5},{5,4},{6,7},{7,6},{8,9},{9,8},{10,11... | collective-permute-start | bytes 1179656 | tf_op jit(solution)/shard_map/ppermute | solution.py:1509
  24.8 13.4 %collective-permute-start.5 = (bf16[256,768]{1,0:T(8,128)(2,1)S(1)}, bf16[256,768]{1,0:T(8,128)(2,1)S(1)}, u32[]{:S(2)}, u32[]{:S(2)}) collective-permute-start(bf16[256,768]{1,0:T(8,128)(2,1)S(1)} %collective-permute-done.1.refs_2_), channel_id=1, source_target_pairs={{2,0},{3,1},{4,2},{5,3},{10,8},{11,9},{12,10},{13,11},{18,16},{19,... | collective-permute-start | bytes 1179656 | tf_op jit(solution)/shard_map/ppermute | solution.py:1688
  26.1 12.1 %collective-permute-start.6 = (bf16[256,768]{1,0:T(8,128)(2,1)S(1)}, bf16[256,768]{1,0:T(8,128)(2,1)S(1)}, u32[]{:S(2)}, u32[]{:S(2)}) collective-permute-start(bf16[256,768]{1,0:T(8,128)(2,1)S(1)} %collective-permute-done.refs_1_), channel_id=1, source_target_pairs={{2,4},{3,5},{4,6},{5,7},{10,12},{11,13},{12,14},{13,15},{18,20},{1... | collective-permute-start | bytes 1179656 | tf_op jit(solution)/shard_map/ppermute | solution.py:1688
  49.5 9.3 %collective-permute-start.10 = (bf16[192,256]{1,0:T(8,128)(2,1)S(1)}, bf16[192,256]{1,0:T(8,128)(2,1)S(1)}, u32[]{:S(2)}, u32[]{:S(2)}) collective-permute-start(bf16[192,256]{1,0:T(8,128)(2,1)S(1)} %get-tuple-element.191), channel_id=1, source_target_pairs={{0,2},{1,3},{2,4},{3,5},{4,6},{5,7},{6,0},{7,1},{8,10},{9,11},{10,... | collective-permute-start | bytes 294920 | tf_op jit(solution)/shard_map/ppermute | solution.py:1505
  51.3 7.4 %collective-permute-start.8 = (bf16[192,256]{1,0:T(8,128)(2,1)S(1)}, bf16[192,256]{1,0:T(8,128)(2,1)S(1)}, u32[]{:S(2)}, u32[]{:S(2)}) collective-permute-start(bf16[192,256]{1,0:T(8,128)(2,1)S(1)} %get-tuple-element.189), channel_id=1, source_target_pairs={{0,6},{1,7},{2,0},{3,1},{4,2},{5,3},{6,4},{7,5},{8,14},{9,15},{10,... | collective-permute-start | bytes 294920 | tf_op jit(solution)/shard_map/ppermute | solution.py:1505
  53.4 8.1 %collective-permute-start.9 = (bf16[192,256]{1,0:T(8,128)(2,1)S(1)}, bf16[192,256]{1,0:T(8,128)(2,1)S(1)}, u32[]{:S(2)}, u32[]{:S(2)}) collective-permute-start(bf16[192,256]{1,0:T(8,128)(2,1)S(1)} %get-tuple-element.190), channel_id=1, source_target_pairs={{0,4},{1,5},{2,6},{3,7},{4,0},{5,1},{6,2},{7,3},{8,12},{9,13},{10,... | collective-permute-start | bytes 294920 | tf_op jit(solution)/shard_map/ppermute | solution.py:1505
  81.2 8.8 %collective-permute-start.19 = (bf16[16,120,768]{2,1,0:T(8,128)(2,1)S(1)}, bf16[16,120,768]{2,1,0:T(8,128)(2,1)S(1)}, u32[]{:S(2)}, u32[]{:S(2)}) collective-permute-start(bf16[16,120,768]{2,1,0:T(8,128)(2,1)S(1)} %get-tuple-element.240), channel_id=1, source_target_pairs={{0,1},{1,0},{2,3},{3,2},{4,5},{5,4},{6,7},{7,6},{8,9},{9,8},{10,11... | collective-permute-start | bytes 8847368 | tf_op jit(solution)/shard_map/ppermute | solution.py:1509
  84.1 5.9 %collective-permute-start.18 = (bf16[16,96,768]{2,1,0:T(8,128)(2,1)S(1)}, bf16[16,96,768]{2,1,0:T(8,128)(2,1)S(1)}, u32[]{:S(2)}, u32[]{:S(2)}) collective-permute-start(bf16[16,96,768]{2,1,0:T(8,128)(2,1)S(1)} %get-tuple-element.238), channel_id=1, source_target_pairs={{0,1},{1,0},{2,3},{3,2},{4,5},{5,4},{6,7},{7,6},{8,9},{9,8},{10,11... | collective-permute-start | bytes 7077896 | tf_op jit(solution)/shard_map/ppermute | solution.py:1509
  84.6 9.2 %collective-permute-start.11 = (bf16[192,256]{1,0:T(8,128)(2,1)S(1)}, bf16[192,256]{1,0:T(8,128)(2,1)S(1)}, u32[]{:S(2)}, u32[]{:S(2)}) collective-permute-start(bf16[192,256]{1,0:T(8,128)(2,1)S(1)} %get-tuple-element.226), channel_id=1, source_target_pairs={{0,2},{1,3},{2,4},{3,5},{4,6},{5,7},{6,0},{7,1},{8,10},{9,11},{10,... | collective-permute-start | bytes 294920 | tf_op jit(solution)/shard_map/ppermute | solution.py:1505
  84.6 9.2 %collective-permute-start.12 = (bf16[192,256]{1,0:T(8,128)(2,1)S(1)}, bf16[192,256]{1,0:T(8,128)(2,1)S(1)}, u32[]{:S(2)}, u32[]{:S(2)}) collective-permute-start(bf16[192,256]{1,0:T(8,128)(2,1)S(1)} %get-tuple-element.227), channel_id=1, source_target_pairs={{0,6},{1,7},{2,0},{3,1},{4,2},{5,3},{6,4},{7,5},{8,14},{9,15},{10,... | collective-permute-start | bytes 294920 | tf_op jit(solution)/shard_map/ppermute | solution.py:1505
  88.5 8.3 %collective-permute-start.13 = (bf16[192,256]{1,0:T(8,128)(2,1)S(1)}, bf16[192,256]{1,0:T(8,128)(2,1)S(1)}, u32[]{:S(2)}, u32[]{:S(2)}) collective-permute-start(bf16[192,256]{1,0:T(8,128)(2,1)S(1)} %get-tuple-element.228), channel_id=1, source_target_pairs={{0,4},{1,5},{2,6},{3,7},{4,0},{5,1},{6,2},{7,3},{8,12},{9,13},{10,... | collective-permute-start | bytes 294920 | tf_op jit(solution)/shard_map/ppermute | solution.py:1505
  91.2 31.2 %collective-permute-start.20 = (bf16[2,2,216,768]{3,2,1,0:T(8,128)(2,1)S(1)}, bf16[2,2,216,768]{3,2,1,0:T(8,128)(2,1)S(1)}, u32[]{:S(2)}, u32[]{:S(2)}) collective-permute-start(bf16[2,2,216,768]{3,2,1,0:T(8,128)(2,1)S(1)} %get-tuple-element.241), channel_id=1, source_target_pairs={{0,8},{8,0},{16,24},{24,16},{1,9},{9,1},{17,25},{25,17},{2,10},{10... | collective-permute-start | bytes 3981320 | tf_op jit(solution)/shard_map/ppermute | solution.py:1513
  91.8 31.2 %collective-permute-start.21 = (bf16[2,2,216,768]{3,2,1,0:T(8,128)(2,1)S(1)}, bf16[2,2,216,768]{3,2,1,0:T(8,128)(2,1)S(1)}, u32[]{:S(2)}, u32[]{:S(2)}) collective-permute-start(bf16[2,2,216,768]{3,2,1,0:T(8,128)(2,1)S(1)} %get-tuple-element.242), channel_id=1, source_target_pairs={{0,16},{8,24},{16,0},{24,8},{1,17},{9,25},{17,1},{25,9},{2,18},{10... | collective-permute-start | bytes 3981320 | tf_op jit(solution)/shard_map/ppermute | solution.py:1513
  110.7 15.7 %collective-permute-start.15 = (bf16[576,256]{1,0:T(8,128)(2,1)S(1)}, bf16[576,256]{1,0:T(8,128)(2,1)S(1)}, u32[]{:S(2)}, u32[]{:S(2)}) collective-permute-start(bf16[576,256]{1,0:T(8,128)(2,1)S(1)} %get-tuple-element.250.refs_5_), channel_id=1, source_target_pairs={{0,6},{1,7},{2,0},{3,1},{4,2},{5,3},{6,4},{7,5},{8,14},{9,15},{10,... | collective-permute-start | bytes 884744 | tf_op jit(solution)/shard_map/ppermute | solution.py:1505
  112.4 24.9 %collective-permute-start.16 = (bf16[576,256]{1,0:T(8,128)(2,1)S(1)}, bf16[576,256]{1,0:T(8,128)(2,1)S(1)}, u32[]{:S(2)}, u32[]{:S(2)}) collective-permute-start(bf16[576,256]{1,0:T(8,128)(2,1)S(1)} %get-tuple-element.252.refs_7_), channel_id=1, source_target_pairs={{0,4},{1,5},{2,6},{3,7},{4,0},{5,1},{6,2},{7,3},{8,12},{9,13},{10,... | collective-permute-start | bytes 884744 | tf_op jit(solution)/shard_map/ppermute | solution.py:1505
  112.4 24.9 %collective-permute-start.17 = (bf16[576,256]{1,0:T(8,128)(2,1)S(1)}, bf16[576,256]{1,0:T(8,128)(2,1)S(1)}, u32[]{:S(2)}, u32[]{:S(2)}) collective-permute-start(bf16[576,256]{1,0:T(8,128)(2,1)S(1)} %get-tuple-element.251.refs_6_), channel_id=1, source_target_pairs={{0,2},{1,3},{2,4},{3,5},{4,6},{5,7},{6,0},{7,1},{8,10},{9,11},{10,... | collective-permute-start | bytes 884744 | tf_op jit(solution)/shard_map/ppermute | solution.py:1505
  124.2 16.2 %collective-permute-start.22 = (bf16[2,216,768]{2,1,0:T(8,128)(2,1)S(1)}, bf16[2,216,768]{2,1,0:T(8,128)(2,1)S(1)}, u32[]{:S(2)}, u32[]{:S(2)}) collective-permute-start(bf16[2,216,768]{2,1,0:T(8,128)(2,1)S(1)} %get-tuple-element.272), channel_id=1, source_target_pairs={{0,16},{8,24},{16,0},{24,8},{1,17},{9,25},{17,1},{25,9},{2,18},{10... | collective-permute-start | bytes 1990664 | tf_op jit(solution)/shard_map/ppermute | solution.py:1513
  126.0 15.5 %collective-permute-start.23 = (bf16[2,216,768]{2,1,0:T(8,128)(2,1)S(1)}, bf16[2,216,768]{2,1,0:T(8,128)(2,1)S(1)}, u32[]{:S(2)}, u32[]{:S(2)}) collective-permute-start(bf16[2,216,768]{2,1,0:T(8,128)(2,1)S(1)} %get-tuple-element.274), channel_id=1, source_target_pairs={{0,8},{8,0},{16,24},{24,16},{1,9},{9,1},{17,25},{25,17},{2,10},{10... | collective-permute-start | bytes 1990664 | tf_op jit(solution)/shard_map/ppermute | solution.py:1513
  137.4 9.3 %collective-permute-start.27 = (bf16[16,24,768]{2,1,0:T(8,128)(2,1)S(1)}, bf16[16,24,768]{2,1,0:T(8,128)(2,1)S(1)}, u32[]{:S(2)}, u32[]{:S(2)}) collective-permute-start(bf16[16,24,768]{2,1,0:T(8,128)(2,1)S(1)} %get-tuple-element.283), channel_id=1, source_target_pairs={{0,1},{1,0},{2,3},{3,2},{4,5},{5,4},{6,7},{7,6},{8,9},{9,8},{10,11... | collective-permute-start | bytes 1769480 | tf_op jit(solution)/shard_map/ppermute | solution.py:1509
  142.8 19.7 %collective-permute-start.24 = (bf16[216,768]{1,0:T(8,128)(2,1)S(1)}, bf16[216,768]{1,0:T(8,128)(2,1)S(1)}, u32[]{:S(2)}, u32[]{:S(2)}) collective-permute-start(bf16[216,768]{1,0:T(8,128)(2,1)S(1)} %get-tuple-element.276), channel_id=1, source_target_pairs={{0,2},{1,3},{2,4},{3,5},{4,6},{5,7},{6,0},{7,1},{8,10},{9,11},{10,... | collective-permute-start | bytes 995336 | tf_op jit(solution)/shard_map/ppermute | solution.py:1505
  142.9 25.6 %collective-permute-start.25 = (bf16[216,768]{1,0:T(8,128)(2,1)S(1)}, bf16[216,768]{1,0:T(8,128)(2,1)S(1)}, u32[]{:S(2)}, u32[]{:S(2)}) collective-permute-start(bf16[216,768]{1,0:T(8,128)(2,1)S(1)} %get-tuple-element.277), channel_id=1, source_target_pairs={{0,4},{1,5},{2,6},{3,7},{4,0},{5,1},{6,2},{7,3},{8,12},{9,13},{10,... | collective-permute-start | bytes 995336 | tf_op jit(solution)/shard_map/ppermute | solution.py:1505
  145.6 23.0 %collective-permute-start.26 = (bf16[216,768]{1,0:T(8,128)(2,1)S(1)}, bf16[216,768]{1,0:T(8,128)(2,1)S(1)}, u32[]{:S(2)}, u32[]{:S(2)}) collective-permute-start(bf16[216,768]{1,0:T(8,128)(2,1)S(1)} %get-tuple-element.278), channel_id=1, source_target_pairs={{0,6},{1,7},{2,0},{3,1},{4,2},{5,3},{6,4},{7,5},{8,14},{9,15},{10,... | collective-permute-start | bytes 995336 | tf_op jit(solution)/shard_map/ppermute | solution.py:1505
  147.3 5.2 %collective-permute-start.28 = (bf16[2,2,24,768]{3,2,1,0:T(8,128)(2,1)S(1)}, bf16[2,2,24,768]{3,2,1,0:T(8,128)(2,1)S(1)}, u32[]{:S(2)}, u32[]{:S(2)}) collective-permute-start(bf16[2,2,24,768]{3,2,1,0:T(8,128)(2,1)S(1)} %get-tuple-element.286), channel_id=1, source_target_pairs={{0,8},{8,0},{16,24},{24,16},{1,9},{9,1},{17,25},{25,17},{2,10},{10... | collective-permute-start | bytes 442376 | tf_op jit(solution)/shard_map/ppermute | solution.py:1513
  148.0 5.1 %collective-permute-start.29 = (bf16[2,2,24,768]{3,2,1,0:T(8,128)(2,1)S(1)}, bf16[2,2,24,768]{3,2,1,0:T(8,128)(2,1)S(1)}, u32[]{:S(2)}, u32[]{:S(2)}) collective-permute-start(bf16[2,2,24,768]{3,2,1,0:T(8,128)(2,1)S(1)} %get-tuple-element.287), channel_id=1, source_target_pairs={{0,16},{8,24},{16,0},{24,8},{1,17},{9,25},{17,1},{25,9},{2,18},{10... | collective-permute-start | bytes 442376 | tf_op jit(solution)/shard_map/ppermute | solution.py:1513
  153.8 4.4 %collective-permute-start.30 = (bf16[2,24,768]{2,1,0:T(8,128)(2,1)S(1)}, bf16[2,24,768]{2,1,0:T(8,128)(2,1)S(1)}, u32[]{:S(2)}, u32[]{:S(2)}) collective-permute-start(bf16[2,24,768]{2,1,0:T(8,128)(2,1)S(1)} %get-tuple-element.289), channel_id=1, source_target_pairs={{0,16},{8,24},{16,0},{24,8},{1,17},{9,25},{17,1},{25,9},{2,18},{10... | collective-permute-start | bytes 221192 | tf_op jit(solution)/shard_map/ppermute | solution.py:1513
  154.6 4.4 %collective-permute-start.31 = (bf16[2,24,768]{2,1,0:T(8,128)(2,1)S(1)}, bf16[2,24,768]{2,1,0:T(8,128)(2,1)S(1)}, u32[]{:S(2)}, u32[]{:S(2)}) collective-permute-start(bf16[2,24,768]{2,1,0:T(8,128)(2,1)S(1)} %get-tuple-element.291), channel_id=1, source_target_pairs={{0,8},{8,0},{16,24},{24,16},{1,9},{9,1},{17,25},{25,17},{2,10},{10... | collective-permute-start | bytes 221192 | tf_op jit(solution)/shard_map/ppermute | solution.py:1513
  159.6 10.4 %collective-permute-start.32 = (bf16[24,768]{1,0:T(8,128)(2,1)S(1)}, bf16[24,768]{1,0:T(8,128)(2,1)S(1)}, u32[]{:S(2)}, u32[]{:S(2)}) collective-permute-start(bf16[24,768]{1,0:T(8,128)(2,1)S(1)} %get-tuple-element.293), channel_id=1, source_target_pairs={{0,2},{1,3},{2,4},{3,5},{4,6},{5,7},{6,0},{7,1},{8,10},{9,11},{10,... | collective-permute-start | bytes 110600 | tf_op jit(solution)/shard_map/ppermute | solution.py:1505
  161.7 14.3 %collective-permute-start.33 = (bf16[24,768]{1,0:T(8,128)(2,1)S(1)}, bf16[24,768]{1,0:T(8,128)(2,1)S(1)}, u32[]{:S(2)}, u32[]{:S(2)}) collective-permute-start(bf16[24,768]{1,0:T(8,128)(2,1)S(1)} %get-tuple-element.294), channel_id=1, source_target_pairs={{0,4},{1,5},{2,6},{3,7},{4,0},{5,1},{6,2},{7,3},{8,12},{9,13},{10,... | collective-permute-start | bytes 110600 | tf_op jit(solution)/shard_map/ppermute | solution.py:1505
  162.5 13.5 %collective-permute-start.34 = (bf16[24,768]{1,0:T(8,128)(2,1)S(1)}, bf16[24,768]{1,0:T(8,128)(2,1)S(1)}, u32[]{:S(2)}, u32[]{:S(2)}) collective-permute-start(bf16[24,768]{1,0:T(8,128)(2,1)S(1)} %get-tuple-element.295), channel_id=1, source_target_pairs={{0,6},{1,7},{2,0},{3,1},{4,2},{5,3},{6,4},{7,5},{8,14},{9,15},{10,... | collective-permute-start | bytes 110600 | tf_op jit(solution)/shard_map/ppermute | solution.py:1505
  (18 other events, 169.5 us)
